TPU v7x, 32 devices: a whole 2x2x4 slice. The times are simulated.
32 devices in a mesh: req: 8 (over z, x), mlp: 4 (over y, core).
Axes of the slice: x: 2, y: 2, z: 4, core: 2. Of those that a mesh axis runs over, the one named last changes fastest.
Arguments:
- hidden_in: bfloat16 [256, 24, 2048], P('mlp', 'req'), may hold values from -6 to 6
- input_gain: float32 [2048], replicated, may hold values from 0.1 to 1.9
- query_weight: bfloat16 [2048, 2048], P(None, 'mlp'), may hold values from -0.125 to 0.125
- keyval_weight: bfloat16 [2048, 1024], P(None, 'mlp'), may hold values from -0.125 to 0.125
- query_gain: float32 [256], replicated, may hold values from 0.5 to 40
- key_gain: float32 [256], replicated, may hold values from 0.1 to 1.9
- out_weight: bfloat16 [2048, 2048], P('mlp'), may hold values from -0.125 to 0.125
- attn_gain: float32 [2048], replicated, may hold values from 0.1 to 1.9
- laurel_left: bfloat16 [2048, 64], replicated, may hold values from -0.125 to 0.125
- laurel_right: bfloat16 [64, 2048], replicated, may hold values from -0.75 to 0.75
- laurel_gain: float32 [2048], replicated, may hold values from 0.1 to 1.9
- ffn_gain: float32 [2048], replicated, may hold values from 0.1 to 1.9
- post_gain: float32 [2048], replicated, may hold values from 0.1 to 1.9
- gate_projection_matrix: bfloat16 [2048, 4096], P(None, 'mlp'), may hold values from -0.125 to 0.125
- up_projection_matrix: bfloat16 [2048, 4096], P(None, 'mlp'), may hold values from -0.125 to 0.125
- down_projection_matrix: bfloat16 [4096, 2048], P('mlp'), may hold values from -0.09375 to 0.09375
- page_pool: bfloat16 [16, 128, 1024], P('req'), may hold values from -6 to 6
- page_owner: int32 [2, 8], replicated, may hold values from 0 to 7, as said below
- page_slot: int32 [2, 8], replicated, may hold values from 0 to 1
- request_group: int32 [24], P('req'), may hold values from 0 to 1, as said below
- suffix_len: int32 [24], P('req'), may hold values from 64 to 256
Outputs:
- hidden_out: bfloat16 [256, 24, 2048], P('mlp', 'req')
- new_pages: bfloat16 [256, 24, 1024], P(None, 'req', 'mlp')
Inputs may be any that keep to these rules, and one draw needn't show every extreme that they name: `request_group`: each group has exactly 12 requests. The pairs (page_owner, page_slot) name every page of the pool exactly once.
All inputs are finite; a program needn't handle non-finite values.
Results may differ from a plain program's by a relative error of at most 0.013.
The roundings to bfloat16 on the way count: a program that leaves them out, or rounds other values in their place, can miss the bound.
Values may be sent and summed in bfloat16 or wider, within the bound.
No kernel may reach another device: no remote copies, remote signals or barrier semaphores. Data moves between devices by JAX's collectives and lax.ppermute only.
A program may use at most 128 MiB of HBM per device.

v0:
```python
import math

import jax
import jax.numpy as jnp
from jax import lax
from jax.sharding import PartitionSpec as P

PAGE = 128
PREFIX_PAGES = 8


EPS = 1e-06
INV_ROOT = 1.0 / math.sqrt(2.0)


def from_partner(value, axis, apart):
    return lax.ppermute(value, axis, [(i, i ^ 1 << apart) for i in range(lax.axis_size(axis))])


def rms_norm(values, norm_gain):
    values = values.astype(jnp.float32)
    return values * lax.rsqrt(jnp.mean(values * values, axis=-1, keepdims=True) + EPS) * norm_gain


def rotary(values, first_row):
    row_count = values.shape[0]
    halfway = values.shape[-1] // 2
    frequency = 1000000.0 ** (-jnp.arange(halfway, dtype=jnp.float32) / halfway)
    positions = (first_row + jnp.arange(row_count)).astype(jnp.float32)
    angles = positions[:, None] * frequency[None, :]
    cos_table = jnp.cos(angles)[:, None, None, :]
    sin_table = jnp.sin(angles)[:, None, None, :]
    first_half = values[..., :halfway]
    second_half = values[..., halfway:]
    return jnp.concatenate(
        [
            first_half * cos_table - second_half * sin_table,
            second_half * cos_table + first_half * sin_table,
        ],
        axis=-1,
    )


def local(
    hidden_in,
    input_gain,
    query_weight,
    keyval_weight,
    query_gain,
    key_gain,
    out_weight,
    attn_gain,
    laurel_left,
    laurel_right,
    laurel_gain,
    ffn_gain,
    post_gain,
    gate_projection_matrix,
    up_projection_matrix,
    down_projection_matrix,
    page_pool,
    page_owner,
    page_slot,
    request_group,
    suffix_len,
):
    mlp_index = lax.axis_index("mlp")
    part_rows = hidden_in.shape[0]
    local_reqs = hidden_in.shape[1]
    head_size = query_gain.shape[0]
    prefix_len = PREFIX_PAGES * PAGE
    parity = mlp_index % 2
    kv_head = mlp_index // 2
    query_cols = query_weight.shape[1]
    heads_here = query_cols // head_size
    active_rows = rms_norm(hidden_in, input_gain).astype(jnp.bfloat16)
    active_part = lax.all_gather(active_rows, "mlp", axis=0, tiled=True)
    first_row = jnp.int32(0)
    row_count = active_part.shape[0]
    project_queries = jnp.einsum(
        "trd,dc->trc", active_part, query_weight, preferred_element_type=jnp.float32
    )
    project_queries = project_queries.reshape(row_count, local_reqs, heads_here, head_size)
    project_queries = rotary(rms_norm(project_queries, query_gain), prefix_len + first_row)
    quarter = jnp.einsum(
        "trd,dc->trc", active_part, keyval_weight, preferred_element_type=jnp.float32
    )
    quarter = quarter.reshape(row_count, local_reqs, 1, head_size)
    as_keys = rotary(rms_norm(quarter, key_gain), prefix_len + first_row)
    as_values = rms_norm(quarter, 1.0)
    quarter = jnp.where(parity == 0, as_keys, as_values)
    joined = jnp.concatenate(
        [
            project_queries.reshape(row_count, local_reqs, query_cols),
            quarter.reshape(row_count, local_reqs, head_size),
        ],
        axis=-1,
    )
    projected = joined.astype(jnp.bfloat16)
    full_rows = projected.shape[0]
    queries = projected[..., :query_cols]
    quarter = projected[..., query_cols:]
    partner = from_partner(quarter, "mlp", 0)
    all_keys = jnp.where(parity == 0, quarter, partner)
    all_values = jnp.where(parity == 0, partner, quarter)
    live_full = jnp.arange(full_rows)[:, None] < suffix_len[None, :]
    new_pages = jnp.where(live_full[:, :, None], quarter, jnp.zeros_like(quarter))
    own_pages = lax.dynamic_slice_in_dim(page_pool, kv_head * 2 * head_size, 2 * head_size, 2)
    pool_pages = page_pool.shape[0]
    whole_pool = lax.all_gather(own_pages, "req", axis=0, tiled=True)
    page_ids = page_owner * pool_pages + page_slot
    group_count = page_ids.shape[0]
    selector = (request_group[:, None] == jnp.arange(group_count, dtype=jnp.int32)[None, :]).astype(
        jnp.int32
    )
    wanted = jnp.dot(selector, page_ids)
    prefix_kv = jnp.take(whole_pool, wanted.reshape(-1), axis=0).reshape(
        local_reqs, prefix_len, 2 * head_size
    )
    causal = jnp.arange(full_rows)[None, :] <= jnp.arange(full_rows)[:, None]
    score_scale = head_size ** (-0.5)

    def attend(req_index):
        query_rows = lax.dynamic_index_in_dim(queries, req_index, 1, keepdims=False).reshape(
            full_rows, heads_here, head_size
        )
        prefix_rows = lax.dynamic_index_in_dim(prefix_kv, req_index, 0, keepdims=False)
        keys_here = jnp.concatenate(
            [
                prefix_rows[:, :head_size],
                lax.dynamic_index_in_dim(all_keys, req_index, 1, keepdims=False),
            ],
            axis=0,
        )
        values_here = jnp.concatenate(
            [
                prefix_rows[:, head_size:],
                lax.dynamic_index_in_dim(all_values, req_index, 1, keepdims=False),
            ],
            axis=0,
        )
        live_count = lax.dynamic_index_in_dim(suffix_len, req_index, 0, keepdims=False)
        suffix_ok = causal & (jnp.arange(full_rows)[None, :] < live_count)
        allowed = jnp.concatenate(
            [jnp.ones((full_rows, prefix_len), dtype=bool), suffix_ok], axis=1
        )
        scores = (
            jnp.einsum("thd,sd->hts", query_rows, keys_here, preferred_element_type=jnp.float32)
            * score_scale
        )
        scores = jnp.where(allowed[None], scores, -jnp.inf)
        row_peak = jnp.max(scores, axis=-1, keepdims=True)
        exp_terms = jnp.exp(scores - row_peak)
        totals = jnp.sum(exp_terms, axis=-1)
        weights = exp_terms.astype(jnp.bfloat16)
        mixed_rows = jnp.einsum(
            "hts,sd->thd", weights, values_here, preferred_element_type=jnp.float32
        )
        mixed_rows = mixed_rows / jnp.transpose(totals)[:, :, None]
        return mixed_rows.reshape(full_rows, query_cols).astype(jnp.bfloat16)

    attended = lax.map(attend, jnp.arange(local_reqs))
    local_row_block = attended
    attn_summed = lax.psum_scatter(
        jnp.einsum(
            "rtc,cd->trd", local_row_block, out_weight, preferred_element_type=jnp.float32
        ).astype(jnp.bfloat16),
        "mlp",
        scatter_dimension=0,
        tiled=True,
    ).astype(jnp.float32)
    laurel_mid = jnp.einsum(
        "trd,dk->trk", active_rows, laurel_left, preferred_element_type=jnp.float32
    ).astype(jnp.bfloat16)
    laurel_out = active_rows.astype(jnp.float32) + rms_norm(
        jnp.einsum("trk,kd->trd", laurel_mid, laurel_right, preferred_element_type=jnp.float32),
        laurel_gain,
    )
    residual = (
        hidden_in.astype(jnp.float32) + rms_norm(attn_summed, attn_gain) + laurel_out
    ) * INV_ROOT
    ffn_in = rms_norm(residual, ffn_gain).astype(jnp.bfloat16)
    incoming_rows = lax.all_gather(ffn_in, "mlp", axis=0, tiled=True)
    gate_portion = jnp.einsum(
        "ghc,cu->ghu", incoming_rows, gate_projection_matrix, preferred_element_type=jnp.float32
    )
    up_portion = jnp.einsum(
        "ghc,cu->ghu", incoming_rows, up_projection_matrix, preferred_element_type=jnp.float32
    )
    expanded = (jax.nn.gelu(gate_portion, approximate=True) * up_portion).astype(jnp.bfloat16)
    local_row_block = expanded
    ffn_summed = lax.psum_scatter(
        jnp.einsum(
            "wjk,kx->wjx",
            local_row_block,
            down_projection_matrix,
            preferred_element_type=jnp.float32,
        ).astype(jnp.bfloat16),
        "mlp",
        scatter_dimension=0,
        tiled=True,
    ).astype(jnp.float32)
    own_positions = mlp_index * part_rows + jnp.arange(part_rows)
    live_part = own_positions[:, None] < suffix_len[None, :]
    output = residual + rms_norm(ffn_summed, post_gain)
    hidden_out = jnp.where(live_part[:, :, None], output, 0.0).astype(jnp.bfloat16)
    return (hidden_out, new_pages)


def solution(mesh):
    placed = (
        P("mlp", "req", None),
        P(),
        P(None, "mlp"),
        P(None, "mlp"),
        P(),
        P(),
        P("mlp", None),
        P(),
        P(),
        P(),
        P(),
        P(),
        P(),
        P(None, "mlp"),
        P(None, "mlp"),
        P("mlp", None),
        P("req", None, None),
        P(),
        P(),
        P("req"),
        P("req"),
    )
    return jax.shard_map(
        local,
        mesh=mesh,
        in_specs=placed,
        out_specs=(P("mlp", "req", None), P(None, "req", "mlp")),
        check_vma=False,
    )
```

profile of v0, /device:TPU:0, one launch (start us, length us, event | category | flops | bytes accessed | tf_op | source)
XLA Modules:
  0.0 296.1 jit_solution(11078036066806763758)
XLA Ops:
  7.3 1.8 constant_dynamic-slice_fusion.3
  9.2 1.4 fusion.56
  10.6 1.8 fusion.58
  13.0 0.6 iota_compare_fusion.2
  13.6 0.5 multiply_cosine_fusion
  14.2 48.7 %all-gather.4.cloned.1.call-done = bf16[16,128,512]{2,1,0:T(8,128)(2,1)} async-done(((bf16[2,128,512]{2,1,0:T(8,128)(2,1)}), bf16[16,128,512]{2,1,0:T(8,128)(2,1)}) %all-gather.4.cloned.1.call-update) | async-done | bytes 2097168 | tf_op jit(solution)/shard_map/all_gather | solution.py:110
  62.9 4.1 %gather_fusion = bf16[24,128,512]{2,1,0:T(8,128)(2,1)} fusion(bf16[16,128,512]{2,1,0:T(8,128)(2,1)} %all-gather.4.cloned.1.call-done, s32[1024]{0:T(1024)S(1)} %pad_clamp_fusion), kind=kCustom, calls=%fused_computation | custom fusion | bytes 6291552 | tf_op jit(solution)/shard_map/jit(_take)/gather | solution.py:117
  67.0 3.4 %bitcast_select_fusion = bf16[3,1024,512]{2,1,0:T(8,128)(2,1)} fusion(pred[3,1024]{1,0:T(4,128)(4,1)S(1)} %bitcast.122, bf16[3,1024,512]{2,1,0:T(8,128)(2,1)} %bitcast.115), kind=kLoop, calls=%fused_computation.47 | loop fusion | flops 1572864 | bytes 6294528 | tf_op jit(solution)/shard_map/jit(_take)/select_n | solution.py:117
  70.4 21.1 %all-gather.6.cloned.1.call-done = bf16[256,3,2048]{2,0,1:T(8,128)(2,1)} async-done(((bf16[64,3,2048]{2,0,1:T(8,128)(2,1)}), bf16[256,3,2048]{2,0,1:T(8,128)(2,1)}) %all-gather.6.cloned.1.call-update) | async-done | bytes 3145744 | tf_op jit(solution)/shard_map/all_gather | solution.py:77
  91.5 5.5 %fusion.45 = f32[256,3,512]{2,0,1:T(8,128)} fusion(bf16[256,3,2048]{2,0,1:T(8,128)(2,1)} %all-gather.6.cloned.1.call-done, bf16[2048,512]{1,0:T(8,128)(2,1)} %param.25), kind=kOutput, calls=%fused_computation.53 | convolution fusion | flops 1610612736 | bytes 6815744 | tf_op jit(solution)/shard_map/trd,dc->trc/dot_general | solution.py:80
  97.0 3.1 %reshape.241 = f32[256,3,2,256]{3,2,0,1:T(2,128)} reshape(f32[256,3,512]{2,0,1:T(8,128)} %fusion.45) | data formatting | bytes 3145728 | tf_op jit(solution)/shard_map/reshape | solution.py:83
  100.1 2.3 multiply_reduce_fusion.2
  102.4 3.6 %copy.57 = f32[256,3,2,256]{0,3,2,1:T(8,128)} copy(f32[256,3,2,256]{3,2,0,1:T(2,128)} %reshape.241) | data formatting | bytes 3145728 | tf_op jit(solution)/shard_map/reshape | solution.py:83
  106.1 4.2 %multiply_reduce_fusion.3 = (f32[256,3]{0,1:T(4,128)S(1)}, f32[256,3,256]{0,2,1:T(8,128)}) fusion(bf16[256,3,2048]{2,0,1:T(8,128)(2,1)} %all-gather.6.cloned.1.call-done, bf16[2048,256]{1,0:T(8,128)(2,1)} %param.26), kind=kOutput, calls=%fused_computation.85 | convolution fusion | flops 805698816 | bytes 4983808 | tf_op jit(solution)/shard_map/trd,dc->trc/dot_general | solution.py:85
  110.4 1.3 multiply_bitcast_fusion
  111.9 1.6 broadcast_select_fusion
  114.3 1.0 pad_maximum_fusion
  115.3 0.9 broadcast_select_fusion.1
  116.2 32.3 %while.11 = (s32[]{:T(128)}, bf16[3,256,512]{1,2,0:T(8,128)(2,1)}, s32[3]{0:T(128)S(1)}, bf16[3,1024,512]{2,1,0:T(8,128)(2,1)}, bf16[256,3,256]{0,2,1:T(8,128)(2...) while((s32[]{:T(128)}, bf16[3,256,512]{1,2,0:T(8,128)(2,1)}, ...), condition=%wide.region_6.7_spmd.clone, body=%wide.region_3.6_spmd.clone.sunk | while | flops 678690048 | bytes 18361092 | solution.py:162
  116.2 0.6 dynamic_slice.46
  118.5 0.6 dynamic_slice.47
  119.1 0.6 iota_compare_fusion.6
  119.8 1.7 constant_dynamic-slice_fusion.6
  121.5 1.0 constant_dynamic-slice_fusion.7
  122.5 0.7 copy.76
  123.3 1.3 dynamic-slice_bitcast_fusion.2
  125.7 0.6 fusion.109
  126.2 0.7 constant_dynamic-update-slice_fusion.2
  127.0 0.6 dynamic_slice.46
  129.2 0.6 dynamic_slice.47
  129.8 0.6 iota_compare_fusion.6
  130.6 1.7 constant_dynamic-slice_fusion.6
  132.3 1.0 constant_dynamic-slice_fusion.7
  133.2 0.7 copy.76
  134.1 1.3 dynamic-slice_bitcast_fusion.2
  135.6 0.5 fusion.107
  136.4 0.6 fusion.109
  137.0 0.7 constant_dynamic-update-slice_fusion.2
  137.7 0.6 dynamic_slice.46
  140.0 0.6 dynamic_slice.47
  140.6 0.6 iota_compare_fusion.6
  141.3 1.7 constant_dynamic-slice_fusion.6
  143.0 1.0 constant_dynamic-slice_fusion.7
  144.0 0.7 copy.76
  144.9 1.3 dynamic-slice_bitcast_fusion.2
  146.3 0.5 fusion.107
  147.2 0.6 fusion.109
  147.8 0.7 constant_dynamic-update-slice_fusion.2
  148.5 4.6 %fusion.43 = bf16[256,3,2048]{2,0,1:T(8,128)(2,1)} fusion(bf16[3,256,512]{1,2,0:T(8,128)(2,1)} %get-tuple-element.49, bf16[512,2048]{1,0:T(8,128)(2,1)S(1)} %copy-done), kind=kOutput, calls=%fused_computation.48 | convolution fusion | flops 1612185600 | bytes 6029312 | tf_op jit(solution)/shard_map/rtc,cd->trd/dot_general | solution.py:165
  153.4 0.7 copy-done.8
  154.1 2.2 multiply_reduce_fusion.1
  156.4 34.8 %reduce-scatter.3.cloned.1.call-done = bf16[64,3,2048]{2,0,1:T(8,128)(2,1)} async-done(((bf16[256,3,2048]{2,0,1:T(8,128)(2,1)}), bf16[64,3,2048]{2,0,1:T(8,128)(2,1)}) %reduce-scatter.3.cloned.1.call-update) | async-done | bytes 786448 | tf_op jit(solution)/shard_map/reduce_scatter | solution.py:164
  191.2 1.4 fusion.49
  192.6 2.5 multiply_reduce_fusion
  195.1 1.1 copy-done.1
  196.3 1.1 multiply_convert_fusion
  197.4 28.6 %all-gather.8.cloned.1.call-done = bf16[256,3,2048]{2,0,1:T(8,128)(2,1)} async-done(((bf16[64,3,2048]{2,0,1:T(8,128)(2,1)}), bf16[256,3,2048]{2,0,1:T(8,128)(2,1)}) %all-gather.8.cloned.1.call-update) | async-done | bytes 3145744 | tf_op jit(solution)/shard_map/all_gather | solution.py:183
  226.1 8.3 %fusion.29 = f32[256,3,1024]{2,0,1:T(8,128)} fusion(bf16[256,3,2048]{2,0,1:T(8,128)(2,1)} %all-gather.8.cloned.1.call-done, bf16[2048,1024]{1,0:T(8,128)(2,1)} %param.36), kind=kOutput, calls=%fused_computation.34 | convolution fusion | flops 3221225472 | bytes 10485760 | tf_op jit(solution)/shard_map/ghc,cu->ghu/dot_general | solution.py:184
  234.3 12.8 %fusion.31 = bf16[256,3,2048]{2,0,1:T(8,128)(2,1)} fusion(bf16[1024,2048]{1,0:T(8,128)(2,1)} %param.38, f32[256,3,1024]{2,0,1:T(8,128)} %fusion.29, bf16[256,3,2048]{2,0,1:T(8,128)(2,1)} %all-gather.8.cloned.1.call-done, bf16[2048,1024]{1,0:T(8,128)(2,1)} %param.37), kind=kOutput, calls=%fused_computation.37 | convolution fusion | flops 6451888128 | bytes 17825792 | tf_op jit(solution)/shard_map/wjk,kx->wjx/dot_general | solution.py:193
  247.2 0.9 copy-done.7
  248.1 0.9 copy.61
  249.0 36.2 %reduce-scatter.5.cloned.1.call-done = bf16[64,3,2048]{2,0,1:T(8,128)(2,1)} async-done(((bf16[256,3,2048]{2,0,1:T(8,128)(2,1)}), bf16[64,3,2048]{2,0,1:T(8,128)(2,1)}) %reduce-scatter.5.cloned.1.call-update) | async-done | bytes 786448 | tf_op jit(solution)/shard_map/reduce_scatter | solution.py:192
  285.2 1.4 fusion.51
  286.6 2.9 fusion.55
  (98 shorter events, 4.8 us)
Async XLA Ops:
  7.2 141.3 %copy-start = (bf16[512,2048]{1,0:T(8,128)(2,1)S(1)}, bf16[512,2048]{1,0:T(8,128)(2,1)}, u32[]{:S(2)}) copy-start(bf16[512,2048]{1,0:T(8,128)(2,1)} %param.29) | copy-start | bytes 6291460
  7.2 3.4 %copy-start.2 = (bf16[64,3,2048]{2,0,1:T(8,128)(2,1)S(1)}, bf16[64,3,2048]{2,0,1:T(8,128)(2,1)}, u32[]{:S(2)}) copy-start(bf16[64,3,2048]{2,0,1:T(8,128)(2,1)} %param.23) | copy-start | bytes 2359300
  7.2 5.3 %copy-start.18 = (s32[3]{0:T(128)S(1)}, s32[3]{0:T(128)}, u32[]{:S(2)}) copy-start(s32[3]{0:T(128)} %param.42) | copy-start | bytes 40
  7.2 5.3 %copy-start.16 = (s32[2,8]{1,0:T(2,128)S(1)}, s32[2,8]{1,0:T(2,128)}, u32[]{:S(2)}) copy-start(s32[2,8]{1,0:T(2,128)} %param.41) | copy-start | bytes 196
  7.2 5.3 %copy-start.17 = (s32[2,8]{1,0:T(2,128)S(1)}, s32[2,8]{1,0:T(2,128)}, u32[]{:S(2)}) copy-start(s32[2,8]{1,0:T(2,128)} %param.40) | copy-start | bytes 196
  7.2 5.8 %copy-start.19 = (s32[3]{0:T(128)S(1)}, s32[3]{0:T(128)}, u32[]{:S(2)}) copy-start(s32[3]{0:T(128)} %param.43) | copy-start | bytes 40
  7.2 55.7 %all-gather.4.cloned.1.call-start = ((), (), s32[]{:S(2)}) async-start(), calls=%async_computation.2 | async-start | bytes 2359296 | tf_op jit(solution)/shard_map/all_gather | solution.py:110
  9.1 82.4 %all-gather.6.cloned.1.call-start = ((), (), s32[]{:S(2)}) async-start(), calls=%async_computation.3 | async-start | bytes 3932160 | tf_op jit(solution)/shard_map/all_gather | solution.py:77
  12.4 178.8 %reduce-scatter.3.cloned.1.call-start = ((), (), s32[]{:S(2)}) async-start(), calls=%async_computation.4 | async-start | bytes 3932160 | tf_op jit(solution)/shard_map/reduce_scatter | solution.py:164
  110.4 1.5 copy-start.6
  111.7 2.0 copy-start.4
  111.8 2.0 copy-start.15
  113.5 1.7 collective-permute-start
  114.3 2.0 copy-start.20
  123.3 1.4 copy-start.3
  123.3 1.4 copy-start.5
  134.1 1.4 copy-start.3
  134.1 1.4 copy-start.5
  144.9 1.4 copy-start.3
  144.9 1.4 copy-start.5
  153.1 0.9 copy-start.8
  153.1 1.0 copy-start.9
  153.1 1.0 copy-start.10
  153.1 39.5 %copy-start.11 = (f32[2048]{0:T(1024)S(1)}, f32[2048]{0:T(1024)}, u32[]{:S(2)}) copy-start(f32[2048]{0:T(1024)} %param.33) | copy-start | bytes 24580
  153.2 39.5 %copy-start.12 = (f32[2048]{0:T(1024)S(1)}, f32[2048]{0:T(1024)}, u32[]{:S(2)}) copy-start(f32[2048]{0:T(1024)} %param.30) | copy-start | bytes 24580
  153.2 72.9 %all-gather.8.cloned.1.call-start = ((), (), s32[]{:S(2)}) async-start(), calls=%async_computation.5 | async-start | bytes 3932160 | tf_op jit(solution)/shard_map/all_gather | solution.py:183
  192.6 3.6 %copy-start.13 = (f32[2048]{0:T(1024)S(1)}, f32[2048]{0:T(1024)}, u32[]{:S(2)}) copy-start(f32[2048]{0:T(1024)} %param.34) | copy-start | bytes 24580
  195.1 1.1 copy-start.1
  197.4 87.9 %reduce-scatter.5.cloned.1.call-start = ((), (), s32[]{:S(2)}) async-start(), calls=%async_computation.6 | async-start | bytes 3932160 | tf_op jit(solution)/shard_map/reduce_scatter | solution.py:192
  247.1 1.0 copy-start.7
  247.1 39.5 %copy-start.14 = (f32[2048]{0:T(1024)S(1)}, f32[2048]{0:T(1024)}, u32[]{:S(2)}) copy-start(f32[2048]{0:T(1024)} %param.35) | copy-start | bytes 24580
Sparse Core Ops, SparseCore 0:
  10.8 52.0 all-gather.3
  64.5 27.0 all-gather.5
  153.3 37.9 reduce-scatter.2
  197.5 28.5 all-gather.7
  247.2 37.9 reduce-scatter.4
where the time goes:
time: 297 us; the launch traced here: 296 us
  waiting for transfers between devices  170 us (57%)
  matrix products  40.9 us (14%)
  local copies, waits for them, and re-layouts  37.5 us (13%)
  other arithmetic  28 us (9%)
  between operations  14.1 us (5%)
  loops' own time  5.32 us (2%)
    all_gather x1, waiting for transfers between devices, local(): whole_pool = lax.all_gather(own_pages, 'req', axis=0, tiled=True)  48.7 us
    reduce_scatter x1, waiting for transfers between devices, local(): lax.psum_scatter(jnp.einsum('wjk,kx->wjx', local_row_block, down_projecti...  36.2 us
    reduce_scatter x1, waiting for transfers between devices, local(): lax.psum_scatter(jnp.einsum('rtc,cd->trd', local_row_block, out_weight, p...  34.8 us
    all_gather x1, waiting for transfers between devices, local(): incoming_rows = lax.all_gather(ffn_in, 'mlp', axis=0, tiled=True)  28.6 us
    all_gather x1, waiting for transfers between devices, local(): active_part = lax.all_gather(active_rows, 'mlp', axis=0, tiled=True)  21.1 us
    dot_general x1, matrix products, local(): jnp.einsum('wjk,kx->wjx', local_row_block, down_projection_matrix, prefer...  12.8 us
    reduce_sum x5, other arithmetic, rms_norm(): jnp.mean(values * values, axis=-1, keepdims=True) + EPS  8.93 us
    dot_general x1, matrix products, local(): jnp.einsum('ghc,cu->ghu', incoming_rows, gate_projection_matrix, preferre...  8.26 us
  transfers between devices with their start and end apart: 6, of which 5 were waited for; matrix products, arithmetic and copies ran while one was open for 6% of the time, Pallas kernels for 0%

commit v1 on v0

v1 whole, which is shorter than its diff:
```python
import functools
import math

import jax
import jax.numpy as jnp
from jax import lax
from jax.experimental import pallas as pl
from jax.experimental.pallas import tpu as pltpu
from jax.sharding import PartitionSpec as P

EPS = 1e-06
INV_ROOT = 1.0 / math.sqrt(2.0)
BF16 = jnp.bfloat16
F32 = jnp.float32
ON_CHIP = pl.BlockSpec(memory_space=pltpu.VMEM)
SCALARS = pl.BlockSpec(memory_space=pltpu.SMEM)
ANYWHERE = pl.BlockSpec(memory_space=pl.ANY)
BLOCK_XOR = (0, 2, 1, 3)


def exchange(value, axis, flip):
    return lax.ppermute(value, axis, [(i, i ^ flip) for i in range(lax.axis_size(axis))])


def normed(values, gain):
    scale = lax.rsqrt(jnp.mean(values * values, axis=-1, keepdims=True) + EPS)
    return values * scale * gain


def rotated(values, cos, sin):
    half = values.shape[-1] // 2
    first, second = values[:, :half], values[:, half:]
    return jnp.concatenate(
        [first * cos - second * sin, second * cos + first * sin], axis=-1
    )


def params(mib):
    return pltpu.CompilerParams(vmem_limit_bytes=mib << 20)


def cost(flops, moved, exps=0):
    return pl.CostEstimate(flops=int(flops), bytes_accessed=int(moved), transcendentals=int(exps))


def active_kernel(hidden_ref, gain_ref, *active_refs):
    for r, active_ref in enumerate(active_refs):
        active_ref[...] = normed(hidden_ref[r].astype(F32), gain_ref[...]).astype(BF16)


def make_active(hidden, gain):
    reqs, rows, width = hidden.shape
    return pl.pallas_call(
        active_kernel,
        out_shape=[jax.ShapeDtypeStruct((rows, width), BF16)] * reqs,
        in_specs=[ON_CHIP, ON_CHIP],
        out_specs=[ON_CHIP] * reqs,
        cost_estimate=cost(6 * hidden.size, 4 * hidden.size),
        name="active",
    )(hidden, gain)


def base_kernel(hidden_ref, *refs):
    reqs = hidden_ref.shape[0]
    active_refs = refs[:reqs]
    left_ref, right_ref, gain_ref = refs[reqs : reqs + 3]
    base_refs = refs[reqs + 3 :]
    for r in range(reqs):
        active = active_refs[r][...]
        mid = lax.dot_general(
            active, left_ref[...], (((1,), (1,)), ((), ())), preferred_element_type=F32
        ).astype(BF16)
        low = jnp.dot(mid, right_ref[...], preferred_element_type=F32)
        base_refs[r][...] = (
            hidden_ref[r].astype(F32) + active.astype(F32) + normed(low, gain_ref[...])
        )


def make_base(hidden, actives, left_t, right, gain):
    reqs, rows, width = hidden.shape
    return pl.pallas_call(
        base_kernel,
        out_shape=[jax.ShapeDtypeStruct((rows, width), F32)] * reqs,
        in_specs=[ON_CHIP] * (reqs + 4),
        out_specs=[ON_CHIP] * reqs,
        cost_estimate=cost(4 * hidden.size * left_t.shape[0], 8 * hidden.size),
        name="base",
    )(hidden, *actives, left_t, right, gain)


def project_kernel(
    req,
    len_ref,
    own_ref,
    y_ref,
    c_ref,
    d_ref,
    wq_ref,
    mine_ref,
    other_ref,
    qgain_ref,
    kgain_ref,
    cos_ref,
    sin_ref,
    *refs,
):
    page_ref, q_ref, k_ref, v_ref = refs[-4:]
    member = lax.axis_index("mlp")
    part = own_ref.shape[0]
    head = qgain_ref.shape[-1]
    rows = jnp.concatenate([own_ref[...], y_ref[...], c_ref[...], d_ref[...]], axis=0)
    starts = [pl.multiple_of((member ^ flip) * part, part) for flip in BLOCK_XOR]
    cos = jnp.concatenate([cos_ref[pl.ds(s, part), :] for s in starts], axis=0)
    sin = jnp.concatenate([sin_ref[pl.ds(s, part), :] for s in starts], axis=0)
    count = rows.shape[0]
    mine = jnp.dot(rows, mine_ref[...], preferred_element_type=F32)
    other = jnp.dot(rows, other_ref[...], preferred_element_type=F32)
    holds_keys = member % 2 == 0
    raw_keys = jnp.where(holds_keys, mine, other)
    raw_values = jnp.where(holds_keys, other, mine)
    keys = rotated(normed(raw_keys, kgain_ref[...]), cos, sin).astype(BF16)
    values = normed(raw_values, 1.0).astype(BF16)
    k_ref[...] = keys
    v_ref[...] = values
    live = len_ref[req]
    for b, start in enumerate(starts):
        block = slice(b * part, (b + 1) * part)
        piece = jnp.where(
            holds_keys, keys[block].astype(F32), values[block].astype(F32)
        )
        position = start + lax.broadcasted_iota(jnp.int32, (part, 1), 0)
        page_ref[0, pl.ds(start, part), :] = jnp.where(position < live, piece, 0.0).astype(BF16)
    heads = wq_ref.shape[1] // head
    for h in range(heads):
        raw = jnp.dot(rows, wq_ref[:, h * head : (h + 1) * head], preferred_element_type=F32)
        q_ref[h * count : (h + 1) * count, :] = rotated(
            normed(raw, qgain_ref[...]), cos, sin
        ).astype(BF16)


def project(req, reqs, lens, blocks, wq, mine, other, qgain, kgain, cos, sin, pages):
    part, width = blocks[0].shape
    count = part * len(blocks)
    head = qgain.shape[-1]
    heads = wq.shape[1] // head
    extra = [] if pages is None else [pages]
    return pl.pallas_call(
        functools.partial(project_kernel, req),
        grid=(1,),
        out_shape=[
            jax.ShapeDtypeStruct((reqs, count, head), BF16),
            jax.ShapeDtypeStruct((heads * count, head), BF16),
            jax.ShapeDtypeStruct((count, head), BF16),
            jax.ShapeDtypeStruct((count, head), BF16),
        ],
        in_specs=[SCALARS] + [ON_CHIP] * 11 + [ANYWHERE] * len(extra),
        out_specs=[
            pl.BlockSpec((1, count, head), lambda i: (req, 0, 0)),
            ON_CHIP,
            ON_CHIP,
            ON_CHIP,
        ],
        input_output_aliases={12: 0} if extra else {},
        compiler_params=params(24),
        cost_estimate=cost(2 * count * width * (heads + 2) * head, 6 << 20),
        name="project",
    )(lens, *blocks, wq, mine, other, qgain, kgain, cos, sin, *extra)


def attend_kernel(
    req,
    sources,
    group_ref,
    owner_ref,
    slot_ref,
    q_ref,
    k_ref,
    v_ref,
    wo_ref,
    *refs,
):
    pool_count = len({name for name, _, _, _ in sources})
    pool_refs = refs[:pool_count]
    own_out, y_out, c_out, d_out = refs[pool_count : pool_count + 4]
    prefix, mixed, place, sems = refs[pool_count + 4 :]
    member = lax.axis_index("mlp")
    me = lax.axis_index("req")
    head = k_ref.shape[1]
    count = k_ref.shape[0]
    part = count // 4
    page = pool_refs[0].shape[1]
    n_pages = owner_ref.shape[1]
    per_part = len(sources) // 2
    group = group_ref[req]
    for s in range(len(sources)):
        place[s] = -1
    for i in range(n_pages):
        flip = owner_ref[group, i] ^ me
        far = slot_ref[group, i] ^ (member % 2)
        place[far * per_part + flip] = i
    for name, index, far, flip in sources:
        where = place[far * per_part + flip]

        @pl.when(where >= 0)
        def _():
            start = pl.multiple_of(where * page, page)
            pltpu.make_async_copy(
                pool_refs[name].at[index], prefix.at[pl.ds(start, page), :], sems.at[where]
            ).start()

    for i in range(n_pages):
        pltpu.make_async_copy(
            pool_refs[0].at[0], prefix.at[i * page : (i + 1) * page, :], sems.at[i]
        ).wait()

    factor = head**-0.5 * math.log2(math.e)
    pre = n_pages * page

    def positions(index):
        block = index // part
        flip = (block & 1) * 2 + (block >> 1)
        return (member ^ flip) * part + index % part

    key_at = positions(lax.broadcasted_iota(jnp.int32, (1, count), 1))
    tile = 2 * part
    heads = q_ref.shape[0] // count
    for h in range(heads):
        for first in range(0, count, tile):
            query_at = positions(first + lax.broadcasted_iota(jnp.int32, (tile, 1), 0))
            start = h * count + first
            q = q_ref[start : start + tile, :]
            contract = (((1,), (1,)), ((), ()))
            before = lax.dot_general(
                q, prefix[:, :head], contract, preferred_element_type=F32
            )
            own = lax.dot_general(q, k_ref[...], contract, preferred_element_type=F32)
            own = jnp.where(key_at <= query_at, own, -jnp.inf)
            peak = jnp.maximum(
                jnp.max(before, axis=-1, keepdims=True), jnp.max(own, axis=-1, keepdims=True)
            )
            before = jnp.exp2((before - peak) * factor)
            own = jnp.exp2((own - peak) * factor)
            total = jnp.sum(before, axis=-1, keepdims=True) + jnp.sum(own, axis=-1, keepdims=True)
            out = jnp.dot(before.astype(BF16), prefix[:, head:], preferred_element_type=F32)
            out += jnp.dot(own.astype(BF16), v_ref[...], preferred_element_type=F32)
            mixed[first : first + tile, h * head : (h + 1) * head] = (
                out * (1.0 / total)
            ).astype(BF16)
    width = wo_ref.shape[1]
    step = 512
    for col in range(0, width, step):
        result = jnp.dot(
            mixed[...], wo_ref[:, col : col + step], preferred_element_type=F32
        ).astype(BF16)
        for b, out_ref in enumerate((own_out, y_out, c_out, d_out)):
            out_ref[:, col : col + step] = result[b * part : (b + 1) * part]


def attend(req, sources, group, owner, slot, q, k, v, wo, pools):
    count, head = k.shape
    part = count // 4
    heads = q.shape[0] // count
    page = pools[0].shape[1]
    n_pages = owner.shape[1]
    keys = n_pages * page + count
    return pl.pallas_call(
        functools.partial(attend_kernel, req, sources),
        out_shape=[jax.ShapeDtypeStruct((part, wo.shape[1]), BF16)] * 4,
        in_specs=[SCALARS] * 3 + [ON_CHIP] * 4 + [ANYWHERE] * len(pools),
        out_specs=[ON_CHIP] * 4,
        scratch_shapes=[
            pltpu.VMEM((n_pages * page, 2 * head), BF16),
            pltpu.VMEM((count, heads * head), BF16),
            pltpu.SMEM((len(sources),), jnp.int32),
            pltpu.SemaphoreType.DMA((n_pages,)),
        ],
        compiler_params=params(24),
        cost_estimate=cost(
            heads * count * head * (4 * keys + 2 * wo.shape[1]), 4 << 20, heads * count * keys
        ),
        name="attend",
    )(group, owner, slot, q, k, v, wo, *pools)


def residual_kernel(base_ref, own_ref, c_ref, y_ref, again_ref, fgain_ref, res_ref, in_ref):
    total = own_ref[...].astype(F32) + c_ref[...].astype(F32) + y_ref[...].astype(F32)
    residual = (base_ref[...] + normed(total, again_ref[...])) * INV_ROOT
    res_ref[...] = residual
    in_ref[...] = normed(residual, fgain_ref[...]).astype(BF16)


def make_residual(base, own, c, y, again, fgain):
    return pl.pallas_call(
        residual_kernel,
        out_shape=[
            jax.ShapeDtypeStruct(base.shape, F32),
            jax.ShapeDtypeStruct(base.shape, BF16),
        ],
        in_specs=[ON_CHIP] * 6,
        out_specs=[ON_CHIP] * 2,
        cost_estimate=cost(12 * base.size, 16 * base.size),
        name="residual",
    )(base, own, c, y, again, fgain)


def feed_kernel(own_ref, y_ref, c_ref, d_ref, gate_ref, up_ref, down_ref, *refs):
    outs, hidden = refs[:4], refs[4]
    rows = jnp.concatenate([own_ref[...], y_ref[...], c_ref[...], d_ref[...]], axis=0)
    part = own_ref.shape[0]
    units = gate_ref.shape[1]
    step = 512
    for u in range(0, units, step):
        gate = jnp.dot(rows, gate_ref[:, u : u + step], preferred_element_type=F32)
        up = jnp.dot(rows, up_ref[:, u : u + step], preferred_element_type=F32)
        hidden[:, u : u + step] = (jax.nn.gelu(gate, approximate=True) * up).astype(BF16)
    for col in range(0, down_ref.shape[1], step):
        result = jnp.dot(
            hidden[...], down_ref[:, col : col + step], preferred_element_type=F32
        ).astype(BF16)
        for b, out_ref in enumerate(outs):
            out_ref[:, col : col + step] = result[b * part : (b + 1) * part]


def feed(blocks, gate, up, down):
    part, width = blocks[0].shape
    count = 4 * part
    units = gate.shape[1]
    return pl.pallas_call(
        feed_kernel,
        out_shape=[jax.ShapeDtypeStruct((part, width), BF16)] * 4,
        in_specs=[ON_CHIP] * 7,
        out_specs=[ON_CHIP] * 4,
        scratch_shapes=[pltpu.VMEM((count, units), BF16)],
        compiler_params=params(32),
        cost_estimate=cost(6 * count * width * units, 12 << 20, count * units),
        name="feed",
    )(*blocks, gate, up, down)


def finish_kernel(req, len_ref, res_ref, own_ref, c_ref, y_ref, gain_ref, *refs):
    out_ref = refs[-1]
    part = res_ref.shape[0]
    total = own_ref[...].astype(F32) + c_ref[...].astype(F32) + y_ref[...].astype(F32)
    output = res_ref[...] + normed(total, gain_ref[...])
    position = lax.axis_index("mlp") * part + lax.broadcasted_iota(jnp.int32, (part, 1), 0)
    out_ref[0] = jnp.where(position < len_ref[req], output, 0.0).astype(BF16)


def finish(req, reqs, lens, residual, own, c, y, gain, before):
    part, width = residual.shape
    extra = [] if before is None else [before]
    return pl.pallas_call(
        functools.partial(finish_kernel, req),
        grid=(1,),
        out_shape=jax.ShapeDtypeStruct((reqs, part, width), BF16),
        in_specs=[SCALARS] + [ON_CHIP] * 5 + [ANYWHERE] * len(extra),
        out_specs=pl.BlockSpec((1, part, width), lambda i: (req, 0, 0)),
        input_output_aliases={6: 0} if extra else {},
        cost_estimate=cost(10 * residual.size, 12 * residual.size),
        name="finish",
    )(lens, residual, own, c, y, gain, *extra)


def gather_pool(page_pool, member, width):
    n_req = lax.axis_size("req")
    page = page_pool.shape[1]
    own = lax.dynamic_slice(page_pool, (member % 2, 0, member // 2 * width), (1, page, width))
    direct = {0: own}
    for flip in range(2, n_req, 2):
        direct[flip] = exchange(own, "req", flip)
    direct[1] = exchange(own, "req", 1)
    direct[3] = exchange(direct[2], "req", 1)
    later = list(range(4, n_req, 2))
    arrays = [
        (jnp.concatenate([own, direct[1], direct[2]]), [0, 1, 2]),
        (jnp.concatenate([direct[f] for f in later]), later),
    ]
    crossed = exchange(arrays[1][0], "req", 1)
    arrays.append(
        (jnp.concatenate([direct[3], crossed]), [3] + [f + 1 for f in later])
    )
    pools, sources = [], []
    for far in (0, 1):
        for array, flips in arrays:
            for index, flip in enumerate(flips):
                sources.append((len(pools), index, far, flip))
            pools.append(exchange(array, "mlp", 1) if far else array)
    return pools, sources


def local(
    hidden_in,
    input_gain,
    query_weight,
    keyval_weight,
    query_gain,
    key_gain,
    out_weight,
    attn_gain,
    laurel_left,
    laurel_right,
    laurel_gain,
    ffn_gain,
    post_gain,
    gate_projection_matrix,
    up_projection_matrix,
    down_projection_matrix,
    page_pool,
    page_owner,
    page_slot,
    request_group,
    suffix_len,
):
    member = lax.axis_index("mlp")
    part, reqs, width = hidden_in.shape
    head = query_gain.shape[0]
    count = part * lax.axis_size("mlp")
    prefix_len = page_owner.shape[1] * page_pool.shape[1]
    row = lambda gain: gain[None, :]

    pools, sources = gather_pool(page_pool, member, 2 * head)

    half = head // 2
    frequency = 1000000.0 ** (-jnp.arange(half, dtype=F32) / half)
    angles = (prefix_len + jnp.arange(count)).astype(F32)[:, None] * frequency[None, :]
    cos, sin = jnp.cos(angles), jnp.sin(angles)

    hidden = jnp.transpose(hidden_in, (1, 0, 2))
    actives = make_active(hidden, row(input_gain))
    other_weight = exchange(keyval_weight, "mlp", 1)
    bases = make_base(
        hidden, actives, laurel_left.T, laurel_right, row(laurel_gain)
    )

    def gather(block):
        y = exchange(block, "mlp", 2)
        return [block, y, exchange(block, "mlp", 1), exchange(y, "mlp", 1)]

    def scatter(partials):
        own, y, c, d = partials
        from_c = exchange(d, "mlp", 1)
        joined = (y.astype(F32) + from_c.astype(F32)).astype(BF16)
        return own, exchange(c, "mlp", 1), exchange(joined, "mlp", 2)

    pages = None
    projected = []
    for r in range(reqs):
        pages, q, k, v = project(
            r,
            reqs,
            suffix_len,
            gather(actives[r]),
            query_weight,
            keyval_weight,
            other_weight,
            row(query_gain),
            row(key_gain),
            cos,
            sin,
            pages,
        )
        projected.append((q, k, v))
    residuals = []
    inputs = []
    for r in range(reqs):
        partials = attend(
            r, sources, request_group, page_owner, page_slot, *projected[r], out_weight, pools
        )
        residual, ffn_in = make_residual(
            bases[r], *scatter(partials), row(attn_gain), row(ffn_gain)
        )
        residuals.append(residual)
        inputs.append(gather(ffn_in))
    result = None
    for r in range(reqs):
        partials = feed(
            inputs[r], gate_projection_matrix, up_projection_matrix, down_projection_matrix
        )
        result = finish(
            r, reqs, suffix_len, residuals[r], *scatter(partials), row(post_gain), result
        )
    return jnp.transpose(result, (1, 0, 2)), jnp.transpose(pages, (1, 0, 2))


def solution(mesh):
    placed = (
        P("mlp", "req", None),
        P(),
        P(None, "mlp"),
        P(None, "mlp"),
        P(),
        P(),
        P("mlp", None),
        P(),
        P(),
        P(),
        P(),
        P(),
        P(),
        P(None, "mlp"),
        P(None, "mlp"),
        P("mlp", None),
        P("req", None, None),
        P(),
        P(),
        P("req"),
        P("req"),
    )
    return jax.shard_map(
        local,
        mesh=mesh,
        in_specs=placed,
        out_specs=(P("mlp", "req", None), P(None, "req", "mlp")),
        check_vma=False,
    )
```

time: 297 us -> 164 us (0.55)
  waiting for transfers between devices: 170 us -> 42.4 us
  Pallas kernels: 0 us -> 55.1 us
  matrix products: 40.9 us -> 0 us
  starting transfers between devices: 0.64 us -> 32.7 us
  other arithmetic: 28 us -> 1.92 us
  between operations: 14.1 us -> 1.25 us
  local copies, waits for them, and re-layouts: 37.5 us -> 30.2 us
  loops' own time: 5.32 us -> 0 us
    all_gather x3 -> x0, waiting for transfers between devices: 98.5 us -> none  [the longest x1 48.7 us: local(): whole_pool = lax.all_gather(own_pages, 'req', axis=0, tiled=True)]
    reduce_scatter x2 -> x0, waiting for transfers between devices: 71.1 us -> none  [the longest x1 36.2 us: local(): lax.psum_scatter(jnp.einsum('wjk,kx->wjx', local_row_block, down_projecti...]
    pallas_call x0 -> x17, Pallas kernels: none -> 55.1 us  [the longest x3 17.3 us: attend(): pl.pallas_call(functools.partial(attend_kernel, req, sources), out_shape=...]
    ppermute x1 -> x46, waiting for transfers between devices: 0.04 us -> 42.4 us  [exchange(): lax.ppermute(value, axis, [(i, i ^ flip) for i in range(lax.axis_size(axi...]
    dot_general x13 -> x0, matrix products: 40.9 us -> none  [the longest x1 12.8 us: local(): jnp.einsum('wjk,kx->wjx', local_row_block, down_projection_matrix, prefer...]
    ppermute x1 -> x46, starting transfers between devices: 0.26 us -> 32.7 us  [exchange(): lax.ppermute(value, axis, [(i, i ^ flip) for i in range(lax.axis_size(axi...]
    unnamed x41 -> x130, local copies, waits for them, and re-layouts: 3.84 us -> 30.2 us
    dynamic_slice x19 -> x1, local copies, waits for them, and re-layouts: 15.8 us -> 0.01 us  [gather_pool(): lax.dynamic_slice(page_pool, (member % 2, 0, member // 2 * width), (1, pa...]
  transfers between devices with their start and end apart: 6 -> 46, of which waited for: 5 -> 14; matrix products, arithmetic and copies ran while one was open for 6% -> 1% of each run, Pallas kernels for 0% -> 29%
where the time goes in v1:
time: 164 us
  Pallas kernels  55.1 us (34%)
  waiting for transfers between devices  42.4 us (26%)
  starting transfers between devices  32.7 us (20%)
  local copies, waits for them, and re-layouts  30.2 us (18%)
  other arithmetic  1.92 us (1%)
    ppermute x46, waiting for transfers between devices, exchange(): lax.ppermute(value, axis, [(i, i ^ flip) for i in range(lax.axis_size(axi...  42.4 us
    ppermute x46, starting transfers between devices, exchange(): lax.ppermute(value, axis, [(i, i ^ flip) for i in range(lax.axis_size(axi...  32.7 us
    unnamed x130, local copies, waits for them, and re-layouts  30.2 us
    pallas_call x3, Pallas kernels, attend(): pl.pallas_call(functools.partial(attend_kernel, req, sources), out_shape=...  17.3 us
    pallas_call x3, Pallas kernels, feed(): pl.pallas_call(feed_kernel, out_shape=[jax.ShapeDtypeStruct((part, width)...  10.5 us
    pallas_call x3, Pallas kernels, project(): pl.pallas_call(functools.partial(project_kernel, req), grid=(1,), out_sha...  7.61 us
    pallas_call x3, Pallas kernels, make_residual(): pl.pallas_call(residual_kernel, out_shape=[jax.ShapeDtypeStruct(base.shap...  7.24 us
    pallas_call x3, Pallas kernels, finish(): pl.pallas_call(functools.partial(finish_kernel, req), grid=(1,), out_shap...  6.71 us
  transfers between devices with their start and end apart: 46, of which 14 were waited for; matrix products, arithmetic and copies ran while one was open for 1% of the time, Pallas kernels for 29%

profile of v1, /device:TPU:0, one launch (start us, length us, event | category | flops | bytes accessed | tf_op | source)
XLA Modules:
  0.0 163.6 jit_solution(4938999938414175579)
XLA Ops:
  0.7 1.0 copy-done
  1.7 4.1 %collective-permute-start.12 = (bf16[1,128,512]{2,1,0:T(8,128)(2,1)S(1)}, bf16[1,128,512]{2,1,0:T(8,128)(2,1)S(1)}, u32[]{:S(2)}, u32[]{:S(2)}) collective-permute-start(bf16[1,128,512]{2,1,0:T(8,128)(2,1)S(1)} %constant_dynamic-slice_fusion), channel_id=1, source_target_pairs={{0,16},{4,20},{8,24},{12,28},{16,0},{20,4},{24,8},{28,12},{1,17},{... | collective-permute-start | bytes 393224 | tf_op jit(solution)/shard_map/ppermute | solution.py:22
  5.8 1.6 collective-permute-start.11
  7.4 1.7 %collective-permute-start.10 = (bf16[1,128,512]{2,1,0:T(8,128)(2,1)S(1)}, bf16[1,128,512]{2,1,0:T(8,128)(2,1)S(1)}, u32[]{:S(2)}, u32[]{:S(2)}) collective-permute-start(bf16[1,128,512]{2,1,0:T(8,128)(2,1)S(1)} %constant_dynamic-slice_fusion), channel_id=1, source_target_pairs={{0,4},{4,0},{8,12},{12,8},{16,20},{20,16},{24,28},{28,24},{1,5},{5... | collective-permute-start | bytes 393224 | tf_op jit(solution)/shard_map/ppermute | solution.py:22
  9.1 2.3 %active.1 = (bf16[64,2048]{1,0:T(8,128)(2,1)}, bf16[64,2048]{1,0:T(8,128)(2,1)}, bf16[64,2048]{1,0:T(8,128)(2,1)}) custom-call(bf16[3,64,2048]{2,1,0:T(8,128)(2,1)} %bitcast.18, f32[1,2048]{1,0:T(1,128)} %bitcast.31), custom_call_target="tpu_custom_call" | custom-call | flops 2359296 | bytes 1572864 | tf_op jit(solution)/shard_map/active/pallas_call | solution.py:53
  11.3 1.5 collective-permute-start
  12.9 0.9 collective-permute-done.12
  13.8 2.2 %collective-permute-start.4 = (bf16[64,2048]{1,0:T(8,128)(2,1)}, bf16[64,2048]{1,0:T(8,128)(2,1)S(1)}, u32[]{:S(2)}, u32[]{:S(2)}) collective-permute-start(bf16[64,2048]{1,0:T(8,128)(2,1)} %get-tuple-element.51.refs_1_.own_ref), channel_id=1, source_target_pairs={{0,2},{1,3},{2,0},{3,1},{4,6},{5,7},{6,4},{7,5},{8,10},{9,11},{10,... | collective-permute-start | bytes 786440 | tf_op jit(solution)/shard_map/ppermute | solution.py:22
  16.1 1.5 collective-permute-start.7
  17.7 1.6 collective-permute-start.15
  19.8 5.3 %collective-permute-done.4.y_ref = bf16[64,2048]{1,0:T(8,128)(2,1)S(1)} collective-permute-done((bf16[64,2048]{1,0:T(8,128)(2,1)}, bf16[64,2048]{1,0:T(8,128)(2,1)S(1)}, u32[]{:S(2)}, u32[]{:S(2)}) %collective-permute-start.4) | collective-permute-done | bytes 262176 | tf_op jit(solution)/shard_map/ppermute | solution.py:22
  25.1 4.7 %collective-permute-done.7.y_ref = bf16[64,2048]{1,0:T(8,128)(2,1)S(1)} collective-permute-done((bf16[64,2048]{1,0:T(8,128)(2,1)}, bf16[64,2048]{1,0:T(8,128)(2,1)S(1)}, u32[]{:S(2)}, u32[]{:S(2)}) %collective-permute-start.7) | collective-permute-done | bytes 262176 | tf_op jit(solution)/shard_map/ppermute | solution.py:22
  31.0 0.8 collective-permute-done.8.c_ref
  33.5 1.2 copy-done.10
  34.7 0.9 copy-done.22
  37.7 2.5 %project.3 = (bf16[3,256,256]{2,1,0:T(8,128)(2,1)}, bf16[512,256]{1,0:T(8,128)(2,1)S(1)}, bf16[256,256]{1,0:T(8,128)(2,1)S(1)}, bf16[256,256]{1,0:T(8,128)(2,1)S(1)}) custom-call(s32[3]{0:T(128)S(1)} %copy-done.44, bf16[64,2048]{1,0:T(8,128)(2,1)S(1)} %copy-done.22, bf16[64,2048]{1,0:T(8,128)(2,1)S(1)} %collective-permute-done.7.y_ref, ...), custom_call_target="tpu_custom_call" | custom-call | flops 1073741824 | bytes 6291456 | tf_op jit(solution)/shard_map/project/pallas_call | solution.py:147
  41.5 2.5 %project.4 = (bf16[3,256,256]{2,1,0:T(8,128)(2,1)}, bf16[512,256]{1,0:T(8,128)(2,1)S(1)}, bf16[256,256]{1,0:T(8,128)(2,1)S(1)}, bf16[256,256]{1,0:T(8,128)(2,1)S(1)}) custom-call(s32[3]{0:T(128)S(1)} %copy-done.44, bf16[64,2048]{1,0:T(8,128)(2,1)S(1)} %copy-done.20, ...), custom_call_target="tpu_custom_call", output_to_operand_aliasing={{0}: (12, {})} | custom-call | flops 1073741824 | bytes 6291456 | tf_op jit(solution)/shard_map/project/pallas_call | solution.py:147
  44.9 2.5 %project.5 = (bf16[3,256,256]{2,1,0:T(8,128)(2,1)}, bf16[512,256]{1,0:T(8,128)(2,1)S(1)}, bf16[256,256]{1,0:T(8,128)(2,1)S(1)}, bf16[256,256]{1,0:T(8,128)(2,1)S(1)}) custom-call(s32[3]{0:T(128)S(1)} %copy-done.45, bf16[64,2048]{1,0:T(8,128)(2,1)S(1)} %copy-done.21, ...), custom_call_target="tpu_custom_call", output_to_operand_aliasing={{0}: (12, {})} | custom-call | flops 1073741824 | bytes 6291456 | tf_op jit(solution)/shard_map/project/pallas_call | solution.py:147
  47.5 5.7 %attend.3 = (bf16[64,2048]{1,0:T(8,128)(2,1)S(1)}, bf16[64,2048]{1,0:T(8,128)(2,1)S(1)}, bf16[64,2048]{1,0:T(8,128)(2,1)S(1)}, bf16[64,2048]{1,0:T(8,128)(2,1)}) custom-call(s32[3]{0:T(128)S(1)} %copy-done.51, s32[2,8]{1,0:T(2,128)S(1)} %copy-done.46, s32[2,8]{1,0:T(2,128)S(1)} %copy-done.47, bf16[512,256]{1,0:T(8,128)(2,1)S(1)} %get-tuple-element.56.q_ref, ...), custom_call_target="tpu_custom_call" | custom-call | flops 1207959552 | bytes 4194304 | tf_op jit(solution)/shard_map/attend/pallas_call | solution.py:266
  53.3 0.7 copy-done.27
  54.7 0.7 copy-done.52
  55.6 3.6 %base.1 = (f32[64,2048]{1,0:T(8,128)}, f32[64,2048]{1,0:T(8,128)}, f32[64,2048]{1,0:T(8,128)}) custom-call(bf16[3,64,2048]{2,1,0:T(8,128)(2,1)} %bitcast.19, bf16[64,2048]{1,0:T(8,128)(2,1)} %get-tuple-element.50.refs_0_.own_ref, bf16[64,2048]{1,0:T(8,128)(2,1)} %get-tuple-element.51.refs_1_.own_ref, bf16[64,2048]{1,0:T(8,128)(2,1)} %get-tuple-element.52.refs_2_.own_ref, ...), custom_call_target="tpu_custom_call" | custom-call | flops 100663296 | bytes 3145728 | tf_op jit(solution)/shard_map/base/pallas_call | solution.py:81
  59.5 1.0 copy-done.13
  60.5 1.0 copy-done.15
  61.5 0.9 copy-done.17
  62.5 0.9 copy-done.19
  63.4 0.9 copy-done.30
  64.4 0.9 copy-done.41
  65.3 0.9 copy-done.43
  66.2 5.9 %attend.4 = (bf16[64,2048]{1,0:T(8,128)(2,1)S(1)}, bf16[64,2048]{1,0:T(8,128)(2,1)S(1)}, bf16[64,2048]{1,0:T(8,128)(2,1)}, bf16[64,2048]{1,0:T(8,128)(2,1)S(1)}) custom-call(s32[3]{0:T(128)S(1)} %copy-done.51, s32[2,8]{1,0:T(2,128)S(1)} %copy-done.46, s32[2,8]{1,0:T(2,128)S(1)} %copy-done.47, bf16[512,256]{1,0:T(8,128)(2,1)S(1)} %copy-done.30, ...), custom_call_target="tpu_custom_call" | custom-call | flops 1207959552 | bytes 4194304 | tf_op jit(solution)/shard_map/attend/pallas_call | solution.py:266
  73.3 5.7 %attend.5 = (bf16[64,2048]{1,0:T(8,128)(2,1)S(1)}, bf16[64,2048]{1,0:T(8,128)(2,1)S(1)}, bf16[64,2048]{1,0:T(8,128)(2,1)}, bf16[64,2048]{1,0:T(8,128)(2,1)S(1)}) custom-call(s32[3]{0:T(128)S(1)} %copy-done.51, s32[2,8]{1,0:T(2,128)S(1)} %copy-done.46, s32[2,8]{1,0:T(2,128)S(1)} %copy-done.47, bf16[512,256]{1,0:T(8,128)(2,1)S(1)} %copy-done.26, ...), custom_call_target="tpu_custom_call" | custom-call | flops 1207959552 | bytes 4194304 | tf_op jit(solution)/shard_map/attend/pallas_call | solution.py:266
  79.5 1.0 add_convert_fusion.5
  80.6 1.6 collective-permute-start.21
  82.9 1.6 collective-permute-start.39
  84.5 5.3 %collective-permute-done.21.y_ref = bf16[64,2048]{1,0:T(8,128)(2,1)S(1)} collective-permute-done((bf16[64,2048]{1,0:T(8,128)(2,1)S(1)}, bf16[64,2048]{1,0:T(8,128)(2,1)S(1)}, u32[]{:S(2)}, u32[]{:S(2)}) %collective-permute-start.21) | collective-permute-done | bytes 262176 | tf_op jit(solution)/shard_map/ppermute | solution.py:22
  89.8 0.7 copy-done.63
  90.5 2.4 %residual.3 = (f32[64,2048]{1,0:T(8,128)}, bf16[64,2048]{1,0:T(8,128)(2,1)}) custom-call(f32[64,2048]{1,0:T(8,128)} %get-tuple-element.53.base_ref, bf16[64,2048]{1,0:T(8,128)(2,1)} %copy-done.34, bf16[64,2048]{1,0:T(8,128)(2,1)} %copy-done.60, bf16[64,2048]{1,0:T(8,128)(2,1)} %copy-done.63, f32[1,2048]{1,0:T(1,128)} %bitcast.25, f32[1,2048]{1,0:T(1,128)} %bitcast.28), custom_call_target="tpu_custom_call" | custom-call | flops 1572864 | bytes 2097152 | tf_op jit(solution)/shard_map/residual/pallas_call | solution.py:293
  92.9 1.5 collective-permute-start.22
  94.4 1.0 collective-permute-done.30.y_ref
  95.4 0.7 copy-done.62
  96.1 2.4 %residual.4 = (f32[64,2048]{1,0:T(8,128)}, bf16[64,2048]{1,0:T(8,128)(2,1)}) custom-call(f32[64,2048]{1,0:T(8,128)} %get-tuple-element.69.base_ref, bf16[64,2048]{1,0:T(8,128)(2,1)} %copy-done.33, bf16[64,2048]{1,0:T(8,128)(2,1)} %collective-permute-done.28.c_ref, bf16[64,2048]{1,0:T(8,128)(2,1)} %copy-done.62, f32[1,2048]{1,0:T(1,128)} %bitcast.26, ...), custom_call_target="tpu_custom_call" | custom-call | flops 1572864 | bytes 2097152 | tf_op jit(solution)/shard_map/residual/pallas_call | solution.py:293
  98.6 1.5 collective-permute-start.31
  100.1 0.9 collective-permute-done.39.y_ref
  101.0 0.7 copy-done.61
  101.7 2.4 %residual.5 = (f32[64,2048]{1,0:T(8,128)}, bf16[64,2048]{1,0:T(8,128)(2,1)}) custom-call(f32[64,2048]{1,0:T(8,128)} %get-tuple-element.83.base_ref, bf16[64,2048]{1,0:T(8,128)(2,1)} %copy-done.32, bf16[64,2048]{1,0:T(8,128)(2,1)} %copy-done.59, bf16[64,2048]{1,0:T(8,128)(2,1)} %copy-done.61, f32[1,2048]{1,0:T(1,128)} %bitcast.27, f32[1,2048]{1,0:T(1,128)} %bitcast.30), custom_call_target="tpu_custom_call" | custom-call | flops 1572864 | bytes 2097152 | tf_op jit(solution)/shard_map/residual/pallas_call | solution.py:293
  104.2 1.5 collective-permute-start.40
  105.7 0.9 collective-permute-done.22.y_ref
  107.2 5.1 %collective-permute-done.31.y_ref = bf16[64,2048]{1,0:T(8,128)(2,1)S(1)} collective-permute-done((bf16[64,2048]{1,0:T(8,128)(2,1)}, bf16[64,2048]{1,0:T(8,128)(2,1)S(1)}, u32[]{:S(2)}, u32[]{:S(2)}) %collective-permute-start.31) | collective-permute-done | bytes 262176 | tf_op jit(solution)/shard_map/ppermute | solution.py:22
  112.3 4.8 %collective-permute-done.40.y_ref = bf16[64,2048]{1,0:T(8,128)(2,1)S(1)} collective-permute-done((bf16[64,2048]{1,0:T(8,128)(2,1)}, bf16[64,2048]{1,0:T(8,128)(2,1)S(1)}, u32[]{:S(2)}, u32[]{:S(2)}) %collective-permute-start.40) | collective-permute-done | bytes 262176 | tf_op jit(solution)/shard_map/ppermute | solution.py:22
  117.1 2.2 %copy-done.1 = bf16[2048,1024]{1,0:T(8,128)(2,1)S(1)} copy-done((bf16[2048,1024]{1,0:T(8,128)(2,1)S(1)}, bf16[2048,1024]{1,0:T(8,128)(2,1)}, u32[]{:S(2)}) %copy-start.1) | copy-done | bytes 4194328
  119.3 2.2 %copy-done.3 = bf16[2048,1024]{1,0:T(8,128)(2,1)S(1)} copy-done((bf16[2048,1024]{1,0:T(8,128)(2,1)S(1)}, bf16[2048,1024]{1,0:T(8,128)(2,1)}, u32[]{:S(2)}) %copy-start.3) | copy-done | bytes 4194328
  121.5 2.2 %copy-done.5 = bf16[1024,2048]{1,0:T(8,128)(2,1)S(1)} copy-done((bf16[1024,2048]{1,0:T(8,128)(2,1)S(1)}, bf16[1024,2048]{1,0:T(8,128)(2,1)}, u32[]{:S(2)}) %copy-start.5) | copy-done | bytes 4194328
  123.7 0.9 copy-done.36
  124.6 3.4 %feed.3 = (bf16[64,2048]{1,0:T(8,128)(2,1)S(1)}, bf16[64,2048]{1,0:T(8,128)(2,1)S(1)}, bf16[64,2048]{1,0:T(8,128)(2,1)S(1)}, bf16[64,2048]{1,0:T(8,128)(2,1)S(1)}) custom-call(bf16[64,2048]{1,0:T(8,128)(2,1)S(1)} %copy-done.36, bf16[64,2048]{1,0:T(8,128)(2,1)S(1)} %collective-permute-done.22.y_ref, bf16[64,2048]{1,0:T(8,128)(2,1)S(1)} %collective-permute-done.23.c_ref, ...), custom_call_target="tpu_custom_call" | custom-call | flops 3221225472 | bytes 12582912 | tf_op jit(solution)/shard_map/feed/pallas_call | solution.py:328
  129.4 3.4 %feed.4 = (bf16[64,2048]{1,0:T(8,128)(2,1)S(1)}, bf16[64,2048]{1,0:T(8,128)(2,1)S(1)}, bf16[64,2048]{1,0:T(8,128)(2,1)S(1)}, bf16[64,2048]{1,0:T(8,128)(2,1)S(1)}) custom-call(bf16[64,2048]{1,0:T(8,128)(2,1)S(1)} %copy-done.37, bf16[64,2048]{1,0:T(8,128)(2,1)S(1)} %collective-permute-done.31.y_ref, bf16[64,2048]{1,0:T(8,128)(2,1)S(1)} %collective-permute-done.32.c_ref, ...), custom_call_target="tpu_custom_call" | custom-call | flops 3221225472 | bytes 12582912 | tf_op jit(solution)/shard_map/feed/pallas_call | solution.py:328
  132.8 0.7 copy-done.24
  134.0 3.7 %feed.5 = (bf16[64,2048]{1,0:T(8,128)(2,1)S(1)}, bf16[64,2048]{1,0:T(8,128)(2,1)S(1)}, bf16[64,2048]{1,0:T(8,128)(2,1)S(1)}, bf16[64,2048]{1,0:T(8,128)(2,1)S(1)}) custom-call(bf16[64,2048]{1,0:T(8,128)(2,1)S(1)} %copy-done.35, bf16[64,2048]{1,0:T(8,128)(2,1)S(1)} %collective-permute-done.40.y_ref, bf16[64,2048]{1,0:T(8,128)(2,1)S(1)} %collective-permute-done.41.c_ref, ...), custom_call_target="tpu_custom_call" | custom-call | flops 3221225472 | bytes 12582912 | tf_op jit(solution)/shard_map/feed/pallas_call | solution.py:328
  138.4 1.4 collective-permute-done.44
  139.8 1.5 collective-permute-start.36
  142.1 1.6 collective-permute-start.27
  143.7 10.9 %collective-permute-done.45.y_ref = bf16[64,2048]{1,0:T(8,128)(2,1)S(1)} collective-permute-done((bf16[64,2048]{1,0:T(8,128)(2,1)S(1)}, bf16[64,2048]{1,0:T(8,128)(2,1)S(1)}, u32[]{:S(2)}, u32[]{:S(2)}) %collective-permute-start.45) | collective-permute-done | bytes 262176 | tf_op jit(solution)/shard_map/ppermute | solution.py:22
  155.3 2.2 %finish.3.refs_0_ = bf16[3,64,2048]{2,1,0:T(8,128)(2,1)} custom-call(s32[3]{0:T(128)} %len_ref.11, f32[64,2048]{1,0:T(8,128)} %get-tuple-element.91.res_ref, bf16[64,2048]{1,0:T(8,128)(2,1)} %copy-done.31, bf16[64,2048]{1,0:T(8,128)(2,1)} %copy-done.55, bf16[64,2048]{1,0:T(8,128)(2,1)} %copy-done.58, f32[1,2048]{1,0:T(1,128)} %bitcast.22), custom_call_target="tpu_custom_call" | custom-call | flops 1310720 | bytes 1572864 | tf_op jit(solution)/shard_map/finish/pallas_call | solution.py:352
  158.3 2.2 %finish.4.refs_0_ = bf16[3,64,2048]{2,1,0:T(8,128)(2,1)} custom-call(s32[3]{0:T(128)} %len_ref.11, f32[64,2048]{1,0:T(8,128)} %get-tuple-element.77.res_ref, bf16[64,2048]{1,0:T(8,128)(2,1)} %copy-done.24, bf16[64,2048]{1,0:T(8,128)(2,1)} %copy-done.54, bf16[64,2048]{1,0:T(8,128)(2,1)} %copy-done.56, ...), custom_call_target="tpu_custom_call", output_to_operand_aliasing={{}: (6, {})} | custom-call | flops 1310720 | bytes 1572864 | tf_op jit(solution)/shard_map/finish/pallas_call | solution.py:352
  161.4 2.2 %finish.5 = bf16[3,64,2048]{2,1,0:T(8,128)(2,1)} custom-call(s32[3]{0:T(128)} %len_ref.11, f32[64,2048]{1,0:T(8,128)} %get-tuple-element.63.res_ref, bf16[64,2048]{1,0:T(8,128)(2,1)} %copy-done.23, bf16[64,2048]{1,0:T(8,128)(2,1)} %copy-done.53, bf16[64,2048]{1,0:T(8,128)(2,1)} %copy-done.57, f32[1,2048]{1,0:T(1,128)} %bitcast.24, ...), custom_call_target="tpu_custom_call", output_to_operand_aliasing={{}: (6, {})} | custom-call | flops 1310720 | bytes 1572864 | tf_op jit(solution)/shard_map/finish/pallas_call | solution.py:352
  (188 shorter events, 17.5 us)
Async XLA Ops:
  0.6 32.8 %copy-start.7 = (bf16[2048,512]{1,0:T(8,128)(2,1)S(1)}, bf16[2048,512]{1,0:T(8,128)(2,1)}, u32[]{:S(2)}) copy-start(bf16[2048,512]{1,0:T(8,128)(2,1)} %wq_ref.5) | copy-start | bytes 6291460
  1.7 12.1 %collective-permute-start.12 = (bf16[1,128,512]{2,1,0:T(8,128)(2,1)S(1)}, bf16[1,128,512]{2,1,0:T(8,128)(2,1)S(1)}, u32[]{:S(2)}, u32[]{:S(2)}) collective-permute-start(bf16[1,128,512]{2,1,0:T(8,128)(2,1)S(1)} %constant_dynamic-slice_fusion), channel_id=1, source_target_pairs={{0,16},{4,20},{8,24},{12,28},{16,0},{20,4},{24,8},{28,12},{1,17},{... | collective-permute-start | bytes 393224 | tf_op jit(solution)/shard_map/ppermute | solution.py:22
  5.8 8.0 %collective-permute-start.11 = (bf16[1,128,512]{2,1,0:T(8,128)(2,1)S(1)}, bf16[1,128,512]{2,1,0:T(8,128)(2,1)S(1)}, u32[]{:S(2)}, u32[]{:S(2)}) collective-permute-start(bf16[1,128,512]{2,1,0:T(8,128)(2,1)S(1)} %constant_dynamic-slice_fusion), channel_id=1, source_target_pairs={{0,8},{4,12},{8,0},{12,4},{16,24},{20,28},{24,16},{28,20},{1,9},{5... | collective-permute-start | bytes 393224 | tf_op jit(solution)/shard_map/ppermute | solution.py:22
  7.4 8.8 %collective-permute-start.13 = (bf16[1,128,512]{2,1,0:T(8,128)(2,1)S(1)}, bf16[1,128,512]{2,1,0:T(8,128)(2,1)S(1)}, u32[]{:S(2)}, u32[]{:S(2)}) collective-permute-start(bf16[1,128,512]{2,1,0:T(8,128)(2,1)S(1)} %constant_dynamic-slice_fusion), channel_id=1, source_target_pairs={{0,24},{4,28},{8,16},{12,20},{16,8},{20,12},{24,0},{28,4},{1,25},{... | collective-permute-start | bytes 393224 | tf_op jit(solution)/shard_map/ppermute | solution.py:22
  7.4 10.3 %collective-permute-start.10 = (bf16[1,128,512]{2,1,0:T(8,128)(2,1)S(1)}, bf16[1,128,512]{2,1,0:T(8,128)(2,1)S(1)}, u32[]{:S(2)}, u32[]{:S(2)}) collective-permute-start(bf16[1,128,512]{2,1,0:T(8,128)(2,1)S(1)} %constant_dynamic-slice_fusion), channel_id=1, source_target_pairs={{0,4},{4,0},{8,12},{12,8},{16,20},{20,16},{24,28},{28,24},{1,5},{5... | collective-permute-start | bytes 393224 | tf_op jit(solution)/shard_map/ppermute | solution.py:22
  11.3 30.2 %copy-start.20 = (bf16[64,2048]{1,0:T(8,128)(2,1)S(1)}, bf16[64,2048]{1,0:T(8,128)(2,1)}, u32[]{:S(2)}) copy-start(bf16[64,2048]{1,0:T(8,128)(2,1)} %get-tuple-element.51.refs_1_.own_ref) | copy-start | bytes 786436
  11.3 8.1 %collective-permute-start = (bf16[64,2048]{1,0:T(8,128)(2,1)}, bf16[64,2048]{1,0:T(8,128)(2,1)S(1)}, u32[]{:S(2)}, u32[]{:S(2)}) collective-permute-start(bf16[64,2048]{1,0:T(8,128)(2,1)} %get-tuple-element.52.refs_2_.own_ref), channel_id=1, source_target_pairs={{0,2},{1,3},{2,0},{3,1},{4,6},{5,7},{6,4},{7,5},{8,10},{9,11},{10,... | collective-permute-start | bytes 786440 | tf_op jit(solution)/shard_map/ppermute | solution.py:22
  13.8 19.3 %collective-permute-start.3 = (bf16[2048,256]{1,0:T(8,128)(2,1)}, bf16[2048,256]{1,0:T(8,128)(2,1)S(1)}, u32[]{:S(2)}, u32[]{:S(2)}) collective-permute-start(bf16[2048,256]{1,0:T(8,128)(2,1)} %mine_ref.5), channel_id=1, source_target_pairs={{0,1},{1,0},{2,3},{3,2},{4,5},{5,4},{6,7},{7,6},{8,9},{9,8},{10,11... | collective-permute-start | bytes 3145736 | tf_op jit(solution)/shard_map/ppermute | solution.py:22
  13.8 11.3 %collective-permute-start.4 = (bf16[64,2048]{1,0:T(8,128)(2,1)}, bf16[64,2048]{1,0:T(8,128)(2,1)S(1)}, u32[]{:S(2)}, u32[]{:S(2)}) collective-permute-start(bf16[64,2048]{1,0:T(8,128)(2,1)} %get-tuple-element.51.refs_1_.own_ref), channel_id=1, source_target_pairs={{0,2},{1,3},{2,0},{3,1},{4,6},{5,7},{6,4},{7,5},{8,10},{9,11},{10,... | collective-permute-start | bytes 786440 | tf_op jit(solution)/shard_map/ppermute | solution.py:22
  16.1 13.7 %collective-permute-start.7 = (bf16[64,2048]{1,0:T(8,128)(2,1)}, bf16[64,2048]{1,0:T(8,128)(2,1)S(1)}, u32[]{:S(2)}, u32[]{:S(2)}) collective-permute-start(bf16[64,2048]{1,0:T(8,128)(2,1)} %get-tuple-element.50.refs_0_.own_ref), channel_id=1, source_target_pairs={{0,2},{1,3},{2,0},{3,1},{4,6},{5,7},{6,4},{7,5},{8,10},{9,11},{10,... | collective-permute-start | bytes 786440 | tf_op jit(solution)/shard_map/ppermute | solution.py:22
  17.7 29.8 %copy-start.16 = (bf16[2,128,512]{2,1,0:T(8,128)(2,1)}, bf16[2,128,512]{2,1,0:T(8,128)(2,1)S(1)}, u32[]{:S(2)}) copy-start(bf16[2,128,512]{2,1,0:T(8,128)(2,1)S(1)} %constant_dynamic-update-slice_fusion.refs_1_) | copy-start | bytes 786436
  17.7 12.6 %collective-permute-start.15 = (bf16[2,128,512]{2,1,0:T(8,128)(2,1)S(1)}, bf16[2,128,512]{2,1,0:T(8,128)(2,1)S(1)}, u32[]{:S(2)}, u32[]{:S(2)}) collective-permute-start(bf16[2,128,512]{2,1,0:T(8,128)(2,1)S(1)} %constant_dynamic-update-slice_fusion.refs_1_), channel_id=1, source_target_pairs={{0,4},{4,0},{8,12},{12,8},{16,20},{20,16},{24,28},{28,24},{1,5},{5... | collective-permute-start | bytes 786440 | tf_op jit(solution)/shard_map/ppermute | solution.py:22
  19.4 10.3 %collective-permute-start.14 = (bf16[1,128,512]{2,1,0:T(8,128)(2,1)S(1)}, bf16[1,128,512]{2,1,0:T(8,128)(2,1)S(1)}, u32[]{:S(2)}, u32[]{:S(2)}) collective-permute-start(bf16[1,128,512]{2,1,0:T(8,128)(2,1)S(1)} %collective-permute-done.11), channel_id=1, source_target_pairs={{0,4},{4,0},{8,12},{12,8},{16,20},{20,16},{24,28},{28,24},{1,5},{5... | collective-permute-start | bytes 393224 | tf_op jit(solution)/shard_map/ppermute | solution.py:22
  25.1 5.4 %collective-permute-start.5 = (bf16[64,2048]{1,0:T(8,128)(2,1)}, bf16[64,2048]{1,0:T(8,128)(2,1)S(1)}, u32[]{:S(2)}, u32[]{:S(2)}) collective-permute-start(bf16[64,2048]{1,0:T(8,128)(2,1)} %get-tuple-element.51.refs_1_.own_ref), channel_id=1, source_target_pairs={{0,1},{1,0},{2,3},{3,2},{4,5},{5,4},{6,7},{7,6},{8,9},{9,8},{10,11... | collective-permute-start | bytes 786440 | tf_op jit(solution)/shard_map/ppermute | solution.py:22
  29.8 2.0 %collective-permute-start.8 = (bf16[64,2048]{1,0:T(8,128)(2,1)}, bf16[64,2048]{1,0:T(8,128)(2,1)S(1)}, u32[]{:S(2)}, u32[]{:S(2)}) collective-permute-start(bf16[64,2048]{1,0:T(8,128)(2,1)} %get-tuple-element.50.refs_0_.own_ref), channel_id=1, source_target_pairs={{0,1},{1,0},{2,3},{3,2},{4,5},{5,4},{6,7},{7,6},{8,9},{9,8},{10,11... | collective-permute-start | bytes 786440 | tf_op jit(solution)/shard_map/ppermute | solution.py:22
  29.8 2.2 %collective-permute-start.6 = (bf16[64,2048]{1,0:T(8,128)(2,1)S(1)}, bf16[64,2048]{1,0:T(8,128)(2,1)S(1)}, u32[]{:S(2)}, u32[]{:S(2)}) collective-permute-start(bf16[64,2048]{1,0:T(8,128)(2,1)S(1)} %collective-permute-done.4.y_ref), channel_id=1, source_target_pairs={{0,1},{1,0},{2,3},{3,2},{4,5},{5,4},{6,7},{7,6},{8,9},{9,8},{10,11... | collective-permute-start | bytes 786440 | tf_op jit(solution)/shard_map/ppermute | solution.py:22
  30.3 2.0 %collective-permute-start.9 = (bf16[64,2048]{1,0:T(8,128)(2,1)S(1)}, bf16[64,2048]{1,0:T(8,128)(2,1)S(1)}, u32[]{:S(2)}, u32[]{:S(2)}) collective-permute-start(bf16[64,2048]{1,0:T(8,128)(2,1)S(1)} %collective-permute-done.7.y_ref), channel_id=1, source_target_pairs={{0,1},{1,0},{2,3},{3,2},{4,5},{5,4},{6,7},{7,6},{8,9},{9,8},{10,11... | collective-permute-start | bytes 786440 | tf_op jit(solution)/shard_map/ppermute | solution.py:22
  30.5 14.4 %collective-permute-start.1 = (bf16[64,2048]{1,0:T(8,128)(2,1)}, bf16[64,2048]{1,0:T(8,128)(2,1)S(1)}, u32[]{:S(2)}, u32[]{:S(2)}) collective-permute-start(bf16[64,2048]{1,0:T(8,128)(2,1)} %get-tuple-element.52.refs_2_.own_ref), channel_id=1, source_target_pairs={{0,1},{1,0},{2,3},{3,2},{4,5},{5,4},{6,7},{7,6},{8,9},{9,8},{10,11... | collective-permute-start | bytes 786440 | tf_op jit(solution)/shard_map/ppermute | solution.py:22
  31.8 15.6 %collective-permute-start.16 = (bf16[3,128,512]{2,1,0:T(8,128)(2,1)S(1)}, bf16[3,128,512]{2,1,0:T(8,128)(2,1)S(1)}, u32[]{:S(2)}, u32[]{:S(2)}) collective-permute-start(bf16[3,128,512]{2,1,0:T(8,128)(2,1)S(1)} %pad_maximum_fusion.refs_0_), channel_id=1, source_target_pairs={{0,1},{1,0},{2,3},{3,2},{4,5},{5,4},{6,7},{7,6},{8,9},{9,8},{10,11... | collective-permute-start | bytes 1179656 | tf_op jit(solution)/shard_map/ppermute | solution.py:22
  32.0 12.9 %collective-permute-start.2 = (bf16[64,2048]{1,0:T(8,128)(2,1)S(1)}, bf16[64,2048]{1,0:T(8,128)(2,1)S(1)}, u32[]{:S(2)}, u32[]{:S(2)}) collective-permute-start(bf16[64,2048]{1,0:T(8,128)(2,1)S(1)} %collective-permute-done.y_ref), channel_id=1, source_target_pairs={{0,1},{1,0},{2,3},{3,2},{4,5},{5,4},{6,7},{7,6},{8,9},{9,8},{10,11... | collective-permute-start | bytes 786440 | tf_op jit(solution)/shard_map/ppermute | solution.py:22
  32.3 15.1 %collective-permute-start.18 = (bf16[3,128,512]{2,1,0:T(8,128)(2,1)S(1)}, bf16[3,128,512]{2,1,0:T(8,128)(2,1)S(1)}, u32[]{:S(2)}, u32[]{:S(2)}) collective-permute-start(bf16[3,128,512]{2,1,0:T(8,128)(2,1)S(1)} %constant_dynamic-update-slice_fusion.2.refs_2_), channel_id=1, source_target_pairs={{0,1},{1,0},{2,3},{3,2},{4,5},{5,4},{6,7},{7,6},{8,9},{9,8},{10,11... | collective-permute-start | bytes 1179656 | tf_op jit(solution)/shard_map/ppermute | solution.py:22
  33.0 14.4 %collective-permute-start.17 = (bf16[2,128,512]{2,1,0:T(8,128)(2,1)S(1)}, bf16[2,128,512]{2,1,0:T(8,128)(2,1)S(1)}, u32[]{:S(2)}, u32[]{:S(2)}) collective-permute-start(bf16[2,128,512]{2,1,0:T(8,128)(2,1)S(1)} %constant_dynamic-update-slice_fusion.refs_1_), channel_id=1, source_target_pairs={{0,1},{1,0},{2,3},{3,2},{4,5},{5,4},{6,7},{7,6},{8,9},{9,8},{10,11... | collective-permute-start | bytes 786440 | tf_op jit(solution)/shard_map/ppermute | solution.py:22
  44.8 8.5 %copy-start.40 = (bf16[256,256]{1,0:T(8,128)(2,1)}, bf16[256,256]{1,0:T(8,128)(2,1)S(1)}, u32[]{:S(2)}) copy-start(bf16[256,256]{1,0:T(8,128)(2,1)S(1)} %get-tuple-element.71.k_ref) | copy-start | bytes 393220
  44.8 8.5 %copy-start.42 = (bf16[256,256]{1,0:T(8,128)(2,1)}, bf16[256,256]{1,0:T(8,128)(2,1)S(1)}, u32[]{:S(2)}) copy-start(bf16[256,256]{1,0:T(8,128)(2,1)S(1)} %get-tuple-element.72.v_ref) | copy-start | bytes 393220
  47.4 12.1 %copy-start.9 = (bf16[512,2048]{1,0:T(8,128)(2,1)S(1)}, bf16[512,2048]{1,0:T(8,128)(2,1)}, u32[]{:S(2)}) copy-start(bf16[512,2048]{1,0:T(8,128)(2,1)} %wo_ref.5) | copy-start | bytes 6291460
  47.4 8.1 %copy-start.18 = (bf16[2,128,512]{2,1,0:T(8,128)(2,1)}, bf16[2,128,512]{2,1,0:T(8,128)(2,1)S(1)}, u32[]{:S(2)}) copy-start(bf16[2,128,512]{2,1,0:T(8,128)(2,1)S(1)} %collective-permute-done.17.refs_4_) | copy-start | bytes 786436
  47.4 5.8 %copy-start.12 = (bf16[3,128,512]{2,1,0:T(8,128)(2,1)}, bf16[3,128,512]{2,1,0:T(8,128)(2,1)S(1)}, u32[]{:S(2)}) copy-start(bf16[3,128,512]{2,1,0:T(8,128)(2,1)S(1)} %collective-permute-done.16.refs_3_) | copy-start | bytes 1179652
  47.5 8.0 %copy-start.14 = (bf16[3,128,512]{2,1,0:T(8,128)(2,1)}, bf16[3,128,512]{2,1,0:T(8,128)(2,1)S(1)}, u32[]{:S(2)}) copy-start(bf16[3,128,512]{2,1,0:T(8,128)(2,1)S(1)} %collective-permute-done.18.refs_5_) | copy-start | bytes 1179652
  55.4 23.7 %collective-permute-start.20 = (bf16[64,2048]{1,0:T(8,128)(2,1)}, bf16[64,2048]{1,0:T(8,128)(2,1)}, u32[]{:S(2)}, u32[]{:S(2)}) collective-permute-start(bf16[64,2048]{1,0:T(8,128)(2,1)} %get-tuple-element.62), channel_id=1, source_target_pairs={{0,1},{1,0},{2,3},{3,2},{4,5},{5,4},{6,7},{7,6},{8,9},{9,8},{10,11... | collective-permute-start | bytes 786440 | tf_op jit(solution)/shard_map/ppermute | solution.py:22
  59.2 23.7 %collective-permute-start.19 = (bf16[64,2048]{1,0:T(8,128)(2,1)}, bf16[64,2048]{1,0:T(8,128)(2,1)S(1)}, u32[]{:S(2)}, u32[]{:S(2)}) collective-permute-start(bf16[64,2048]{1,0:T(8,128)(2,1)} %copy-done.52), channel_id=1, source_target_pairs={{0,1},{1,0},{2,3},{3,2},{4,5},{5,4},{6,7},{7,6},{8,9},{9,8},{10,11... | collective-permute-start | bytes 786440 | tf_op jit(solution)/shard_map/ppermute | solution.py:22
  66.2 7.1 %copy-start.26 = (bf16[512,256]{1,0:T(8,128)(2,1)S(1)}, bf16[512,256]{1,0:T(8,128)(2,1)}, u32[]{:S(2)}) copy-start(bf16[512,256]{1,0:T(8,128)(2,1)} %copy-done.25) | copy-start | bytes 786436
  66.2 7.1 %copy-start.39 = (bf16[256,256]{1,0:T(8,128)(2,1)S(1)}, bf16[256,256]{1,0:T(8,128)(2,1)}, u32[]{:S(2)}) copy-start(bf16[256,256]{1,0:T(8,128)(2,1)} %copy-done.38) | copy-start | bytes 393220
  66.2 13.4 %copy-start.28 = (bf16[64,2048]{1,0:T(8,128)(2,1)S(1)}, bf16[64,2048]{1,0:T(8,128)(2,1)}, u32[]{:S(2)}) copy-start(bf16[64,2048]{1,0:T(8,128)(2,1)} %copy-done.27) | copy-start | bytes 786436
  72.7 21.7 %collective-permute-start.28 = (bf16[64,2048]{1,0:T(8,128)(2,1)}, bf16[64,2048]{1,0:T(8,128)(2,1)}, u32[]{:S(2)}, u32[]{:S(2)}) collective-permute-start(bf16[64,2048]{1,0:T(8,128)(2,1)} %get-tuple-element.74), channel_id=1, source_target_pairs={{0,1},{1,0},{2,3},{3,2},{4,5},{5,4},{6,7},{7,6},{8,9},{9,8},{10,11... | collective-permute-start | bytes 786440 | tf_op jit(solution)/shard_map/ppermute | solution.py:22
  72.9 7.7 %collective-permute-start.29 = (bf16[64,2048]{1,0:T(8,128)(2,1)S(1)}, bf16[64,2048]{1,0:T(8,128)(2,1)S(1)}, u32[]{:S(2)}, u32[]{:S(2)}) collective-permute-start(bf16[64,2048]{1,0:T(8,128)(2,1)S(1)} %get-tuple-element.76), channel_id=1, source_target_pairs={{0,1},{1,0},{2,3},{3,2},{4,5},{5,4},{6,7},{7,6},{8,9},{9,8},{10,11... | collective-permute-start | bytes 786440 | tf_op jit(solution)/shard_map/ppermute | solution.py:22
  79.0 21.1 %collective-permute-start.37 = (bf16[64,2048]{1,0:T(8,128)(2,1)}, bf16[64,2048]{1,0:T(8,128)(2,1)S(1)}, u32[]{:S(2)}, u32[]{:S(2)}) collective-permute-start(bf16[64,2048]{1,0:T(8,128)(2,1)} %get-tuple-element.88), channel_id=1, source_target_pairs={{0,1},{1,0},{2,3},{3,2},{4,5},{5,4},{6,7},{7,6},{8,9},{9,8},{10,11... | collective-permute-start | bytes 786440 | tf_op jit(solution)/shard_map/ppermute | solution.py:22
  79.2 3.1 %collective-permute-start.38 = (bf16[64,2048]{1,0:T(8,128)(2,1)S(1)}, bf16[64,2048]{1,0:T(8,128)(2,1)S(1)}, u32[]{:S(2)}, u32[]{:S(2)}) collective-permute-start(bf16[64,2048]{1,0:T(8,128)(2,1)S(1)} %get-tuple-element.90), channel_id=1, source_target_pairs={{0,1},{1,0},{2,3},{3,2},{4,5},{5,4},{6,7},{7,6},{8,9},{9,8},{10,11... | collective-permute-start | bytes 786440 | tf_op jit(solution)/shard_map/ppermute | solution.py:22
  80.6 9.2 %collective-permute-start.21 = (bf16[64,2048]{1,0:T(8,128)(2,1)S(1)}, bf16[64,2048]{1,0:T(8,128)(2,1)S(1)}, u32[]{:S(2)}, u32[]{:S(2)}) collective-permute-start(bf16[64,2048]{1,0:T(8,128)(2,1)S(1)} %add_convert_fusion.5), channel_id=1, source_target_pairs={{0,2},{1,3},{2,0},{3,1},{4,6},{5,7},{6,4},{7,5},{8,10},{9,11},{10,... | collective-permute-start | bytes 786440 | tf_op jit(solution)/shard_map/ppermute | solution.py:22
  82.3 13.2 %collective-permute-start.30 = (bf16[64,2048]{1,0:T(8,128)(2,1)S(1)}, bf16[64,2048]{1,0:T(8,128)(2,1)S(1)}, u32[]{:S(2)}, u32[]{:S(2)}) collective-permute-start(bf16[64,2048]{1,0:T(8,128)(2,1)S(1)} %add_convert_fusion.3), channel_id=1, source_target_pairs={{0,2},{1,3},{2,0},{3,1},{4,6},{5,7},{6,4},{7,5},{8,10},{9,11},{10,... | collective-permute-start | bytes 786440 | tf_op jit(solution)/shard_map/ppermute | solution.py:22
  82.9 6.9 %copy-start.60 = (bf16[64,2048]{1,0:T(8,128)(2,1)}, bf16[64,2048]{1,0:T(8,128)(2,1)S(1)}, u32[]{:S(2)}) copy-start(bf16[64,2048]{1,0:T(8,128)(2,1)S(1)} %collective-permute-done.19.c_ref) | copy-start | bytes 786436
  82.9 18.1 %collective-permute-start.39 = (bf16[64,2048]{1,0:T(8,128)(2,1)S(1)}, bf16[64,2048]{1,0:T(8,128)(2,1)S(1)}, u32[]{:S(2)}, u32[]{:S(2)}) collective-permute-start(bf16[64,2048]{1,0:T(8,128)(2,1)S(1)} %add_convert_fusion.1), channel_id=1, source_target_pairs={{0,2},{1,3},{2,0},{3,1},{4,6},{5,7},{6,4},{7,5},{8,10},{9,11},{10,... | collective-permute-start | bytes 786440 | tf_op jit(solution)/shard_map/ppermute | solution.py:22
  92.9 13.7 %collective-permute-start.22 = (bf16[64,2048]{1,0:T(8,128)(2,1)}, bf16[64,2048]{1,0:T(8,128)(2,1)S(1)}, u32[]{:S(2)}, u32[]{:S(2)}) collective-permute-start(bf16[64,2048]{1,0:T(8,128)(2,1)} %get-tuple-element.64.own_ref), channel_id=1, source_target_pairs={{0,2},{1,3},{2,0},{3,1},{4,6},{5,7},{6,4},{7,5},{8,10},{9,11},{10,... | collective-permute-start | bytes 786440 | tf_op jit(solution)/shard_map/ppermute | solution.py:22
  94.4 12.7 %collective-permute-start.23 = (bf16[64,2048]{1,0:T(8,128)(2,1)}, bf16[64,2048]{1,0:T(8,128)(2,1)S(1)}, u32[]{:S(2)}, u32[]{:S(2)}) collective-permute-start(bf16[64,2048]{1,0:T(8,128)(2,1)} %get-tuple-element.64.own_ref), channel_id=1, source_target_pairs={{0,1},{1,0},{2,3},{3,2},{4,5},{5,4},{6,7},{7,6},{8,9},{9,8},{10,11... | collective-permute-start | bytes 786440 | tf_op jit(solution)/shard_map/ppermute | solution.py:22
  98.6 13.7 %collective-permute-start.31 = (bf16[64,2048]{1,0:T(8,128)(2,1)}, bf16[64,2048]{1,0:T(8,128)(2,1)S(1)}, u32[]{:S(2)}, u32[]{:S(2)}) collective-permute-start(bf16[64,2048]{1,0:T(8,128)(2,1)} %get-tuple-element.78.own_ref), channel_id=1, source_target_pairs={{0,2},{1,3},{2,0},{3,1},{4,6},{5,7},{6,4},{7,5},{8,10},{9,11},{10,... | collective-permute-start | bytes 786440 | tf_op jit(solution)/shard_map/ppermute | solution.py:22
  101.7 27.0 %copy-start.37 = (bf16[64,2048]{1,0:T(8,128)(2,1)S(1)}, bf16[64,2048]{1,0:T(8,128)(2,1)}, u32[]{:S(2)}) copy-start(bf16[64,2048]{1,0:T(8,128)(2,1)} %get-tuple-element.78.own_ref) | copy-start | bytes 786436
  104.2 12.9 %collective-permute-start.40 = (bf16[64,2048]{1,0:T(8,128)(2,1)}, bf16[64,2048]{1,0:T(8,128)(2,1)S(1)}, u32[]{:S(2)}, u32[]{:S(2)}) collective-permute-start(bf16[64,2048]{1,0:T(8,128)(2,1)} %get-tuple-element.92.own_ref), channel_id=1, source_target_pairs={{0,2},{1,3},{2,0},{3,1},{4,6},{5,7},{6,4},{7,5},{8,10},{9,11},{10,... | collective-permute-start | bytes 786440 | tf_op jit(solution)/shard_map/ppermute | solution.py:22
  106.6 10.4 %collective-permute-start.24 = (bf16[64,2048]{1,0:T(8,128)(2,1)S(1)}, bf16[64,2048]{1,0:T(8,128)(2,1)S(1)}, u32[]{:S(2)}, u32[]{:S(2)}) collective-permute-start(bf16[64,2048]{1,0:T(8,128)(2,1)S(1)} %collective-permute-done.22.y_ref), channel_id=1, source_target_pairs={{0,1},{1,0},{2,3},{3,2},{4,5},{5,4},{6,7},{7,6},{8,9},{9,8},{10,11... | collective-permute-start | bytes 786440 | tf_op jit(solution)/shard_map/ppermute | solution.py:22
  106.6 22.0 %collective-permute-start.32 = (bf16[64,2048]{1,0:T(8,128)(2,1)}, bf16[64,2048]{1,0:T(8,128)(2,1)S(1)}, u32[]{:S(2)}, u32[]{:S(2)}) collective-permute-start(bf16[64,2048]{1,0:T(8,128)(2,1)} %get-tuple-element.78.own_ref), channel_id=1, source_target_pairs={{0,1},{1,0},{2,3},{3,2},{4,5},{5,4},{6,7},{7,6},{8,9},{9,8},{10,11... | collective-permute-start | bytes 786440 | tf_op jit(solution)/shard_map/ppermute | solution.py:22
  107.2 26.9 %collective-permute-start.41 = (bf16[64,2048]{1,0:T(8,128)(2,1)}, bf16[64,2048]{1,0:T(8,128)(2,1)S(1)}, u32[]{:S(2)}, u32[]{:S(2)}) collective-permute-start(bf16[64,2048]{1,0:T(8,128)(2,1)} %get-tuple-element.92.own_ref), channel_id=1, source_target_pairs={{0,1},{1,0},{2,3},{3,2},{4,5},{5,4},{6,7},{7,6},{8,9},{9,8},{10,11... | collective-permute-start | bytes 786440 | tf_op jit(solution)/shard_map/ppermute | solution.py:22
  112.3 16.5 %collective-permute-start.33 = (bf16[64,2048]{1,0:T(8,128)(2,1)S(1)}, bf16[64,2048]{1,0:T(8,128)(2,1)S(1)}, u32[]{:S(2)}, u32[]{:S(2)}) collective-permute-start(bf16[64,2048]{1,0:T(8,128)(2,1)S(1)} %collective-permute-done.31.y_ref), channel_id=1, source_target_pairs={{0,1},{1,0},{2,3},{3,2},{4,5},{5,4},{6,7},{7,6},{8,9},{9,8},{10,11... | collective-permute-start | bytes 786440 | tf_op jit(solution)/shard_map/ppermute | solution.py:22
  117.1 17.0 %collective-permute-start.42 = (bf16[64,2048]{1,0:T(8,128)(2,1)S(1)}, bf16[64,2048]{1,0:T(8,128)(2,1)S(1)}, u32[]{:S(2)}, u32[]{:S(2)}) collective-permute-start(bf16[64,2048]{1,0:T(8,128)(2,1)S(1)} %collective-permute-done.40.y_ref), channel_id=1, source_target_pairs={{0,1},{1,0},{2,3},{3,2},{4,5},{5,4},{6,7},{7,6},{8,9},{9,8},{10,11... | collective-permute-start | bytes 786440 | tf_op jit(solution)/shard_map/ppermute | solution.py:22
  124.6 4.8 %copy-start.6 = (bf16[1024,2048]{1,0:T(8,128)(2,1)S(1)}, bf16[1024,2048]{1,0:T(8,128)(2,1)}, u32[]{:S(2)}) copy-start(bf16[1024,2048]{1,0:T(8,128)(2,1)} %down_ref.5) | copy-start | bytes 12582916
  128.0 4.8 %copy-start.23 = (bf16[64,2048]{1,0:T(8,128)(2,1)}, bf16[64,2048]{1,0:T(8,128)(2,1)S(1)}, u32[]{:S(2)}) copy-start(bf16[64,2048]{1,0:T(8,128)(2,1)S(1)} %get-tuple-element.65.own_ref) | copy-start | bytes 786436
  128.0 32.5 %collective-permute-start.25 = (bf16[64,2048]{1,0:T(8,128)(2,1)S(1)}, bf16[64,2048]{1,0:T(8,128)(2,1)S(1)}, u32[]{:S(2)}, u32[]{:S(2)}) collective-permute-start(bf16[64,2048]{1,0:T(8,128)(2,1)S(1)} %get-tuple-element.66), channel_id=1, source_target_pairs={{0,1},{1,0},{2,3},{3,2},{4,5},{5,4},{6,7},{7,6},{8,9},{9,8},{10,11... | collective-permute-start | bytes 786440 | tf_op jit(solution)/shard_map/ppermute | solution.py:22
  128.6 5.4 %copy-start.35 = (bf16[64,2048]{1,0:T(8,128)(2,1)S(1)}, bf16[64,2048]{1,0:T(8,128)(2,1)}, u32[]{:S(2)}) copy-start(bf16[64,2048]{1,0:T(8,128)(2,1)} %get-tuple-element.92.own_ref) | copy-start | bytes 786436
  128.6 12.8 %collective-permute-start.26 = (bf16[64,2048]{1,0:T(8,128)(2,1)S(1)}, bf16[64,2048]{1,0:T(8,128)(2,1)S(1)}, u32[]{:S(2)}, u32[]{:S(2)}) collective-permute-start(bf16[64,2048]{1,0:T(8,128)(2,1)S(1)} %get-tuple-element.68), channel_id=1, source_target_pairs={{0,1},{1,0},{2,3},{3,2},{4,5},{5,4},{6,7},{7,6},{8,9},{9,8},{10,11... | collective-permute-start | bytes 786440 | tf_op jit(solution)/shard_map/ppermute | solution.py:22
  133.5 24.0 %collective-permute-start.34 = (bf16[64,2048]{1,0:T(8,128)(2,1)S(1)}, bf16[64,2048]{1,0:T(8,128)(2,1)S(1)}, u32[]{:S(2)}, u32[]{:S(2)}) collective-permute-start(bf16[64,2048]{1,0:T(8,128)(2,1)S(1)} %get-tuple-element.80), channel_id=1, source_target_pairs={{0,1},{1,0},{2,3},{3,2},{4,5},{5,4},{6,7},{7,6},{8,9},{9,8},{10,11... | collective-permute-start | bytes 786440 | tf_op jit(solution)/shard_map/ppermute | solution.py:22
  134.0 4.3 %collective-permute-start.35 = (bf16[64,2048]{1,0:T(8,128)(2,1)S(1)}, bf16[64,2048]{1,0:T(8,128)(2,1)S(1)}, u32[]{:S(2)}, u32[]{:S(2)}) collective-permute-start(bf16[64,2048]{1,0:T(8,128)(2,1)S(1)} %get-tuple-element.82), channel_id=1, source_target_pairs={{0,1},{1,0},{2,3},{3,2},{4,5},{5,4},{6,7},{7,6},{8,9},{9,8},{10,11... | collective-permute-start | bytes 786440 | tf_op jit(solution)/shard_map/ppermute | solution.py:22
  137.7 4.4 %collective-permute-start.43 = (bf16[64,2048]{1,0:T(8,128)(2,1)S(1)}, bf16[64,2048]{1,0:T(8,128)(2,1)S(1)}, u32[]{:S(2)}, u32[]{:S(2)}) collective-permute-start(bf16[64,2048]{1,0:T(8,128)(2,1)S(1)} %get-tuple-element.94), channel_id=1, source_target_pairs={{0,1},{1,0},{2,3},{3,2},{4,5},{5,4},{6,7},{7,6},{8,9},{9,8},{10,11... | collective-permute-start | bytes 786440 | tf_op jit(solution)/shard_map/ppermute | solution.py:22
  138.3 1.5 collective-permute-start.44
  139.8 17.7 %collective-permute-start.36 = (bf16[64,2048]{1,0:T(8,128)(2,1)S(1)}, bf16[64,2048]{1,0:T(8,128)(2,1)S(1)}, u32[]{:S(2)}, u32[]{:S(2)}) collective-permute-start(bf16[64,2048]{1,0:T(8,128)(2,1)S(1)} %add_convert_fusion.2), channel_id=1, source_target_pairs={{0,2},{1,3},{2,0},{3,1},{4,6},{5,7},{6,4},{7,5},{8,10},{9,11},{10,... | collective-permute-start | bytes 786440 | tf_op jit(solution)/shard_map/ppermute | solution.py:22
  141.4 13.1 %collective-permute-start.45 = (bf16[64,2048]{1,0:T(8,128)(2,1)S(1)}, bf16[64,2048]{1,0:T(8,128)(2,1)S(1)}, u32[]{:S(2)}, u32[]{:S(2)}) collective-permute-start(bf16[64,2048]{1,0:T(8,128)(2,1)S(1)} %add_convert_fusion), channel_id=1, source_target_pairs={{0,2},{1,3},{2,0},{3,1},{4,6},{5,7},{6,4},{7,5},{8,10},{9,11},{10,... | collective-permute-start | bytes 786440 | tf_op jit(solution)/shard_map/ppermute | solution.py:22
  142.1 12.5 %copy-start.55 = (bf16[64,2048]{1,0:T(8,128)(2,1)}, bf16[64,2048]{1,0:T(8,128)(2,1)S(1)}, u32[]{:S(2)}) copy-start(bf16[64,2048]{1,0:T(8,128)(2,1)S(1)} %collective-permute-done.43.c_ref) | copy-start | bytes 786436
  142.1 18.5 %collective-permute-start.27 = (bf16[64,2048]{1,0:T(8,128)(2,1)S(1)}, bf16[64,2048]{1,0:T(8,128)(2,1)S(1)}, u32[]{:S(2)}, u32[]{:S(2)}) collective-permute-start(bf16[64,2048]{1,0:T(8,128)(2,1)S(1)} %add_convert_fusion.4), channel_id=1, source_target_pairs={{0,2},{1,3},{2,0},{3,1},{4,6},{5,7},{6,4},{7,5},{8,10},{9,11},{10,... | collective-permute-start | bytes 786440 | tf_op jit(solution)/shard_map/ppermute | solution.py:22
  (46 other events, 72.5 us)

commit v2 on v1

v2 whole, which is shorter than its diff:
```python
import functools
import math

import jax
import jax.numpy as jnp
from jax import lax
from jax.experimental import pallas as pl
from jax.experimental.pallas import tpu as pltpu
from jax.sharding import PartitionSpec as P

EPS = 1e-06
INV_ROOT = 1.0 / math.sqrt(2.0)
BF16 = jnp.bfloat16
F32 = jnp.float32
ON_CHIP = pl.BlockSpec(memory_space=pltpu.VMEM)
SCALARS = pl.BlockSpec(memory_space=pltpu.SMEM)
ANYWHERE = pl.BlockSpec(memory_space=pl.ANY)
BLOCK_XOR = (0, 2, 1, 3)
SPLIT = 2
TILE = 256


def exchange(value, axis, flip):
    return lax.ppermute(value, axis, [(i, i ^ flip) for i in range(lax.axis_size(axis))])


def after(value, *earlier):
    return lax.optimization_barrier((value, *earlier))[0]


def normed(values, gain):
    scale = lax.rsqrt(jnp.mean(values * values, axis=-1, keepdims=True) + EPS)
    return values * scale * gain


def rotated(values, cos, sin):
    half = values.shape[-1] // 2
    first, second = values[:, :half], values[:, half:]
    return jnp.concatenate(
        [first * cos - second * sin, second * cos + first * sin], axis=-1
    )


def params(mib):
    return pltpu.CompilerParams(vmem_limit_bytes=mib << 20)


def cost(flops, moved, exps=0):
    return pl.CostEstimate(flops=1, bytes_accessed=1, transcendentals=0)


def active_rows(hidden, gain):
    return normed(hidden.astype(F32), gain).astype(BF16)


def base_kernel(hidden_ref, gains_ref, left_ref, right_ref, out_ref):
    for r in range(hidden_ref.shape[0]):
        hidden = hidden_ref[r]
        active = active_rows(hidden, gains_ref[0:1, :])
        mid = lax.dot_general(
            active, left_ref[...], (((1,), (1,)), ((), ())), preferred_element_type=F32
        ).astype(BF16)
        low = jnp.dot(mid, right_ref[...], preferred_element_type=F32)
        out_ref[r] = hidden.astype(F32) + active.astype(F32) + normed(low, gains_ref[1:2, :])


def make_base(hidden, gains, left_t, right):
    return pl.pallas_call(
        base_kernel,
        out_shape=jax.ShapeDtypeStruct(hidden.shape, F32),
        in_specs=[ON_CHIP] * 4,
        out_specs=ON_CHIP,
        cost_estimate=cost(4 * hidden.size * left_t.shape[0], 8 * hidden.size),
        compiler_params=params(8),
        name="base",
    )(hidden, gains, left_t, right)


def project_kernel(
    len_ref,
    hidden_ref,
    y_ref,
    c_ref,
    d_ref,
    gains_ref,
    wq_ref,
    mine_ref,
    other_ref,
    head_gains_ref,
    cos_ref,
    sin_ref,
    page_ref,
    q_ref,
    kv_ref,
):
    member = lax.axis_index("mlp")
    reqs, part, _ = hidden_ref.shape
    head = head_gains_ref.shape[-1]
    qgain, kgain = head_gains_ref[0:1, :], head_gains_ref[1:2, :]
    starts = [pl.multiple_of((member ^ flip) * part, part) for flip in BLOCK_XOR]
    cos = jnp.concatenate([cos_ref[pl.ds(s, part), :] for s in starts], axis=0)
    sin = jnp.concatenate([sin_ref[pl.ds(s, part), :] for s in starts], axis=0)
    holds_keys = member % 2 == 0
    heads = wq_ref.shape[1] // head
    for r in range(reqs):
        rows = jnp.concatenate(
            [
                active_rows(ref[r], gains_ref[0:1, :])
                for ref in (hidden_ref, y_ref, c_ref, d_ref)
            ],
            axis=0,
        )
        count = rows.shape[0]
        mine = jnp.dot(rows, mine_ref[...], preferred_element_type=F32)
        other = jnp.dot(rows, other_ref[...], preferred_element_type=F32)
        keys = rotated(normed(jnp.where(holds_keys, mine, other), kgain), cos, sin)
        values = normed(jnp.where(holds_keys, other, mine), 1.0)
        kv_ref[r, :, :head] = keys.astype(BF16)
        kv_ref[r, :, head:] = values.astype(BF16)
        quarter = jnp.where(holds_keys, keys, values)
        live = len_ref[r]
        for b, start in enumerate(starts):
            position = start + lax.broadcasted_iota(jnp.int32, (part, 1), 0)
            page_ref[r, pl.ds(start, part), :] = jnp.where(
                position < live, quarter[b * part : (b + 1) * part], 0.0
            ).astype(BF16)
        for h in range(heads):
            raw = jnp.dot(
                rows, wq_ref[:, h * head : (h + 1) * head], preferred_element_type=F32
            )
            q_ref[r, h * count : (h + 1) * count, :] = rotated(
                normed(raw, qgain), cos, sin
            ).astype(BF16)


def project(lens, hidden, y, c, d, gains, wq, mine, other, head_gains, cos, sin):
    reqs, part, width = hidden.shape
    count = part * len(BLOCK_XOR)
    head = head_gains.shape[-1]
    heads = wq.shape[1] // head
    return pl.pallas_call(
        project_kernel,
        out_shape=[
            jax.ShapeDtypeStruct((reqs, count, head), BF16),
            jax.ShapeDtypeStruct((reqs, heads * count, head), BF16),
            jax.ShapeDtypeStruct((reqs, count, 2 * head), BF16),
        ],
        in_specs=[SCALARS] + [ON_CHIP] * 11,
        out_specs=[ON_CHIP] * 3,
        compiler_params=params(10),
        cost_estimate=cost(2 * reqs * count * width * (heads + 2) * head, 6 << 20),
        name="project",
    )(lens, hidden, y, c, d, gains, wq, mine, other, head_gains, cos, sin)


def attend_kernel(
    req,
    sources,
    group_ref,
    owner_ref,
    slot_ref,
    q_ref,
    kv_ref,
    wo_ref,
    *refs,
):
    pool_count = len({name for name, _, _, _ in sources})
    pool_refs = refs[:pool_count]
    outs = refs[pool_count:-4]
    keyval, mixed, place, sems = refs[-4:]
    member = lax.axis_index("mlp")
    me = lax.axis_index("req")
    count, head = kv_ref.shape[1], kv_ref.shape[2] // 2
    part = count // 4
    page = pool_refs[0].shape[1]
    n_pages = owner_ref.shape[1]
    per_part = len(sources) // 2
    group = group_ref[req]
    for s in range(len(sources)):
        place[s] = -1
    for i in range(n_pages):
        flip = owner_ref[group, i] ^ me
        far = slot_ref[group, i] ^ (member % 2)
        place[far * per_part + flip] = i
    for name, index, far, flip in sources:
        where = place[far * per_part + flip]

        @pl.when(where >= 0)
        def _():
            start = pl.multiple_of(where * page, page)
            pltpu.make_async_copy(
                pool_refs[name].at[index], keyval.at[pl.ds(start, page), :], sems.at[where]
            ).start()

    pre = n_pages * page
    keyval[pre:, :] = kv_ref[req]
    for i in range(n_pages):
        pltpu.make_async_copy(
            pool_refs[0].at[0], keyval.at[i * page : (i + 1) * page, :], sems.at[i]
        ).wait()

    factor = head**-0.5 * math.log2(math.e)

    def positions(index):
        block = index // part
        flip = (block & 1) * 2 + (block >> 1)
        return (member ^ flip) * part + index % part

    key_at = positions(lax.broadcasted_iota(jnp.int32, (1, count), 1))
    tile = TILE
    heads = q_ref.shape[1] // count
    for first in range(0, count, tile):
        query_at = positions(first + lax.broadcasted_iota(jnp.int32, (tile, 1), 0))
        seen = key_at <= query_at
        for h in range(heads):
            start = h * count + first
            scores = lax.dot_general(
                q_ref[req, start : start + tile, :],
                keyval[:, :head],
                (((1,), (1,)), ((), ())),
                preferred_element_type=F32,
            )
            scores = jnp.concatenate(
                [scores[:, :pre], jnp.where(seen, scores[:, pre:], -jnp.inf)], axis=1
            )
            peak = jnp.max(scores, axis=-1, keepdims=True)
            exps = jnp.exp2((scores - peak) * factor)
            total = jnp.sum(exps, axis=-1, keepdims=True)
            out = jnp.dot(exps.astype(BF16), keyval[:, head:], preferred_element_type=F32)
            mixed[first : first + tile, h * head : (h + 1) * head] = (
                out * (1.0 / total)
            ).astype(BF16)
    width = wo_ref.shape[1]
    step = 512
    for col in range(0, width, step):
        result = jnp.dot(
            mixed[...], wo_ref[:, col : col + step], preferred_element_type=F32
        ).astype(BF16)
        store_rows(outs, col, result)


def store_rows(outs, col, result):
    first = 0
    for out_ref in outs:
        rows = out_ref.shape[0]
        out_ref[:, col : col + result.shape[1]] = result[first : first + rows]
        first += rows


def partial_shapes(part, width):
    return [jax.ShapeDtypeStruct((2 * part, width), BF16)] + [
        jax.ShapeDtypeStruct((part // SPLIT, width), BF16)
    ] * (2 * SPLIT)


def attend(req, sources, group, owner, slot, q, kv, wo, pools):
    count, head = kv.shape[1], kv.shape[2] // 2
    part = count // 4
    heads = q.shape[1] // count
    page = pools[0].shape[1]
    n_pages = owner.shape[1]
    keys = n_pages * page + count
    return pl.pallas_call(
        functools.partial(attend_kernel, req, sources),
        out_shape=partial_shapes(part, wo.shape[1]),
        in_specs=[SCALARS] * 3 + [ON_CHIP] * 3 + [ANYWHERE] * len(pools),
        out_specs=[ON_CHIP] * (1 + 2 * SPLIT),
        scratch_shapes=[
            pltpu.VMEM((keys, 2 * head), BF16),
            pltpu.VMEM((count, heads * head), BF16),
            pltpu.SMEM((len(sources),), jnp.int32),
            pltpu.SemaphoreType.DMA((n_pages,)),
        ],
        compiler_params=params(8),
        cost_estimate=cost(
            heads * count * head * (4 * keys + 2 * wo.shape[1]), 4 << 20, heads * count * keys
        ),
        name="attend",
    )(group, owner, slot, q, kv, wo, *pools)


def pair_kernel(keep_ref, *refs):
    count = 2 * SPLIT
    others, outs = refs[:count], refs[count:]
    total = keep_ref[...].astype(F32) + jnp.concatenate(
        [ref[...].astype(F32) for ref in others], axis=0
    )
    store_rows(outs, 0, total.astype(BF16))


def pair_sum(keep, others, parts):
    rows, width = keep.shape
    return pl.pallas_call(
        pair_kernel,
        out_shape=[jax.ShapeDtypeStruct((rows // parts, width), BF16)] * parts,
        in_specs=[ON_CHIP] * (1 + len(others)),
        out_specs=[ON_CHIP] * parts,
        cost_estimate=cost(2 * keep.size, 6 * keep.size),
        compiler_params=params(6),
        name="pair_sum",
    )(keep, *others)


def residual_kernel(req, own_base_ref, y_base_ref, near_ref, far_ref, gains_ref, res_ref, *in_refs):
    part = res_ref.shape[0]
    for b, base_ref in enumerate((own_base_ref, y_base_ref)):
        mine = slice(b * part, (b + 1) * part)
        theirs = slice((1 - b) * part, (2 - b) * part)
        total = near_ref[mine, :].astype(F32) + far_ref[theirs, :].astype(F32)
        residual = (base_ref[req] + normed(total, gains_ref[2:3, :])) * INV_ROOT
        if b == 0:
            res_ref[...] = residual
        rows = normed(residual, gains_ref[3:4, :]).astype(BF16)
        store_rows(in_refs[b * SPLIT : (b + 1) * SPLIT], 0, rows)


def make_residual(req, own_base, y_base, near, far, gains):
    rows, width = near.shape
    part = rows // 2
    return pl.pallas_call(
        functools.partial(residual_kernel, req),
        out_shape=[
            jax.ShapeDtypeStruct((part, width), F32),
        ]
        + [jax.ShapeDtypeStruct((part // SPLIT, width), BF16)] * (2 * SPLIT),
        in_specs=[ON_CHIP] * 5,
        out_specs=[ON_CHIP] * (1 + 2 * SPLIT),
        cost_estimate=cost(12 * near.size, 16 * near.size),
        compiler_params=params(4),
        name="residual",
    )(own_base, y_base, near, far, gains)


def feed_kernel(gate_ref, up_ref, down_ref, *refs):
    count = 4 * SPLIT
    outs, hidden = refs[count:-1], refs[-1]
    rows = jnp.concatenate([ref[...] for ref in refs[:count]], axis=0)
    units = gate_ref.shape[1]
    step = 512
    for u in range(0, units, step):
        gate = jnp.dot(rows, gate_ref[:, u : u + step], preferred_element_type=F32)
        up = jnp.dot(rows, up_ref[:, u : u + step], preferred_element_type=F32)
        hidden[:, u : u + step] = (jax.nn.gelu(gate, approximate=True) * up).astype(BF16)
    for col in range(0, down_ref.shape[1], step):
        result = jnp.dot(
            hidden[...], down_ref[:, col : col + step], preferred_element_type=F32
        ).astype(BF16)
        store_rows(outs, col, result)


def feed(pieces, gate, up, down):
    width, units = gate.shape
    part = pieces[0].shape[0] * SPLIT
    return pl.pallas_call(
        feed_kernel,
        out_shape=partial_shapes(part, width),
        in_specs=[ON_CHIP] * (3 + len(pieces)),
        out_specs=[ON_CHIP] * (1 + 2 * SPLIT),
        scratch_shapes=[pltpu.VMEM((4 * part, units), BF16)],
        compiler_params=params(8),
        cost_estimate=cost(24 * part * width * units, 12 << 20, 4 * part * units),
        name="feed",
    )(gate, up, down, *pieces)


def finish_kernel(req, len_ref, res_ref, near_ref, far_ref, gains_ref, *refs):
    out_ref = refs[-1]
    part = res_ref.shape[0]
    total = near_ref[...].astype(F32) + far_ref[...].astype(F32)
    output = res_ref[...] + normed(total, gains_ref[4:5, :])
    position = lax.axis_index("mlp") * part + lax.broadcasted_iota(jnp.int32, (part, 1), 0)
    out_ref[0] = jnp.where(position < len_ref[req], output, 0.0).astype(BF16)


def finish(req, reqs, lens, residual, near, far, gains, before):
    part, width = residual.shape
    extra = [] if before is None else [before]
    return pl.pallas_call(
        functools.partial(finish_kernel, req),
        grid=(1,),
        out_shape=jax.ShapeDtypeStruct((reqs, part, width), BF16),
        in_specs=[SCALARS] + [ON_CHIP] * 4 + [ANYWHERE] * len(extra),
        out_specs=pl.BlockSpec((1, part, width), lambda i: (req, 0, 0)),
        input_output_aliases={5: 0} if extra else {},
        cost_estimate=cost(10 * residual.size, 12 * residual.size),
        compiler_params=params(4),
        name="finish",
    )(lens, residual, near, far, gains, *extra)


def local(
    hidden_in,
    input_gain,
    query_weight,
    keyval_weight,
    query_gain,
    key_gain,
    out_weight,
    attn_gain,
    laurel_left,
    laurel_right,
    laurel_gain,
    ffn_gain,
    post_gain,
    gate_projection_matrix,
    up_projection_matrix,
    down_projection_matrix,
    page_pool,
    page_owner,
    page_slot,
    request_group,
    suffix_len,
):
    member = lax.axis_index("mlp")
    part, reqs, width = hidden_in.shape
    head = query_gain.shape[0]
    count = part * lax.axis_size("mlp")
    prefix_len = page_owner.shape[1] * page_pool.shape[1]

    hidden = jnp.transpose(hidden_in, (1, 0, 2))
    gains = jnp.stack([input_gain, laurel_gain, attn_gain, ffn_gain, post_gain])
    head_gains = jnp.stack([query_gain, key_gain])
    half = head // 2
    frequency = 1000000.0 ** (-jnp.arange(half, dtype=F32) / half)
    angles = (prefix_len + jnp.arange(count)).astype(F32)[:, None] * frequency[None, :]
    cos, sin = jnp.cos(angles), jnp.sin(angles)

    page_rows = page_pool.shape[1]
    own_page = lax.dynamic_slice(
        page_pool, (member % 2, 0, member // 2 * 2 * head), (1, page_rows, 2 * head)
    )
    even = list(range(0, lax.axis_size("req"), 2))
    even_pages = [own_page] + [exchange(own_page, "req", flip) for flip in even[1:]]
    hidden_y = exchange(hidden, "mlp", 2)
    hidden_c = exchange(hidden, "mlp", 1)
    other_weight = exchange(after(keyval_weight, hidden_c), "mlp", 1)
    own_base = make_base(hidden, gains, laurel_left.T, laurel_right)
    even_pages[1] = after(even_pages[1], own_base, cos, head_gains)
    even_pages = jnp.concatenate(even_pages)
    odd_pages = exchange(even_pages, "req", 1)
    even_other = exchange(even_pages, "mlp", 1)
    hidden_y = after(hidden_y, even_pages)
    hidden_d = exchange(hidden_y, "mlp", 1)
    y_base = make_base(hidden_y, gains, laurel_left.T, laurel_right)
    pages, q_all, kv_all = project(
        suffix_len,
        hidden,
        after(hidden_y, y_base),
        hidden_c,
        hidden_d,
        gains,
        query_weight,
        keyval_weight,
        other_weight,
        head_gains,
        cos,
        sin,
    )
    odd_pages = after(odd_pages, q_all)
    odd_other = exchange(odd_pages, "mlp", 1)
    pools = [even_pages, odd_pages, even_other, odd_other]
    sources = [
        (p, i, p // 2, flip + p % 2) for p in range(len(pools)) for i, flip in enumerate(even)
    ]

    def attend_one(r, *earlier):
        return attend(
            r,
            sources,
            request_group,
            page_owner,
            page_slot,
            after(q_all, *earlier),
            kv_all,
            out_weight,
            pools,
        )

    def swap(pieces):
        return [exchange(piece, "mlp", 1) for piece in pieces]

    def residual_one(r, *earlier):
        residual, *pieces = make_residual(
            r, own_base, y_base, near[r], after(far[r], *earlier), gains
        )
        residuals[r] = residual
        inputs[r] = pieces + swap(pieces)
        return pieces[0]

    def feed_one(r, *earlier):
        first, *rest = inputs[r]
        return feed(
            [after(first, *earlier), *rest],
            gate_projection_matrix,
            up_projection_matrix,
            down_projection_matrix,
        )

    def finish_one(r, earlier, before):
        near_own, far_own = done[r]
        return finish(
            r,
            reqs,
            suffix_len,
            residuals[r],
            near_own,
            after(far_own, earlier),
            gains,
            before,
        )

    near, far, residuals, inputs = {}, {}, {}, {}
    last = q_all
    for r in range(reqs):
        keep, *pieces = attend_one(r, last)
        others = swap(pieces)
        last = keep
        if r >= 2:
            last = residual_one(r - 2, last)
        (near[r],) = pair_sum(after(keep, last), others, 1)
        far[r] = exchange(near[r], "mlp", 2)
        last = near[r]
    done, result = {}, None
    for r in range(reqs):
        keep, *pieces = feed_one(r, last)
        others = swap(pieces)
        last = keep
        if r + 1 < reqs:
            last = residual_one(r + 1, last)
        else:
            last = result = finish_one(0, last, None)
        near_own, near_y = pair_sum(after(keep, last), others, 2)
        done[r] = (near_own, exchange(near_y, "mlp", 2))
        last = near_own
    for r in range(1, reqs):
        result = finish_one(r, last, result)
    return jnp.transpose(result, (1, 0, 2)), jnp.transpose(pages, (1, 0, 2))


def solution(mesh):
    placed = (
        P("mlp", "req", None),
        P(),
        P(None, "mlp"),
        P(None, "mlp"),
        P(),
        P(),
        P("mlp", None),
        P(),
        P(),
        P(),
        P(),
        P(),
        P(),
        P(None, "mlp"),
        P(None, "mlp"),
        P("mlp", None),
        P("req", None, None),
        P(),
        P(),
        P("req"),
        P("req"),
    )
    return jax.shard_map(
        local,
        mesh=mesh,
        in_specs=placed,
        out_specs=(P("mlp", "req", None), P(None, "req", "mlp")),
        check_vma=False,
    )
```

time: 164 us -> 107 us (0.65)
  local copies, waits for them, and re-layouts: 30.2 us -> 4.62 us
  Pallas kernels: 55.1 us -> 38.9 us
  waiting for transfers between devices: 42.4 us -> 33.1 us
  starting transfers between devices: 32.7 us -> 26.4 us
    unnamed x130 -> x42, local copies, waits for them, and re-layouts: 30.2 us -> 3.12 us
    pallas_call x11 -> x15, Pallas kernels: 31.2 us -> 21.5 us  [the longest x3 10.5 us: feed(): pl.pallas_call(feed_kernel, out_shape=partial_shapes(part, width), in_spe...]
    ppermute x46 -> x52, waiting for transfers between devices: 42.4 us -> 33.1 us  [exchange(): lax.ppermute(value, axis, [(i, i ^ flip) for i in range(lax.axis_size(axi...]
    ppermute x46 -> x52, starting transfers between devices: 32.7 us -> 26.4 us  [exchange(): lax.ppermute(value, axis, [(i, i ^ flip) for i in range(lax.axis_size(axi...]
    pallas_call x3, Pallas kernels: 17.3 us -> 13 us  [attend(): pl.pallas_call(functools.partial(attend_kernel, req, sources), out_shape=...]
    pallas_call x3, Pallas kernels: 6.71 us -> 4.44 us  [finish(): pl.pallas_call(functools.partial(finish_kernel, req), grid=(1,), out_shap...]
  transfers between devices with their start and end apart: 46 -> 52, of which waited for: 14 -> 26; matrix products, arithmetic and copies ran while one was open for 1% -> 4% of each run, Pallas kernels for 29% -> 31%
where the time goes in v2:
time: 107 us
  Pallas kernels  38.9 us (36%)
  waiting for transfers between devices  33.1 us (31%)
  starting transfers between devices  26.4 us (25%)
  local copies, waits for them, and re-layouts  4.62 us (4%)
  other arithmetic  2.42 us (2%)
  between operations  1.09 us (1%)
    ppermute x52, waiting for transfers between devices, exchange(): lax.ppermute(value, axis, [(i, i ^ flip) for i in range(lax.axis_size(axi...  33.1 us
    ppermute x52, starting transfers between devices, exchange(): lax.ppermute(value, axis, [(i, i ^ flip) for i in range(lax.axis_size(axi...  26.4 us
    pallas_call x3, Pallas kernels, attend(): pl.pallas_call(functools.partial(attend_kernel, req, sources), out_shape=...  13 us
    pallas_call x3, Pallas kernels, feed(): pl.pallas_call(feed_kernel, out_shape=partial_shapes(part, width), in_spe...  10.5 us
    pallas_call x1, Pallas kernels, project(): pl.pallas_call(project_kernel, out_shape=[jax.ShapeDtypeStruct((reqs, cou...  5.63 us
    pallas_call x3, Pallas kernels, finish(): pl.pallas_call(functools.partial(finish_kernel, req), grid=(1,), out_shap...  4.44 us
    unnamed x42, local copies, waits for them, and re-layouts  3.12 us
    pallas_call x2, Pallas kernels, make_base(): pl.pallas_call(base_kernel, out_shape=jax.ShapeDtypeStruct(hidden.shape,...  2.72 us
  transfers between devices with their start and end apart: 52, of which 26 were waited for; matrix products, arithmetic and copies ran while one was open for 4% of the time, Pallas kernels for 31%

profile of v2, /device:TPU:0, one launch (start us, length us, event | category | flops | bytes accessed | tf_op | source)
XLA Modules:
  0.0 106.5 jit_solution(4707023379076449431)
XLA Ops:
  0.7 0.5 collective-permute-start.4
  1.2 2.6 %collective-permute-start = (bf16[3,64,2048]{2,1,0:T(8,128)(2,1)}, bf16[3,64,2048]{2,1,0:T(8,128)(2,1)S(1)}, u32[]{:S(2)}, u32[]{:S(2)}) collective-permute-start(bf16[3,64,2048]{2,1,0:T(8,128)(2,1)} %bitcast.12), channel_id=1, source_target_pairs={{0,2},{1,3},{2,0},{3,1},{4,6},{5,7},{6,4},{7,5},{8,10},{9,11},{10,... | collective-permute-start | bytes 2359304 | tf_op jit(solution)/shard_map/ppermute | solution.py:24
  3.8 0.7 constant_dynamic-slice_fusion
  4.5 1.6 %collective-permute-start.1 = (bf16[1,128,512]{2,1,0:T(8,128)(2,1)}, bf16[1,128,512]{2,1,0:T(8,128)(2,1)}, u32[]{:S(2)}, u32[]{:S(2)}) collective-permute-start(bf16[1,128,512]{2,1,0:T(8,128)(2,1)} %constant_dynamic-slice_fusion), channel_id=1, source_target_pairs={{0,8},{4,12},{8,0},{12,4},{16,24},{20,28},{24,16},{28,20},{1,9},{5... | collective-permute-start | bytes 393224 | tf_op jit(solution)/shard_map/ppermute | solution.py:24
  6.0 2.6 %collective-permute-start.2 = (bf16[1,128,512]{2,1,0:T(8,128)(2,1)}, bf16[1,128,512]{2,1,0:T(8,128)(2,1)}, u32[]{:S(2)}, u32[]{:S(2)}) collective-permute-start(bf16[1,128,512]{2,1,0:T(8,128)(2,1)} %constant_dynamic-slice_fusion), channel_id=1, source_target_pairs={{0,16},{4,20},{8,24},{12,28},{16,0},{20,4},{24,8},{28,12},{1,17},{... | collective-permute-start | bytes 393224 | tf_op jit(solution)/shard_map/ppermute | solution.py:24
  9.0 1.2 %multiply_sine_fusion = (f32[256,128]{1,0:T(8,128)}, f32[256,128]{1,0:T(8,128)}) fusion(f32[128]{0:T(128)S(1)} %multiply_power_fusion, f32[256]{0:T(256)S(1)} %add_convert_fusion), kind=kLoop, calls=%fused_computation.1 | loop fusion | flops 32768 | bytes 263680 | tf_op jit(solution)/shard_map/sin | solution.py:426
  10.2 0.8 stack.32.gains_ref
  11.0 1.1 %copy-done.5 = bf16[64,3,2048]{2,0,1:T(8,128)(2,1)S(1)} copy-done((bf16[64,3,2048]{2,0,1:T(8,128)(2,1)S(1)}, bf16[64,3,2048]{2,0,1:T(8,128)(2,1)}, u32[]{:S(2)}) %copy-start.5) | copy-done | bytes 786456
  12.2 0.9 copy-done.8
  13.1 0.9 copy-done.10
  14.1 1.4 %base.2.own_base_ref = f32[3,64,2048]{2,1,0:T(8,128)S(1)} custom-call(bf16[3,64,2048]{2,1,0:T(8,128)(2,1)S(1)} %bitcast.13, f32[5,2048]{1,0:T(8,128)S(1)} %stack.32.gains_ref, bf16[64,2048]{1,0:T(8,128)(2,1)S(1)} %bitcast.15, bf16[64,2048]{1,0:T(8,128)(2,1)S(1)} %copy-done.10), custom_call_target="tpu_custom_call" | custom-call | flops 1 | bytes 1 | tf_op jit(solution)/shard_map/base/pallas_call | solution.py:68
  15.5 3.7 %collective-permute-done.2 = bf16[1,128,512]{2,1,0:T(8,128)(2,1)} collective-permute-done((bf16[1,128,512]{2,1,0:T(8,128)(2,1)}, bf16[1,128,512]{2,1,0:T(8,128)(2,1)}, u32[]{:S(2)}, u32[]{:S(2)}) %collective-permute-start.2) | collective-permute-done | bytes 131104 | tf_op jit(solution)/shard_map/ppermute | solution.py:24
  19.2 1.2 %pad_maximum_fusion.refs_0_ = bf16[4,128,512]{2,1,0:T(8,128)(2,1)S(1)} fusion(bf16[1,128,512]{2,1,0:T(8,128)(2,1)} %collective-permute-done.3, bf16[1,128,512]{2,1,0:T(8,128)(2,1)} %collective-permute-done.2, bf16[1,128,512]{2,1,0:T(8,128)(2,1)} %collective-permute-done.1, bf16[1,128,512]{2,1,0:T(8,128)(2,1)} %constant_dynamic-slice_fusion), kind=kLoop, calls=%fused_computation | loop fusion | flops 786432 | bytes 1048576 | tf_op jit(solution)/shard_map/concatenate | solution.py:439
  20.4 1.7 %collective-permute-done.hidden_ref.y_ref = bf16[3,64,2048]{2,1,0:T(8,128)(2,1)S(1)} collective-permute-done((bf16[3,64,2048]{2,1,0:T(8,128)(2,1)}, bf16[3,64,2048]{2,1,0:T(8,128)(2,1)S(1)}, u32[]{:S(2)}, u32[]{:S(2)}) %collective-permute-start) | collective-permute-done | bytes 786464 | tf_op jit(solution)/shard_map/ppermute | solution.py:24
  22.1 1.7 %collective-permute-start.7 = (bf16[4,128,512]{2,1,0:T(8,128)(2,1)S(1)}, bf16[4,128,512]{2,1,0:T(8,128)(2,1)S(1)}, u32[]{:S(2)}, u32[]{:S(2)}) collective-permute-start(bf16[4,128,512]{2,1,0:T(8,128)(2,1)S(1)} %pad_maximum_fusion.refs_0_), channel_id=1, source_target_pairs={{0,4},{4,0},{8,12},{12,8},{16,20},{20,16},{24,28},{28,24},{1,5},{5... | collective-permute-start | bytes 1572872 | tf_op jit(solution)/shard_map/ppermute | solution.py:24
  24.1 1.4 %base.3.y_base_ref = f32[3,64,2048]{2,1,0:T(8,128)S(1)} custom-call(bf16[3,64,2048]{2,1,0:T(8,128)(2,1)S(1)} %collective-permute-done.hidden_ref.y_ref, f32[5,2048]{1,0:T(8,128)S(1)} %stack.32.gains_ref, bf16[64,2048]{1,0:T(8,128)(2,1)S(1)} %bitcast.16, bf16[64,2048]{1,0:T(8,128)(2,1)S(1)} %copy-done.11), custom_call_target="tpu_custom_call" | custom-call | flops 1 | bytes 1 | tf_op jit(solution)/shard_map/base/pallas_call | solution.py:68
  25.6 5.6 %project.1 = (bf16[3,256,256]{2,1,0:T(8,128)(2,1)}, bf16[3,512,256]{2,1,0:T(8,128)(2,1)S(1)}, bf16[3,256,512]{2,1,0:T(8,128)(2,1)S(1)}) custom-call(s32[3]{0:T(128)S(1)} %copy-done.17, bf16[3,64,2048]{2,1,0:T(8,128)(2,1)S(1)} %bitcast.14, bf16[3,64,2048]{2,1,0:T(8,128)(2,1)S(1)} %collective-permute-done.hidden_ref.y_ref, ...), custom_call_target="tpu_custom_call" | custom-call | flops 1 | bytes 1 | tf_op jit(solution)/shard_map/project/pallas_call | solution.py:141
  31.2 5.2 %collective-permute-done.7.refs_1_ = bf16[4,128,512]{2,1,0:T(8,128)(2,1)S(1)} collective-permute-done((bf16[4,128,512]{2,1,0:T(8,128)(2,1)S(1)}, bf16[4,128,512]{2,1,0:T(8,128)(2,1)S(1)}, u32[]{:S(2)}, u32[]{:S(2)}) %collective-permute-start.7) | collective-permute-done | bytes 524320 | tf_op jit(solution)/shard_map/ppermute | solution.py:24
  36.5 1.9 %collective-permute-done.9.refs_3_ = bf16[4,128,512]{2,1,0:T(8,128)(2,1)S(1)} collective-permute-done((bf16[4,128,512]{2,1,0:T(8,128)(2,1)S(1)}, bf16[4,128,512]{2,1,0:T(8,128)(2,1)S(1)}, u32[]{:S(2)}, u32[]{:S(2)}) %collective-permute-start.9) | collective-permute-done | bytes 524320 | tf_op jit(solution)/shard_map/ppermute | solution.py:24
  38.4 4.3 %attend.3 = (bf16[128,2048]{1,0:T(8,128)(2,1)S(1)}, bf16[32,2048]{1,0:T(8,128)(2,1)S(1)}, bf16[32,2048]{1,0:T(8,128)(2,1)S(1)}, bf16[32,2048]{1,0:T(8,128)(2,1)S(1)}, bf16[32,2048]{1,0:T(8,128)(2,1)S(1)}) custom-call(s32[3]{0:T(128)S(1)} %copy-done.18, s32[2,8]{1,0:T(2,128)S(1)} %copy-done.15, s32[2,8]{1,0:T(2,128)S(1)} %copy-done.16, ...), custom_call_target="tpu_custom_call" | custom-call | flops 1 | bytes 1 | tf_op jit(solution)/shard_map/attend/pallas_call | solution.py:263
  42.9 0.4 collective-permute-start.11
  43.4 0.4 collective-permute-start.13
  43.8 0.3 collective-permute-done.10.refs_0_
  44.3 0.3 collective-permute-done.12.refs_2_
  44.9 1.8 %collective-permute-start.18 = (bf16[128,2048]{1,0:T(8,128)(2,1)S(1)}, bf16[128,2048]{1,0:T(8,128)(2,1)S(1)}, u32[]{:S(2)}, u32[]{:S(2)}) collective-permute-start(bf16[128,2048]{1,0:T(8,128)(2,1)S(1)} %pair_sum.6.near_ref), channel_id=1, source_target_pairs={{0,2},{1,3},{2,0},{3,1},{4,6},{5,7},{6,4},{7,5},{8,10},{9,11},{10,... | collective-permute-start | bytes 1572872 | tf_op jit(solution)/shard_map/ppermute | solution.py:24
  46.7 4.4 %attend.4 = (bf16[128,2048]{1,0:T(8,128)(2,1)S(1)}, bf16[32,2048]{1,0:T(8,128)(2,1)S(1)}, bf16[32,2048]{1,0:T(8,128)(2,1)S(1)}, bf16[32,2048]{1,0:T(8,128)(2,1)S(1)}, bf16[32,2048]{1,0:T(8,128)(2,1)S(1)}) custom-call(s32[3]{0:T(128)S(1)} %copy-done.18, s32[2,8]{1,0:T(2,128)S(1)} %copy-done.15, s32[2,8]{1,0:T(2,128)S(1)} %copy-done.16, ...), custom_call_target="tpu_custom_call" | custom-call | flops 1 | bytes 1 | tf_op jit(solution)/shard_map/attend/pallas_call | solution.py:263
  51.3 0.5 collective-permute-start.15
  51.8 0.4 collective-permute-start.17
  52.3 0.3 collective-permute-done.14.refs_0_
  52.8 0.3 collective-permute-done.16.refs_2_
  53.4 0.3 collective-permute-start.24
  53.8 4.3 %attend.5 = (bf16[128,2048]{1,0:T(8,128)(2,1)S(1)}, bf16[32,2048]{1,0:T(8,128)(2,1)S(1)}, bf16[32,2048]{1,0:T(8,128)(2,1)S(1)}, bf16[32,2048]{1,0:T(8,128)(2,1)S(1)}, bf16[32,2048]{1,0:T(8,128)(2,1)S(1)}) custom-call(s32[3]{0:T(128)S(1)} %copy-done.18, s32[2,8]{1,0:T(2,128)S(1)} %copy-done.15, s32[2,8]{1,0:T(2,128)S(1)} %copy-done.16, ...), custom_call_target="tpu_custom_call" | custom-call | flops 1 | bytes 1 | tf_op jit(solution)/shard_map/attend/pallas_call | solution.py:263
  58.2 0.4 collective-permute-start.20
  58.7 1.0 collective-permute-done.18.far_ref
  59.7 0.6 residual.3
  60.4 0.6 collective-permute-start.25
  61.0 0.4 collective-permute-start.27
  61.9 1.8 %collective-permute-start.23 = (bf16[128,2048]{1,0:T(8,128)(2,1)S(1)}, bf16[128,2048]{1,0:T(8,128)(2,1)S(1)}, u32[]{:S(2)}, u32[]{:S(2)}) collective-permute-start(bf16[128,2048]{1,0:T(8,128)(2,1)S(1)} %pair_sum.8.near_ref), channel_id=1, source_target_pairs={{0,2},{1,3},{2,0},{3,1},{4,6},{5,7},{6,4},{7,5},{8,10},{9,11},{10,... | collective-permute-start | bytes 1572872 | tf_op jit(solution)/shard_map/ppermute | solution.py:24
  63.7 3.4 %feed.3 = (bf16[128,2048]{1,0:T(8,128)(2,1)S(1)}, bf16[32,2048]{1,0:T(8,128)(2,1)S(1)}, bf16[32,2048]{1,0:T(8,128)(2,1)S(1)}, bf16[32,2048]{1,0:T(8,128)(2,1)S(1)}, bf16[32,2048]{1,0:T(8,128)(2,1)S(1)}) custom-call(bf16[2048,1024]{1,0:T(8,128)(2,1)S(1)} %copy-done.1, bf16[2048,1024]{1,0:T(8,128)(2,1)S(1)} %copy-done.2, bf16[1024,2048]{1,0:T(8,128)(2,1)S(1)} %copy-done.3, ...), custom_call_target="tpu_custom_call" | custom-call | flops 1 | bytes 1 | tf_op jit(solution)/shard_map/feed/pallas_call | solution.py:354
  67.3 0.4 collective-permute-start.30
  67.8 3.1 %collective-permute-done.24.far_ref = bf16[128,2048]{1,0:T(8,128)(2,1)S(1)} collective-permute-done((bf16[128,2048]{1,0:T(8,128)(2,1)S(1)}, bf16[128,2048]{1,0:T(8,128)(2,1)S(1)}, u32[]{:S(2)}, u32[]{:S(2)}) %collective-permute-start.24) | collective-permute-done | bytes 524320 | tf_op jit(solution)/shard_map/ppermute | solution.py:24
  71.0 0.6 residual.4
  71.6 0.6 collective-permute-start.33
  72.3 0.4 collective-permute-start.35
  73.2 0.4 collective-permute-done.34.refs_5_
  73.7 0.3 collective-permute-done.36.refs_7_
  74.0 3.4 %feed.4 = (bf16[128,2048]{1,0:T(8,128)(2,1)S(1)}, bf16[32,2048]{1,0:T(8,128)(2,1)S(1)}, bf16[32,2048]{1,0:T(8,128)(2,1)S(1)}, bf16[32,2048]{1,0:T(8,128)(2,1)S(1)}, bf16[32,2048]{1,0:T(8,128)(2,1)S(1)}) custom-call(bf16[2048,1024]{1,0:T(8,128)(2,1)S(1)} %copy-done.1, bf16[2048,1024]{1,0:T(8,128)(2,1)S(1)} %copy-done.2, bf16[1024,2048]{1,0:T(8,128)(2,1)S(1)} %copy-done.3, ...), custom_call_target="tpu_custom_call" | custom-call | flops 1 | bytes 1 | tf_op jit(solution)/shard_map/feed/pallas_call | solution.py:354
  77.7 0.3 collective-permute-start.38
  78.2 0.3 collective-permute-start.40
  78.6 3.1 %collective-permute-done.23.far_ref = bf16[128,2048]{1,0:T(8,128)(2,1)S(1)} collective-permute-done((bf16[128,2048]{1,0:T(8,128)(2,1)S(1)}, bf16[128,2048]{1,0:T(8,128)(2,1)S(1)}, u32[]{:S(2)}, u32[]{:S(2)}) %collective-permute-start.23) | collective-permute-done | bytes 524320 | tf_op jit(solution)/shard_map/ppermute | solution.py:24
  81.6 1.7 %collective-permute-start.45 = (bf16[64,2048]{1,0:T(8,128)(2,1)S(1)}, bf16[64,2048]{1,0:T(8,128)(2,1)S(1)}, u32[]{:S(2)}, u32[]{:S(2)}) collective-permute-start(bf16[64,2048]{1,0:T(8,128)(2,1)S(1)} %get-tuple-element.138), channel_id=1, source_target_pairs={{0,2},{1,3},{2,0},{3,1},{4,6},{5,7},{6,4},{7,5},{8,10},{9,11},{10,... | collective-permute-start | bytes 786440 | tf_op jit(solution)/shard_map/ppermute | solution.py:24
  83.4 0.6 residual.5
  84.1 0.5 collective-permute-start.42
  84.7 0.4 collective-permute-start.44
  85.6 0.3 collective-permute-done.43.refs_6_
  86.1 3.7 %feed.5 = (bf16[128,2048]{1,0:T(8,128)(2,1)S(1)}, bf16[32,2048]{1,0:T(8,128)(2,1)S(1)}, bf16[32,2048]{1,0:T(8,128)(2,1)S(1)}, bf16[32,2048]{1,0:T(8,128)(2,1)S(1)}, bf16[32,2048]{1,0:T(8,128)(2,1)S(1)}) custom-call(bf16[2048,1024]{1,0:T(8,128)(2,1)S(1)} %copy-done.1, bf16[2048,1024]{1,0:T(8,128)(2,1)S(1)} %copy-done.2, bf16[1024,2048]{1,0:T(8,128)(2,1)S(1)} %copy-done.3, ...), custom_call_target="tpu_custom_call" | custom-call | flops 1 | bytes 1 | tf_op jit(solution)/shard_map/feed/pallas_call | solution.py:354
  89.8 0.4 collective-permute-start.46
  90.4 0.3 collective-permute-start.48
  91.2 1.5 %finish.3.refs_0_ = bf16[3,64,2048]{2,1,0:T(8,128)(2,1)} custom-call(s32[3]{0:T(128)S(1)} %copy-done.17, f32[64,2048]{1,0:T(8,128)S(1)} %get-tuple-element.137.res_ref, bf16[64,2048]{1,0:T(8,128)(2,1)S(1)} %get-tuple-element.117.near_ref, bf16[64,2048]{1,0:T(8,128)(2,1)S(1)} %collective-permute-done.45.far_ref, f32[5,2048]{1,0:T(8,128)S(1)} %stack.32.gains_ref), custom_call_target="tpu_custom_call" | custom-call | flops 1 | bytes 1 | tf_op jit(solution)/shard_map/finish/pallas_call | solution.py:378
  92.8 1.8 %collective-permute-start.50 = (bf16[64,2048]{1,0:T(8,128)(2,1)S(1)}, bf16[64,2048]{1,0:T(8,128)(2,1)S(1)}, u32[]{:S(2)}, u32[]{:S(2)}) collective-permute-start(bf16[64,2048]{1,0:T(8,128)(2,1)S(1)} %get-tuple-element.146), channel_id=1, source_target_pairs={{0,2},{1,3},{2,0},{3,1},{4,6},{5,7},{6,4},{7,5},{8,10},{9,11},{10,... | collective-permute-start | bytes 786440 | tf_op jit(solution)/shard_map/ppermute | solution.py:24
  94.6 5.4 %collective-permute-done.51.far_ref = bf16[64,2048]{1,0:T(8,128)(2,1)S(1)} collective-permute-done((bf16[64,2048]{1,0:T(8,128)(2,1)S(1)}, bf16[64,2048]{1,0:T(8,128)(2,1)S(1)}, u32[]{:S(2)}, u32[]{:S(2)}) %collective-permute-start.51) | collective-permute-done | bytes 262176 | tf_op jit(solution)/shard_map/ppermute | solution.py:24
  100.0 1.5 %finish.4.refs_0_ = bf16[3,64,2048]{2,1,0:T(8,128)(2,1)} custom-call(s32[3]{0:T(128)S(1)} %copy-done.17, f32[64,2048]{1,0:T(8,128)S(1)} %get-tuple-element.148.res_ref, bf16[64,2048]{1,0:T(8,128)(2,1)S(1)} %get-tuple-element.131.near_ref, bf16[64,2048]{1,0:T(8,128)(2,1)S(1)} %collective-permute-done.51.far_ref, ...), custom_call_target="tpu_custom_call", output_to_operand_aliasing={{}: (5, {})} | custom-call | flops 1 | bytes 1 | tf_op jit(solution)/shard_map/finish/pallas_call | solution.py:378
  101.5 3.5 %collective-permute-done.50.far_ref = bf16[64,2048]{1,0:T(8,128)(2,1)S(1)} collective-permute-done((bf16[64,2048]{1,0:T(8,128)(2,1)S(1)}, bf16[64,2048]{1,0:T(8,128)(2,1)S(1)}, u32[]{:S(2)}, u32[]{:S(2)}) %collective-permute-start.50) | collective-permute-done | bytes 262176 | tf_op jit(solution)/shard_map/ppermute | solution.py:24
  105.0 1.5 %finish.5 = bf16[3,64,2048]{2,1,0:T(8,128)(2,1)} custom-call(s32[3]{0:T(128)S(1)} %copy-done.17, f32[64,2048]{1,0:T(8,128)S(1)} %get-tuple-element.124.res_ref, bf16[64,2048]{1,0:T(8,128)(2,1)S(1)} %get-tuple-element.145.near_ref, bf16[64,2048]{1,0:T(8,128)(2,1)S(1)} %collective-permute-done.50.far_ref, ...), custom_call_target="tpu_custom_call", output_to_operand_aliasing={{}: (5, {})} | custom-call | flops 1 | bytes 1 | tf_op jit(solution)/shard_map/finish/pallas_call | solution.py:378
  (110 shorter events, 6.0 us)
Async XLA Ops:
  0.6 14.8 %copy-start.20 = (f32[256]{0:T(256)S(1)}, f32[256]{0:T(256)}, u32[]{:S(2)}) copy-start(f32[256]{0:T(256)} %param.25) | copy-start | bytes 3076
  0.7 14.8 %copy-start.19 = (f32[256]{0:T(256)S(1)}, f32[256]{0:T(256)}, u32[]{:S(2)}) copy-start(f32[256]{0:T(256)} %param.26) | copy-start | bytes 3076
  0.7 8.2 %collective-permute-start.4 = (bf16[3,64,2048]{2,1,0:T(8,128)(2,1)}, bf16[3,64,2048]{2,1,0:T(8,128)(2,1)S(1)}, u32[]{:S(2)}, u32[]{:S(2)}) collective-permute-start(bf16[3,64,2048]{2,1,0:T(8,128)(2,1)} %bitcast.11), channel_id=1, source_target_pairs={{0,1},{1,0},{2,3},{3,2},{4,5},{5,4},{6,7},{7,6},{8,9},{9,8},{10,11... | collective-permute-start | bytes 2359304 | tf_op jit(solution)/shard_map/ppermute | solution.py:24
  1.2 20.9 %collective-permute-start = (bf16[3,64,2048]{2,1,0:T(8,128)(2,1)}, bf16[3,64,2048]{2,1,0:T(8,128)(2,1)S(1)}, u32[]{:S(2)}, u32[]{:S(2)}) collective-permute-start(bf16[3,64,2048]{2,1,0:T(8,128)(2,1)} %bitcast.12), channel_id=1, source_target_pairs={{0,2},{1,3},{2,0},{3,1},{4,6},{5,7},{6,4},{7,5},{8,10},{9,11},{10,... | collective-permute-start | bytes 2359304 | tf_op jit(solution)/shard_map/ppermute | solution.py:24
  4.5 11.1 %collective-permute-start.1 = (bf16[1,128,512]{2,1,0:T(8,128)(2,1)}, bf16[1,128,512]{2,1,0:T(8,128)(2,1)}, u32[]{:S(2)}, u32[]{:S(2)}) collective-permute-start(bf16[1,128,512]{2,1,0:T(8,128)(2,1)} %constant_dynamic-slice_fusion), channel_id=1, source_target_pairs={{0,8},{4,12},{8,0},{12,4},{16,24},{20,28},{24,16},{28,20},{1,9},{5... | collective-permute-start | bytes 393224 | tf_op jit(solution)/shard_map/ppermute | solution.py:24
  6.0 13.2 %collective-permute-start.2 = (bf16[1,128,512]{2,1,0:T(8,128)(2,1)}, bf16[1,128,512]{2,1,0:T(8,128)(2,1)}, u32[]{:S(2)}, u32[]{:S(2)}) collective-permute-start(bf16[1,128,512]{2,1,0:T(8,128)(2,1)} %constant_dynamic-slice_fusion), channel_id=1, source_target_pairs={{0,16},{4,20},{8,24},{12,28},{16,0},{20,4},{24,8},{28,12},{1,17},{... | collective-permute-start | bytes 393224 | tf_op jit(solution)/shard_map/ppermute | solution.py:24
  8.6 10.6 %collective-permute-start.3 = (bf16[1,128,512]{2,1,0:T(8,128)(2,1)}, bf16[1,128,512]{2,1,0:T(8,128)(2,1)}, u32[]{:S(2)}, u32[]{:S(2)}) collective-permute-start(bf16[1,128,512]{2,1,0:T(8,128)(2,1)} %constant_dynamic-slice_fusion), channel_id=1, source_target_pairs={{0,24},{4,28},{8,16},{12,20},{16,8},{20,12},{24,0},{28,4},{1,25},{... | collective-permute-start | bytes 393224 | tf_op jit(solution)/shard_map/ppermute | solution.py:24
  8.9 16.6 %collective-permute-start.6 = (bf16[2048,256]{1,0:T(8,128)(2,1)}, bf16[2048,256]{1,0:T(8,128)(2,1)S(1)}, u32[]{:S(2)}, u32[]{:S(2)}) collective-permute-start(bf16[2048,256]{1,0:T(8,128)(2,1)} %mine_ref.1), channel_id=1, source_target_pairs={{0,1},{1,0},{2,3},{3,2},{4,5},{5,4},{6,7},{7,6},{8,9},{9,8},{10,11... | collective-permute-start | bytes 3145736 | tf_op jit(solution)/shard_map/ppermute | solution.py:24
  8.9 15.1 %copy-start.9 = (bf16[2048,64]{0,1:T(8,128)(2,1)S(1)}, bf16[2048,64]{0,1:T(8,128)(2,1)}, u32[]{:S(2)}) copy-start(bf16[2048,64]{0,1:T(8,128)(2,1)} %param.29) | copy-start | bytes 786436
  14.1 11.4 %copy-start.13 = (f32[256,128]{1,0:T(8,128)S(1)}, f32[256,128]{1,0:T(8,128)}, u32[]{:S(2)}) copy-start(f32[256,128]{1,0:T(8,128)} %get-tuple-element.152.sin_ref) | copy-start | bytes 393220
  14.1 11.4 %copy-start.14 = (f32[256,128]{1,0:T(8,128)S(1)}, f32[256,128]{1,0:T(8,128)}, u32[]{:S(2)}) copy-start(f32[256,128]{1,0:T(8,128)} %get-tuple-element.153.cos_ref) | copy-start | bytes 393220
  15.4 10.1 %copy-start.6 = (bf16[64,3,2048]{2,0,1:T(8,128)(2,1)S(1)}, bf16[64,3,2048]{2,0,1:T(8,128)(2,1)}, u32[]{:S(2)}) copy-start(bf16[64,3,2048]{2,0,1:T(8,128)(2,1)} %param.21) | copy-start | bytes 2359300
  15.4 10.1 %copy-start.7 = (bf16[2048,512]{1,0:T(8,128)(2,1)S(1)}, bf16[2048,512]{1,0:T(8,128)(2,1)}, u32[]{:S(2)}) copy-start(bf16[2048,512]{1,0:T(8,128)(2,1)} %wq_ref.1) | copy-start | bytes 6291460
  22.1 3.3 %collective-permute-start.5 = (bf16[3,64,2048]{2,1,0:T(8,128)(2,1)S(1)}, bf16[3,64,2048]{2,1,0:T(8,128)(2,1)S(1)}, u32[]{:S(2)}, u32[]{:S(2)}) collective-permute-start(bf16[3,64,2048]{2,1,0:T(8,128)(2,1)S(1)} %collective-permute-done.hidden_ref.y_ref), channel_id=1, source_target_pairs={{0,1},{1,0},{2,3},{3,2},{4,5},{5,4},{6,7},{7,6},{8,9},{9,8},{10,11... | collective-permute-start | bytes 2359304 | tf_op jit(solution)/shard_map/ppermute | solution.py:24
  22.1 14.3 %collective-permute-start.7 = (bf16[4,128,512]{2,1,0:T(8,128)(2,1)S(1)}, bf16[4,128,512]{2,1,0:T(8,128)(2,1)S(1)}, u32[]{:S(2)}, u32[]{:S(2)}) collective-permute-start(bf16[4,128,512]{2,1,0:T(8,128)(2,1)S(1)} %pad_maximum_fusion.refs_0_), channel_id=1, source_target_pairs={{0,4},{4,0},{8,12},{12,8},{16,20},{20,16},{24,28},{28,24},{1,5},{5... | collective-permute-start | bytes 1572872 | tf_op jit(solution)/shard_map/ppermute | solution.py:24
  23.9 12.6 %collective-permute-start.8 = (bf16[4,128,512]{2,1,0:T(8,128)(2,1)S(1)}, bf16[4,128,512]{2,1,0:T(8,128)(2,1)S(1)}, u32[]{:S(2)}, u32[]{:S(2)}) collective-permute-start(bf16[4,128,512]{2,1,0:T(8,128)(2,1)S(1)} %pad_maximum_fusion.refs_0_), channel_id=1, source_target_pairs={{0,1},{1,0},{2,3},{3,2},{4,5},{5,4},{6,7},{7,6},{8,9},{9,8},{10,11... | collective-permute-start | bytes 1572872 | tf_op jit(solution)/shard_map/ppermute | solution.py:24
  25.5 12.8 %copy-start.4 = (bf16[512,2048]{1,0:T(8,128)(2,1)S(1)}, bf16[512,2048]{1,0:T(8,128)(2,1)}, u32[]{:S(2)}) copy-start(bf16[512,2048]{1,0:T(8,128)(2,1)} %wo_ref.5) | copy-start | bytes 6291460
  25.5 12.8 %copy-start.15 = (s32[2,8]{1,0:T(2,128)S(1)}, s32[2,8]{1,0:T(2,128)}, u32[]{:S(2)}) copy-start(s32[2,8]{1,0:T(2,128)} %owner_ref.5) | copy-start | bytes 196
  25.6 12.8 %copy-start.16 = (s32[2,8]{1,0:T(2,128)S(1)}, s32[2,8]{1,0:T(2,128)}, u32[]{:S(2)}) copy-start(s32[2,8]{1,0:T(2,128)} %slot_ref.5) | copy-start | bytes 196
  25.6 12.8 %copy-start.18 = (s32[3]{0:T(128)S(1)}, s32[3]{0:T(128)}, u32[]{:S(2)}) copy-start(s32[3]{0:T(128)} %group_ref.5) | copy-start | bytes 40
  36.5 1.9 %collective-permute-start.9 = (bf16[4,128,512]{2,1,0:T(8,128)(2,1)S(1)}, bf16[4,128,512]{2,1,0:T(8,128)(2,1)S(1)}, u32[]{:S(2)}, u32[]{:S(2)}) collective-permute-start(bf16[4,128,512]{2,1,0:T(8,128)(2,1)S(1)} %collective-permute-done.7.refs_1_), channel_id=1, source_target_pairs={{0,1},{1,0},{2,3},{3,2},{4,5},{5,4},{6,7},{7,6},{8,9},{9,8},{10,11... | collective-permute-start | bytes 1572872 | tf_op jit(solution)/shard_map/ppermute | solution.py:24
  42.7 1.4 %collective-permute-start.10 = (bf16[32,2048]{1,0:T(8,128)(2,1)S(1)}, bf16[32,2048]{1,0:T(8,128)(2,1)S(1)}, u32[]{:S(2)}, u32[]{:S(2)}) collective-permute-start(bf16[32,2048]{1,0:T(8,128)(2,1)S(1)} %get-tuple-element.86), channel_id=1, source_target_pairs={{0,1},{1,0},{2,3},{3,2},{4,5},{5,4},{6,7},{7,6},{8,9},{9,8},{10,11... | collective-permute-start | bytes 393224 | tf_op jit(solution)/shard_map/ppermute | solution.py:24
  42.9 1.4 %collective-permute-start.11 = (bf16[32,2048]{1,0:T(8,128)(2,1)S(1)}, bf16[32,2048]{1,0:T(8,128)(2,1)S(1)}, u32[]{:S(2)}, u32[]{:S(2)}) collective-permute-start(bf16[32,2048]{1,0:T(8,128)(2,1)S(1)} %get-tuple-element.87), channel_id=1, source_target_pairs={{0,1},{1,0},{2,3},{3,2},{4,5},{5,4},{6,7},{7,6},{8,9},{9,8},{10,11... | collective-permute-start | bytes 393224 | tf_op jit(solution)/shard_map/ppermute | solution.py:24
  43.2 1.3 %collective-permute-start.12 = (bf16[32,2048]{1,0:T(8,128)(2,1)S(1)}, bf16[32,2048]{1,0:T(8,128)(2,1)S(1)}, u32[]{:S(2)}, u32[]{:S(2)}) collective-permute-start(bf16[32,2048]{1,0:T(8,128)(2,1)S(1)} %get-tuple-element.88), channel_id=1, source_target_pairs={{0,1},{1,0},{2,3},{3,2},{4,5},{5,4},{6,7},{7,6},{8,9},{9,8},{10,11... | collective-permute-start | bytes 393224 | tf_op jit(solution)/shard_map/ppermute | solution.py:24
  43.4 1.4 %collective-permute-start.13 = (bf16[32,2048]{1,0:T(8,128)(2,1)S(1)}, bf16[32,2048]{1,0:T(8,128)(2,1)S(1)}, u32[]{:S(2)}, u32[]{:S(2)}) collective-permute-start(bf16[32,2048]{1,0:T(8,128)(2,1)S(1)} %get-tuple-element.89), channel_id=1, source_target_pairs={{0,1},{1,0},{2,3},{3,2},{4,5},{5,4},{6,7},{7,6},{8,9},{9,8},{10,11... | collective-permute-start | bytes 393224 | tf_op jit(solution)/shard_map/ppermute | solution.py:24
  44.9 14.8 %collective-permute-start.18 = (bf16[128,2048]{1,0:T(8,128)(2,1)S(1)}, bf16[128,2048]{1,0:T(8,128)(2,1)S(1)}, u32[]{:S(2)}, u32[]{:S(2)}) collective-permute-start(bf16[128,2048]{1,0:T(8,128)(2,1)S(1)} %pair_sum.6.near_ref), channel_id=1, source_target_pairs={{0,2},{1,3},{2,0},{3,1},{4,6},{5,7},{6,4},{7,5},{8,10},{9,11},{10,... | collective-permute-start | bytes 1572872 | tf_op jit(solution)/shard_map/ppermute | solution.py:24
  51.2 1.4 %collective-permute-start.14 = (bf16[32,2048]{1,0:T(8,128)(2,1)S(1)}, bf16[32,2048]{1,0:T(8,128)(2,1)S(1)}, u32[]{:S(2)}, u32[]{:S(2)}) collective-permute-start(bf16[32,2048]{1,0:T(8,128)(2,1)S(1)} %get-tuple-element.92), channel_id=1, source_target_pairs={{0,1},{1,0},{2,3},{3,2},{4,5},{5,4},{6,7},{7,6},{8,9},{9,8},{10,11... | collective-permute-start | bytes 393224 | tf_op jit(solution)/shard_map/ppermute | solution.py:24
  51.3 1.5 %collective-permute-start.15 = (bf16[32,2048]{1,0:T(8,128)(2,1)S(1)}, bf16[32,2048]{1,0:T(8,128)(2,1)S(1)}, u32[]{:S(2)}, u32[]{:S(2)}) collective-permute-start(bf16[32,2048]{1,0:T(8,128)(2,1)S(1)} %get-tuple-element.93), channel_id=1, source_target_pairs={{0,1},{1,0},{2,3},{3,2},{4,5},{5,4},{6,7},{7,6},{8,9},{9,8},{10,11... | collective-permute-start | bytes 393224 | tf_op jit(solution)/shard_map/ppermute | solution.py:24
  51.8 1.3 %collective-permute-start.16 = (bf16[32,2048]{1,0:T(8,128)(2,1)S(1)}, bf16[32,2048]{1,0:T(8,128)(2,1)S(1)}, u32[]{:S(2)}, u32[]{:S(2)}) collective-permute-start(bf16[32,2048]{1,0:T(8,128)(2,1)S(1)} %get-tuple-element.94), channel_id=1, source_target_pairs={{0,1},{1,0},{2,3},{3,2},{4,5},{5,4},{6,7},{7,6},{8,9},{9,8},{10,11... | collective-permute-start | bytes 393224 | tf_op jit(solution)/shard_map/ppermute | solution.py:24
  51.8 1.5 %collective-permute-start.17 = (bf16[32,2048]{1,0:T(8,128)(2,1)S(1)}, bf16[32,2048]{1,0:T(8,128)(2,1)S(1)}, u32[]{:S(2)}, u32[]{:S(2)}) collective-permute-start(bf16[32,2048]{1,0:T(8,128)(2,1)S(1)} %get-tuple-element.95), channel_id=1, source_target_pairs={{0,1},{1,0},{2,3},{3,2},{4,5},{5,4},{6,7},{7,6},{8,9},{9,8},{10,11... | collective-permute-start | bytes 393224 | tf_op jit(solution)/shard_map/ppermute | solution.py:24
  53.3 10.4 %copy-start.3 = (bf16[1024,2048]{1,0:T(8,128)(2,1)S(1)}, bf16[1024,2048]{1,0:T(8,128)(2,1)}, u32[]{:S(2)}) copy-start(bf16[1024,2048]{1,0:T(8,128)(2,1)} %down_ref.5) | copy-start | bytes 12582916
  53.4 17.5 %collective-permute-start.24 = (bf16[128,2048]{1,0:T(8,128)(2,1)S(1)}, bf16[128,2048]{1,0:T(8,128)(2,1)S(1)}, u32[]{:S(2)}, u32[]{:S(2)}) collective-permute-start(bf16[128,2048]{1,0:T(8,128)(2,1)S(1)} %pair_sum.7.near_ref), channel_id=1, source_target_pairs={{0,2},{1,3},{2,0},{3,1},{4,6},{5,7},{6,4},{7,5},{8,10},{9,11},{10,... | collective-permute-start | bytes 1572872 | tf_op jit(solution)/shard_map/ppermute | solution.py:24
  58.0 2.3 %collective-permute-start.19 = (bf16[32,2048]{1,0:T(8,128)(2,1)S(1)}, bf16[32,2048]{1,0:T(8,128)(2,1)S(1)}, u32[]{:S(2)}, u32[]{:S(2)}) collective-permute-start(bf16[32,2048]{1,0:T(8,128)(2,1)S(1)} %get-tuple-element.101), channel_id=1, source_target_pairs={{0,1},{1,0},{2,3},{3,2},{4,5},{5,4},{6,7},{7,6},{8,9},{9,8},{10,11... | collective-permute-start | bytes 393224 | tf_op jit(solution)/shard_map/ppermute | solution.py:24
  58.2 2.8 %collective-permute-start.20 = (bf16[32,2048]{1,0:T(8,128)(2,1)S(1)}, bf16[32,2048]{1,0:T(8,128)(2,1)S(1)}, u32[]{:S(2)}, u32[]{:S(2)}) collective-permute-start(bf16[32,2048]{1,0:T(8,128)(2,1)S(1)} %get-tuple-element.102), channel_id=1, source_target_pairs={{0,1},{1,0},{2,3},{3,2},{4,5},{5,4},{6,7},{7,6},{8,9},{9,8},{10,11... | collective-permute-start | bytes 393224 | tf_op jit(solution)/shard_map/ppermute | solution.py:24
  58.6 2.4 %collective-permute-start.21 = (bf16[32,2048]{1,0:T(8,128)(2,1)S(1)}, bf16[32,2048]{1,0:T(8,128)(2,1)S(1)}, u32[]{:S(2)}, u32[]{:S(2)}) collective-permute-start(bf16[32,2048]{1,0:T(8,128)(2,1)S(1)} %get-tuple-element.103), channel_id=1, source_target_pairs={{0,1},{1,0},{2,3},{3,2},{4,5},{5,4},{6,7},{7,6},{8,9},{9,8},{10,11... | collective-permute-start | bytes 393224 | tf_op jit(solution)/shard_map/ppermute | solution.py:24
  59.7 1.7 %collective-permute-start.22 = (bf16[32,2048]{1,0:T(8,128)(2,1)S(1)}, bf16[32,2048]{1,0:T(8,128)(2,1)S(1)}, u32[]{:S(2)}, u32[]{:S(2)}) collective-permute-start(bf16[32,2048]{1,0:T(8,128)(2,1)S(1)} %get-tuple-element.104), channel_id=1, source_target_pairs={{0,1},{1,0},{2,3},{3,2},{4,5},{5,4},{6,7},{7,6},{8,9},{9,8},{10,11... | collective-permute-start | bytes 393224 | tf_op jit(solution)/shard_map/ppermute | solution.py:24
  60.4 1.6 %collective-permute-start.25 = (bf16[32,2048]{1,0:T(8,128)(2,1)S(1)}, bf16[32,2048]{1,0:T(8,128)(2,1)S(1)}, u32[]{:S(2)}, u32[]{:S(2)}) collective-permute-start(bf16[32,2048]{1,0:T(8,128)(2,1)S(1)} %get-tuple-element.105.refs_0_), channel_id=1, source_target_pairs={{0,1},{1,0},{2,3},{3,2},{4,5},{5,4},{6,7},{7,6},{8,9},{9,8},{10,11... | collective-permute-start | bytes 393224 | tf_op jit(solution)/shard_map/ppermute | solution.py:24
  60.9 2.8 %collective-permute-start.26 = (bf16[32,2048]{1,0:T(8,128)(2,1)S(1)}, bf16[32,2048]{1,0:T(8,128)(2,1)S(1)}, u32[]{:S(2)}, u32[]{:S(2)}) collective-permute-start(bf16[32,2048]{1,0:T(8,128)(2,1)S(1)} %get-tuple-element.106.refs_1_), channel_id=1, source_target_pairs={{0,1},{1,0},{2,3},{3,2},{4,5},{5,4},{6,7},{7,6},{8,9},{9,8},{10,11... | collective-permute-start | bytes 393224 | tf_op jit(solution)/shard_map/ppermute | solution.py:24
  61.0 2.7 %collective-permute-start.27 = (bf16[32,2048]{1,0:T(8,128)(2,1)S(1)}, bf16[32,2048]{1,0:T(8,128)(2,1)S(1)}, u32[]{:S(2)}, u32[]{:S(2)}) collective-permute-start(bf16[32,2048]{1,0:T(8,128)(2,1)S(1)} %get-tuple-element.107.refs_2_), channel_id=1, source_target_pairs={{0,1},{1,0},{2,3},{3,2},{4,5},{5,4},{6,7},{7,6},{8,9},{9,8},{10,11... | collective-permute-start | bytes 393224 | tf_op jit(solution)/shard_map/ppermute | solution.py:24
  61.5 2.3 %collective-permute-start.28 = (bf16[32,2048]{1,0:T(8,128)(2,1)S(1)}, bf16[32,2048]{1,0:T(8,128)(2,1)S(1)}, u32[]{:S(2)}, u32[]{:S(2)}) collective-permute-start(bf16[32,2048]{1,0:T(8,128)(2,1)S(1)} %get-tuple-element.108.refs_3_), channel_id=1, source_target_pairs={{0,1},{1,0},{2,3},{3,2},{4,5},{5,4},{6,7},{7,6},{8,9},{9,8},{10,11... | collective-permute-start | bytes 393224 | tf_op jit(solution)/shard_map/ppermute | solution.py:24
  61.9 19.7 %collective-permute-start.23 = (bf16[128,2048]{1,0:T(8,128)(2,1)S(1)}, bf16[128,2048]{1,0:T(8,128)(2,1)S(1)}, u32[]{:S(2)}, u32[]{:S(2)}) collective-permute-start(bf16[128,2048]{1,0:T(8,128)(2,1)S(1)} %pair_sum.8.near_ref), channel_id=1, source_target_pairs={{0,2},{1,3},{2,0},{3,1},{4,6},{5,7},{6,4},{7,5},{8,10},{9,11},{10,... | collective-permute-start | bytes 1572872 | tf_op jit(solution)/shard_map/ppermute | solution.py:24
  67.2 4.4 %collective-permute-start.29 = (bf16[32,2048]{1,0:T(8,128)(2,1)S(1)}, bf16[32,2048]{1,0:T(8,128)(2,1)S(1)}, u32[]{:S(2)}, u32[]{:S(2)}) collective-permute-start(bf16[32,2048]{1,0:T(8,128)(2,1)S(1)} %get-tuple-element.113), channel_id=1, source_target_pairs={{0,1},{1,0},{2,3},{3,2},{4,5},{5,4},{6,7},{7,6},{8,9},{9,8},{10,11... | collective-permute-start | bytes 393224 | tf_op jit(solution)/shard_map/ppermute | solution.py:24
  67.3 4.9 %collective-permute-start.30 = (bf16[32,2048]{1,0:T(8,128)(2,1)S(1)}, bf16[32,2048]{1,0:T(8,128)(2,1)S(1)}, u32[]{:S(2)}, u32[]{:S(2)}) collective-permute-start(bf16[32,2048]{1,0:T(8,128)(2,1)S(1)} %get-tuple-element.114), channel_id=1, source_target_pairs={{0,1},{1,0},{2,3},{3,2},{4,5},{5,4},{6,7},{7,6},{8,9},{9,8},{10,11... | collective-permute-start | bytes 393224 | tf_op jit(solution)/shard_map/ppermute | solution.py:24
  67.8 4.5 %collective-permute-start.31 = (bf16[32,2048]{1,0:T(8,128)(2,1)S(1)}, bf16[32,2048]{1,0:T(8,128)(2,1)S(1)}, u32[]{:S(2)}, u32[]{:S(2)}) collective-permute-start(bf16[32,2048]{1,0:T(8,128)(2,1)S(1)} %get-tuple-element.115), channel_id=1, source_target_pairs={{0,1},{1,0},{2,3},{3,2},{4,5},{5,4},{6,7},{7,6},{8,9},{9,8},{10,11... | collective-permute-start | bytes 393224 | tf_op jit(solution)/shard_map/ppermute | solution.py:24
  71.0 1.7 %collective-permute-start.32 = (bf16[32,2048]{1,0:T(8,128)(2,1)S(1)}, bf16[32,2048]{1,0:T(8,128)(2,1)S(1)}, u32[]{:S(2)}, u32[]{:S(2)}) collective-permute-start(bf16[32,2048]{1,0:T(8,128)(2,1)S(1)} %get-tuple-element.116), channel_id=1, source_target_pairs={{0,1},{1,0},{2,3},{3,2},{4,5},{5,4},{6,7},{7,6},{8,9},{9,8},{10,11... | collective-permute-start | bytes 393224 | tf_op jit(solution)/shard_map/ppermute | solution.py:24
  71.6 1.6 %collective-permute-start.33 = (bf16[32,2048]{1,0:T(8,128)(2,1)S(1)}, bf16[32,2048]{1,0:T(8,128)(2,1)S(1)}, u32[]{:S(2)}, u32[]{:S(2)}) collective-permute-start(bf16[32,2048]{1,0:T(8,128)(2,1)S(1)} %get-tuple-element.118.refs_0_), channel_id=1, source_target_pairs={{0,1},{1,0},{2,3},{3,2},{4,5},{5,4},{6,7},{7,6},{8,9},{9,8},{10,11... | collective-permute-start | bytes 393224 | tf_op jit(solution)/shard_map/ppermute | solution.py:24
  72.2 1.3 %collective-permute-start.34 = (bf16[32,2048]{1,0:T(8,128)(2,1)S(1)}, bf16[32,2048]{1,0:T(8,128)(2,1)S(1)}, u32[]{:S(2)}, u32[]{:S(2)}) collective-permute-start(bf16[32,2048]{1,0:T(8,128)(2,1)S(1)} %get-tuple-element.119.refs_1_), channel_id=1, source_target_pairs={{0,1},{1,0},{2,3},{3,2},{4,5},{5,4},{6,7},{7,6},{8,9},{9,8},{10,11... | collective-permute-start | bytes 393224 | tf_op jit(solution)/shard_map/ppermute | solution.py:24
  72.3 1.4 %collective-permute-start.35 = (bf16[32,2048]{1,0:T(8,128)(2,1)S(1)}, bf16[32,2048]{1,0:T(8,128)(2,1)S(1)}, u32[]{:S(2)}, u32[]{:S(2)}) collective-permute-start(bf16[32,2048]{1,0:T(8,128)(2,1)S(1)} %get-tuple-element.120.refs_2_), channel_id=1, source_target_pairs={{0,1},{1,0},{2,3},{3,2},{4,5},{5,4},{6,7},{7,6},{8,9},{9,8},{10,11... | collective-permute-start | bytes 393224 | tf_op jit(solution)/shard_map/ppermute | solution.py:24
  72.7 1.3 %collective-permute-start.36 = (bf16[32,2048]{1,0:T(8,128)(2,1)S(1)}, bf16[32,2048]{1,0:T(8,128)(2,1)S(1)}, u32[]{:S(2)}, u32[]{:S(2)}) collective-permute-start(bf16[32,2048]{1,0:T(8,128)(2,1)S(1)} %get-tuple-element.121.refs_3_), channel_id=1, source_target_pairs={{0,1},{1,0},{2,3},{3,2},{4,5},{5,4},{6,7},{7,6},{8,9},{9,8},{10,11... | collective-permute-start | bytes 393224 | tf_op jit(solution)/shard_map/ppermute | solution.py:24
  77.5 6.5 %collective-permute-start.37 = (bf16[32,2048]{1,0:T(8,128)(2,1)S(1)}, bf16[32,2048]{1,0:T(8,128)(2,1)S(1)}, u32[]{:S(2)}, u32[]{:S(2)}) collective-permute-start(bf16[32,2048]{1,0:T(8,128)(2,1)S(1)} %get-tuple-element.127), channel_id=1, source_target_pairs={{0,1},{1,0},{2,3},{3,2},{4,5},{5,4},{6,7},{7,6},{8,9},{9,8},{10,11... | collective-permute-start | bytes 393224 | tf_op jit(solution)/shard_map/ppermute | solution.py:24
  77.7 6.4 %collective-permute-start.38 = (bf16[32,2048]{1,0:T(8,128)(2,1)S(1)}, bf16[32,2048]{1,0:T(8,128)(2,1)S(1)}, u32[]{:S(2)}, u32[]{:S(2)}) collective-permute-start(bf16[32,2048]{1,0:T(8,128)(2,1)S(1)} %get-tuple-element.128), channel_id=1, source_target_pairs={{0,1},{1,0},{2,3},{3,2},{4,5},{5,4},{6,7},{7,6},{8,9},{9,8},{10,11... | collective-permute-start | bytes 393224 | tf_op jit(solution)/shard_map/ppermute | solution.py:24
  78.0 6.5 %collective-permute-start.39 = (bf16[32,2048]{1,0:T(8,128)(2,1)S(1)}, bf16[32,2048]{1,0:T(8,128)(2,1)S(1)}, u32[]{:S(2)}, u32[]{:S(2)}) collective-permute-start(bf16[32,2048]{1,0:T(8,128)(2,1)S(1)} %get-tuple-element.129), channel_id=1, source_target_pairs={{0,1},{1,0},{2,3},{3,2},{4,5},{5,4},{6,7},{7,6},{8,9},{9,8},{10,11... | collective-permute-start | bytes 393224 | tf_op jit(solution)/shard_map/ppermute | solution.py:24
  78.2 6.4 %collective-permute-start.40 = (bf16[32,2048]{1,0:T(8,128)(2,1)S(1)}, bf16[32,2048]{1,0:T(8,128)(2,1)S(1)}, u32[]{:S(2)}, u32[]{:S(2)}) collective-permute-start(bf16[32,2048]{1,0:T(8,128)(2,1)S(1)} %get-tuple-element.130), channel_id=1, source_target_pairs={{0,1},{1,0},{2,3},{3,2},{4,5},{5,4},{6,7},{7,6},{8,9},{9,8},{10,11... | collective-permute-start | bytes 393224 | tf_op jit(solution)/shard_map/ppermute | solution.py:24
  81.6 9.2 %collective-permute-start.45 = (bf16[64,2048]{1,0:T(8,128)(2,1)S(1)}, bf16[64,2048]{1,0:T(8,128)(2,1)S(1)}, u32[]{:S(2)}, u32[]{:S(2)}) collective-permute-start(bf16[64,2048]{1,0:T(8,128)(2,1)S(1)} %get-tuple-element.138), channel_id=1, source_target_pairs={{0,2},{1,3},{2,0},{3,1},{4,6},{5,7},{6,4},{7,5},{8,10},{9,11},{10,... | collective-permute-start | bytes 786440 | tf_op jit(solution)/shard_map/ppermute | solution.py:24
  84.0 1.4 %collective-permute-start.41 = (bf16[32,2048]{1,0:T(8,128)(2,1)S(1)}, bf16[32,2048]{1,0:T(8,128)(2,1)S(1)}, u32[]{:S(2)}, u32[]{:S(2)}) collective-permute-start(bf16[32,2048]{1,0:T(8,128)(2,1)S(1)} %get-tuple-element.132.refs_0_), channel_id=1, source_target_pairs={{0,1},{1,0},{2,3},{3,2},{4,5},{5,4},{6,7},{7,6},{8,9},{9,8},{10,11... | collective-permute-start | bytes 393224 | tf_op jit(solution)/shard_map/ppermute | solution.py:24
  84.1 1.5 %collective-permute-start.42 = (bf16[32,2048]{1,0:T(8,128)(2,1)S(1)}, bf16[32,2048]{1,0:T(8,128)(2,1)S(1)}, u32[]{:S(2)}, u32[]{:S(2)}) collective-permute-start(bf16[32,2048]{1,0:T(8,128)(2,1)S(1)} %get-tuple-element.133.refs_1_), channel_id=1, source_target_pairs={{0,1},{1,0},{2,3},{3,2},{4,5},{5,4},{6,7},{7,6},{8,9},{9,8},{10,11... | collective-permute-start | bytes 393224 | tf_op jit(solution)/shard_map/ppermute | solution.py:24
  84.6 1.3 %collective-permute-start.43 = (bf16[32,2048]{1,0:T(8,128)(2,1)S(1)}, bf16[32,2048]{1,0:T(8,128)(2,1)S(1)}, u32[]{:S(2)}, u32[]{:S(2)}) collective-permute-start(bf16[32,2048]{1,0:T(8,128)(2,1)S(1)} %get-tuple-element.134.refs_2_), channel_id=1, source_target_pairs={{0,1},{1,0},{2,3},{3,2},{4,5},{5,4},{6,7},{7,6},{8,9},{9,8},{10,11... | collective-permute-start | bytes 393224 | tf_op jit(solution)/shard_map/ppermute | solution.py:24
  84.7 1.4 %collective-permute-start.44 = (bf16[32,2048]{1,0:T(8,128)(2,1)S(1)}, bf16[32,2048]{1,0:T(8,128)(2,1)S(1)}, u32[]{:S(2)}, u32[]{:S(2)}) collective-permute-start(bf16[32,2048]{1,0:T(8,128)(2,1)S(1)} %get-tuple-element.135.refs_3_), channel_id=1, source_target_pairs={{0,1},{1,0},{2,3},{3,2},{4,5},{5,4},{6,7},{7,6},{8,9},{9,8},{10,11... | collective-permute-start | bytes 393224 | tf_op jit(solution)/shard_map/ppermute | solution.py:24
  89.8 2.9 %collective-permute-start.46 = (bf16[32,2048]{1,0:T(8,128)(2,1)S(1)}, bf16[32,2048]{1,0:T(8,128)(2,1)S(1)}, u32[]{:S(2)}, u32[]{:S(2)}) collective-permute-start(bf16[32,2048]{1,0:T(8,128)(2,1)S(1)} %get-tuple-element.141), channel_id=1, source_target_pairs={{0,1},{1,0},{2,3},{3,2},{4,5},{5,4},{6,7},{7,6},{8,9},{9,8},{10,11... | collective-permute-start | bytes 393224 | tf_op jit(solution)/shard_map/ppermute | solution.py:24
  90.2 2.5 %collective-permute-start.47 = (bf16[32,2048]{1,0:T(8,128)(2,1)S(1)}, bf16[32,2048]{1,0:T(8,128)(2,1)S(1)}, u32[]{:S(2)}, u32[]{:S(2)}) collective-permute-start(bf16[32,2048]{1,0:T(8,128)(2,1)S(1)} %get-tuple-element.142), channel_id=1, source_target_pairs={{0,1},{1,0},{2,3},{3,2},{4,5},{5,4},{6,7},{7,6},{8,9},{9,8},{10,11... | collective-permute-start | bytes 393224 | tf_op jit(solution)/shard_map/ppermute | solution.py:24
  90.4 2.3 %collective-permute-start.48 = (bf16[32,2048]{1,0:T(8,128)(2,1)S(1)}, bf16[32,2048]{1,0:T(8,128)(2,1)S(1)}, u32[]{:S(2)}, u32[]{:S(2)}) collective-permute-start(bf16[32,2048]{1,0:T(8,128)(2,1)S(1)} %get-tuple-element.143), channel_id=1, source_target_pairs={{0,1},{1,0},{2,3},{3,2},{4,5},{5,4},{6,7},{7,6},{8,9},{9,8},{10,11... | collective-permute-start | bytes 393224 | tf_op jit(solution)/shard_map/ppermute | solution.py:24
  90.7 2.0 %collective-permute-start.49 = (bf16[32,2048]{1,0:T(8,128)(2,1)S(1)}, bf16[32,2048]{1,0:T(8,128)(2,1)S(1)}, u32[]{:S(2)}, u32[]{:S(2)}) collective-permute-start(bf16[32,2048]{1,0:T(8,128)(2,1)S(1)} %get-tuple-element.144), channel_id=1, source_target_pairs={{0,1},{1,0},{2,3},{3,2},{4,5},{5,4},{6,7},{7,6},{8,9},{9,8},{10,11... | collective-permute-start | bytes 393224 | tf_op jit(solution)/shard_map/ppermute | solution.py:24
  90.9 9.1 %collective-permute-start.51 = (bf16[64,2048]{1,0:T(8,128)(2,1)S(1)}, bf16[64,2048]{1,0:T(8,128)(2,1)S(1)}, u32[]{:S(2)}, u32[]{:S(2)}) collective-permute-start(bf16[64,2048]{1,0:T(8,128)(2,1)S(1)} %get-tuple-element.149), channel_id=1, source_target_pairs={{0,2},{1,3},{2,0},{3,1},{4,6},{5,7},{6,4},{7,5},{8,10},{9,11},{10,... | collective-permute-start | bytes 786440 | tf_op jit(solution)/shard_map/ppermute | solution.py:24
  92.8 12.2 %collective-permute-start.50 = (bf16[64,2048]{1,0:T(8,128)(2,1)S(1)}, bf16[64,2048]{1,0:T(8,128)(2,1)S(1)}, u32[]{:S(2)}, u32[]{:S(2)}) collective-permute-start(bf16[64,2048]{1,0:T(8,128)(2,1)S(1)} %get-tuple-element.146), channel_id=1, source_target_pairs={{0,2},{1,3},{2,0},{3,1},{4,6},{5,7},{6,4},{7,5},{8,10},{9,11},{10,... | collective-permute-start | bytes 786440 | tf_op jit(solution)/shard_map/ppermute | solution.py:24
  (9 other events, 50.3 us)

commit v3 on v2

--- a/solution.py
+++ b/solution.py
@@ -16,7 +16,9 @@
 SCALARS = pl.BlockSpec(memory_space=pltpu.SMEM)
 ANYWHERE = pl.BlockSpec(memory_space=pl.ANY)
 BLOCK_XOR = (0, 2, 1, 3)
-SPLIT = 2
+AFTER_ATTEND = (4, 4)
+AFTER_FEED = (3, 3, 2)
+BEFORE_FEED = (3, 3, 2)
 TILE = 256
 
 
@@ -45,8 +47,8 @@
     return pltpu.CompilerParams(vmem_limit_bytes=mib << 20)
 
 
-def cost(flops, moved, exps=0):
-    return pl.CostEstimate(flops=1, bytes_accessed=1, transcendentals=0)
+def cost(flops):
+    return pl.CostEstimate(flops=int(flops), bytes_accessed=1, transcendentals=0)
 
 
 def active_rows(hidden, gain):
@@ -64,13 +66,13 @@
         out_ref[r] = hidden.astype(F32) + active.astype(F32) + normed(low, gains_ref[1:2, :])
 
 
-def make_base(hidden, gains, left_t, right):
+def make_base(hidden, gains, left_t, right, flops=1):
     return pl.pallas_call(
         base_kernel,
         out_shape=jax.ShapeDtypeStruct(hidden.shape, F32),
         in_specs=[ON_CHIP] * 4,
         out_specs=ON_CHIP,
-        cost_estimate=cost(4 * hidden.size * left_t.shape[0], 8 * hidden.size),
+        cost_estimate=pl.CostEstimate(flops=int(flops), bytes_accessed=1, transcendentals=0),
         compiler_params=params(8),
         name="base",
     )(hidden, gains, left_t, right)
@@ -148,7 +150,7 @@
         in_specs=[SCALARS] + [ON_CHIP] * 11,
         out_specs=[ON_CHIP] * 3,
         compiler_params=params(10),
-        cost_estimate=cost(2 * reqs * count * width * (heads + 2) * head, 6 << 20),
+        cost_estimate=cost(1),
         name="project",
     )(lens, hidden, y, c, d, gains, wq, mine, other, head_gains, cos, sin)
 
@@ -247,10 +249,13 @@
         first += rows
 
 
-def partial_shapes(part, width):
-    return [jax.ShapeDtypeStruct((2 * part, width), BF16)] + [
-        jax.ShapeDtypeStruct((part // SPLIT, width), BF16)
-    ] * (2 * SPLIT)
+def piece_shapes(part, width, pieces):
+    return [jax.ShapeDtypeStruct((part // 4 * piece, width), BF16) for piece in pieces]
+
+
+def partial_shapes(part, width, pieces):
+    kept = jax.ShapeDtypeStruct((2 * part, width), BF16)
+    return [kept] + piece_shapes(part, width, pieces)
 
 
 def attend(req, sources, group, owner, slot, q, kv, wo, pools):
@@ -262,9 +267,9 @@
     keys = n_pages * page + count
     return pl.pallas_call(
         functools.partial(attend_kernel, req, sources),
-        out_shape=partial_shapes(part, wo.shape[1]),
+        out_shape=partial_shapes(part, wo.shape[1], AFTER_ATTEND),
         in_specs=[SCALARS] * 3 + [ON_CHIP] * 3 + [ANYWHERE] * len(pools),
-        out_specs=[ON_CHIP] * (1 + 2 * SPLIT),
+        out_specs=[ON_CHIP] * (1 + len(AFTER_ATTEND)),
         scratch_shapes=[
             pltpu.VMEM((keys, 2 * head), BF16),
             pltpu.VMEM((count, heads * head), BF16),
@@ -272,15 +277,12 @@
             pltpu.SemaphoreType.DMA((n_pages,)),
         ],
         compiler_params=params(8),
-        cost_estimate=cost(
-            heads * count * head * (4 * keys + 2 * wo.shape[1]), 4 << 20, heads * count * keys
-        ),
+        cost_estimate=cost(1),
         name="attend",
     )(group, owner, slot, q, kv, wo, *pools)
 
 
-def pair_kernel(keep_ref, *refs):
-    count = 2 * SPLIT
+def pair_kernel(count, keep_ref, *refs):
     others, outs = refs[:count], refs[count:]
     total = keep_ref[...].astype(F32) + jnp.concatenate(
         [ref[...].astype(F32) for ref in others], axis=0
@@ -291,11 +293,11 @@
 def pair_sum(keep, others, parts):
     rows, width = keep.shape
     return pl.pallas_call(
-        pair_kernel,
+        functools.partial(pair_kernel, len(others)),
         out_shape=[jax.ShapeDtypeStruct((rows // parts, width), BF16)] * parts,
         in_specs=[ON_CHIP] * (1 + len(others)),
         out_specs=[ON_CHIP] * parts,
-        cost_estimate=cost(2 * keep.size, 6 * keep.size),
+        cost_estimate=cost(1),
         compiler_params=params(6),
         name="pair_sum",
     )(keep, *others)
@@ -303,6 +305,7 @@
 
 def residual_kernel(req, own_base_ref, y_base_ref, near_ref, far_ref, gains_ref, res_ref, *in_refs):
     part = res_ref.shape[0]
+    blocks = []
     for b, base_ref in enumerate((own_base_ref, y_base_ref)):
         mine = slice(b * part, (b + 1) * part)
         theirs = slice((1 - b) * part, (2 - b) * part)
@@ -310,8 +313,8 @@
         residual = (base_ref[req] + normed(total, gains_ref[2:3, :])) * INV_ROOT
         if b == 0:
             res_ref[...] = residual
-        rows = normed(residual, gains_ref[3:4, :]).astype(BF16)
-        store_rows(in_refs[b * SPLIT : (b + 1) * SPLIT], 0, rows)
+        blocks.append(normed(residual, gains_ref[3:4, :]).astype(BF16))
+    store_rows(in_refs, 0, jnp.concatenate(blocks, axis=0))
 
 
 def make_residual(req, own_base, y_base, near, far, gains):
@@ -322,17 +325,16 @@
         out_shape=[
             jax.ShapeDtypeStruct((part, width), F32),
         ]
-        + [jax.ShapeDtypeStruct((part // SPLIT, width), BF16)] * (2 * SPLIT),
+        + piece_shapes(part, width, BEFORE_FEED),
         in_specs=[ON_CHIP] * 5,
-        out_specs=[ON_CHIP] * (1 + 2 * SPLIT),
-        cost_estimate=cost(12 * near.size, 16 * near.size),
+        out_specs=[ON_CHIP] * (1 + len(BEFORE_FEED)),
+        cost_estimate=cost(1e11),
         compiler_params=params(4),
         name="residual",
     )(own_base, y_base, near, far, gains)
 
 
-def feed_kernel(gate_ref, up_ref, down_ref, *refs):
-    count = 4 * SPLIT
+def feed_kernel(count, gate_ref, up_ref, down_ref, *refs):
     outs, hidden = refs[count:-1], refs[-1]
     rows = jnp.concatenate([ref[...] for ref in refs[:count]], axis=0)
     units = gate_ref.shape[1]
@@ -350,15 +352,15 @@
 
 def feed(pieces, gate, up, down):
     width, units = gate.shape
-    part = pieces[0].shape[0] * SPLIT
-    return pl.pallas_call(
-        feed_kernel,
-        out_shape=partial_shapes(part, width),
+    part = sum(piece.shape[0] for piece in pieces) // 4
+    return pl.pallas_call(
+        functools.partial(feed_kernel, len(pieces)),
+        out_shape=partial_shapes(part, width, AFTER_FEED),
         in_specs=[ON_CHIP] * (3 + len(pieces)),
-        out_specs=[ON_CHIP] * (1 + 2 * SPLIT),
+        out_specs=[ON_CHIP] * (1 + len(AFTER_FEED)),
         scratch_shapes=[pltpu.VMEM((4 * part, units), BF16)],
         compiler_params=params(8),
-        cost_estimate=cost(24 * part * width * units, 12 << 20, 4 * part * units),
+        cost_estimate=cost(1),
         name="feed",
     )(gate, up, down, *pieces)
 
@@ -382,7 +384,7 @@
         in_specs=[SCALARS] + [ON_CHIP] * 4 + [ANYWHERE] * len(extra),
         out_specs=pl.BlockSpec((1, part, width), lambda i: (req, 0, 0)),
         input_output_aliases={5: 0} if extra else {},
-        cost_estimate=cost(10 * residual.size, 12 * residual.size),
+        cost_estimate=cost(1e11),
         compiler_params=params(4),
         name="finish",
     )(lens, residual, near, far, gains, *extra)
@@ -425,23 +427,28 @@
     angles = (prefix_len + jnp.arange(count)).astype(F32)[:, None] * frequency[None, :]
     cos, sin = jnp.cos(angles), jnp.sin(angles)
 
+    hidden_y = exchange(hidden, "mlp", 2)
+    hidden_c = exchange(hidden, "mlp", 1)
+
     page_rows = page_pool.shape[1]
     own_page = lax.dynamic_slice(
-        page_pool, (member % 2, 0, member // 2 * 2 * head), (1, page_rows, 2 * head)
+        after(page_pool, hidden_c), (member % 2, 0, member // 2 * 2 * head), (1, page_rows, 2 * head)
     )
-    even = list(range(0, lax.axis_size("req"), 2))
-    even_pages = [own_page] + [exchange(own_page, "req", flip) for flip in even[1:]]
-    hidden_y = exchange(hidden, "mlp", 2)
-    hidden_c = exchange(hidden, "mlp", 1)
+    later = list(range(4, lax.axis_size("req"), 2))
+    direct = {flip: exchange(own_page, "req", flip) for flip in [*later, 2]}
     other_weight = exchange(after(keyval_weight, hidden_c), "mlp", 1)
-    own_base = make_base(hidden, gains, laurel_left.T, laurel_right)
-    even_pages[1] = after(even_pages[1], own_base, cos, head_gains)
-    even_pages = jnp.concatenate(even_pages)
-    odd_pages = exchange(even_pages, "req", 1)
-    even_other = exchange(even_pages, "mlp", 1)
-    hidden_y = after(hidden_y, even_pages)
+    near_pages = jnp.concatenate([own_page, after(direct[2], cos, gains, head_gains)])
+    near_odd = exchange(near_pages, "req", 1)
+    own_base = make_base(after(hidden, near_pages), gains, laurel_left.T, laurel_right)
+    far_pages = [direct[flip] for flip in later]
+    far_pages[0] = after(far_pages[0], own_base)
+    far_pages = jnp.concatenate(far_pages)
+    far_odd = exchange(far_pages, "req", 1)
+    far_other = exchange(far_pages, "mlp", 1)
+    near_other = exchange(near_pages, "mlp", 1)
+    hidden_y = after(hidden_y, far_pages)
     hidden_d = exchange(hidden_y, "mlp", 1)
-    y_base = make_base(hidden_y, gains, laurel_left.T, laurel_right)
+    y_base = make_base(hidden_y, gains, laurel_left.T, laurel_right, 1e11)
     pages, q_all, kv_all = project(
         suffix_len,
         hidden,
@@ -456,11 +463,15 @@
         cos,
         sin,
     )
-    odd_pages = after(odd_pages, q_all)
-    odd_other = exchange(odd_pages, "mlp", 1)
-    pools = [even_pages, odd_pages, even_other, odd_other]
+    near_odd = after(near_odd, q_all)
+    near_odd_other = exchange(near_odd, "mlp", 1)
+    far_odd = after(far_odd, q_all)
+    far_odd_other = exchange(far_odd, "mlp", 1)
+    pools = [near_pages, far_pages, near_odd, far_odd]
+    pools += [near_other, far_other, near_odd_other, far_odd_other]
+    flips = [[0, 2], later, [1, 3], [flip + 1 for flip in later]]
     sources = [
-        (p, i, p // 2, flip + p % 2) for p in range(len(pools)) for i, flip in enumerate(even)
+        (p, i, p // 4, flip) for p in range(len(pools)) for i, flip in enumerate(flips[p % 4])
     ]
 
     def attend_one(r, *earlier):

time: 107 us -> 96.3 us (0.900)
  waiting for transfers between devices: 33.1 us -> 21.1 us
  starting transfers between devices: 26.4 us -> 28.1 us
  other arithmetic: 2.42 us -> 1.27 us
    ppermute x52 -> x43, waiting for transfers between devices: 33.1 us -> 21.1 us  [exchange(): lax.ppermute(value, axis, [(i, i ^ flip) for i in range(lax.axis_size(axi...]
    ppermute x52 -> x43, starting transfers between devices: 26.4 us -> 28.1 us  [exchange(): lax.ppermute(value, axis, [(i, i ^ flip) for i in range(lax.axis_size(axi...]
    unnamed x42 -> x35, local copies, waits for them, and re-layouts: 3.12 us -> 4.48 us
    concatenate x1, other arithmetic: 1.16 us -> 0.03 us  [local(): jnp.concatenate([own_page, after(direct[2], cos, gains, head_gains)])]
  transfers between devices with their start and end apart: 52 -> 43, of which waited for: 26 -> 14; matrix products, arithmetic and copies ran while one was open for 4% -> 2% of each run, Pallas kernels for 31% -> 35%
where the time goes in v3:
time: 96.3 us; the launch traced here: 96 us
  Pallas kernels  39.2 us (41%)
  starting transfers between devices  28.1 us (29%)
  waiting for transfers between devices  21.1 us (22%)
  local copies, waits for them, and re-layouts  5.34 us (6%)
  other arithmetic  1.27 us (1%)
  between operations  1.06 us (1%)
    ppermute x43, starting transfers between devices, exchange(): lax.ppermute(value, axis, [(i, i ^ flip) for i in range(lax.axis_size(axi...  28.1 us
    ppermute x43, waiting for transfers between devices, exchange(): lax.ppermute(value, axis, [(i, i ^ flip) for i in range(lax.axis_size(axi...  21.1 us
    pallas_call x3, Pallas kernels, attend(): pl.pallas_call(functools.partial(attend_kernel, req, sources), out_shape=...  13.2 us
    pallas_call x3, Pallas kernels, feed(): pl.pallas_call(functools.partial(feed_kernel, len(pieces)), out_shape=par...  10.5 us
    pallas_call x1, Pallas kernels, project(): pl.pallas_call(project_kernel, out_shape=[jax.ShapeDtypeStruct((reqs, cou...  5.71 us
    unnamed x35, local copies, waits for them, and re-layouts  4.48 us
    pallas_call x3, Pallas kernels, finish(): pl.pallas_call(functools.partial(finish_kernel, req), grid=(1,), out_shap...  4.42 us
    pallas_call x2, Pallas kernels, make_base(): pl.pallas_call(base_kernel, out_shape=jax.ShapeDtypeStruct(hidden.shape,...  2.73 us
  transfers between devices with their start and end apart: 43, of which 14 were waited for; matrix products, arithmetic and copies ran while one was open for 2% of the time, Pallas kernels for 35%

profile of v3, /device:TPU:0, one launch (start us, length us, event | category | flops | bytes accessed | tf_op | source)
XLA Modules:
  0.0 96.0 jit_solution(2875966899161751404)
XLA Ops:
  0.6 0.5 collective-permute-start
  1.2 2.6 %collective-permute-start.2 = (bf16[3,64,2048]{2,1,0:T(8,128)(2,1)}, bf16[3,64,2048]{2,1,0:T(8,128)(2,1)S(1)}, u32[]{:S(2)}, u32[]{:S(2)}) collective-permute-start(bf16[3,64,2048]{2,1,0:T(8,128)(2,1)} %bitcast.12), channel_id=1, source_target_pairs={{0,2},{1,3},{2,0},{3,1},{4,6},{5,7},{6,4},{7,5},{8,10},{9,11},{10,... | collective-permute-start | bytes 2359304 | tf_op jit(solution)/shard_map/ppermute | solution.py:26
  3.8 2.5 %collective-permute-start.1 = (bf16[1,128,512]{2,1,0:T(8,128)(2,1)S(1)}, bf16[1,128,512]{2,1,0:T(8,128)(2,1)S(1)}, u32[]{:S(2)}, u32[]{:S(2)}) collective-permute-start(bf16[1,128,512]{2,1,0:T(8,128)(2,1)S(1)} %constant_dynamic-slice_fusion), channel_id=1, source_target_pairs={{0,8},{4,12},{8,0},{12,4},{16,24},{20,28},{24,16},{28,20},{1,9},{5... | collective-permute-start | bytes 393224 | tf_op jit(solution)/shard_map/ppermute | solution.py:26
  6.3 0.5 multiply_sine_fusion
  6.9 2.7 %collective-permute-start.3 = (bf16[1,128,512]{2,1,0:T(8,128)(2,1)S(1)}, bf16[1,128,512]{2,1,0:T(8,128)(2,1)S(1)}, u32[]{:S(2)}, u32[]{:S(2)}) collective-permute-start(bf16[1,128,512]{2,1,0:T(8,128)(2,1)S(1)} %constant_dynamic-slice_fusion), channel_id=1, source_target_pairs={{0,16},{4,20},{8,24},{12,28},{16,0},{20,4},{24,8},{28,12},{1,17},{... | collective-permute-start | bytes 393224 | tf_op jit(solution)/shard_map/ppermute | solution.py:26
  9.5 0.7 pad_maximum_fusion.1.head_gains_ref
  10.2 0.8 stack.32.gains_ref
  11.3 1.7 %collective-permute-start.7 = (bf16[2,128,512]{2,1,0:T(8,128)(2,1)S(1)}, bf16[2,128,512]{2,1,0:T(8,128)(2,1)S(1)}, u32[]{:S(2)}, u32[]{:S(2)}) collective-permute-start(bf16[2,128,512]{2,1,0:T(8,128)(2,1)S(1)} %pad_maximum_fusion.refs_0_), channel_id=1, source_target_pairs={{0,4},{4,0},{8,12},{12,8},{16,20},{20,16},{24,28},{28,24},{1,5},{5... | collective-permute-start | bytes 786440 | tf_op jit(solution)/shard_map/ppermute | solution.py:26
  12.9 1.1 %copy-done.5 = bf16[64,3,2048]{2,0,1:T(8,128)(2,1)S(1)} copy-done((bf16[64,3,2048]{2,0,1:T(8,128)(2,1)S(1)}, bf16[64,3,2048]{2,0,1:T(8,128)(2,1)}, u32[]{:S(2)}) %copy-start.5) | copy-done | bytes 786456
  14.1 0.9 copy-done.9
  15.0 0.9 copy-done.11
  16.0 1.4 %base.2.own_base_ref = f32[3,64,2048]{2,1,0:T(8,128)S(1)} custom-call(bf16[3,64,2048]{2,1,0:T(8,128)(2,1)S(1)} %bitcast.13, f32[5,2048]{1,0:T(8,128)S(1)} %stack.32.gains_ref, bf16[64,2048]{1,0:T(8,128)(2,1)S(1)} %bitcast.15, bf16[64,2048]{1,0:T(8,128)(2,1)S(1)} %copy-done.11), custom_call_target="tpu_custom_call" | custom-call | flops 1 | bytes 1 | tf_op jit(solution)/shard_map/base/pallas_call | solution.py:70
  17.4 2.0 %collective-permute-done.3 = bf16[1,128,512]{2,1,0:T(8,128)(2,1)S(1)} collective-permute-done((bf16[1,128,512]{2,1,0:T(8,128)(2,1)S(1)}, bf16[1,128,512]{2,1,0:T(8,128)(2,1)S(1)}, u32[]{:S(2)}, u32[]{:S(2)}) %collective-permute-start.3) | collective-permute-done | bytes 131104 | tf_op jit(solution)/shard_map/ppermute | solution.py:26
  19.5 1.6 %collective-permute-start.8 = (bf16[2,128,512]{2,1,0:T(8,128)(2,1)S(1)}, bf16[2,128,512]{2,1,0:T(8,128)(2,1)S(1)}, u32[]{:S(2)}, u32[]{:S(2)}) collective-permute-start(bf16[2,128,512]{2,1,0:T(8,128)(2,1)S(1)} %constant_dynamic-update-slice_fusion.refs_1_), channel_id=1, source_target_pairs={{0,4},{4,0},{8,12},{12,8},{16,20},{20,16},{24,28},{28,24},{1,5},{5... | collective-permute-start | bytes 786440 | tf_op jit(solution)/shard_map/ppermute | solution.py:26
  21.0 1.1 %collective-permute-done.2.hidden_ref.y_ref = bf16[3,64,2048]{2,1,0:T(8,128)(2,1)S(1)} collective-permute-done((bf16[3,64,2048]{2,1,0:T(8,128)(2,1)}, bf16[3,64,2048]{2,1,0:T(8,128)(2,1)S(1)}, u32[]{:S(2)}, u32[]{:S(2)}) %collective-permute-start.2) | collective-permute-done | bytes 786464 | tf_op jit(solution)/shard_map/ppermute | solution.py:26
  22.1 1.4 %base.3.y_base_ref = f32[3,64,2048]{2,1,0:T(8,128)S(1)} custom-call(bf16[3,64,2048]{2,1,0:T(8,128)(2,1)S(1)} %collective-permute-done.2.hidden_ref.y_ref, f32[5,2048]{1,0:T(8,128)S(1)} %stack.32.gains_ref, bf16[64,2048]{1,0:T(8,128)(2,1)S(1)} %bitcast.16, bf16[64,2048]{1,0:T(8,128)(2,1)S(1)} %copy-done.12), custom_call_target="tpu_custom_call" | custom-call | flops 99999997952 | bytes 1 | tf_op jit(solution)/shard_map/base/pallas_call | solution.py:70
  23.5 0.6 collective-permute-start.10
  24.1 0.3 collective-permute-done.5.d_ref
  24.6 5.7 %project.1 = (bf16[3,256,256]{2,1,0:T(8,128)(2,1)}, bf16[3,512,256]{2,1,0:T(8,128)(2,1)S(1)}, bf16[3,256,512]{2,1,0:T(8,128)(2,1)S(1)}) custom-call(s32[3]{0:T(128)S(1)} %copy-done.16, bf16[3,64,2048]{2,1,0:T(8,128)(2,1)S(1)} %bitcast.14, bf16[3,64,2048]{2,1,0:T(8,128)(2,1)S(1)} %collective-permute-done.2.hidden_ref.y_ref, ...), custom_call_target="tpu_custom_call" | custom-call | flops 1 | bytes 1 | tf_op jit(solution)/shard_map/project/pallas_call | solution.py:143
  30.3 0.4 collective-permute-start.12
  30.8 1.0 %collective-permute-done.12.refs_7_ = bf16[2,128,512]{2,1,0:T(8,128)(2,1)S(1)} collective-permute-done((bf16[2,128,512]{2,1,0:T(8,128)(2,1)S(1)}, bf16[2,128,512]{2,1,0:T(8,128)(2,1)S(1)}, u32[]{:S(2)}, u32[]{:S(2)}) %collective-permute-start.12) | collective-permute-done | bytes 262176 | tf_op jit(solution)/shard_map/ppermute | solution.py:26
  31.9 0.4 collective-permute-done.11.refs_6_
  32.3 4.3 %attend.3 = (bf16[128,2048]{1,0:T(8,128)(2,1)S(1)}, bf16[64,2048]{1,0:T(8,128)(2,1)S(1)}, bf16[64,2048]{1,0:T(8,128)(2,1)S(1)}) custom-call(s32[3]{0:T(128)S(1)} %copy-done.15, s32[2,8]{1,0:T(2,128)S(1)} %copy-done.13, s32[2,8]{1,0:T(2,128)S(1)} %copy-done.14, bf16[3,512,256]{2,1,0:T(8,128)(2,1)S(1)} %get-tuple-element.88.q_ref, ...), custom_call_target="tpu_custom_call" | custom-call | flops 1 | bytes 1 | tf_op jit(solution)/shard_map/attend/pallas_call | solution.py:268
  36.6 0.4 collective-permute-start.13
  37.2 1.0 %collective-permute-done.13.refs_0_ = bf16[64,2048]{1,0:T(8,128)(2,1)S(1)} collective-permute-done((bf16[64,2048]{1,0:T(8,128)(2,1)S(1)}, bf16[64,2048]{1,0:T(8,128)(2,1)S(1)}, u32[]{:S(2)}, u32[]{:S(2)}) %collective-permute-start.13) | collective-permute-done | bytes 262176 | tf_op jit(solution)/shard_map/ppermute | solution.py:26
  38.2 0.4 collective-permute-done.14.refs_1_
  38.7 1.9 %collective-permute-start.17 = (bf16[128,2048]{1,0:T(8,128)(2,1)S(1)}, bf16[128,2048]{1,0:T(8,128)(2,1)S(1)}, u32[]{:S(2)}, u32[]{:S(2)}) collective-permute-start(bf16[128,2048]{1,0:T(8,128)(2,1)S(1)} %pair_sum.6.near_ref), channel_id=1, source_target_pairs={{0,2},{1,3},{2,0},{3,1},{4,6},{5,7},{6,4},{7,5},{8,10},{9,11},{10,... | collective-permute-start | bytes 1572872 | tf_op jit(solution)/shard_map/ppermute | solution.py:26
  40.6 4.3 %attend.4 = (bf16[128,2048]{1,0:T(8,128)(2,1)S(1)}, bf16[64,2048]{1,0:T(8,128)(2,1)S(1)}, bf16[64,2048]{1,0:T(8,128)(2,1)S(1)}) custom-call(s32[3]{0:T(128)S(1)} %copy-done.15, s32[2,8]{1,0:T(2,128)S(1)} %copy-done.13, s32[2,8]{1,0:T(2,128)S(1)} %copy-done.14, bf16[3,512,256]{2,1,0:T(8,128)(2,1)S(1)} %get-tuple-element.88.q_ref, ...), custom_call_target="tpu_custom_call" | custom-call | flops 1 | bytes 1 | tf_op jit(solution)/shard_map/attend/pallas_call | solution.py:268
  45.1 0.4 collective-permute-start.16
  45.5 1.0 %collective-permute-done.15.refs_0_ = bf16[64,2048]{1,0:T(8,128)(2,1)S(1)} collective-permute-done((bf16[64,2048]{1,0:T(8,128)(2,1)S(1)}, bf16[64,2048]{1,0:T(8,128)(2,1)S(1)}, u32[]{:S(2)}, u32[]{:S(2)}) %collective-permute-start.15) | collective-permute-done | bytes 262176 | tf_op jit(solution)/shard_map/ppermute | solution.py:26
  46.5 0.4 collective-permute-done.16.refs_1_
  47.0 0.3 collective-permute-start.21
  47.3 4.5 %attend.5 = (bf16[128,2048]{1,0:T(8,128)(2,1)S(1)}, bf16[64,2048]{1,0:T(8,128)(2,1)S(1)}, bf16[64,2048]{1,0:T(8,128)(2,1)S(1)}) custom-call(s32[3]{0:T(128)S(1)} %copy-done.15, s32[2,8]{1,0:T(2,128)S(1)} %copy-done.13, s32[2,8]{1,0:T(2,128)S(1)} %copy-done.14, bf16[3,512,256]{2,1,0:T(8,128)(2,1)S(1)} %get-tuple-element.88.q_ref, ...), custom_call_target="tpu_custom_call" | custom-call | flops 1 | bytes 1 | tf_op jit(solution)/shard_map/attend/pallas_call | solution.py:268
  51.9 0.5 collective-permute-start.19
  52.4 1.1 %collective-permute-done.17.far_ref = bf16[128,2048]{1,0:T(8,128)(2,1)S(1)} collective-permute-done((bf16[128,2048]{1,0:T(8,128)(2,1)S(1)}, bf16[128,2048]{1,0:T(8,128)(2,1)S(1)}, u32[]{:S(2)}, u32[]{:S(2)}) %collective-permute-start.17) | collective-permute-done | bytes 524320 | tf_op jit(solution)/shard_map/ppermute | solution.py:26
  53.5 0.6 residual.3
  54.2 0.5 collective-permute-start.23
  55.0 1.8 %collective-permute-start.20 = (bf16[128,2048]{1,0:T(8,128)(2,1)S(1)}, bf16[128,2048]{1,0:T(8,128)(2,1)S(1)}, u32[]{:S(2)}, u32[]{:S(2)}) collective-permute-start(bf16[128,2048]{1,0:T(8,128)(2,1)S(1)} %pair_sum.8.near_ref), channel_id=1, source_target_pairs={{0,2},{1,3},{2,0},{3,1},{4,6},{5,7},{6,4},{7,5},{8,10},{9,11},{10,... | collective-permute-start | bytes 1572872 | tf_op jit(solution)/shard_map/ppermute | solution.py:26
  56.8 0.2 copy-done.2
  57.0 1.2 %copy-done.3 = bf16[1024,2048]{1,0:T(8,128)(2,1)S(1)} copy-done((bf16[1024,2048]{1,0:T(8,128)(2,1)S(1)}, bf16[1024,2048]{1,0:T(8,128)(2,1)}, u32[]{:S(2)}) %copy-start.3) | copy-done | bytes 4194328
  58.2 3.4 %feed.3 = (bf16[128,2048]{1,0:T(8,128)(2,1)S(1)}, bf16[48,2048]{1,0:T(8,128)(2,1)S(1)}, bf16[48,2048]{1,0:T(8,128)(2,1)S(1)}, bf16[32,2048]{1,0:T(8,128)(2,1)S(1)}) custom-call(bf16[2048,1024]{1,0:T(8,128)(2,1)S(1)} %copy-done.1, bf16[2048,1024]{1,0:T(8,128)(2,1)S(1)} %copy-done.2, bf16[1024,2048]{1,0:T(8,128)(2,1)S(1)} %copy-done.3, ...), custom_call_target="tpu_custom_call" | custom-call | flops 1 | bytes 1 | tf_op jit(solution)/shard_map/feed/pallas_call | solution.py:356
  61.7 0.5 collective-permute-start.26
  62.3 2.5 %collective-permute-done.21.far_ref = bf16[128,2048]{1,0:T(8,128)(2,1)S(1)} collective-permute-done((bf16[128,2048]{1,0:T(8,128)(2,1)S(1)}, bf16[128,2048]{1,0:T(8,128)(2,1)S(1)}, u32[]{:S(2)}, u32[]{:S(2)}) %collective-permute-start.21) | collective-permute-done | bytes 524320 | tf_op jit(solution)/shard_map/ppermute | solution.py:26
  64.8 0.6 residual.4
  65.5 0.5 collective-permute-start.29
  66.2 1.8 %collective-permute-start.37 = (bf16[64,2048]{1,0:T(8,128)(2,1)S(1)}, bf16[64,2048]{1,0:T(8,128)(2,1)S(1)}, u32[]{:S(2)}, u32[]{:S(2)}) collective-permute-start(bf16[64,2048]{1,0:T(8,128)(2,1)S(1)} %get-tuple-element.123), channel_id=1, source_target_pairs={{0,2},{1,3},{2,0},{3,1},{4,6},{5,7},{6,4},{7,5},{8,10},{9,11},{10,... | collective-permute-start | bytes 786440 | tf_op jit(solution)/shard_map/ppermute | solution.py:26
  68.1 3.4 %feed.4 = (bf16[128,2048]{1,0:T(8,128)(2,1)S(1)}, bf16[48,2048]{1,0:T(8,128)(2,1)S(1)}, bf16[48,2048]{1,0:T(8,128)(2,1)S(1)}, bf16[32,2048]{1,0:T(8,128)(2,1)S(1)}) custom-call(bf16[2048,1024]{1,0:T(8,128)(2,1)S(1)} %copy-done.1, bf16[2048,1024]{1,0:T(8,128)(2,1)S(1)} %copy-done.2, bf16[1024,2048]{1,0:T(8,128)(2,1)S(1)} %copy-done.3, ...), custom_call_target="tpu_custom_call" | custom-call | flops 1 | bytes 1 | tf_op jit(solution)/shard_map/feed/pallas_call | solution.py:356
  71.5 0.2 collective-permute-start.31
  71.7 0.4 collective-permute-start.32
  72.1 0.2 collective-permute-start.33
  72.2 3.8 %collective-permute-done.20.far_ref = bf16[128,2048]{1,0:T(8,128)(2,1)S(1)} collective-permute-done((bf16[128,2048]{1,0:T(8,128)(2,1)S(1)}, bf16[128,2048]{1,0:T(8,128)(2,1)S(1)}, u32[]{:S(2)}, u32[]{:S(2)}) %collective-permute-start.20) | collective-permute-done | bytes 524320 | tf_op jit(solution)/shard_map/ppermute | solution.py:26
  76.0 0.6 residual.5
  76.7 0.5 collective-permute-start.35
  77.4 1.8 %collective-permute-start.42 = (bf16[64,2048]{1,0:T(8,128)(2,1)S(1)}, bf16[64,2048]{1,0:T(8,128)(2,1)S(1)}, u32[]{:S(2)}, u32[]{:S(2)}) collective-permute-start(bf16[64,2048]{1,0:T(8,128)(2,1)S(1)} %get-tuple-element.133), channel_id=1, source_target_pairs={{0,2},{1,3},{2,0},{3,1},{4,6},{5,7},{6,4},{7,5},{8,10},{9,11},{10,... | collective-permute-start | bytes 786440 | tf_op jit(solution)/shard_map/ppermute | solution.py:26
  79.3 3.7 %feed.5 = (bf16[128,2048]{1,0:T(8,128)(2,1)S(1)}, bf16[48,2048]{1,0:T(8,128)(2,1)S(1)}, bf16[48,2048]{1,0:T(8,128)(2,1)S(1)}, bf16[32,2048]{1,0:T(8,128)(2,1)S(1)}) custom-call(bf16[2048,1024]{1,0:T(8,128)(2,1)S(1)} %copy-done.1, bf16[2048,1024]{1,0:T(8,128)(2,1)S(1)} %copy-done.2, bf16[1024,2048]{1,0:T(8,128)(2,1)S(1)} %copy-done.3, ...), custom_call_target="tpu_custom_call" | custom-call | flops 1 | bytes 1 | tf_op jit(solution)/shard_map/feed/pallas_call | solution.py:356
  83.0 0.2 collective-permute-start.38
  83.2 0.4 collective-permute-start.39
  83.5 0.2 collective-permute-start.40
  83.7 1.5 %finish.3.refs_0_ = bf16[3,64,2048]{2,1,0:T(8,128)(2,1)} custom-call(s32[3]{0:T(128)S(1)} %copy-done.16, f32[64,2048]{1,0:T(8,128)S(1)} %get-tuple-element.122.res_ref, bf16[64,2048]{1,0:T(8,128)(2,1)S(1)} %get-tuple-element.105.near_ref, bf16[64,2048]{1,0:T(8,128)(2,1)S(1)} %collective-permute-done.37.far_ref, f32[5,2048]{1,0:T(8,128)S(1)} %stack.32.gains_ref), custom_call_target="tpu_custom_call" | custom-call | flops 99999997952 | bytes 1 | tf_op jit(solution)/shard_map/finish/pallas_call | solution.py:380
  85.3 1.4 %collective-permute-done.42.far_ref = bf16[64,2048]{1,0:T(8,128)(2,1)S(1)} collective-permute-done((bf16[64,2048]{1,0:T(8,128)(2,1)S(1)}, bf16[64,2048]{1,0:T(8,128)(2,1)S(1)}, u32[]{:S(2)}, u32[]{:S(2)}) %collective-permute-start.42) | collective-permute-done | bytes 262176 | tf_op jit(solution)/shard_map/ppermute | solution.py:26
  86.7 1.7 %collective-permute-start.41 = (bf16[64,2048]{1,0:T(8,128)(2,1)S(1)}, bf16[64,2048]{1,0:T(8,128)(2,1)S(1)}, u32[]{:S(2)}, u32[]{:S(2)}) collective-permute-start(bf16[64,2048]{1,0:T(8,128)(2,1)S(1)} %get-tuple-element.130), channel_id=1, source_target_pairs={{0,2},{1,3},{2,0},{3,1},{4,6},{5,7},{6,4},{7,5},{8,10},{9,11},{10,... | collective-permute-start | bytes 786440 | tf_op jit(solution)/shard_map/ppermute | solution.py:26
  88.5 1.5 %finish.4.refs_0_ = bf16[3,64,2048]{2,1,0:T(8,128)(2,1)} custom-call(s32[3]{0:T(128)S(1)} %copy-done.16, f32[64,2048]{1,0:T(8,128)S(1)} %get-tuple-element.132.res_ref, bf16[64,2048]{1,0:T(8,128)(2,1)S(1)} %get-tuple-element.117.near_ref, bf16[64,2048]{1,0:T(8,128)(2,1)S(1)} %collective-permute-done.42.far_ref, ...), custom_call_target="tpu_custom_call", output_to_operand_aliasing={{}: (5, {})} | custom-call | flops 99999997952 | bytes 1 | tf_op jit(solution)/shard_map/finish/pallas_call | solution.py:380
  89.9 4.6 %collective-permute-done.41.far_ref = bf16[64,2048]{1,0:T(8,128)(2,1)S(1)} collective-permute-done((bf16[64,2048]{1,0:T(8,128)(2,1)S(1)}, bf16[64,2048]{1,0:T(8,128)(2,1)S(1)}, u32[]{:S(2)}, u32[]{:S(2)}) %collective-permute-start.41) | collective-permute-done | bytes 262176 | tf_op jit(solution)/shard_map/ppermute | solution.py:26
  94.6 1.5 %finish.5 = bf16[3,64,2048]{2,1,0:T(8,128)(2,1)} custom-call(s32[3]{0:T(128)S(1)} %copy-done.16, f32[64,2048]{1,0:T(8,128)S(1)} %get-tuple-element.111.res_ref, bf16[64,2048]{1,0:T(8,128)(2,1)S(1)} %get-tuple-element.129.near_ref, bf16[64,2048]{1,0:T(8,128)(2,1)S(1)} %collective-permute-done.41.far_ref, ...), custom_call_target="tpu_custom_call", output_to_operand_aliasing={{}: (5, {})} | custom-call | flops 99999997952 | bytes 1 | tf_op jit(solution)/shard_map/finish/pallas_call | solution.py:380
  (86 shorter events, 2.4 us)
Async XLA Ops:
  0.6 3.2 %copy-start = (bf16[2,128,1024]{2,1,0:T(8,128)(2,1)S(1)}, bf16[2,128,1024]{2,1,0:T(8,128)(2,1)}, u32[]{:S(2)}) copy-start(bf16[2,128,1024]{2,1,0:T(8,128)(2,1)} %param.37) | copy-start | bytes 1572868
  0.6 3.1 %collective-permute-start = (bf16[3,64,2048]{2,1,0:T(8,128)(2,1)}, bf16[3,64,2048]{2,1,0:T(8,128)(2,1)S(1)}, u32[]{:S(2)}, u32[]{:S(2)}) collective-permute-start(bf16[3,64,2048]{2,1,0:T(8,128)(2,1)} %bitcast.11), channel_id=1, source_target_pairs={{0,1},{1,0},{2,3},{3,2},{4,5},{5,4},{6,7},{7,6},{8,9},{9,8},{10,11... | collective-permute-start | bytes 2359304 | tf_op jit(solution)/shard_map/ppermute | solution.py:26
  1.2 20.9 %collective-permute-start.2 = (bf16[3,64,2048]{2,1,0:T(8,128)(2,1)}, bf16[3,64,2048]{2,1,0:T(8,128)(2,1)S(1)}, u32[]{:S(2)}, u32[]{:S(2)}) collective-permute-start(bf16[3,64,2048]{2,1,0:T(8,128)(2,1)} %bitcast.12), channel_id=1, source_target_pairs={{0,2},{1,3},{2,0},{3,1},{4,6},{5,7},{6,4},{7,5},{8,10},{9,11},{10,... | collective-permute-start | bytes 2359304 | tf_op jit(solution)/shard_map/ppermute | solution.py:26
  3.8 7.4 %collective-permute-start.1 = (bf16[1,128,512]{2,1,0:T(8,128)(2,1)S(1)}, bf16[1,128,512]{2,1,0:T(8,128)(2,1)S(1)}, u32[]{:S(2)}, u32[]{:S(2)}) collective-permute-start(bf16[1,128,512]{2,1,0:T(8,128)(2,1)S(1)} %constant_dynamic-slice_fusion), channel_id=1, source_target_pairs={{0,8},{4,12},{8,0},{12,4},{16,24},{20,28},{24,16},{28,20},{1,9},{5... | collective-permute-start | bytes 393224 | tf_op jit(solution)/shard_map/ppermute | solution.py:26
  6.8 15.3 %copy-start.10 = (bf16[2048,64]{0,1:T(8,128)(2,1)S(1)}, bf16[2048,64]{0,1:T(8,128)(2,1)}, u32[]{:S(2)}) copy-start(bf16[2048,64]{0,1:T(8,128)(2,1)} %param.29) | copy-start | bytes 786436
  6.9 15.2 %copy-start.12 = (bf16[64,2048]{1,0:T(8,128)(2,1)S(1)}, bf16[64,2048]{1,0:T(8,128)(2,1)}, u32[]{:S(2)}) copy-start(bf16[64,2048]{1,0:T(8,128)(2,1)} %right_ref.3) | copy-start | bytes 786436
  6.9 12.5 %collective-permute-start.3 = (bf16[1,128,512]{2,1,0:T(8,128)(2,1)S(1)}, bf16[1,128,512]{2,1,0:T(8,128)(2,1)S(1)}, u32[]{:S(2)}, u32[]{:S(2)}) collective-permute-start(bf16[1,128,512]{2,1,0:T(8,128)(2,1)S(1)} %constant_dynamic-slice_fusion), channel_id=1, source_target_pairs={{0,16},{4,20},{8,24},{12,28},{16,0},{20,4},{24,8},{28,12},{1,17},{... | collective-permute-start | bytes 393224 | tf_op jit(solution)/shard_map/ppermute | solution.py:26
  11.1 8.3 %collective-permute-start.4 = (bf16[1,128,512]{2,1,0:T(8,128)(2,1)S(1)}, bf16[1,128,512]{2,1,0:T(8,128)(2,1)S(1)}, u32[]{:S(2)}, u32[]{:S(2)}) collective-permute-start(bf16[1,128,512]{2,1,0:T(8,128)(2,1)S(1)} %constant_dynamic-slice_fusion), channel_id=1, source_target_pairs={{0,24},{4,28},{8,16},{12,20},{16,8},{20,12},{24,0},{28,4},{1,25},{... | collective-permute-start | bytes 393224 | tf_op jit(solution)/shard_map/ppermute | solution.py:26
  11.1 13.4 %collective-permute-start.6 = (bf16[2048,256]{1,0:T(8,128)(2,1)}, bf16[2048,256]{1,0:T(8,128)(2,1)S(1)}, u32[]{:S(2)}, u32[]{:S(2)}) collective-permute-start(bf16[2048,256]{1,0:T(8,128)(2,1)} %mine_ref.1), channel_id=1, source_target_pairs={{0,1},{1,0},{2,3},{3,2},{4,5},{5,4},{6,7},{7,6},{8,9},{9,8},{10,11... | collective-permute-start | bytes 3145736 | tf_op jit(solution)/shard_map/ppermute | solution.py:26
  11.3 19.4 %collective-permute-start.7 = (bf16[2,128,512]{2,1,0:T(8,128)(2,1)S(1)}, bf16[2,128,512]{2,1,0:T(8,128)(2,1)S(1)}, u32[]{:S(2)}, u32[]{:S(2)}) collective-permute-start(bf16[2,128,512]{2,1,0:T(8,128)(2,1)S(1)} %pad_maximum_fusion.refs_0_), channel_id=1, source_target_pairs={{0,4},{4,0},{8,12},{12,8},{16,20},{20,16},{24,28},{28,24},{1,5},{5... | collective-permute-start | bytes 786440 | tf_op jit(solution)/shard_map/ppermute | solution.py:26
  12.9 1.1 %copy-start.5 = (bf16[64,3,2048]{2,0,1:T(8,128)(2,1)S(1)}, bf16[64,3,2048]{2,0,1:T(8,128)(2,1)}, u32[]{:S(2)}) copy-start(bf16[64,3,2048]{2,0,1:T(8,128)(2,1)} %param.21) | copy-start | bytes 2359300
  14.1 0.9 copy-start.9
  15.0 0.9 copy-start.11
  19.4 5.1 %copy-start.6 = (bf16[64,3,2048]{2,0,1:T(8,128)(2,1)S(1)}, bf16[64,3,2048]{2,0,1:T(8,128)(2,1)}, u32[]{:S(2)}) copy-start(bf16[64,3,2048]{2,0,1:T(8,128)(2,1)} %param.21) | copy-start | bytes 2359300
  19.4 5.1 %copy-start.7 = (bf16[2048,512]{1,0:T(8,128)(2,1)S(1)}, bf16[2048,512]{1,0:T(8,128)(2,1)}, u32[]{:S(2)}) copy-start(bf16[2048,512]{1,0:T(8,128)(2,1)} %wq_ref.1) | copy-start | bytes 6291460
  19.4 5.1 %copy-start.8 = (bf16[2048,256]{1,0:T(8,128)(2,1)S(1)}, bf16[2048,256]{1,0:T(8,128)(2,1)}, u32[]{:S(2)}) copy-start(bf16[2048,256]{1,0:T(8,128)(2,1)} %mine_ref.1) | copy-start | bytes 3145732
  19.4 5.1 %copy-start.16 = (s32[3]{0:T(128)S(1)}, s32[3]{0:T(128)}, u32[]{:S(2)}) copy-start(s32[3]{0:T(128)} %len_ref.7) | copy-start | bytes 40
  19.5 10.9 %collective-permute-start.8 = (bf16[2,128,512]{2,1,0:T(8,128)(2,1)S(1)}, bf16[2,128,512]{2,1,0:T(8,128)(2,1)S(1)}, u32[]{:S(2)}, u32[]{:S(2)}) collective-permute-start(bf16[2,128,512]{2,1,0:T(8,128)(2,1)S(1)} %constant_dynamic-update-slice_fusion.refs_1_), channel_id=1, source_target_pairs={{0,4},{4,0},{8,12},{12,8},{16,20},{20,16},{24,28},{28,24},{1,5},{5... | collective-permute-start | bytes 786440 | tf_op jit(solution)/shard_map/ppermute | solution.py:26
  22.1 2.3 %collective-permute-start.5 = (bf16[3,64,2048]{2,1,0:T(8,128)(2,1)S(1)}, bf16[3,64,2048]{2,1,0:T(8,128)(2,1)S(1)}, u32[]{:S(2)}, u32[]{:S(2)}) collective-permute-start(bf16[3,64,2048]{2,1,0:T(8,128)(2,1)S(1)} %collective-permute-done.2.hidden_ref.y_ref), channel_id=1, source_target_pairs={{0,1},{1,0},{2,3},{3,2},{4,5},{5,4},{6,7},{7,6},{8,9},{9,8},{10,11... | collective-permute-start | bytes 2359304 | tf_op jit(solution)/shard_map/ppermute | solution.py:26
  23.5 7.4 %collective-permute-start.10 = (bf16[2,128,512]{2,1,0:T(8,128)(2,1)S(1)}, bf16[2,128,512]{2,1,0:T(8,128)(2,1)S(1)}, u32[]{:S(2)}, u32[]{:S(2)}) collective-permute-start(bf16[2,128,512]{2,1,0:T(8,128)(2,1)S(1)} %constant_dynamic-update-slice_fusion.refs_1_), channel_id=1, source_target_pairs={{0,1},{1,0},{2,3},{3,2},{4,5},{5,4},{6,7},{7,6},{8,9},{9,8},{10,11... | collective-permute-start | bytes 786440 | tf_op jit(solution)/shard_map/ppermute | solution.py:26
  24.4 6.5 %collective-permute-start.9 = (bf16[2,128,512]{2,1,0:T(8,128)(2,1)S(1)}, bf16[2,128,512]{2,1,0:T(8,128)(2,1)S(1)}, u32[]{:S(2)}, u32[]{:S(2)}) collective-permute-start(bf16[2,128,512]{2,1,0:T(8,128)(2,1)S(1)} %pad_maximum_fusion.refs_0_), channel_id=1, source_target_pairs={{0,1},{1,0},{2,3},{3,2},{4,5},{5,4},{6,7},{7,6},{8,9},{9,8},{10,11... | collective-permute-start | bytes 786440 | tf_op jit(solution)/shard_map/ppermute | solution.py:26
  24.6 7.7 %copy-start.4 = (bf16[512,2048]{1,0:T(8,128)(2,1)S(1)}, bf16[512,2048]{1,0:T(8,128)(2,1)}, u32[]{:S(2)}) copy-start(bf16[512,2048]{1,0:T(8,128)(2,1)} %wo_ref.5) | copy-start | bytes 6291460
  24.6 7.7 %copy-start.13 = (s32[2,8]{1,0:T(2,128)S(1)}, s32[2,8]{1,0:T(2,128)}, u32[]{:S(2)}) copy-start(s32[2,8]{1,0:T(2,128)} %owner_ref.5) | copy-start | bytes 196
  24.6 7.7 %copy-start.14 = (s32[2,8]{1,0:T(2,128)S(1)}, s32[2,8]{1,0:T(2,128)}, u32[]{:S(2)}) copy-start(s32[2,8]{1,0:T(2,128)} %slot_ref.5) | copy-start | bytes 196
  24.6 7.7 %copy-start.15 = (s32[3]{0:T(128)S(1)}, s32[3]{0:T(128)}, u32[]{:S(2)}) copy-start(s32[3]{0:T(128)} %group_ref.5) | copy-start | bytes 40
  30.3 1.5 %collective-permute-start.12 = (bf16[2,128,512]{2,1,0:T(8,128)(2,1)S(1)}, bf16[2,128,512]{2,1,0:T(8,128)(2,1)S(1)}, u32[]{:S(2)}, u32[]{:S(2)}) collective-permute-start(bf16[2,128,512]{2,1,0:T(8,128)(2,1)S(1)} %collective-permute-done.8.refs_3_), channel_id=1, source_target_pairs={{0,1},{1,0},{2,3},{3,2},{4,5},{5,4},{6,7},{7,6},{8,9},{9,8},{10,11... | collective-permute-start | bytes 786440 | tf_op jit(solution)/shard_map/ppermute | solution.py:26
  30.7 1.5 %collective-permute-start.11 = (bf16[2,128,512]{2,1,0:T(8,128)(2,1)S(1)}, bf16[2,128,512]{2,1,0:T(8,128)(2,1)S(1)}, u32[]{:S(2)}, u32[]{:S(2)}) collective-permute-start(bf16[2,128,512]{2,1,0:T(8,128)(2,1)S(1)} %collective-permute-done.7.refs_2_), channel_id=1, source_target_pairs={{0,1},{1,0},{2,3},{3,2},{4,5},{5,4},{6,7},{7,6},{8,9},{9,8},{10,11... | collective-permute-start | bytes 786440 | tf_op jit(solution)/shard_map/ppermute | solution.py:26
  36.6 1.6 %collective-permute-start.13 = (bf16[64,2048]{1,0:T(8,128)(2,1)S(1)}, bf16[64,2048]{1,0:T(8,128)(2,1)S(1)}, u32[]{:S(2)}, u32[]{:S(2)}) collective-permute-start(bf16[64,2048]{1,0:T(8,128)(2,1)S(1)} %get-tuple-element.82), channel_id=1, source_target_pairs={{0,1},{1,0},{2,3},{3,2},{4,5},{5,4},{6,7},{7,6},{8,9},{9,8},{10,11... | collective-permute-start | bytes 786440 | tf_op jit(solution)/shard_map/ppermute | solution.py:26
  37.0 1.5 %collective-permute-start.14 = (bf16[64,2048]{1,0:T(8,128)(2,1)S(1)}, bf16[64,2048]{1,0:T(8,128)(2,1)S(1)}, u32[]{:S(2)}, u32[]{:S(2)}) collective-permute-start(bf16[64,2048]{1,0:T(8,128)(2,1)S(1)} %get-tuple-element.83), channel_id=1, source_target_pairs={{0,1},{1,0},{2,3},{3,2},{4,5},{5,4},{6,7},{7,6},{8,9},{9,8},{10,11... | collective-permute-start | bytes 786440 | tf_op jit(solution)/shard_map/ppermute | solution.py:26
  38.7 14.8 %collective-permute-start.17 = (bf16[128,2048]{1,0:T(8,128)(2,1)S(1)}, bf16[128,2048]{1,0:T(8,128)(2,1)S(1)}, u32[]{:S(2)}, u32[]{:S(2)}) collective-permute-start(bf16[128,2048]{1,0:T(8,128)(2,1)S(1)} %pair_sum.6.near_ref), channel_id=1, source_target_pairs={{0,2},{1,3},{2,0},{3,1},{4,6},{5,7},{6,4},{7,5},{8,10},{9,11},{10,... | collective-permute-start | bytes 1572872 | tf_op jit(solution)/shard_map/ppermute | solution.py:26
  44.9 1.6 %collective-permute-start.15 = (bf16[64,2048]{1,0:T(8,128)(2,1)S(1)}, bf16[64,2048]{1,0:T(8,128)(2,1)S(1)}, u32[]{:S(2)}, u32[]{:S(2)}) collective-permute-start(bf16[64,2048]{1,0:T(8,128)(2,1)S(1)} %get-tuple-element.86), channel_id=1, source_target_pairs={{0,1},{1,0},{2,3},{3,2},{4,5},{5,4},{6,7},{7,6},{8,9},{9,8},{10,11... | collective-permute-start | bytes 786440 | tf_op jit(solution)/shard_map/ppermute | solution.py:26
  45.1 1.8 %collective-permute-start.16 = (bf16[64,2048]{1,0:T(8,128)(2,1)S(1)}, bf16[64,2048]{1,0:T(8,128)(2,1)S(1)}, u32[]{:S(2)}, u32[]{:S(2)}) collective-permute-start(bf16[64,2048]{1,0:T(8,128)(2,1)S(1)} %get-tuple-element.87), channel_id=1, source_target_pairs={{0,1},{1,0},{2,3},{3,2},{4,5},{5,4},{6,7},{7,6},{8,9},{9,8},{10,11... | collective-permute-start | bytes 786440 | tf_op jit(solution)/shard_map/ppermute | solution.py:26
  47.0 17.7 %collective-permute-start.21 = (bf16[128,2048]{1,0:T(8,128)(2,1)S(1)}, bf16[128,2048]{1,0:T(8,128)(2,1)S(1)}, u32[]{:S(2)}, u32[]{:S(2)}) collective-permute-start(bf16[128,2048]{1,0:T(8,128)(2,1)S(1)} %pair_sum.7.near_ref), channel_id=1, source_target_pairs={{0,2},{1,3},{2,0},{3,1},{4,6},{5,7},{6,4},{7,5},{8,10},{9,11},{10,... | collective-permute-start | bytes 1572872 | tf_op jit(solution)/shard_map/ppermute | solution.py:26
  51.9 2.9 %collective-permute-start.18 = (bf16[64,2048]{1,0:T(8,128)(2,1)S(1)}, bf16[64,2048]{1,0:T(8,128)(2,1)S(1)}, u32[]{:S(2)}, u32[]{:S(2)}) collective-permute-start(bf16[64,2048]{1,0:T(8,128)(2,1)S(1)} %get-tuple-element.93), channel_id=1, source_target_pairs={{0,1},{1,0},{2,3},{3,2},{4,5},{5,4},{6,7},{7,6},{8,9},{9,8},{10,11... | collective-permute-start | bytes 786440 | tf_op jit(solution)/shard_map/ppermute | solution.py:26
  51.9 2.9 %collective-permute-start.19 = (bf16[64,2048]{1,0:T(8,128)(2,1)S(1)}, bf16[64,2048]{1,0:T(8,128)(2,1)S(1)}, u32[]{:S(2)}, u32[]{:S(2)}) collective-permute-start(bf16[64,2048]{1,0:T(8,128)(2,1)S(1)} %get-tuple-element.94), channel_id=1, source_target_pairs={{0,1},{1,0},{2,3},{3,2},{4,5},{5,4},{6,7},{7,6},{8,9},{9,8},{10,11... | collective-permute-start | bytes 786440 | tf_op jit(solution)/shard_map/ppermute | solution.py:26
  53.5 3.3 %copy-start.1 = (bf16[2048,1024]{1,0:T(8,128)(2,1)S(1)}, bf16[2048,1024]{1,0:T(8,128)(2,1)}, u32[]{:S(2)}) copy-start(bf16[2048,1024]{1,0:T(8,128)(2,1)} %gate_ref.5) | copy-start | bytes 12582916
  53.5 3.5 %copy-start.2 = (bf16[2048,1024]{1,0:T(8,128)(2,1)S(1)}, bf16[2048,1024]{1,0:T(8,128)(2,1)}, u32[]{:S(2)}) copy-start(bf16[2048,1024]{1,0:T(8,128)(2,1)} %up_ref.5) | copy-start | bytes 12582916
  53.5 4.7 %copy-start.3 = (bf16[1024,2048]{1,0:T(8,128)(2,1)S(1)}, bf16[1024,2048]{1,0:T(8,128)(2,1)}, u32[]{:S(2)}) copy-start(bf16[1024,2048]{1,0:T(8,128)(2,1)} %down_ref.5) | copy-start | bytes 12582916
  54.2 2.7 %collective-permute-start.22 = (bf16[48,2048]{1,0:T(8,128)(2,1)S(1)}, bf16[48,2048]{1,0:T(8,128)(2,1)S(1)}, u32[]{:S(2)}, u32[]{:S(2)}) collective-permute-start(bf16[48,2048]{1,0:T(8,128)(2,1)S(1)} %get-tuple-element.95.refs_0_), channel_id=1, source_target_pairs={{0,1},{1,0},{2,3},{3,2},{4,5},{5,4},{6,7},{7,6},{8,9},{9,8},{10,11... | collective-permute-start | bytes 589832 | tf_op jit(solution)/shard_map/ppermute | solution.py:26
  54.2 2.6 %collective-permute-start.23 = (bf16[48,2048]{1,0:T(8,128)(2,1)S(1)}, bf16[48,2048]{1,0:T(8,128)(2,1)S(1)}, u32[]{:S(2)}, u32[]{:S(2)}) collective-permute-start(bf16[48,2048]{1,0:T(8,128)(2,1)S(1)} %get-tuple-element.96.refs_1_), channel_id=1, source_target_pairs={{0,1},{1,0},{2,3},{3,2},{4,5},{5,4},{6,7},{7,6},{8,9},{9,8},{10,11... | collective-permute-start | bytes 589832 | tf_op jit(solution)/shard_map/ppermute | solution.py:26
  54.7 2.1 %collective-permute-start.24 = (bf16[32,2048]{1,0:T(8,128)(2,1)S(1)}, bf16[32,2048]{1,0:T(8,128)(2,1)S(1)}, u32[]{:S(2)}, u32[]{:S(2)}) collective-permute-start(bf16[32,2048]{1,0:T(8,128)(2,1)S(1)} %get-tuple-element.97.refs_2_), channel_id=1, source_target_pairs={{0,1},{1,0},{2,3},{3,2},{4,5},{5,4},{6,7},{7,6},{8,9},{9,8},{10,11... | collective-permute-start | bytes 393224 | tf_op jit(solution)/shard_map/ppermute | solution.py:26
  55.0 21.0 %collective-permute-start.20 = (bf16[128,2048]{1,0:T(8,128)(2,1)S(1)}, bf16[128,2048]{1,0:T(8,128)(2,1)S(1)}, u32[]{:S(2)}, u32[]{:S(2)}) collective-permute-start(bf16[128,2048]{1,0:T(8,128)(2,1)S(1)} %pair_sum.8.near_ref), channel_id=1, source_target_pairs={{0,2},{1,3},{2,0},{3,1},{4,6},{5,7},{6,4},{7,5},{8,10},{9,11},{10,... | collective-permute-start | bytes 1572872 | tf_op jit(solution)/shard_map/ppermute | solution.py:26
  61.6 4.4 %collective-permute-start.25 = (bf16[48,2048]{1,0:T(8,128)(2,1)S(1)}, bf16[48,2048]{1,0:T(8,128)(2,1)S(1)}, u32[]{:S(2)}, u32[]{:S(2)}) collective-permute-start(bf16[48,2048]{1,0:T(8,128)(2,1)S(1)} %get-tuple-element.102), channel_id=1, source_target_pairs={{0,1},{1,0},{2,3},{3,2},{4,5},{5,4},{6,7},{7,6},{8,9},{9,8},{10,11... | collective-permute-start | bytes 589832 | tf_op jit(solution)/shard_map/ppermute | solution.py:26
  61.7 4.4 %collective-permute-start.26 = (bf16[48,2048]{1,0:T(8,128)(2,1)S(1)}, bf16[48,2048]{1,0:T(8,128)(2,1)S(1)}, u32[]{:S(2)}, u32[]{:S(2)}) collective-permute-start(bf16[48,2048]{1,0:T(8,128)(2,1)S(1)} %get-tuple-element.103), channel_id=1, source_target_pairs={{0,1},{1,0},{2,3},{3,2},{4,5},{5,4},{6,7},{7,6},{8,9},{9,8},{10,11... | collective-permute-start | bytes 589832 | tf_op jit(solution)/shard_map/ppermute | solution.py:26
  62.2 3.3 %collective-permute-start.27 = (bf16[32,2048]{1,0:T(8,128)(2,1)S(1)}, bf16[32,2048]{1,0:T(8,128)(2,1)S(1)}, u32[]{:S(2)}, u32[]{:S(2)}) collective-permute-start(bf16[32,2048]{1,0:T(8,128)(2,1)S(1)} %get-tuple-element.104), channel_id=1, source_target_pairs={{0,1},{1,0},{2,3},{3,2},{4,5},{5,4},{6,7},{7,6},{8,9},{9,8},{10,11... | collective-permute-start | bytes 393224 | tf_op jit(solution)/shard_map/ppermute | solution.py:26
  65.4 2.6 %collective-permute-start.28 = (bf16[48,2048]{1,0:T(8,128)(2,1)S(1)}, bf16[48,2048]{1,0:T(8,128)(2,1)S(1)}, u32[]{:S(2)}, u32[]{:S(2)}) collective-permute-start(bf16[48,2048]{1,0:T(8,128)(2,1)S(1)} %get-tuple-element.106.refs_0_), channel_id=1, source_target_pairs={{0,1},{1,0},{2,3},{3,2},{4,5},{5,4},{6,7},{7,6},{8,9},{9,8},{10,11... | collective-permute-start | bytes 589832 | tf_op jit(solution)/shard_map/ppermute | solution.py:26
  65.5 2.6 %collective-permute-start.29 = (bf16[48,2048]{1,0:T(8,128)(2,1)S(1)}, bf16[48,2048]{1,0:T(8,128)(2,1)S(1)}, u32[]{:S(2)}, u32[]{:S(2)}) collective-permute-start(bf16[48,2048]{1,0:T(8,128)(2,1)S(1)} %get-tuple-element.107.refs_1_), channel_id=1, source_target_pairs={{0,1},{1,0},{2,3},{3,2},{4,5},{5,4},{6,7},{7,6},{8,9},{9,8},{10,11... | collective-permute-start | bytes 589832 | tf_op jit(solution)/shard_map/ppermute | solution.py:26
  66.0 2.1 %collective-permute-start.30 = (bf16[32,2048]{1,0:T(8,128)(2,1)S(1)}, bf16[32,2048]{1,0:T(8,128)(2,1)S(1)}, u32[]{:S(2)}, u32[]{:S(2)}) collective-permute-start(bf16[32,2048]{1,0:T(8,128)(2,1)S(1)} %get-tuple-element.108.refs_2_), channel_id=1, source_target_pairs={{0,1},{1,0},{2,3},{3,2},{4,5},{5,4},{6,7},{7,6},{8,9},{9,8},{10,11... | collective-permute-start | bytes 393224 | tf_op jit(solution)/shard_map/ppermute | solution.py:26
  66.2 16.8 %collective-permute-start.37 = (bf16[64,2048]{1,0:T(8,128)(2,1)S(1)}, bf16[64,2048]{1,0:T(8,128)(2,1)S(1)}, u32[]{:S(2)}, u32[]{:S(2)}) collective-permute-start(bf16[64,2048]{1,0:T(8,128)(2,1)S(1)} %get-tuple-element.123), channel_id=1, source_target_pairs={{0,2},{1,3},{2,0},{3,1},{4,6},{5,7},{6,4},{7,5},{8,10},{9,11},{10,... | collective-permute-start | bytes 786440 | tf_op jit(solution)/shard_map/ppermute | solution.py:26
  71.5 5.7 %collective-permute-start.31 = (bf16[48,2048]{1,0:T(8,128)(2,1)S(1)}, bf16[48,2048]{1,0:T(8,128)(2,1)S(1)}, u32[]{:S(2)}, u32[]{:S(2)}) collective-permute-start(bf16[48,2048]{1,0:T(8,128)(2,1)S(1)} %get-tuple-element.114), channel_id=1, source_target_pairs={{0,1},{1,0},{2,3},{3,2},{4,5},{5,4},{6,7},{7,6},{8,9},{9,8},{10,11... | collective-permute-start | bytes 589832 | tf_op jit(solution)/shard_map/ppermute | solution.py:26
  71.7 5.6 %collective-permute-start.32 = (bf16[48,2048]{1,0:T(8,128)(2,1)S(1)}, bf16[48,2048]{1,0:T(8,128)(2,1)S(1)}, u32[]{:S(2)}, u32[]{:S(2)}) collective-permute-start(bf16[48,2048]{1,0:T(8,128)(2,1)S(1)} %get-tuple-element.115), channel_id=1, source_target_pairs={{0,1},{1,0},{2,3},{3,2},{4,5},{5,4},{6,7},{7,6},{8,9},{9,8},{10,11... | collective-permute-start | bytes 589832 | tf_op jit(solution)/shard_map/ppermute | solution.py:26
  72.1 4.7 %collective-permute-start.33 = (bf16[32,2048]{1,0:T(8,128)(2,1)S(1)}, bf16[32,2048]{1,0:T(8,128)(2,1)S(1)}, u32[]{:S(2)}, u32[]{:S(2)}) collective-permute-start(bf16[32,2048]{1,0:T(8,128)(2,1)S(1)} %get-tuple-element.116), channel_id=1, source_target_pairs={{0,1},{1,0},{2,3},{3,2},{4,5},{5,4},{6,7},{7,6},{8,9},{9,8},{10,11... | collective-permute-start | bytes 393224 | tf_op jit(solution)/shard_map/ppermute | solution.py:26
  76.6 2.6 %collective-permute-start.34 = (bf16[48,2048]{1,0:T(8,128)(2,1)S(1)}, bf16[48,2048]{1,0:T(8,128)(2,1)S(1)}, u32[]{:S(2)}, u32[]{:S(2)}) collective-permute-start(bf16[48,2048]{1,0:T(8,128)(2,1)S(1)} %get-tuple-element.118.refs_0_), channel_id=1, source_target_pairs={{0,1},{1,0},{2,3},{3,2},{4,5},{5,4},{6,7},{7,6},{8,9},{9,8},{10,11... | collective-permute-start | bytes 589832 | tf_op jit(solution)/shard_map/ppermute | solution.py:26
  76.7 2.6 %collective-permute-start.35 = (bf16[48,2048]{1,0:T(8,128)(2,1)S(1)}, bf16[48,2048]{1,0:T(8,128)(2,1)S(1)}, u32[]{:S(2)}, u32[]{:S(2)}) collective-permute-start(bf16[48,2048]{1,0:T(8,128)(2,1)S(1)} %get-tuple-element.119.refs_1_), channel_id=1, source_target_pairs={{0,1},{1,0},{2,3},{3,2},{4,5},{5,4},{6,7},{7,6},{8,9},{9,8},{10,11... | collective-permute-start | bytes 589832 | tf_op jit(solution)/shard_map/ppermute | solution.py:26
  77.2 2.1 %collective-permute-start.36 = (bf16[32,2048]{1,0:T(8,128)(2,1)S(1)}, bf16[32,2048]{1,0:T(8,128)(2,1)S(1)}, u32[]{:S(2)}, u32[]{:S(2)}) collective-permute-start(bf16[32,2048]{1,0:T(8,128)(2,1)S(1)} %get-tuple-element.120.refs_2_), channel_id=1, source_target_pairs={{0,1},{1,0},{2,3},{3,2},{4,5},{5,4},{6,7},{7,6},{8,9},{9,8},{10,11... | collective-permute-start | bytes 393224 | tf_op jit(solution)/shard_map/ppermute | solution.py:26
  77.4 9.3 %collective-permute-start.42 = (bf16[64,2048]{1,0:T(8,128)(2,1)S(1)}, bf16[64,2048]{1,0:T(8,128)(2,1)S(1)}, u32[]{:S(2)}, u32[]{:S(2)}) collective-permute-start(bf16[64,2048]{1,0:T(8,128)(2,1)S(1)} %get-tuple-element.133), channel_id=1, source_target_pairs={{0,2},{1,3},{2,0},{3,1},{4,6},{5,7},{6,4},{7,5},{8,10},{9,11},{10,... | collective-permute-start | bytes 786440 | tf_op jit(solution)/shard_map/ppermute | solution.py:26
  83.0 2.2 %collective-permute-start.38 = (bf16[48,2048]{1,0:T(8,128)(2,1)S(1)}, bf16[48,2048]{1,0:T(8,128)(2,1)S(1)}, u32[]{:S(2)}, u32[]{:S(2)}) collective-permute-start(bf16[48,2048]{1,0:T(8,128)(2,1)S(1)} %get-tuple-element.126), channel_id=1, source_target_pairs={{0,1},{1,0},{2,3},{3,2},{4,5},{5,4},{6,7},{7,6},{8,9},{9,8},{10,11... | collective-permute-start | bytes 589832 | tf_op jit(solution)/shard_map/ppermute | solution.py:26
  83.2 2.0 %collective-permute-start.39 = (bf16[48,2048]{1,0:T(8,128)(2,1)S(1)}, bf16[48,2048]{1,0:T(8,128)(2,1)S(1)}, u32[]{:S(2)}, u32[]{:S(2)}) collective-permute-start(bf16[48,2048]{1,0:T(8,128)(2,1)S(1)} %get-tuple-element.127), channel_id=1, source_target_pairs={{0,1},{1,0},{2,3},{3,2},{4,5},{5,4},{6,7},{7,6},{8,9},{9,8},{10,11... | collective-permute-start | bytes 589832 | tf_op jit(solution)/shard_map/ppermute | solution.py:26
  83.5 1.6 %collective-permute-start.40 = (bf16[32,2048]{1,0:T(8,128)(2,1)S(1)}, bf16[32,2048]{1,0:T(8,128)(2,1)S(1)}, u32[]{:S(2)}, u32[]{:S(2)}) collective-permute-start(bf16[32,2048]{1,0:T(8,128)(2,1)S(1)} %get-tuple-element.128), channel_id=1, source_target_pairs={{0,1},{1,0},{2,3},{3,2},{4,5},{5,4},{6,7},{7,6},{8,9},{9,8},{10,11... | collective-permute-start | bytes 393224 | tf_op jit(solution)/shard_map/ppermute | solution.py:26
  86.7 7.8 %collective-permute-start.41 = (bf16[64,2048]{1,0:T(8,128)(2,1)S(1)}, bf16[64,2048]{1,0:T(8,128)(2,1)S(1)}, u32[]{:S(2)}, u32[]{:S(2)}) collective-permute-start(bf16[64,2048]{1,0:T(8,128)(2,1)S(1)} %get-tuple-element.130), channel_id=1, source_target_pairs={{0,2},{1,3},{2,0},{3,1},{4,6},{5,7},{6,4},{7,5},{8,10},{9,11},{10,... | collective-permute-start | bytes 786440 | tf_op jit(solution)/shard_map/ppermute | solution.py:26

commit v4 on v3

--- a/solution.py
+++ b/solution.py
@@ -20,6 +20,7 @@
 AFTER_FEED = (3, 3, 2)
 BEFORE_FEED = (3, 3, 2)
 TILE = 256
+FIRST_CUT = 1
 
 
 def exchange(value, axis, flip):
@@ -79,6 +80,8 @@
 
 
 def project_kernel(
+    reqs,
+    pages_in,
     len_ref,
     hidden_ref,
     y_ref,
@@ -86,17 +89,15 @@
     d_ref,
     gains_ref,
     wq_ref,
-    mine_ref,
-    other_ref,
+    wkv_ref,
     head_gains_ref,
     cos_ref,
     sin_ref,
-    page_ref,
-    q_ref,
-    kv_ref,
+    *refs,
 ):
+    page_ref, q_ref, quarter_ref = refs[pages_in:]
     member = lax.axis_index("mlp")
-    reqs, part, _ = hidden_ref.shape
+    part = hidden_ref.shape[1]
     head = head_gains_ref.shape[-1]
     qgain, kgain = head_gains_ref[0:1, :], head_gains_ref[1:2, :]
     starts = [pl.multiple_of((member ^ flip) * part, part) for flip in BLOCK_XOR]
@@ -104,7 +105,7 @@
     sin = jnp.concatenate([sin_ref[pl.ds(s, part), :] for s in starts], axis=0)
     holds_keys = member % 2 == 0
     heads = wq_ref.shape[1] // head
-    for r in range(reqs):
+    for i, r in enumerate(reqs):
         rows = jnp.concatenate(
             [
                 active_rows(ref[r], gains_ref[0:1, :])
@@ -113,56 +114,64 @@
             axis=0,
         )
         count = rows.shape[0]
-        mine = jnp.dot(rows, mine_ref[...], preferred_element_type=F32)
-        other = jnp.dot(rows, other_ref[...], preferred_element_type=F32)
-        keys = rotated(normed(jnp.where(holds_keys, mine, other), kgain), cos, sin)
-        values = normed(jnp.where(holds_keys, other, mine), 1.0)
-        kv_ref[r, :, :head] = keys.astype(BF16)
-        kv_ref[r, :, head:] = values.astype(BF16)
-        quarter = jnp.where(holds_keys, keys, values)
+        raw = jnp.dot(rows, wkv_ref[...], preferred_element_type=F32)
+        quarter = jnp.where(holds_keys, rotated(normed(raw, kgain), cos, sin), normed(raw, 1.0))
+        quarter_ref[i] = quarter.astype(BF16)
         live = len_ref[r]
         for b, start in enumerate(starts):
             position = start + lax.broadcasted_iota(jnp.int32, (part, 1), 0)
-            page_ref[r, pl.ds(start, part), :] = jnp.where(
+            page_ref[i, pl.ds(start, part), :] = jnp.where(
                 position < live, quarter[b * part : (b + 1) * part], 0.0
             ).astype(BF16)
         for h in range(heads):
             raw = jnp.dot(
                 rows, wq_ref[:, h * head : (h + 1) * head], preferred_element_type=F32
             )
-            q_ref[r, h * count : (h + 1) * count, :] = rotated(
+            q_ref[i, h * count : (h + 1) * count, :] = rotated(
                 normed(raw, qgain), cos, sin
             ).astype(BF16)
 
 
-def project(lens, hidden, y, c, d, gains, wq, mine, other, head_gains, cos, sin):
-    reqs, part, width = hidden.shape
+def project(reqs, pages, lens, hidden, y, c, d, gains, wq, wkv, head_gains, cos, sin):
+    part = hidden.shape[1]
     count = part * len(BLOCK_XOR)
     head = head_gains.shape[-1]
     heads = wq.shape[1] // head
+    here = len(reqs)
+    extra = [] if pages is None else [pages]
     return pl.pallas_call(
-        project_kernel,
+        functools.partial(project_kernel, reqs, len(extra)),
+        grid=(1,),
         out_shape=[
-            jax.ShapeDtypeStruct((reqs, count, head), BF16),
-            jax.ShapeDtypeStruct((reqs, heads * count, head), BF16),
-            jax.ShapeDtypeStruct((reqs, count, 2 * head), BF16),
+            jax.ShapeDtypeStruct((hidden.shape[0], count, head), BF16),
+            jax.ShapeDtypeStruct((here, heads * count, head), BF16),
+            jax.ShapeDtypeStruct((here, count, head), BF16),
         ],
-        in_specs=[SCALARS] + [ON_CHIP] * 11,
-        out_specs=[ON_CHIP] * 3,
+        in_specs=[SCALARS] + [ON_CHIP] * 10 + [ANYWHERE] * len(extra),
+        out_specs=[
+            pl.BlockSpec((here, count, head), lambda i: (reqs[0] // here, 0, 0)),
+            ON_CHIP,
+            ON_CHIP,
+        ],
+        input_output_aliases={11: 0} if extra else {},
         compiler_params=params(10),
         cost_estimate=cost(1),
         name="project",
-    )(lens, hidden, y, c, d, gains, wq, mine, other, head_gains, cos, sin)
+    )(lens, hidden, y, c, d, gains, wq, wkv, head_gains, cos, sin, *extra)
 
 
 def attend_kernel(
     req,
+    index,
+    offset,
+    rows,
     sources,
     group_ref,
     owner_ref,
     slot_ref,
     q_ref,
-    kv_ref,
+    mine_ref,
+    other_ref,
     wo_ref,
     *refs,
 ):
@@ -172,8 +181,8 @@
     keyval, mixed, place, sems = refs[-4:]
     member = lax.axis_index("mlp")
     me = lax.axis_index("req")
-    count, head = kv_ref.shape[1], kv_ref.shape[2] // 2
-    part = count // 4
+    count, head = mine_ref.shape[1:]
+    part = count // len(BLOCK_XOR)
     page = pool_refs[0].shape[1]
     n_pages = owner_ref.shape[1]
     per_part = len(sources) // 2
@@ -184,54 +193,77 @@
         flip = owner_ref[group, i] ^ me
         far = slot_ref[group, i] ^ (member % 2)
         place[far * per_part + flip] = i
-    for name, index, far, flip in sources:
+    for name, entry, far, flip in sources:
         where = place[far * per_part + flip]
 
         @pl.when(where >= 0)
         def _():
             start = pl.multiple_of(where * page, page)
             pltpu.make_async_copy(
-                pool_refs[name].at[index], keyval.at[pl.ds(start, page), :], sems.at[where]
+                pool_refs[name].at[entry], keyval.at[pl.ds(start, page), :], sems.at[where]
             ).start()
 
     pre = n_pages * page
-    keyval[pre:, :] = kv_ref[req]
+    holds_keys = member % 2 == 0
+
+    half = count // 2
+
+    def place_suffix(mine_cols, other_cols):
+        keyval[pre:, mine_cols] = mine_ref[index]
+        keyval[pre : pre + half, other_cols] = other_ref[index, half:, :]
+        keyval[pre + half :, other_cols] = other_ref[index, :half, :]
+
+    @pl.when(holds_keys)
+    def _():
+        place_suffix(slice(0, head), slice(head, 2 * head))
+
+    @pl.when(jnp.logical_not(holds_keys))
+    def _():
+        place_suffix(slice(head, 2 * head), slice(0, head))
+
     for i in range(n_pages):
         pltpu.make_async_copy(
             pool_refs[0].at[0], keyval.at[i * page : (i + 1) * page, :], sems.at[i]
         ).wait()
 
     factor = head**-0.5 * math.log2(math.e)
-
-    def positions(index):
-        block = index // part
-        flip = (block & 1) * 2 + (block >> 1)
-        return (member ^ flip) * part + index % part
-
-    key_at = positions(lax.broadcasted_iota(jnp.int32, (1, count), 1))
-    tile = TILE
+    column = lax.broadcasted_iota(jnp.int32, (1, count), 1)
+    block = column // part
+    key_at = (member ^ ((block & 1) * 2 + (block >> 1))) * part + column % part
     heads = q_ref.shape[1] // count
-    for first in range(0, count, tile):
-        query_at = positions(first + lax.broadcasted_iota(jnp.int32, (tile, 1), 0))
-        seen = key_at <= query_at
-        for h in range(heads):
-            start = h * count + first
-            scores = lax.dot_general(
-                q_ref[req, start : start + tile, :],
-                keyval[:, :head],
-                (((1,), (1,)), ((), ())),
-                preferred_element_type=F32,
-            )
-            scores = jnp.concatenate(
-                [scores[:, :pre], jnp.where(seen, scores[:, pre:], -jnp.inf)], axis=1
-            )
-            peak = jnp.max(scores, axis=-1, keepdims=True)
-            exps = jnp.exp2((scores - peak) * factor)
-            total = jnp.sum(exps, axis=-1, keepdims=True)
-            out = jnp.dot(exps.astype(BF16), keyval[:, head:], preferred_element_type=F32)
-            mixed[first : first + tile, h * head : (h + 1) * head] = (
-                out * (1.0 / total)
-            ).astype(BF16)
+    pieces = [(h, b) for h in range(heads) for b in range(len(BLOCK_XOR))]
+    per_step = max(1, TILE // rows)
+    for first in range(0, len(pieces), per_step):
+        step = pieces[first : first + per_step]
+        starts = [h * count + b * part + offset for h, b in step]
+        queries = jnp.concatenate([q_ref[index, s : s + rows, :] for s in starts], axis=0)
+        query_at = jnp.concatenate(
+            [
+                (member ^ BLOCK_XOR[b]) * part
+                + offset
+                + lax.broadcasted_iota(jnp.int32, (rows, 1), 0)
+                for _, b in step
+            ],
+            axis=0,
+        )
+        scores = lax.dot_general(
+            queries,
+            keyval[:, :head],
+            (((1,), (1,)), ((), ())),
+            preferred_element_type=F32,
+        )
+        scores = jnp.concatenate(
+            [scores[:, :pre], jnp.where(key_at <= query_at, scores[:, pre:], -jnp.inf)], axis=1
+        )
+        peak = jnp.max(scores, axis=-1, keepdims=True)
+        exps = jnp.exp2((scores - peak) * factor)
+        total = jnp.sum(exps, axis=-1, keepdims=True)
+        out = jnp.dot(exps.astype(BF16), keyval[:, head:], preferred_element_type=F32)
+        out = (out * (1.0 / total)).astype(BF16)
+        for i, (h, b) in enumerate(step):
+            mixed[b * rows : (b + 1) * rows, h * head : (h + 1) * head] = out[
+                i * rows : (i + 1) * rows
+            ]
     width = wo_ref.shape[1]
     step = 512
     for col in range(0, width, step):
@@ -258,28 +290,27 @@
     return [kept] + piece_shapes(part, width, pieces)
 
 
-def attend(req, sources, group, owner, slot, q, kv, wo, pools):
-    count, head = kv.shape[1], kv.shape[2] // 2
-    part = count // 4
+def attend(req, index, offset, rows, sources, group, owner, slot, q, mine, other, wo, pools):
+    count, head = mine.shape[1:]
     heads = q.shape[1] // count
     page = pools[0].shape[1]
     n_pages = owner.shape[1]
     keys = n_pages * page + count
     return pl.pallas_call(
-        functools.partial(attend_kernel, req, sources),
-        out_shape=partial_shapes(part, wo.shape[1], AFTER_ATTEND),
-        in_specs=[SCALARS] * 3 + [ON_CHIP] * 3 + [ANYWHERE] * len(pools),
+        functools.partial(attend_kernel, req, index, offset, rows, sources),
+        out_shape=partial_shapes(rows, wo.shape[1], AFTER_ATTEND),
+        in_specs=[SCALARS] * 3 + [ON_CHIP] * 4 + [ANYWHERE] * len(pools),
         out_specs=[ON_CHIP] * (1 + len(AFTER_ATTEND)),
         scratch_shapes=[
             pltpu.VMEM((keys, 2 * head), BF16),
-            pltpu.VMEM((count, heads * head), BF16),
+            pltpu.VMEM((len(BLOCK_XOR) * rows, heads * head), BF16),
             pltpu.SMEM((len(sources),), jnp.int32),
             pltpu.SemaphoreType.DMA((n_pages,)),
         ],
         compiler_params=params(8),
         cost_estimate=cost(1),
         name="attend",
-    )(group, owner, slot, q, kv, wo, *pools)
+    )(group, owner, slot, q, mine, other, wo, *pools)
 
 
 def pair_kernel(count, keep_ref, *refs):
@@ -303,13 +334,18 @@
     )(keep, *others)
 
 
-def residual_kernel(req, own_base_ref, y_base_ref, near_ref, far_ref, gains_ref, res_ref, *in_refs):
-    part = res_ref.shape[0]
+def residual_kernel(req, count, gains_ref, own_base_ref, y_base_ref, *refs):
+    near_refs, far_refs = refs[:count], refs[count : 2 * count]
+    res_ref, in_refs = refs[2 * count], refs[2 * count + 1 :]
     blocks = []
     for b, base_ref in enumerate((own_base_ref, y_base_ref)):
-        mine = slice(b * part, (b + 1) * part)
-        theirs = slice((1 - b) * part, (2 - b) * part)
-        total = near_ref[mine, :].astype(F32) + far_ref[theirs, :].astype(F32)
+        sums = []
+        for near_ref, far_ref in zip(near_refs, far_refs):
+            rows = near_ref.shape[0] // 2
+            mine = slice(b * rows, (b + 1) * rows)
+            theirs = slice((1 - b) * rows, (2 - b) * rows)
+            sums.append(near_ref[mine, :].astype(F32) + far_ref[theirs, :].astype(F32))
+        total = jnp.concatenate(sums, axis=0)
         residual = (base_ref[req] + normed(total, gains_ref[2:3, :])) * INV_ROOT
         if b == 0:
             res_ref[...] = residual
@@ -317,21 +353,18 @@
     store_rows(in_refs, 0, jnp.concatenate(blocks, axis=0))
 
 
-def make_residual(req, own_base, y_base, near, far, gains):
-    rows, width = near.shape
-    part = rows // 2
+def make_residual(req, gains, own_base, y_base, near, far):
+    part, width = own_base.shape[1:]
     return pl.pallas_call(
-        functools.partial(residual_kernel, req),
-        out_shape=[
-            jax.ShapeDtypeStruct((part, width), F32),
-        ]
+        functools.partial(residual_kernel, req, len(near)),
+        out_shape=[jax.ShapeDtypeStruct((part, width), F32)]
         + piece_shapes(part, width, BEFORE_FEED),
-        in_specs=[ON_CHIP] * 5,
+        in_specs=[ON_CHIP] * (3 + 2 * len(near)),
         out_specs=[ON_CHIP] * (1 + len(BEFORE_FEED)),
         cost_estimate=cost(1e11),
         compiler_params=params(4),
         name="residual",
-    )(own_base, y_base, near, far, gains)
+    )(gains, own_base, y_base, *near, *far)
 
 
 def feed_kernel(count, gate_ref, up_ref, down_ref, *refs):
@@ -384,7 +417,7 @@
         in_specs=[SCALARS] + [ON_CHIP] * 4 + [ANYWHERE] * len(extra),
         out_specs=pl.BlockSpec((1, part, width), lambda i: (req, 0, 0)),
         input_output_aliases={5: 0} if extra else {},
-        cost_estimate=cost(1e11),
+        cost_estimate=cost(1e11 if req == 0 else 1),
         compiler_params=params(4),
         name="finish",
     )(lens, residual, near, far, gains, *extra)
@@ -436,7 +469,6 @@
     )
     later = list(range(4, lax.axis_size("req"), 2))
     direct = {flip: exchange(own_page, "req", flip) for flip in [*later, 2]}
-    other_weight = exchange(after(keyval_weight, hidden_c), "mlp", 1)
     near_pages = jnp.concatenate([own_page, after(direct[2], cos, gains, head_gains)])
     near_odd = exchange(near_pages, "req", 1)
     own_base = make_base(after(hidden, near_pages), gains, laurel_left.T, laurel_right)
@@ -449,23 +481,30 @@
     hidden_y = after(hidden_y, far_pages)
     hidden_d = exchange(hidden_y, "mlp", 1)
     y_base = make_base(hidden_y, gains, laurel_left.T, laurel_right, 1e11)
-    pages, q_all, kv_all = project(
-        suffix_len,
-        hidden,
-        after(hidden_y, y_base),
-        hidden_c,
-        hidden_d,
-        gains,
-        query_weight,
-        keyval_weight,
-        other_weight,
-        head_gains,
-        cos,
-        sin,
-    )
-    near_odd = after(near_odd, q_all)
+    hidden_y = after(hidden_y, y_base)
+
+    def project_some(some, pages, *earlier):
+        return project(
+            some,
+            pages,
+            suffix_len,
+            after(hidden, *earlier),
+            hidden_y,
+            hidden_c,
+            hidden_d,
+            gains,
+            query_weight,
+            keyval_weight,
+            head_gains,
+            cos,
+            sin,
+        )
+
+    pages, q_first, kv_first = project_some([0], None)
+    projected = [(q_first, kv_first, exchange(kv_first, "mlp", 1), 0)]
+    near_odd = after(near_odd, q_first)
     near_odd_other = exchange(near_odd, "mlp", 1)
-    far_odd = after(far_odd, q_all)
+    far_odd = after(far_odd, q_first)
     far_odd_other = exchange(far_odd, "mlp", 1)
     pools = [near_pages, far_pages, near_odd, far_odd]
     pools += [near_other, far_other, near_odd_other, far_odd_other]
@@ -474,15 +513,23 @@
         (p, i, p // 4, flip) for p in range(len(pools)) for i, flip in enumerate(flips[p % 4])
     ]
 
-    def attend_one(r, *earlier):
+    pages, q_next, kv_next = project_some([1], pages, q_first)
+    projected.append((q_next, kv_next, exchange(kv_next, "mlp", 1), 0))
+
+    def attend_one(r, offset, rows, *earlier):
+        q, mine, other, index = projected[r]
         return attend(
             r,
+            index,
+            offset,
+            rows,
             sources,
             request_group,
             page_owner,
             page_slot,
-            after(q_all, *earlier),
-            kv_all,
+            after(q, *earlier),
+            mine,
+            other,
             out_weight,
             pools,
         )
@@ -491,8 +538,9 @@
         return [exchange(piece, "mlp", 1) for piece in pieces]
 
     def residual_one(r, *earlier):
+        first, *rest = far[r]
         residual, *pieces = make_residual(
-            r, own_base, y_base, near[r], after(far[r], *earlier), gains
+            r, gains, own_base, y_base, near[r], [after(first, *earlier), *rest]
         )
         residuals[r] = residual
         inputs[r] = pieces + swap(pieces)
@@ -521,16 +569,24 @@
         )
 
     near, far, residuals, inputs = {}, {}, {}, {}
-    last = q_all
+    last = q_next
     for r in range(reqs):
-        keep, *pieces = attend_one(r, last)
-        others = swap(pieces)
-        last = keep
-        if r >= 2:
-            last = residual_one(r - 2, last)
-        (near[r],) = pair_sum(after(keep, last), others, 1)
-        far[r] = exchange(near[r], "mlp", 2)
-        last = near[r]
+        rows = part // FIRST_CUT if r == 0 else part
+        near[r], far[r] = [], []
+        for offset in range(0, part, rows):
+            keep, *pieces = attend_one(r, offset, rows, last)
+            others = swap(pieces)
+            last = keep
+            if r >= 2:
+                last = residual_one(r - 2, last)
+            (joined,) = pair_sum(after(keep, last), others, 1)
+            near[r].append(joined)
+            far[r].append(exchange(joined, "mlp", 2))
+            last = joined
+        if r + 2 < reqs:
+            pages, q_next, kv_next = project_some([r + 2], pages, last)
+            projected.append((q_next, kv_next, exchange(kv_next, "mlp", 1), 0))
+            last = q_next
     done, result = {}, None
     for r in range(reqs):
         keep, *pieces = feed_one(r, last)

time: 96.3 us -> 93.2 us (0.968)
  waiting for transfers between devices: 21.1 us -> 16.7 us
    ppermute x43 -> x45, waiting for transfers between devices: 21.1 us -> 16.7 us  [exchange(): lax.ppermute(value, axis, [(i, i ^ flip) for i in range(lax.axis_size(axi...]
    pallas_call x7 -> x9, Pallas kernels: 20.7 us -> 21.7 us  [the longest x3 13.2 us: attend(): pl.pallas_call(functools.partial(attend_kernel, req, index, offset, rows,...]
    ppermute x43 -> x45, starting transfers between devices: 28.1 us -> 28.7 us  [exchange(): lax.ppermute(value, axis, [(i, i ^ flip) for i in range(lax.axis_size(axi...]
    unnamed x35 -> x37, local copies, waits for them, and re-layouts: 4.48 us -> 4.42 us
  transfers between devices with their start and end apart: 43 -> 45, of which waited for: 14 -> 11; matrix products, arithmetic and copies ran while one was open for 2% -> 2% of each run, Pallas kernels for 35% -> 37%
where the time goes in v4:
time: 93.2 us; the launch traced here: 93 us
  Pallas kernels  40 us (43%)
  starting transfers between devices  28.7 us (31%)
  waiting for transfers between devices  16.7 us (18%)
  local copies, waits for them, and re-layouts  5.28 us (6%)
  other arithmetic  1.27 us (1%)
  between operations  1.05 us (1%)
    ppermute x45, starting transfers between devices, exchange(): lax.ppermute(value, axis, [(i, i ^ flip) for i in range(lax.axis_size(axi...  28.7 us
    ppermute x45, waiting for transfers between devices, exchange(): lax.ppermute(value, axis, [(i, i ^ flip) for i in range(lax.axis_size(axi...  16.7 us
    pallas_call x3, Pallas kernels, attend(): pl.pallas_call(functools.partial(attend_kernel, req, index, offset, rows,...  13.2 us
    pallas_call x3, Pallas kernels, feed(): pl.pallas_call(functools.partial(feed_kernel, len(pieces)), out_shape=par...  10.5 us
    pallas_call x3, Pallas kernels, project(): pl.pallas_call(functools.partial(project_kernel, reqs, len(extra)), grid=...  6.63 us
    unnamed x37, local copies, waits for them, and re-layouts  4.42 us
    pallas_call x3, Pallas kernels, finish(): pl.pallas_call(functools.partial(finish_kernel, req), grid=(1,), out_shap...  4.41 us
    pallas_call x2, Pallas kernels, make_base(): pl.pallas_call(base_kernel, out_shape=jax.ShapeDtypeStruct(hidden.shape,...  2.73 us
  transfers between devices with their start and end apart: 45, of which 11 were waited for; matrix products, arithmetic and copies ran while one was open for 2% of the time, Pallas kernels for 37%

profile of v4, /device:TPU:0, one launch (start us, length us, event | category | flops | bytes accessed | tf_op | source)
XLA Modules:
  0.0 93.0 jit_solution(9037334841096197269)
XLA Ops:
  0.6 0.5 collective-permute-start
  1.2 2.6 %collective-permute-start.2 = (bf16[3,64,2048]{2,1,0:T(8,128)(2,1)}, bf16[3,64,2048]{2,1,0:T(8,128)(2,1)S(1)}, u32[]{:S(2)}, u32[]{:S(2)}) collective-permute-start(bf16[3,64,2048]{2,1,0:T(8,128)(2,1)} %bitcast.12), channel_id=1, source_target_pairs={{0,2},{1,3},{2,0},{3,1},{4,6},{5,7},{6,4},{7,5},{8,10},{9,11},{10,... | collective-permute-start | bytes 2359304 | tf_op jit(solution)/shard_map/ppermute | solution.py:27
  3.8 2.5 %collective-permute-start.1 = (bf16[1,128,512]{2,1,0:T(8,128)(2,1)S(1)}, bf16[1,128,512]{2,1,0:T(8,128)(2,1)S(1)}, u32[]{:S(2)}, u32[]{:S(2)}) collective-permute-start(bf16[1,128,512]{2,1,0:T(8,128)(2,1)S(1)} %constant_dynamic-slice_fusion), channel_id=1, source_target_pairs={{0,8},{4,12},{8,0},{12,4},{16,24},{20,28},{24,16},{28,20},{1,9},{5... | collective-permute-start | bytes 393224 | tf_op jit(solution)/shard_map/ppermute | solution.py:27
  6.3 0.5 multiply_sine_fusion
  6.9 2.7 %collective-permute-start.3 = (bf16[1,128,512]{2,1,0:T(8,128)(2,1)S(1)}, bf16[1,128,512]{2,1,0:T(8,128)(2,1)S(1)}, u32[]{:S(2)}, u32[]{:S(2)}) collective-permute-start(bf16[1,128,512]{2,1,0:T(8,128)(2,1)S(1)} %constant_dynamic-slice_fusion), channel_id=1, source_target_pairs={{0,16},{4,20},{8,24},{12,28},{16,0},{20,4},{24,8},{28,12},{1,17},{... | collective-permute-start | bytes 393224 | tf_op jit(solution)/shard_map/ppermute | solution.py:27
  9.5 0.7 pad_maximum_fusion.1.head_gains_ref
  10.2 0.8 stack.32.gains_ref
  11.2 1.8 %collective-permute-start.7 = (bf16[2,128,512]{2,1,0:T(8,128)(2,1)S(1)}, bf16[2,128,512]{2,1,0:T(8,128)(2,1)S(1)}, u32[]{:S(2)}, u32[]{:S(2)}) collective-permute-start(bf16[2,128,512]{2,1,0:T(8,128)(2,1)S(1)} %pad_maximum_fusion.refs_0_), channel_id=1, source_target_pairs={{0,4},{4,0},{8,12},{12,8},{16,20},{20,16},{24,28},{28,24},{1,5},{5... | collective-permute-start | bytes 786440 | tf_op jit(solution)/shard_map/ppermute | solution.py:27
  12.9 1.1 %copy-done.6 = bf16[64,3,2048]{2,0,1:T(8,128)(2,1)S(1)} copy-done((bf16[64,3,2048]{2,0,1:T(8,128)(2,1)S(1)}, bf16[64,3,2048]{2,0,1:T(8,128)(2,1)}, u32[]{:S(2)}) %copy-start.6) | copy-done | bytes 786456
  14.1 0.9 %copy-done.9 = bf16[2048,64]{0,1:T(8,128)(2,1)S(1)} copy-done((bf16[2048,64]{0,1:T(8,128)(2,1)S(1)}, bf16[2048,64]{0,1:T(8,128)(2,1)}, u32[]{:S(2)}) %copy-start.9) | copy-done | bytes 262168
  15.0 0.9 %copy-done.11 = bf16[64,2048]{1,0:T(8,128)(2,1)S(1)} copy-done((bf16[64,2048]{1,0:T(8,128)(2,1)S(1)}, bf16[64,2048]{1,0:T(8,128)(2,1)}, u32[]{:S(2)}) %copy-start.11) | copy-done | bytes 262168
  16.0 1.4 %base.2.own_base_ref = f32[3,64,2048]{2,1,0:T(8,128)S(1)} custom-call(bf16[3,64,2048]{2,1,0:T(8,128)(2,1)S(1)} %bitcast.13, f32[5,2048]{1,0:T(8,128)S(1)} %stack.32.gains_ref, bf16[64,2048]{1,0:T(8,128)(2,1)S(1)} %bitcast.17, bf16[64,2048]{1,0:T(8,128)(2,1)S(1)} %copy-done.11), custom_call_target="tpu_custom_call" | custom-call | flops 1 | bytes 1 | tf_op jit(solution)/shard_map/base/pallas_call | solution.py:71
  17.3 2.0 %collective-permute-done.3 = bf16[1,128,512]{2,1,0:T(8,128)(2,1)S(1)} collective-permute-done((bf16[1,128,512]{2,1,0:T(8,128)(2,1)S(1)}, bf16[1,128,512]{2,1,0:T(8,128)(2,1)S(1)}, u32[]{:S(2)}, u32[]{:S(2)}) %collective-permute-start.3) | collective-permute-done | bytes 131104 | tf_op jit(solution)/shard_map/ppermute | solution.py:27
  19.5 1.6 %collective-permute-start.8 = (bf16[2,128,512]{2,1,0:T(8,128)(2,1)S(1)}, bf16[2,128,512]{2,1,0:T(8,128)(2,1)S(1)}, u32[]{:S(2)}, u32[]{:S(2)}) collective-permute-start(bf16[2,128,512]{2,1,0:T(8,128)(2,1)S(1)} %constant_dynamic-update-slice_fusion.refs_1_), channel_id=1, source_target_pairs={{0,4},{4,0},{8,12},{12,8},{16,20},{20,16},{24,28},{28,24},{1,5},{5... | collective-permute-start | bytes 786440 | tf_op jit(solution)/shard_map/ppermute | solution.py:27
  21.0 1.1 %collective-permute-done.2.hidden_ref.y_ref = bf16[3,64,2048]{2,1,0:T(8,128)(2,1)S(1)} collective-permute-done((bf16[3,64,2048]{2,1,0:T(8,128)(2,1)}, bf16[3,64,2048]{2,1,0:T(8,128)(2,1)S(1)}, u32[]{:S(2)}, u32[]{:S(2)}) %collective-permute-start.2) | collective-permute-done | bytes 786464 | tf_op jit(solution)/shard_map/ppermute | solution.py:27
  22.1 1.4 %base.3.y_base_ref = f32[3,64,2048]{2,1,0:T(8,128)S(1)} custom-call(bf16[3,64,2048]{2,1,0:T(8,128)(2,1)S(1)} %collective-permute-done.2.hidden_ref.y_ref, f32[5,2048]{1,0:T(8,128)S(1)} %stack.32.gains_ref, bf16[64,2048]{1,0:T(8,128)(2,1)S(1)} %bitcast.18, bf16[64,2048]{1,0:T(8,128)(2,1)S(1)} %copy-done.12), custom_call_target="tpu_custom_call" | custom-call | flops 99999997952 | bytes 1 | tf_op jit(solution)/shard_map/base/pallas_call | solution.py:71
  23.5 0.6 collective-permute-start.10
  24.1 0.3 collective-permute-done.5.d_ref
  24.4 2.5 %project.3 = (bf16[3,256,256]{2,1,0:T(8,128)(2,1)}, bf16[1,512,256]{2,1,0:T(8,128)(2,1)S(1)}, bf16[1,256,256]{2,1,0:T(8,128)(2,1)S(1)}) custom-call(s32[3]{0:T(128)S(1)} %copy-done.13, bf16[3,64,2048]{2,1,0:T(8,128)(2,1)S(1)} %bitcast.14, bf16[3,64,2048]{2,1,0:T(8,128)(2,1)S(1)} %collective-permute-done.2.hidden_ref.y_ref, ...), custom_call_target="tpu_custom_call" | custom-call | flops 1 | bytes 1 | tf_op jit(solution)/shard_map/project/pallas_call | solution.py:142
  27.1 0.3 collective-permute-start.11
  27.7 2.0 %project.4 = (bf16[3,256,256]{2,1,0:T(8,128)(2,1)}, bf16[1,512,256]{2,1,0:T(8,128)(2,1)S(1)}, bf16[1,256,256]{2,1,0:T(8,128)(2,1)S(1)}) custom-call(s32[3]{0:T(128)S(1)} %copy-done.13, bf16[3,64,2048]{2,1,0:T(8,128)(2,1)S(1)} %bitcast.15, bf16[3,64,2048]{2,1,0:T(8,128)(2,1)S(1)} %collective-permute-done.2.hidden_ref.y_ref, ...), custom_call_target="tpu_custom_call", output_to_operand_aliasing={{0}: (11, {})} | custom-call | flops 1 | bytes 1 | tf_op jit(solution)/shard_map/project/pallas_call | solution.py:142
  29.8 4.4 %attend.3 = (bf16[128,2048]{1,0:T(8,128)(2,1)S(1)}, bf16[64,2048]{1,0:T(8,128)(2,1)S(1)}, bf16[64,2048]{1,0:T(8,128)(2,1)S(1)}) custom-call(s32[3]{0:T(128)S(1)} %copy-done.17, s32[2,8]{1,0:T(2,128)S(1)} %copy-done.15, s32[2,8]{1,0:T(2,128)S(1)} %copy-done.16, bf16[1,512,256]{2,1,0:T(8,128)(2,1)S(1)} %get-tuple-element.86.q_ref, ...), custom_call_target="tpu_custom_call" | custom-call | flops 1 | bytes 1 | tf_op jit(solution)/shard_map/attend/pallas_call | solution.py:299
  34.2 0.4 collective-permute-start.13
  34.5 0.2 collective-permute-start.14
  34.8 1.0 %collective-permute-done.13.refs_0_ = bf16[64,2048]{1,0:T(8,128)(2,1)S(1)} collective-permute-done((bf16[64,2048]{1,0:T(8,128)(2,1)S(1)}, bf16[64,2048]{1,0:T(8,128)(2,1)S(1)}, u32[]{:S(2)}, u32[]{:S(2)}) %collective-permute-start.13) | collective-permute-done | bytes 262176 | tf_op jit(solution)/shard_map/ppermute | solution.py:27
  35.8 0.4 collective-permute-done.14.refs_1_
  36.3 1.8 %collective-permute-start.19 = (bf16[128,2048]{1,0:T(8,128)(2,1)S(1)}, bf16[128,2048]{1,0:T(8,128)(2,1)S(1)}, u32[]{:S(2)}, u32[]{:S(2)}) collective-permute-start(bf16[128,2048]{1,0:T(8,128)(2,1)S(1)} %pair_sum.6.refs_0_), channel_id=1, source_target_pairs={{0,2},{1,3},{2,0},{3,1},{4,6},{5,7},{6,4},{7,5},{8,10},{9,11},{10,... | collective-permute-start | bytes 1572872 | tf_op jit(solution)/shard_map/ppermute | solution.py:27
  38.1 2.0 %project.5 = (bf16[3,256,256]{2,1,0:T(8,128)(2,1)}, bf16[1,512,256]{2,1,0:T(8,128)(2,1)S(1)}, bf16[1,256,256]{2,1,0:T(8,128)(2,1)S(1)}) custom-call(s32[3]{0:T(128)S(1)} %copy-done.13, bf16[3,64,2048]{2,1,0:T(8,128)(2,1)S(1)} %bitcast.16, bf16[3,64,2048]{2,1,0:T(8,128)(2,1)S(1)} %collective-permute-done.2.hidden_ref.y_ref, ...), custom_call_target="tpu_custom_call", output_to_operand_aliasing={{0}: (11, {})} | custom-call | flops 1 | bytes 1 | tf_op jit(solution)/shard_map/project/pallas_call | solution.py:142
  40.2 4.5 %attend.4 = (bf16[128,2048]{1,0:T(8,128)(2,1)S(1)}, bf16[64,2048]{1,0:T(8,128)(2,1)S(1)}, bf16[64,2048]{1,0:T(8,128)(2,1)S(1)}) custom-call(s32[3]{0:T(128)S(1)} %copy-done.17, s32[2,8]{1,0:T(2,128)S(1)} %copy-done.15, s32[2,8]{1,0:T(2,128)S(1)} %copy-done.16, bf16[1,512,256]{2,1,0:T(8,128)(2,1)S(1)} %get-tuple-element.96.q_ref, ...), custom_call_target="tpu_custom_call" | custom-call | flops 1 | bytes 1 | tf_op jit(solution)/shard_map/attend/pallas_call | solution.py:299
  44.7 0.6 collective-permute-start.16
  45.3 0.4 collective-permute-start.18
  45.8 0.7 collective-permute-done.16.refs_0_
  46.4 0.4 collective-permute-done.17.refs_1_
  46.9 0.4 collective-permute-start.23
  47.3 4.3 %attend.5 = (bf16[128,2048]{1,0:T(8,128)(2,1)S(1)}, bf16[64,2048]{1,0:T(8,128)(2,1)S(1)}, bf16[64,2048]{1,0:T(8,128)(2,1)S(1)}) custom-call(s32[3]{0:T(128)S(1)} %copy-done.17, s32[2,8]{1,0:T(2,128)S(1)} %copy-done.15, s32[2,8]{1,0:T(2,128)S(1)} %copy-done.16, bf16[1,512,256]{2,1,0:T(8,128)(2,1)S(1)} %get-tuple-element.101.q_ref, ...), custom_call_target="tpu_custom_call" | custom-call | flops 1 | bytes 1 | tf_op jit(solution)/shard_map/attend/pallas_call | solution.py:299
  51.6 0.2 collective-permute-start.20
  51.8 0.4 collective-permute-start.21
  52.2 0.6 residual.3
  52.8 0.2 collective-permute-start.24
  53.0 0.4 collective-permute-start.25
  53.7 1.8 %collective-permute-start.22 = (bf16[128,2048]{1,0:T(8,128)(2,1)S(1)}, bf16[128,2048]{1,0:T(8,128)(2,1)S(1)}, u32[]{:S(2)}, u32[]{:S(2)}) collective-permute-start(bf16[128,2048]{1,0:T(8,128)(2,1)S(1)} %pair_sum.8.refs_0_), channel_id=1, source_target_pairs={{0,2},{1,3},{2,0},{3,1},{4,6},{5,7},{6,4},{7,5},{8,10},{9,11},{10,... | collective-permute-start | bytes 1572872 | tf_op jit(solution)/shard_map/ppermute | solution.py:27
  55.6 1.2 %copy-done.3 = bf16[1024,2048]{1,0:T(8,128)(2,1)S(1)} copy-done((bf16[1024,2048]{1,0:T(8,128)(2,1)S(1)}, bf16[1024,2048]{1,0:T(8,128)(2,1)}, u32[]{:S(2)}) %copy-start.3) | copy-done | bytes 4194328
  56.8 3.4 %feed.3 = (bf16[128,2048]{1,0:T(8,128)(2,1)S(1)}, bf16[48,2048]{1,0:T(8,128)(2,1)S(1)}, bf16[48,2048]{1,0:T(8,128)(2,1)S(1)}, bf16[32,2048]{1,0:T(8,128)(2,1)S(1)}) custom-call(bf16[2048,1024]{1,0:T(8,128)(2,1)S(1)} %copy-done.1, bf16[2048,1024]{1,0:T(8,128)(2,1)S(1)} %copy-done.2, bf16[1024,2048]{1,0:T(8,128)(2,1)S(1)} %copy-done.3, ...), custom_call_target="tpu_custom_call" | custom-call | flops 1 | bytes 1 | tf_op jit(solution)/shard_map/feed/pallas_call | solution.py:389
  60.3 0.2 collective-permute-start.27
  60.5 0.4 collective-permute-start.28
  61.0 1.2 %collective-permute-done.23.refs_1_ = bf16[128,2048]{1,0:T(8,128)(2,1)S(1)} collective-permute-done((bf16[128,2048]{1,0:T(8,128)(2,1)S(1)}, bf16[128,2048]{1,0:T(8,128)(2,1)S(1)}, u32[]{:S(2)}, u32[]{:S(2)}) %collective-permute-start.23) | collective-permute-done | bytes 524320 | tf_op jit(solution)/shard_map/ppermute | solution.py:27
  62.2 0.6 residual.4
  62.9 0.5 collective-permute-start.31
  63.6 2.0 %collective-permute-start.39 = (bf16[64,2048]{1,0:T(8,128)(2,1)S(1)}, bf16[64,2048]{1,0:T(8,128)(2,1)S(1)}, u32[]{:S(2)}, u32[]{:S(2)}) collective-permute-start(bf16[64,2048]{1,0:T(8,128)(2,1)S(1)} %get-tuple-element.137), channel_id=1, source_target_pairs={{0,2},{1,3},{2,0},{3,1},{4,6},{5,7},{6,4},{7,5},{8,10},{9,11},{10,... | collective-permute-start | bytes 786440 | tf_op jit(solution)/shard_map/ppermute | solution.py:27
  65.6 3.4 %feed.4 = (bf16[128,2048]{1,0:T(8,128)(2,1)S(1)}, bf16[48,2048]{1,0:T(8,128)(2,1)S(1)}, bf16[48,2048]{1,0:T(8,128)(2,1)S(1)}, bf16[32,2048]{1,0:T(8,128)(2,1)S(1)}) custom-call(bf16[2048,1024]{1,0:T(8,128)(2,1)S(1)} %copy-done.1, bf16[2048,1024]{1,0:T(8,128)(2,1)S(1)} %copy-done.2, bf16[1024,2048]{1,0:T(8,128)(2,1)S(1)} %copy-done.3, ...), custom_call_target="tpu_custom_call" | custom-call | flops 1 | bytes 1 | tf_op jit(solution)/shard_map/feed/pallas_call | solution.py:389
  69.0 0.2 collective-permute-start.33
  69.2 0.4 collective-permute-start.34
  69.8 3.6 %collective-permute-done.22.refs_1_ = bf16[128,2048]{1,0:T(8,128)(2,1)S(1)} collective-permute-done((bf16[128,2048]{1,0:T(8,128)(2,1)S(1)}, bf16[128,2048]{1,0:T(8,128)(2,1)S(1)}, u32[]{:S(2)}, u32[]{:S(2)}) %collective-permute-start.22) | collective-permute-done | bytes 524320 | tf_op jit(solution)/shard_map/ppermute | solution.py:27
  73.4 0.6 residual.5
  74.1 0.5 collective-permute-start.37
  74.8 2.0 %collective-permute-start.44 = (bf16[64,2048]{1,0:T(8,128)(2,1)S(1)}, bf16[64,2048]{1,0:T(8,128)(2,1)S(1)}, u32[]{:S(2)}, u32[]{:S(2)}) collective-permute-start(bf16[64,2048]{1,0:T(8,128)(2,1)S(1)} %get-tuple-element.147), channel_id=1, source_target_pairs={{0,2},{1,3},{2,0},{3,1},{4,6},{5,7},{6,4},{7,5},{8,10},{9,11},{10,... | collective-permute-start | bytes 786440 | tf_op jit(solution)/shard_map/ppermute | solution.py:27
  76.8 3.7 %feed.5 = (bf16[128,2048]{1,0:T(8,128)(2,1)S(1)}, bf16[48,2048]{1,0:T(8,128)(2,1)S(1)}, bf16[48,2048]{1,0:T(8,128)(2,1)S(1)}, bf16[32,2048]{1,0:T(8,128)(2,1)S(1)}) custom-call(bf16[2048,1024]{1,0:T(8,128)(2,1)S(1)} %copy-done.1, bf16[2048,1024]{1,0:T(8,128)(2,1)S(1)} %copy-done.2, bf16[1024,2048]{1,0:T(8,128)(2,1)S(1)} %copy-done.3, ...), custom_call_target="tpu_custom_call" | custom-call | flops 1 | bytes 1 | tf_op jit(solution)/shard_map/feed/pallas_call | solution.py:389
  80.5 0.2 collective-permute-start.40
  80.7 0.4 collective-permute-start.41
  81.3 1.5 %finish.3.refs_0_ = bf16[3,64,2048]{2,1,0:T(8,128)(2,1)} custom-call(s32[3]{0:T(128)S(1)} %copy-done.14, f32[64,2048]{1,0:T(8,128)S(1)} %get-tuple-element.136.res_ref, bf16[64,2048]{1,0:T(8,128)(2,1)S(1)} %get-tuple-element.119.near_ref, bf16[64,2048]{1,0:T(8,128)(2,1)S(1)} %collective-permute-done.39.far_ref, f32[5,2048]{1,0:T(8,128)S(1)} %stack.32.gains_ref), custom_call_target="tpu_custom_call" | custom-call | flops 99999997952 | bytes 1 | tf_op jit(solution)/shard_map/finish/pallas_call | solution.py:413
  82.9 1.2 %collective-permute-start.43 = (bf16[64,2048]{1,0:T(8,128)(2,1)S(1)}, bf16[64,2048]{1,0:T(8,128)(2,1)S(1)}, u32[]{:S(2)}, u32[]{:S(2)}) collective-permute-start(bf16[64,2048]{1,0:T(8,128)(2,1)S(1)} %get-tuple-element.144), channel_id=1, source_target_pairs={{0,2},{1,3},{2,0},{3,1},{4,6},{5,7},{6,4},{7,5},{8,10},{9,11},{10,... | collective-permute-start | bytes 786440 | tf_op jit(solution)/shard_map/ppermute | solution.py:27
  84.2 1.5 %finish.4.refs_0_ = bf16[3,64,2048]{2,1,0:T(8,128)(2,1)} custom-call(s32[3]{0:T(128)S(1)} %copy-done.14, f32[64,2048]{1,0:T(8,128)S(1)} %get-tuple-element.146.res_ref, bf16[64,2048]{1,0:T(8,128)(2,1)S(1)} %get-tuple-element.131.near_ref, bf16[64,2048]{1,0:T(8,128)(2,1)S(1)} %collective-permute-done.44.far_ref, ...), custom_call_target="tpu_custom_call", output_to_operand_aliasing={{}: (5, {})} | custom-call | flops 1 | bytes 1 | tf_op jit(solution)/shard_map/finish/pallas_call | solution.py:413
  85.7 5.8 %collective-permute-done.43.far_ref = bf16[64,2048]{1,0:T(8,128)(2,1)S(1)} collective-permute-done((bf16[64,2048]{1,0:T(8,128)(2,1)S(1)}, bf16[64,2048]{1,0:T(8,128)(2,1)S(1)}, u32[]{:S(2)}, u32[]{:S(2)}) %collective-permute-start.43) | collective-permute-done | bytes 262176 | tf_op jit(solution)/shard_map/ppermute | solution.py:27
  91.5 1.5 %finish.5 = bf16[3,64,2048]{2,1,0:T(8,128)(2,1)} custom-call(s32[3]{0:T(128)S(1)} %copy-done.14, f32[64,2048]{1,0:T(8,128)S(1)} %get-tuple-element.125.res_ref, bf16[64,2048]{1,0:T(8,128)(2,1)S(1)} %get-tuple-element.143.near_ref, bf16[64,2048]{1,0:T(8,128)(2,1)S(1)} %collective-permute-done.43.far_ref, ...), custom_call_target="tpu_custom_call", output_to_operand_aliasing={{}: (5, {})} | custom-call | flops 1 | bytes 1 | tf_op jit(solution)/shard_map/finish/pallas_call | solution.py:413
  (94 shorter events, 2.7 us)
Async XLA Ops:
  0.6 3.2 %copy-start = (bf16[2,128,1024]{2,1,0:T(8,128)(2,1)S(1)}, bf16[2,128,1024]{2,1,0:T(8,128)(2,1)}, u32[]{:S(2)}) copy-start(bf16[2,128,1024]{2,1,0:T(8,128)(2,1)} %param.37) | copy-start | bytes 1572868
  0.6 3.1 %collective-permute-start = (bf16[3,64,2048]{2,1,0:T(8,128)(2,1)}, bf16[3,64,2048]{2,1,0:T(8,128)(2,1)S(1)}, u32[]{:S(2)}, u32[]{:S(2)}) collective-permute-start(bf16[3,64,2048]{2,1,0:T(8,128)(2,1)} %bitcast.11), channel_id=1, source_target_pairs={{0,1},{1,0},{2,3},{3,2},{4,5},{5,4},{6,7},{7,6},{8,9},{9,8},{10,11... | collective-permute-start | bytes 2359304 | tf_op jit(solution)/shard_map/ppermute | solution.py:27
  1.2 20.9 %collective-permute-start.2 = (bf16[3,64,2048]{2,1,0:T(8,128)(2,1)}, bf16[3,64,2048]{2,1,0:T(8,128)(2,1)S(1)}, u32[]{:S(2)}, u32[]{:S(2)}) collective-permute-start(bf16[3,64,2048]{2,1,0:T(8,128)(2,1)} %bitcast.12), channel_id=1, source_target_pairs={{0,2},{1,3},{2,0},{3,1},{4,6},{5,7},{6,4},{7,5},{8,10},{9,11},{10,... | collective-permute-start | bytes 2359304 | tf_op jit(solution)/shard_map/ppermute | solution.py:27
  3.8 7.3 %collective-permute-start.1 = (bf16[1,128,512]{2,1,0:T(8,128)(2,1)S(1)}, bf16[1,128,512]{2,1,0:T(8,128)(2,1)S(1)}, u32[]{:S(2)}, u32[]{:S(2)}) collective-permute-start(bf16[1,128,512]{2,1,0:T(8,128)(2,1)S(1)} %constant_dynamic-slice_fusion), channel_id=1, source_target_pairs={{0,8},{4,12},{8,0},{12,4},{16,24},{20,28},{24,16},{28,20},{1,9},{5... | collective-permute-start | bytes 393224 | tf_op jit(solution)/shard_map/ppermute | solution.py:27
  6.8 15.3 %copy-start.10 = (bf16[2048,64]{0,1:T(8,128)(2,1)S(1)}, bf16[2048,64]{0,1:T(8,128)(2,1)}, u32[]{:S(2)}) copy-start(bf16[2048,64]{0,1:T(8,128)(2,1)} %param.29) | copy-start | bytes 786436
  6.9 15.2 %copy-start.12 = (bf16[64,2048]{1,0:T(8,128)(2,1)S(1)}, bf16[64,2048]{1,0:T(8,128)(2,1)}, u32[]{:S(2)}) copy-start(bf16[64,2048]{1,0:T(8,128)(2,1)} %right_ref.3) | copy-start | bytes 786436
  6.9 12.5 %collective-permute-start.3 = (bf16[1,128,512]{2,1,0:T(8,128)(2,1)S(1)}, bf16[1,128,512]{2,1,0:T(8,128)(2,1)S(1)}, u32[]{:S(2)}, u32[]{:S(2)}) collective-permute-start(bf16[1,128,512]{2,1,0:T(8,128)(2,1)S(1)} %constant_dynamic-slice_fusion), channel_id=1, source_target_pairs={{0,16},{4,20},{8,24},{12,28},{16,0},{20,4},{24,8},{28,12},{1,17},{... | collective-permute-start | bytes 393224 | tf_op jit(solution)/shard_map/ppermute | solution.py:27
  11.1 8.3 %collective-permute-start.4 = (bf16[1,128,512]{2,1,0:T(8,128)(2,1)S(1)}, bf16[1,128,512]{2,1,0:T(8,128)(2,1)S(1)}, u32[]{:S(2)}, u32[]{:S(2)}) collective-permute-start(bf16[1,128,512]{2,1,0:T(8,128)(2,1)S(1)} %constant_dynamic-slice_fusion), channel_id=1, source_target_pairs={{0,24},{4,28},{8,16},{12,20},{16,8},{20,12},{24,0},{28,4},{1,25},{... | collective-permute-start | bytes 393224 | tf_op jit(solution)/shard_map/ppermute | solution.py:27
  11.2 16.0 %collective-permute-start.7 = (bf16[2,128,512]{2,1,0:T(8,128)(2,1)S(1)}, bf16[2,128,512]{2,1,0:T(8,128)(2,1)S(1)}, u32[]{:S(2)}, u32[]{:S(2)}) collective-permute-start(bf16[2,128,512]{2,1,0:T(8,128)(2,1)S(1)} %pad_maximum_fusion.refs_0_), channel_id=1, source_target_pairs={{0,4},{4,0},{8,12},{12,8},{16,20},{20,16},{24,28},{28,24},{1,5},{5... | collective-permute-start | bytes 786440 | tf_op jit(solution)/shard_map/ppermute | solution.py:27
  12.9 1.1 %copy-start.6 = (bf16[64,3,2048]{2,0,1:T(8,128)(2,1)S(1)}, bf16[64,3,2048]{2,0,1:T(8,128)(2,1)}, u32[]{:S(2)}) copy-start(bf16[64,3,2048]{2,0,1:T(8,128)(2,1)} %param.21) | copy-start | bytes 2359300
  14.1 0.9 %copy-start.9 = (bf16[2048,64]{0,1:T(8,128)(2,1)S(1)}, bf16[2048,64]{0,1:T(8,128)(2,1)}, u32[]{:S(2)}) copy-start(bf16[2048,64]{0,1:T(8,128)(2,1)} %param.29) | copy-start | bytes 786436
  15.0 0.9 %copy-start.11 = (bf16[64,2048]{1,0:T(8,128)(2,1)S(1)}, bf16[64,2048]{1,0:T(8,128)(2,1)}, u32[]{:S(2)}) copy-start(bf16[64,2048]{1,0:T(8,128)(2,1)} %right_ref.3) | copy-start | bytes 786436
  19.4 5.0 %copy-start.5 = (bf16[2048,512]{1,0:T(8,128)(2,1)S(1)}, bf16[2048,512]{1,0:T(8,128)(2,1)}, u32[]{:S(2)}) copy-start(bf16[2048,512]{1,0:T(8,128)(2,1)} %wq_ref.5) | copy-start | bytes 6291460
  19.4 5.0 %copy-start.7 = (bf16[64,3,2048]{2,0,1:T(8,128)(2,1)S(1)}, bf16[64,3,2048]{2,0,1:T(8,128)(2,1)}, u32[]{:S(2)}) copy-start(bf16[64,3,2048]{2,0,1:T(8,128)(2,1)} %param.21) | copy-start | bytes 2359300
  19.4 5.0 %copy-start.8 = (bf16[2048,256]{1,0:T(8,128)(2,1)S(1)}, bf16[2048,256]{1,0:T(8,128)(2,1)}, u32[]{:S(2)}) copy-start(bf16[2048,256]{1,0:T(8,128)(2,1)} %wkv_ref.5) | copy-start | bytes 3145732
  19.4 5.0 %copy-start.13 = (s32[3]{0:T(128)S(1)}, s32[3]{0:T(128)}, u32[]{:S(2)}) copy-start(s32[3]{0:T(128)} %len_ref.11) | copy-start | bytes 40
  19.5 7.5 %collective-permute-start.8 = (bf16[2,128,512]{2,1,0:T(8,128)(2,1)S(1)}, bf16[2,128,512]{2,1,0:T(8,128)(2,1)S(1)}, u32[]{:S(2)}, u32[]{:S(2)}) collective-permute-start(bf16[2,128,512]{2,1,0:T(8,128)(2,1)S(1)} %constant_dynamic-update-slice_fusion.refs_1_), channel_id=1, source_target_pairs={{0,4},{4,0},{8,12},{12,8},{16,20},{20,16},{24,28},{28,24},{1,5},{5... | collective-permute-start | bytes 786440 | tf_op jit(solution)/shard_map/ppermute | solution.py:27
  22.1 2.3 %collective-permute-start.5 = (bf16[3,64,2048]{2,1,0:T(8,128)(2,1)S(1)}, bf16[3,64,2048]{2,1,0:T(8,128)(2,1)S(1)}, u32[]{:S(2)}, u32[]{:S(2)}) collective-permute-start(bf16[3,64,2048]{2,1,0:T(8,128)(2,1)S(1)} %collective-permute-done.2.hidden_ref.y_ref), channel_id=1, source_target_pairs={{0,1},{1,0},{2,3},{3,2},{4,5},{5,4},{6,7},{7,6},{8,9},{9,8},{10,11... | collective-permute-start | bytes 2359304 | tf_op jit(solution)/shard_map/ppermute | solution.py:27
  23.5 6.2 %collective-permute-start.10 = (bf16[2,128,512]{2,1,0:T(8,128)(2,1)S(1)}, bf16[2,128,512]{2,1,0:T(8,128)(2,1)S(1)}, u32[]{:S(2)}, u32[]{:S(2)}) collective-permute-start(bf16[2,128,512]{2,1,0:T(8,128)(2,1)S(1)} %constant_dynamic-update-slice_fusion.refs_1_), channel_id=1, source_target_pairs={{0,1},{1,0},{2,3},{3,2},{4,5},{5,4},{6,7},{7,6},{8,9},{9,8},{10,11... | collective-permute-start | bytes 786440 | tf_op jit(solution)/shard_map/ppermute | solution.py:27
  24.1 5.7 %collective-permute-start.9 = (bf16[2,128,512]{2,1,0:T(8,128)(2,1)S(1)}, bf16[2,128,512]{2,1,0:T(8,128)(2,1)S(1)}, u32[]{:S(2)}, u32[]{:S(2)}) collective-permute-start(bf16[2,128,512]{2,1,0:T(8,128)(2,1)S(1)} %pad_maximum_fusion.refs_0_), channel_id=1, source_target_pairs={{0,1},{1,0},{2,3},{3,2},{4,5},{5,4},{6,7},{7,6},{8,9},{9,8},{10,11... | collective-permute-start | bytes 786440 | tf_op jit(solution)/shard_map/ppermute | solution.py:27
  26.9 2.8 %collective-permute-start.12 = (bf16[2,128,512]{2,1,0:T(8,128)(2,1)S(1)}, bf16[2,128,512]{2,1,0:T(8,128)(2,1)S(1)}, u32[]{:S(2)}, u32[]{:S(2)}) collective-permute-start(bf16[2,128,512]{2,1,0:T(8,128)(2,1)S(1)} %collective-permute-done.8.refs_3_), channel_id=1, source_target_pairs={{0,1},{1,0},{2,3},{3,2},{4,5},{5,4},{6,7},{7,6},{8,9},{9,8},{10,11... | collective-permute-start | bytes 786440 | tf_op jit(solution)/shard_map/ppermute | solution.py:27
  27.1 2.6 %collective-permute-start.11 = (bf16[2,128,512]{2,1,0:T(8,128)(2,1)S(1)}, bf16[2,128,512]{2,1,0:T(8,128)(2,1)S(1)}, u32[]{:S(2)}, u32[]{:S(2)}) collective-permute-start(bf16[2,128,512]{2,1,0:T(8,128)(2,1)S(1)} %collective-permute-done.7.refs_2_), channel_id=1, source_target_pairs={{0,1},{1,0},{2,3},{3,2},{4,5},{5,4},{6,7},{7,6},{8,9},{9,8},{10,11... | collective-permute-start | bytes 786440 | tf_op jit(solution)/shard_map/ppermute | solution.py:27
  27.5 2.3 %collective-permute-start.6 = (bf16[1,256,256]{2,1,0:T(8,128)(2,1)S(1)}, bf16[1,256,256]{2,1,0:T(8,128)(2,1)S(1)}, u32[]{:S(2)}, u32[]{:S(2)}) collective-permute-start(bf16[1,256,256]{2,1,0:T(8,128)(2,1)S(1)} %get-tuple-element.87.mine_ref), channel_id=1, source_target_pairs={{0,1},{1,0},{2,3},{3,2},{4,5},{5,4},{6,7},{7,6},{8,9},{9,8},{10,11... | collective-permute-start | bytes 393224 | tf_op jit(solution)/shard_map/ppermute | solution.py:27
  27.6 2.1 %copy-start.4 = (bf16[512,2048]{1,0:T(8,128)(2,1)S(1)}, bf16[512,2048]{1,0:T(8,128)(2,1)}, u32[]{:S(2)}) copy-start(bf16[512,2048]{1,0:T(8,128)(2,1)} %wo_ref.5) | copy-start | bytes 6291460
  27.6 2.1 %copy-start.15 = (s32[2,8]{1,0:T(2,128)S(1)}, s32[2,8]{1,0:T(2,128)}, u32[]{:S(2)}) copy-start(s32[2,8]{1,0:T(2,128)} %owner_ref.5) | copy-start | bytes 196
  27.7 2.1 %copy-start.16 = (s32[2,8]{1,0:T(2,128)S(1)}, s32[2,8]{1,0:T(2,128)}, u32[]{:S(2)}) copy-start(s32[2,8]{1,0:T(2,128)} %slot_ref.5) | copy-start | bytes 196
  27.7 2.1 %copy-start.17 = (s32[3]{0:T(128)S(1)}, s32[3]{0:T(128)}, u32[]{:S(2)}) copy-start(s32[3]{0:T(128)} %group_ref.5) | copy-start | bytes 40
  34.2 1.6 %collective-permute-start.13 = (bf16[64,2048]{1,0:T(8,128)(2,1)S(1)}, bf16[64,2048]{1,0:T(8,128)(2,1)S(1)}, u32[]{:S(2)}, u32[]{:S(2)}) collective-permute-start(bf16[64,2048]{1,0:T(8,128)(2,1)S(1)} %get-tuple-element.91), channel_id=1, source_target_pairs={{0,1},{1,0},{2,3},{3,2},{4,5},{5,4},{6,7},{7,6},{8,9},{9,8},{10,11... | collective-permute-start | bytes 786440 | tf_op jit(solution)/shard_map/ppermute | solution.py:27
  34.5 1.6 %collective-permute-start.14 = (bf16[64,2048]{1,0:T(8,128)(2,1)S(1)}, bf16[64,2048]{1,0:T(8,128)(2,1)S(1)}, u32[]{:S(2)}, u32[]{:S(2)}) collective-permute-start(bf16[64,2048]{1,0:T(8,128)(2,1)S(1)} %get-tuple-element.92), channel_id=1, source_target_pairs={{0,1},{1,0},{2,3},{3,2},{4,5},{5,4},{6,7},{7,6},{8,9},{9,8},{10,11... | collective-permute-start | bytes 786440 | tf_op jit(solution)/shard_map/ppermute | solution.py:27
  36.3 15.9 %collective-permute-start.19 = (bf16[128,2048]{1,0:T(8,128)(2,1)S(1)}, bf16[128,2048]{1,0:T(8,128)(2,1)S(1)}, u32[]{:S(2)}, u32[]{:S(2)}) collective-permute-start(bf16[128,2048]{1,0:T(8,128)(2,1)S(1)} %pair_sum.6.refs_0_), channel_id=1, source_target_pairs={{0,2},{1,3},{2,0},{3,1},{4,6},{5,7},{6,4},{7,5},{8,10},{9,11},{10,... | collective-permute-start | bytes 1572872 | tf_op jit(solution)/shard_map/ppermute | solution.py:27
  38.1 2.0 %collective-permute-start.15 = (bf16[1,256,256]{2,1,0:T(8,128)(2,1)S(1)}, bf16[1,256,256]{2,1,0:T(8,128)(2,1)S(1)}, u32[]{:S(2)}, u32[]{:S(2)}) collective-permute-start(bf16[1,256,256]{2,1,0:T(8,128)(2,1)S(1)} %get-tuple-element.97.mine_ref), channel_id=1, source_target_pairs={{0,1},{1,0},{2,3},{3,2},{4,5},{5,4},{6,7},{7,6},{8,9},{9,8},{10,11... | collective-permute-start | bytes 393224 | tf_op jit(solution)/shard_map/ppermute | solution.py:27
  44.7 1.8 %collective-permute-start.16 = (bf16[64,2048]{1,0:T(8,128)(2,1)S(1)}, bf16[64,2048]{1,0:T(8,128)(2,1)S(1)}, u32[]{:S(2)}, u32[]{:S(2)}) collective-permute-start(bf16[64,2048]{1,0:T(8,128)(2,1)S(1)} %get-tuple-element.99), channel_id=1, source_target_pairs={{0,1},{1,0},{2,3},{3,2},{4,5},{5,4},{6,7},{7,6},{8,9},{9,8},{10,11... | collective-permute-start | bytes 786440 | tf_op jit(solution)/shard_map/ppermute | solution.py:27
  45.3 1.5 %collective-permute-start.17 = (bf16[64,2048]{1,0:T(8,128)(2,1)S(1)}, bf16[64,2048]{1,0:T(8,128)(2,1)S(1)}, u32[]{:S(2)}, u32[]{:S(2)}) collective-permute-start(bf16[64,2048]{1,0:T(8,128)(2,1)S(1)} %get-tuple-element.100), channel_id=1, source_target_pairs={{0,1},{1,0},{2,3},{3,2},{4,5},{5,4},{6,7},{7,6},{8,9},{9,8},{10,11... | collective-permute-start | bytes 786440 | tf_op jit(solution)/shard_map/ppermute | solution.py:27
  45.3 1.9 %collective-permute-start.18 = (bf16[1,256,256]{2,1,0:T(8,128)(2,1)S(1)}, bf16[1,256,256]{2,1,0:T(8,128)(2,1)S(1)}, u32[]{:S(2)}, u32[]{:S(2)}) collective-permute-start(bf16[1,256,256]{2,1,0:T(8,128)(2,1)S(1)} %get-tuple-element.102.mine_ref), channel_id=1, source_target_pairs={{0,1},{1,0},{2,3},{3,2},{4,5},{5,4},{6,7},{7,6},{8,9},{9,8},{10,11... | collective-permute-start | bytes 393224 | tf_op jit(solution)/shard_map/ppermute | solution.py:27
  46.9 15.2 %collective-permute-start.23 = (bf16[128,2048]{1,0:T(8,128)(2,1)S(1)}, bf16[128,2048]{1,0:T(8,128)(2,1)S(1)}, u32[]{:S(2)}, u32[]{:S(2)}) collective-permute-start(bf16[128,2048]{1,0:T(8,128)(2,1)S(1)} %pair_sum.7.refs_0_), channel_id=1, source_target_pairs={{0,2},{1,3},{2,0},{3,1},{4,6},{5,7},{6,4},{7,5},{8,10},{9,11},{10,... | collective-permute-start | bytes 1572872 | tf_op jit(solution)/shard_map/ppermute | solution.py:27
  51.6 1.8 %collective-permute-start.20 = (bf16[64,2048]{1,0:T(8,128)(2,1)S(1)}, bf16[64,2048]{1,0:T(8,128)(2,1)S(1)}, u32[]{:S(2)}, u32[]{:S(2)}) collective-permute-start(bf16[64,2048]{1,0:T(8,128)(2,1)S(1)} %get-tuple-element.107), channel_id=1, source_target_pairs={{0,1},{1,0},{2,3},{3,2},{4,5},{5,4},{6,7},{7,6},{8,9},{9,8},{10,11... | collective-permute-start | bytes 786440 | tf_op jit(solution)/shard_map/ppermute | solution.py:27
  51.8 1.8 %collective-permute-start.21 = (bf16[64,2048]{1,0:T(8,128)(2,1)S(1)}, bf16[64,2048]{1,0:T(8,128)(2,1)S(1)}, u32[]{:S(2)}, u32[]{:S(2)}) collective-permute-start(bf16[64,2048]{1,0:T(8,128)(2,1)S(1)} %get-tuple-element.108), channel_id=1, source_target_pairs={{0,1},{1,0},{2,3},{3,2},{4,5},{5,4},{6,7},{7,6},{8,9},{9,8},{10,11... | collective-permute-start | bytes 786440 | tf_op jit(solution)/shard_map/ppermute | solution.py:27
  52.2 3.4 %copy-start.1 = (bf16[2048,1024]{1,0:T(8,128)(2,1)S(1)}, bf16[2048,1024]{1,0:T(8,128)(2,1)}, u32[]{:S(2)}) copy-start(bf16[2048,1024]{1,0:T(8,128)(2,1)} %gate_ref.5) | copy-start | bytes 12582916
  52.2 3.5 %copy-start.2 = (bf16[2048,1024]{1,0:T(8,128)(2,1)S(1)}, bf16[2048,1024]{1,0:T(8,128)(2,1)}, u32[]{:S(2)}) copy-start(bf16[2048,1024]{1,0:T(8,128)(2,1)} %up_ref.5) | copy-start | bytes 12582916
  52.2 4.7 %copy-start.3 = (bf16[1024,2048]{1,0:T(8,128)(2,1)S(1)}, bf16[1024,2048]{1,0:T(8,128)(2,1)}, u32[]{:S(2)}) copy-start(bf16[1024,2048]{1,0:T(8,128)(2,1)} %down_ref.5) | copy-start | bytes 12582916
  52.8 2.7 %collective-permute-start.24 = (bf16[48,2048]{1,0:T(8,128)(2,1)S(1)}, bf16[48,2048]{1,0:T(8,128)(2,1)S(1)}, u32[]{:S(2)}, u32[]{:S(2)}) collective-permute-start(bf16[48,2048]{1,0:T(8,128)(2,1)S(1)} %get-tuple-element.109.refs_0_), channel_id=1, source_target_pairs={{0,1},{1,0},{2,3},{3,2},{4,5},{5,4},{6,7},{7,6},{8,9},{9,8},{10,11... | collective-permute-start | bytes 589832 | tf_op jit(solution)/shard_map/ppermute | solution.py:27
  53.0 2.5 %collective-permute-start.25 = (bf16[48,2048]{1,0:T(8,128)(2,1)S(1)}, bf16[48,2048]{1,0:T(8,128)(2,1)S(1)}, u32[]{:S(2)}, u32[]{:S(2)}) collective-permute-start(bf16[48,2048]{1,0:T(8,128)(2,1)S(1)} %get-tuple-element.110.refs_1_), channel_id=1, source_target_pairs={{0,1},{1,0},{2,3},{3,2},{4,5},{5,4},{6,7},{7,6},{8,9},{9,8},{10,11... | collective-permute-start | bytes 589832 | tf_op jit(solution)/shard_map/ppermute | solution.py:27
  53.4 2.1 %collective-permute-start.26 = (bf16[32,2048]{1,0:T(8,128)(2,1)S(1)}, bf16[32,2048]{1,0:T(8,128)(2,1)S(1)}, u32[]{:S(2)}, u32[]{:S(2)}) collective-permute-start(bf16[32,2048]{1,0:T(8,128)(2,1)S(1)} %get-tuple-element.111.refs_2_), channel_id=1, source_target_pairs={{0,1},{1,0},{2,3},{3,2},{4,5},{5,4},{6,7},{7,6},{8,9},{9,8},{10,11... | collective-permute-start | bytes 393224 | tf_op jit(solution)/shard_map/ppermute | solution.py:27
  53.7 19.7 %collective-permute-start.22 = (bf16[128,2048]{1,0:T(8,128)(2,1)S(1)}, bf16[128,2048]{1,0:T(8,128)(2,1)S(1)}, u32[]{:S(2)}, u32[]{:S(2)}) collective-permute-start(bf16[128,2048]{1,0:T(8,128)(2,1)S(1)} %pair_sum.8.refs_0_), channel_id=1, source_target_pairs={{0,2},{1,3},{2,0},{3,1},{4,6},{5,7},{6,4},{7,5},{8,10},{9,11},{10,... | collective-permute-start | bytes 1572872 | tf_op jit(solution)/shard_map/ppermute | solution.py:27
  60.3 3.1 %collective-permute-start.27 = (bf16[48,2048]{1,0:T(8,128)(2,1)S(1)}, bf16[48,2048]{1,0:T(8,128)(2,1)S(1)}, u32[]{:S(2)}, u32[]{:S(2)}) collective-permute-start(bf16[48,2048]{1,0:T(8,128)(2,1)S(1)} %get-tuple-element.116), channel_id=1, source_target_pairs={{0,1},{1,0},{2,3},{3,2},{4,5},{5,4},{6,7},{7,6},{8,9},{9,8},{10,11... | collective-permute-start | bytes 589832 | tf_op jit(solution)/shard_map/ppermute | solution.py:27
  60.5 3.0 %collective-permute-start.28 = (bf16[48,2048]{1,0:T(8,128)(2,1)S(1)}, bf16[48,2048]{1,0:T(8,128)(2,1)S(1)}, u32[]{:S(2)}, u32[]{:S(2)}) collective-permute-start(bf16[48,2048]{1,0:T(8,128)(2,1)S(1)} %get-tuple-element.117), channel_id=1, source_target_pairs={{0,1},{1,0},{2,3},{3,2},{4,5},{5,4},{6,7},{7,6},{8,9},{9,8},{10,11... | collective-permute-start | bytes 589832 | tf_op jit(solution)/shard_map/ppermute | solution.py:27
  60.8 2.1 %collective-permute-start.29 = (bf16[32,2048]{1,0:T(8,128)(2,1)S(1)}, bf16[32,2048]{1,0:T(8,128)(2,1)S(1)}, u32[]{:S(2)}, u32[]{:S(2)}) collective-permute-start(bf16[32,2048]{1,0:T(8,128)(2,1)S(1)} %get-tuple-element.118), channel_id=1, source_target_pairs={{0,1},{1,0},{2,3},{3,2},{4,5},{5,4},{6,7},{7,6},{8,9},{9,8},{10,11... | collective-permute-start | bytes 393224 | tf_op jit(solution)/shard_map/ppermute | solution.py:27
  62.8 2.8 %collective-permute-start.30 = (bf16[48,2048]{1,0:T(8,128)(2,1)S(1)}, bf16[48,2048]{1,0:T(8,128)(2,1)S(1)}, u32[]{:S(2)}, u32[]{:S(2)}) collective-permute-start(bf16[48,2048]{1,0:T(8,128)(2,1)S(1)} %get-tuple-element.120.refs_0_), channel_id=1, source_target_pairs={{0,1},{1,0},{2,3},{3,2},{4,5},{5,4},{6,7},{7,6},{8,9},{9,8},{10,11... | collective-permute-start | bytes 589832 | tf_op jit(solution)/shard_map/ppermute | solution.py:27
  62.9 2.7 %collective-permute-start.31 = (bf16[48,2048]{1,0:T(8,128)(2,1)S(1)}, bf16[48,2048]{1,0:T(8,128)(2,1)S(1)}, u32[]{:S(2)}, u32[]{:S(2)}) collective-permute-start(bf16[48,2048]{1,0:T(8,128)(2,1)S(1)} %get-tuple-element.121.refs_1_), channel_id=1, source_target_pairs={{0,1},{1,0},{2,3},{3,2},{4,5},{5,4},{6,7},{7,6},{8,9},{9,8},{10,11... | collective-permute-start | bytes 589832 | tf_op jit(solution)/shard_map/ppermute | solution.py:27
  63.4 2.2 %collective-permute-start.32 = (bf16[32,2048]{1,0:T(8,128)(2,1)S(1)}, bf16[32,2048]{1,0:T(8,128)(2,1)S(1)}, u32[]{:S(2)}, u32[]{:S(2)}) collective-permute-start(bf16[32,2048]{1,0:T(8,128)(2,1)S(1)} %get-tuple-element.122.refs_2_), channel_id=1, source_target_pairs={{0,1},{1,0},{2,3},{3,2},{4,5},{5,4},{6,7},{7,6},{8,9},{9,8},{10,11... | collective-permute-start | bytes 393224 | tf_op jit(solution)/shard_map/ppermute | solution.py:27
  63.6 16.9 %collective-permute-start.39 = (bf16[64,2048]{1,0:T(8,128)(2,1)S(1)}, bf16[64,2048]{1,0:T(8,128)(2,1)S(1)}, u32[]{:S(2)}, u32[]{:S(2)}) collective-permute-start(bf16[64,2048]{1,0:T(8,128)(2,1)S(1)} %get-tuple-element.137), channel_id=1, source_target_pairs={{0,2},{1,3},{2,0},{3,1},{4,6},{5,7},{6,4},{7,5},{8,10},{9,11},{10,... | collective-permute-start | bytes 786440 | tf_op jit(solution)/shard_map/ppermute | solution.py:27
  69.0 5.6 %collective-permute-start.33 = (bf16[48,2048]{1,0:T(8,128)(2,1)S(1)}, bf16[48,2048]{1,0:T(8,128)(2,1)S(1)}, u32[]{:S(2)}, u32[]{:S(2)}) collective-permute-start(bf16[48,2048]{1,0:T(8,128)(2,1)S(1)} %get-tuple-element.128), channel_id=1, source_target_pairs={{0,1},{1,0},{2,3},{3,2},{4,5},{5,4},{6,7},{7,6},{8,9},{9,8},{10,11... | collective-permute-start | bytes 589832 | tf_op jit(solution)/shard_map/ppermute | solution.py:27
  69.2 5.5 %collective-permute-start.34 = (bf16[48,2048]{1,0:T(8,128)(2,1)S(1)}, bf16[48,2048]{1,0:T(8,128)(2,1)S(1)}, u32[]{:S(2)}, u32[]{:S(2)}) collective-permute-start(bf16[48,2048]{1,0:T(8,128)(2,1)S(1)} %get-tuple-element.129), channel_id=1, source_target_pairs={{0,1},{1,0},{2,3},{3,2},{4,5},{5,4},{6,7},{7,6},{8,9},{9,8},{10,11... | collective-permute-start | bytes 589832 | tf_op jit(solution)/shard_map/ppermute | solution.py:27
  69.6 4.5 %collective-permute-start.35 = (bf16[32,2048]{1,0:T(8,128)(2,1)S(1)}, bf16[32,2048]{1,0:T(8,128)(2,1)S(1)}, u32[]{:S(2)}, u32[]{:S(2)}) collective-permute-start(bf16[32,2048]{1,0:T(8,128)(2,1)S(1)} %get-tuple-element.130), channel_id=1, source_target_pairs={{0,1},{1,0},{2,3},{3,2},{4,5},{5,4},{6,7},{7,6},{8,9},{9,8},{10,11... | collective-permute-start | bytes 393224 | tf_op jit(solution)/shard_map/ppermute | solution.py:27
  74.0 2.8 %collective-permute-start.36 = (bf16[48,2048]{1,0:T(8,128)(2,1)S(1)}, bf16[48,2048]{1,0:T(8,128)(2,1)S(1)}, u32[]{:S(2)}, u32[]{:S(2)}) collective-permute-start(bf16[48,2048]{1,0:T(8,128)(2,1)S(1)} %get-tuple-element.132.refs_0_), channel_id=1, source_target_pairs={{0,1},{1,0},{2,3},{3,2},{4,5},{5,4},{6,7},{7,6},{8,9},{9,8},{10,11... | collective-permute-start | bytes 589832 | tf_op jit(solution)/shard_map/ppermute | solution.py:27
  74.1 2.7 %collective-permute-start.37 = (bf16[48,2048]{1,0:T(8,128)(2,1)S(1)}, bf16[48,2048]{1,0:T(8,128)(2,1)S(1)}, u32[]{:S(2)}, u32[]{:S(2)}) collective-permute-start(bf16[48,2048]{1,0:T(8,128)(2,1)S(1)} %get-tuple-element.133.refs_1_), channel_id=1, source_target_pairs={{0,1},{1,0},{2,3},{3,2},{4,5},{5,4},{6,7},{7,6},{8,9},{9,8},{10,11... | collective-permute-start | bytes 589832 | tf_op jit(solution)/shard_map/ppermute | solution.py:27
  74.6 2.2 %collective-permute-start.38 = (bf16[32,2048]{1,0:T(8,128)(2,1)S(1)}, bf16[32,2048]{1,0:T(8,128)(2,1)S(1)}, u32[]{:S(2)}, u32[]{:S(2)}) collective-permute-start(bf16[32,2048]{1,0:T(8,128)(2,1)S(1)} %get-tuple-element.134.refs_2_), channel_id=1, source_target_pairs={{0,1},{1,0},{2,3},{3,2},{4,5},{5,4},{6,7},{7,6},{8,9},{9,8},{10,11... | collective-permute-start | bytes 393224 | tf_op jit(solution)/shard_map/ppermute | solution.py:27
  74.8 6.4 %copy-start.14 = (s32[3]{0:T(128)S(1)}, s32[3]{0:T(128)}, u32[]{:S(2)}) copy-start(s32[3]{0:T(128)} %len_ref.11) | copy-start | bytes 40
  74.8 9.3 %collective-permute-start.44 = (bf16[64,2048]{1,0:T(8,128)(2,1)S(1)}, bf16[64,2048]{1,0:T(8,128)(2,1)S(1)}, u32[]{:S(2)}, u32[]{:S(2)}) collective-permute-start(bf16[64,2048]{1,0:T(8,128)(2,1)S(1)} %get-tuple-element.147), channel_id=1, source_target_pairs={{0,2},{1,3},{2,0},{3,1},{4,6},{5,7},{6,4},{7,5},{8,10},{9,11},{10,... | collective-permute-start | bytes 786440 | tf_op jit(solution)/shard_map/ppermute | solution.py:27
  80.5 2.2 %collective-permute-start.40 = (bf16[48,2048]{1,0:T(8,128)(2,1)S(1)}, bf16[48,2048]{1,0:T(8,128)(2,1)S(1)}, u32[]{:S(2)}, u32[]{:S(2)}) collective-permute-start(bf16[48,2048]{1,0:T(8,128)(2,1)S(1)} %get-tuple-element.140), channel_id=1, source_target_pairs={{0,1},{1,0},{2,3},{3,2},{4,5},{5,4},{6,7},{7,6},{8,9},{9,8},{10,11... | collective-permute-start | bytes 589832 | tf_op jit(solution)/shard_map/ppermute | solution.py:27
  80.7 2.0 %collective-permute-start.41 = (bf16[48,2048]{1,0:T(8,128)(2,1)S(1)}, bf16[48,2048]{1,0:T(8,128)(2,1)S(1)}, u32[]{:S(2)}, u32[]{:S(2)}) collective-permute-start(bf16[48,2048]{1,0:T(8,128)(2,1)S(1)} %get-tuple-element.141), channel_id=1, source_target_pairs={{0,1},{1,0},{2,3},{3,2},{4,5},{5,4},{6,7},{7,6},{8,9},{9,8},{10,11... | collective-permute-start | bytes 589832 | tf_op jit(solution)/shard_map/ppermute | solution.py:27
  81.1 1.6 %collective-permute-start.42 = (bf16[32,2048]{1,0:T(8,128)(2,1)S(1)}, bf16[32,2048]{1,0:T(8,128)(2,1)S(1)}, u32[]{:S(2)}, u32[]{:S(2)}) collective-permute-start(bf16[32,2048]{1,0:T(8,128)(2,1)S(1)} %get-tuple-element.142), channel_id=1, source_target_pairs={{0,1},{1,0},{2,3},{3,2},{4,5},{5,4},{6,7},{7,6},{8,9},{9,8},{10,11... | collective-permute-start | bytes 393224 | tf_op jit(solution)/shard_map/ppermute | solution.py:27
  82.9 8.6 %collective-permute-start.43 = (bf16[64,2048]{1,0:T(8,128)(2,1)S(1)}, bf16[64,2048]{1,0:T(8,128)(2,1)S(1)}, u32[]{:S(2)}, u32[]{:S(2)}) collective-permute-start(bf16[64,2048]{1,0:T(8,128)(2,1)S(1)} %get-tuple-element.144), channel_id=1, source_target_pairs={{0,2},{1,3},{2,0},{3,1},{4,6},{5,7},{6,4},{7,5},{8,10},{9,11},{10,... | collective-permute-start | bytes 786440 | tf_op jit(solution)/shard_map/ppermute | solution.py:27

commit v5 on v4

--- a/solution.py
+++ b/solution.py
@@ -79,11 +79,29 @@
     )(hidden, gains, left_t, right)
 
 
+def active_kernel(hidden_ref, c_ref, gains_ref, own_ref, c_out_ref):
+    for r in range(hidden_ref.shape[0]):
+        own_ref[r] = active_rows(hidden_ref[r], gains_ref[0:1, :])
+        c_out_ref[r] = active_rows(c_ref[r], gains_ref[0:1, :])
+
+
+def make_active(hidden, c, gains):
+    return pl.pallas_call(
+        active_kernel,
+        out_shape=[jax.ShapeDtypeStruct(hidden.shape, BF16)] * 2,
+        in_specs=[ON_CHIP] * 3,
+        out_specs=[ON_CHIP] * 2,
+        cost_estimate=cost(1),
+        compiler_params=params(4),
+        name="active",
+    )(hidden, c, gains)
+
+
 def project_kernel(
     reqs,
     pages_in,
     len_ref,
-    hidden_ref,
+    own_ref,
     y_ref,
     c_ref,
     d_ref,
@@ -97,7 +115,7 @@
 ):
     page_ref, q_ref, quarter_ref = refs[pages_in:]
     member = lax.axis_index("mlp")
-    part = hidden_ref.shape[1]
+    part = own_ref.shape[1]
     head = head_gains_ref.shape[-1]
     qgain, kgain = head_gains_ref[0:1, :], head_gains_ref[1:2, :]
     starts = [pl.multiple_of((member ^ flip) * part, part) for flip in BLOCK_XOR]
@@ -108,8 +126,10 @@
     for i, r in enumerate(reqs):
         rows = jnp.concatenate(
             [
-                active_rows(ref[r], gains_ref[0:1, :])
-                for ref in (hidden_ref, y_ref, c_ref, d_ref)
+                own_ref[r],
+                active_rows(y_ref[r], gains_ref[0:1, :]),
+                c_ref[r],
+                active_rows(d_ref[r], gains_ref[0:1, :]),
             ],
             axis=0,
         )
@@ -473,7 +493,8 @@
     near_odd = exchange(near_pages, "req", 1)
     own_base = make_base(after(hidden, near_pages), gains, laurel_left.T, laurel_right)
     far_pages = [direct[flip] for flip in later]
-    far_pages[0] = after(far_pages[0], own_base)
+    own_active, c_active = make_active(after(hidden, own_base), hidden_c, gains)
+    far_pages[0] = after(far_pages[0], own_active)
     far_pages = jnp.concatenate(far_pages)
     far_odd = exchange(far_pages, "req", 1)
     far_other = exchange(far_pages, "mlp", 1)
@@ -488,9 +509,9 @@
             some,
             pages,
             suffix_len,
-            after(hidden, *earlier),
+            after(own_active, *earlier),
             hidden_y,
-            hidden_c,
+            c_active,
             hidden_d,
             gains,
             query_weight,

time: 93.2 us -> 93.4 us (level)
  Pallas kernels: 40 us -> 41.2 us
  waiting for transfers between devices: 16.7 us -> 15.5 us
    ppermute x45, waiting for transfers between devices: 16.7 us -> 15.5 us  [exchange(): lax.ppermute(value, axis, [(i, i ^ flip) for i in range(lax.axis_size(axi...]
    unnamed x37 -> x33, local copies, waits for them, and re-layouts: 4.42 us -> 4.4 us
  transfers between devices with their start and end apart: 45 -> 45, of which waited for: 11 -> 11; matrix products, arithmetic and copies ran while one was open for 2% -> 2% of each run, Pallas kernels for 37% -> 38%
where the time goes in v5:
time: 93.4 us; the launch traced here: 93.1 us
  Pallas kernels  41.2 us (44%)
  starting transfers between devices  28.8 us (31%)
  waiting for transfers between devices  15.5 us (17%)
  local copies, waits for them, and re-layouts  5.26 us (6%)
  other arithmetic  1.27 us (1%)
  between operations  1.02 us (1%)
    ppermute x45, starting transfers between devices, exchange(): lax.ppermute(value, axis, [(i, i ^ flip) for i in range(lax.axis_size(axi...  28.8 us
    ppermute x45, waiting for transfers between devices, exchange(): lax.ppermute(value, axis, [(i, i ^ flip) for i in range(lax.axis_size(axi...  15.5 us
    pallas_call x3, Pallas kernels, attend(): pl.pallas_call(functools.partial(attend_kernel, req, index, offset, rows,...  13.1 us
    pallas_call x3, Pallas kernels, feed(): pl.pallas_call(functools.partial(feed_kernel, len(pieces)), out_shape=par...  10.5 us
    pallas_call x3, Pallas kernels, project(): pl.pallas_call(functools.partial(project_kernel, reqs, len(extra)), grid=...  7.18 us
    pallas_call x3, Pallas kernels, finish(): pl.pallas_call(functools.partial(finish_kernel, req), grid=(1,), out_shap...  4.44 us
    unnamed x33, local copies, waits for them, and re-layouts  4.4 us
    pallas_call x2, Pallas kernels, make_base(): pl.pallas_call(base_kernel, out_shape=jax.ShapeDtypeStruct(hidden.shape,...  2.73 us
  transfers between devices with their start and end apart: 45, of which 11 were waited for; matrix products, arithmetic and copies ran while one was open for 2% of the time, Pallas kernels for 38%

profile of v5, /device:TPU:0, one launch (start us, length us, event | category | flops | bytes accessed | tf_op | source)
XLA Modules:
  0.0 93.1 jit_solution(12036895831975964703)
XLA Ops:
  0.6 0.5 collective-permute-start
  1.2 2.6 %collective-permute-start.2 = (bf16[3,64,2048]{2,1,0:T(8,128)(2,1)}, bf16[3,64,2048]{2,1,0:T(8,128)(2,1)S(1)}, u32[]{:S(2)}, u32[]{:S(2)}) collective-permute-start(bf16[3,64,2048]{2,1,0:T(8,128)(2,1)} %bitcast.12), channel_id=1, source_target_pairs={{0,2},{1,3},{2,0},{3,1},{4,6},{5,7},{6,4},{7,5},{8,10},{9,11},{10,... | collective-permute-start | bytes 2359304 | tf_op jit(solution)/shard_map/ppermute | solution.py:27
  3.8 2.5 %collective-permute-start.1 = (bf16[1,128,512]{2,1,0:T(8,128)(2,1)S(1)}, bf16[1,128,512]{2,1,0:T(8,128)(2,1)S(1)}, u32[]{:S(2)}, u32[]{:S(2)}) collective-permute-start(bf16[1,128,512]{2,1,0:T(8,128)(2,1)S(1)} %constant_dynamic-slice_fusion), channel_id=1, source_target_pairs={{0,8},{4,12},{8,0},{12,4},{16,24},{20,28},{24,16},{28,20},{1,9},{5... | collective-permute-start | bytes 393224 | tf_op jit(solution)/shard_map/ppermute | solution.py:27
  6.3 0.5 multiply_sine_fusion
  6.8 2.7 %collective-permute-start.3 = (bf16[1,128,512]{2,1,0:T(8,128)(2,1)S(1)}, bf16[1,128,512]{2,1,0:T(8,128)(2,1)S(1)}, u32[]{:S(2)}, u32[]{:S(2)}) collective-permute-start(bf16[1,128,512]{2,1,0:T(8,128)(2,1)S(1)} %constant_dynamic-slice_fusion), channel_id=1, source_target_pairs={{0,16},{4,20},{8,24},{12,28},{16,0},{20,4},{24,8},{28,12},{1,17},{... | collective-permute-start | bytes 393224 | tf_op jit(solution)/shard_map/ppermute | solution.py:27
  9.5 0.7 pad_maximum_fusion.1.head_gains_ref
  10.2 0.8 stack.32.gains_ref
  11.2 1.8 %collective-permute-start.7 = (bf16[2,128,512]{2,1,0:T(8,128)(2,1)S(1)}, bf16[2,128,512]{2,1,0:T(8,128)(2,1)S(1)}, u32[]{:S(2)}, u32[]{:S(2)}) collective-permute-start(bf16[2,128,512]{2,1,0:T(8,128)(2,1)S(1)} %pad_maximum_fusion.refs_0_), channel_id=1, source_target_pairs={{0,4},{4,0},{8,12},{12,8},{16,20},{20,16},{24,28},{28,24},{1,5},{5... | collective-permute-start | bytes 786440 | tf_op jit(solution)/shard_map/ppermute | solution.py:27
  12.9 1.1 %copy-done.7 = bf16[64,3,2048]{2,0,1:T(8,128)(2,1)S(1)} copy-done((bf16[64,3,2048]{2,0,1:T(8,128)(2,1)S(1)}, bf16[64,3,2048]{2,0,1:T(8,128)(2,1)}, u32[]{:S(2)}) %copy-start.7) | copy-done | bytes 786456
  14.0 0.9 %copy-done.8 = bf16[2048,64]{0,1:T(8,128)(2,1)S(1)} copy-done((bf16[2048,64]{0,1:T(8,128)(2,1)S(1)}, bf16[2048,64]{0,1:T(8,128)(2,1)}, u32[]{:S(2)}) %copy-start.8) | copy-done | bytes 262168
  15.0 0.9 %copy-done.10 = bf16[64,2048]{1,0:T(8,128)(2,1)S(1)} copy-done((bf16[64,2048]{1,0:T(8,128)(2,1)S(1)}, bf16[64,2048]{1,0:T(8,128)(2,1)}, u32[]{:S(2)}) %copy-start.10) | copy-done | bytes 262168
  15.9 1.4 %base.2.own_base_ref = f32[3,64,2048]{2,1,0:T(8,128)S(1)} custom-call(bf16[3,64,2048]{2,1,0:T(8,128)(2,1)S(1)} %bitcast.13, f32[5,2048]{1,0:T(8,128)S(1)} %stack.32.gains_ref, bf16[64,2048]{1,0:T(8,128)(2,1)S(1)} %bitcast.15, bf16[64,2048]{1,0:T(8,128)(2,1)S(1)} %copy-done.10), custom_call_target="tpu_custom_call" | custom-call | flops 1 | bytes 1 | tf_op jit(solution)/shard_map/base/pallas_call | solution.py:71
  17.3 0.6 active.1
  18.0 1.4 %collective-permute-done.3 = bf16[1,128,512]{2,1,0:T(8,128)(2,1)S(1)} collective-permute-done((bf16[1,128,512]{2,1,0:T(8,128)(2,1)S(1)}, bf16[1,128,512]{2,1,0:T(8,128)(2,1)S(1)}, u32[]{:S(2)}, u32[]{:S(2)}) %collective-permute-start.3) | collective-permute-done | bytes 131104 | tf_op jit(solution)/shard_map/ppermute | solution.py:27
  19.4 1.6 %collective-permute-start.8 = (bf16[2,128,512]{2,1,0:T(8,128)(2,1)S(1)}, bf16[2,128,512]{2,1,0:T(8,128)(2,1)S(1)}, u32[]{:S(2)}, u32[]{:S(2)}) collective-permute-start(bf16[2,128,512]{2,1,0:T(8,128)(2,1)S(1)} %constant_dynamic-update-slice_fusion.refs_1_), channel_id=1, source_target_pairs={{0,4},{4,0},{8,12},{12,8},{16,20},{20,16},{24,28},{28,24},{1,5},{5... | collective-permute-start | bytes 786440 | tf_op jit(solution)/shard_map/ppermute | solution.py:27
  21.0 1.1 %collective-permute-done.2.hidden_ref.y_ref = bf16[3,64,2048]{2,1,0:T(8,128)(2,1)S(1)} collective-permute-done((bf16[3,64,2048]{2,1,0:T(8,128)(2,1)}, bf16[3,64,2048]{2,1,0:T(8,128)(2,1)S(1)}, u32[]{:S(2)}, u32[]{:S(2)}) %collective-permute-start.2) | collective-permute-done | bytes 786464 | tf_op jit(solution)/shard_map/ppermute | solution.py:27
  22.1 1.4 %base.3.y_base_ref = f32[3,64,2048]{2,1,0:T(8,128)S(1)} custom-call(bf16[3,64,2048]{2,1,0:T(8,128)(2,1)S(1)} %collective-permute-done.2.hidden_ref.y_ref, f32[5,2048]{1,0:T(8,128)S(1)} %stack.32.gains_ref, bf16[64,2048]{1,0:T(8,128)(2,1)S(1)} %bitcast.16, bf16[64,2048]{1,0:T(8,128)(2,1)S(1)} %copy-done.11), custom_call_target="tpu_custom_call" | custom-call | flops 99999997952 | bytes 1 | tf_op jit(solution)/shard_map/base/pallas_call | solution.py:71
  23.5 0.6 collective-permute-start.10
  24.1 0.3 collective-permute-done.5.d_ref
  24.4 2.4 %project.3 = (bf16[3,256,256]{2,1,0:T(8,128)(2,1)}, bf16[1,512,256]{2,1,0:T(8,128)(2,1)S(1)}, bf16[1,256,256]{2,1,0:T(8,128)(2,1)S(1)}) custom-call(s32[3]{0:T(128)S(1)} %copy-done.12, bf16[3,64,2048]{2,1,0:T(8,128)(2,1)S(1)} %get-tuple-element.99.own_ref, bf16[3,64,2048]{2,1,0:T(8,128)(2,1)S(1)} %collective-permute-done.2.hidden_ref.y_ref, ...), custom_call_target="tpu_custom_call" | custom-call | flops 1 | bytes 1 | tf_op jit(solution)/shard_map/project/pallas_call | solution.py:162
  27.0 0.3 collective-permute-start.11
  27.5 2.4 %project.4 = (bf16[3,256,256]{2,1,0:T(8,128)(2,1)}, bf16[1,512,256]{2,1,0:T(8,128)(2,1)S(1)}, bf16[1,256,256]{2,1,0:T(8,128)(2,1)S(1)}) custom-call(s32[3]{0:T(128)S(1)} %copy-done.12, bf16[3,64,2048]{2,1,0:T(8,128)(2,1)S(1)} %get-tuple-element.99.own_ref, ...), custom_call_target="tpu_custom_call", output_to_operand_aliasing={{0}: (11, {})} | custom-call | flops 1 | bytes 1 | tf_op jit(solution)/shard_map/project/pallas_call | solution.py:162
  30.0 4.3 %attend.3 = (bf16[128,2048]{1,0:T(8,128)(2,1)S(1)}, bf16[64,2048]{1,0:T(8,128)(2,1)S(1)}, bf16[64,2048]{1,0:T(8,128)(2,1)S(1)}) custom-call(s32[3]{0:T(128)S(1)} %copy-done.15, s32[2,8]{1,0:T(2,128)S(1)} %copy-done.13, s32[2,8]{1,0:T(2,128)S(1)} %copy-done.14, bf16[1,512,256]{2,1,0:T(8,128)(2,1)S(1)} %get-tuple-element.92.q_ref, ...), custom_call_target="tpu_custom_call" | custom-call | flops 1 | bytes 1 | tf_op jit(solution)/shard_map/attend/pallas_call | solution.py:319
  34.3 0.5 collective-permute-start.13
  34.9 1.0 %collective-permute-done.13.refs_0_ = bf16[64,2048]{1,0:T(8,128)(2,1)S(1)} collective-permute-done((bf16[64,2048]{1,0:T(8,128)(2,1)S(1)}, bf16[64,2048]{1,0:T(8,128)(2,1)S(1)}, u32[]{:S(2)}, u32[]{:S(2)}) %collective-permute-start.13) | collective-permute-done | bytes 262176 | tf_op jit(solution)/shard_map/ppermute | solution.py:27
  35.9 0.4 collective-permute-done.14.refs_1_
  36.4 1.8 %collective-permute-start.19 = (bf16[128,2048]{1,0:T(8,128)(2,1)S(1)}, bf16[128,2048]{1,0:T(8,128)(2,1)S(1)}, u32[]{:S(2)}, u32[]{:S(2)}) collective-permute-start(bf16[128,2048]{1,0:T(8,128)(2,1)S(1)} %pair_sum.6.refs_0_), channel_id=1, source_target_pairs={{0,2},{1,3},{2,0},{3,1},{4,6},{5,7},{6,4},{7,5},{8,10},{9,11},{10,... | collective-permute-start | bytes 1572872 | tf_op jit(solution)/shard_map/ppermute | solution.py:27
  38.3 2.4 %project.5 = (bf16[3,256,256]{2,1,0:T(8,128)(2,1)}, bf16[1,512,256]{2,1,0:T(8,128)(2,1)S(1)}, bf16[1,256,256]{2,1,0:T(8,128)(2,1)S(1)}) custom-call(s32[3]{0:T(128)S(1)} %copy-done.12, bf16[3,64,2048]{2,1,0:T(8,128)(2,1)S(1)} %get-tuple-element.99.own_ref, ...), custom_call_target="tpu_custom_call", output_to_operand_aliasing={{0}: (11, {})} | custom-call | flops 1 | bytes 1 | tf_op jit(solution)/shard_map/project/pallas_call | solution.py:162
  40.7 4.5 %attend.4 = (bf16[128,2048]{1,0:T(8,128)(2,1)S(1)}, bf16[64,2048]{1,0:T(8,128)(2,1)S(1)}, bf16[64,2048]{1,0:T(8,128)(2,1)S(1)}) custom-call(s32[3]{0:T(128)S(1)} %copy-done.15, s32[2,8]{1,0:T(2,128)S(1)} %copy-done.13, s32[2,8]{1,0:T(2,128)S(1)} %copy-done.14, bf16[1,512,256]{2,1,0:T(8,128)(2,1)S(1)} %get-tuple-element.102.q_ref, ...), custom_call_target="tpu_custom_call" | custom-call | flops 1 | bytes 1 | tf_op jit(solution)/shard_map/attend/pallas_call | solution.py:319
  45.2 0.6 collective-permute-start.16
  45.9 0.4 collective-permute-start.18
  46.3 0.7 collective-permute-done.16.refs_0_
  47.0 0.4 collective-permute-done.17.refs_1_
  47.5 0.4 collective-permute-start.23
  47.8 4.3 %attend.5 = (bf16[128,2048]{1,0:T(8,128)(2,1)S(1)}, bf16[64,2048]{1,0:T(8,128)(2,1)S(1)}, bf16[64,2048]{1,0:T(8,128)(2,1)S(1)}) custom-call(s32[3]{0:T(128)S(1)} %copy-done.15, s32[2,8]{1,0:T(2,128)S(1)} %copy-done.13, s32[2,8]{1,0:T(2,128)S(1)} %copy-done.14, bf16[1,512,256]{2,1,0:T(8,128)(2,1)S(1)} %get-tuple-element.107.q_ref, ...), custom_call_target="tpu_custom_call" | custom-call | flops 1 | bytes 1 | tf_op jit(solution)/shard_map/attend/pallas_call | solution.py:319
  52.1 0.3 collective-permute-start.20
  52.4 0.3 collective-permute-start.21
  52.7 0.6 residual.3
  53.4 0.3 collective-permute-start.24
  53.6 0.3 collective-permute-start.25
  54.3 1.8 %collective-permute-start.22 = (bf16[128,2048]{1,0:T(8,128)(2,1)S(1)}, bf16[128,2048]{1,0:T(8,128)(2,1)S(1)}, u32[]{:S(2)}, u32[]{:S(2)}) collective-permute-start(bf16[128,2048]{1,0:T(8,128)(2,1)S(1)} %pair_sum.8.refs_0_), channel_id=1, source_target_pairs={{0,2},{1,3},{2,0},{3,1},{4,6},{5,7},{6,4},{7,5},{8,10},{9,11},{10,... | collective-permute-start | bytes 1572872 | tf_op jit(solution)/shard_map/ppermute | solution.py:27
  56.2 1.2 %copy-done.3 = bf16[1024,2048]{1,0:T(8,128)(2,1)S(1)} copy-done((bf16[1024,2048]{1,0:T(8,128)(2,1)S(1)}, bf16[1024,2048]{1,0:T(8,128)(2,1)}, u32[]{:S(2)}) %copy-start.3) | copy-done | bytes 4194328
  57.4 3.4 %feed.3 = (bf16[128,2048]{1,0:T(8,128)(2,1)S(1)}, bf16[48,2048]{1,0:T(8,128)(2,1)S(1)}, bf16[48,2048]{1,0:T(8,128)(2,1)S(1)}, bf16[32,2048]{1,0:T(8,128)(2,1)S(1)}) custom-call(bf16[2048,1024]{1,0:T(8,128)(2,1)S(1)} %copy-done.1, bf16[2048,1024]{1,0:T(8,128)(2,1)S(1)} %copy-done.2, bf16[1024,2048]{1,0:T(8,128)(2,1)S(1)} %copy-done.3, ...), custom_call_target="tpu_custom_call" | custom-call | flops 1 | bytes 1 | tf_op jit(solution)/shard_map/feed/pallas_call | solution.py:409
  60.8 0.2 collective-permute-start.27
  61.1 0.3 collective-permute-start.28
  61.6 0.7 collective-permute-done.23.refs_1_
  62.3 0.6 residual.4
  63.0 0.5 collective-permute-start.31
  63.7 2.0 %collective-permute-start.39 = (bf16[64,2048]{1,0:T(8,128)(2,1)S(1)}, bf16[64,2048]{1,0:T(8,128)(2,1)S(1)}, u32[]{:S(2)}, u32[]{:S(2)}) collective-permute-start(bf16[64,2048]{1,0:T(8,128)(2,1)S(1)} %get-tuple-element.143), channel_id=1, source_target_pairs={{0,2},{1,3},{2,0},{3,1},{4,6},{5,7},{6,4},{7,5},{8,10},{9,11},{10,... | collective-permute-start | bytes 786440 | tf_op jit(solution)/shard_map/ppermute | solution.py:27
  65.7 3.4 %feed.4 = (bf16[128,2048]{1,0:T(8,128)(2,1)S(1)}, bf16[48,2048]{1,0:T(8,128)(2,1)S(1)}, bf16[48,2048]{1,0:T(8,128)(2,1)S(1)}, bf16[32,2048]{1,0:T(8,128)(2,1)S(1)}) custom-call(bf16[2048,1024]{1,0:T(8,128)(2,1)S(1)} %copy-done.1, bf16[2048,1024]{1,0:T(8,128)(2,1)S(1)} %copy-done.2, bf16[1024,2048]{1,0:T(8,128)(2,1)S(1)} %copy-done.3, ...), custom_call_target="tpu_custom_call" | custom-call | flops 1 | bytes 1 | tf_op jit(solution)/shard_map/feed/pallas_call | solution.py:409
  69.2 0.2 collective-permute-start.33
  69.4 0.3 collective-permute-start.34
  69.9 3.6 %collective-permute-done.22.refs_1_ = bf16[128,2048]{1,0:T(8,128)(2,1)S(1)} collective-permute-done((bf16[128,2048]{1,0:T(8,128)(2,1)S(1)}, bf16[128,2048]{1,0:T(8,128)(2,1)S(1)}, u32[]{:S(2)}, u32[]{:S(2)}) %collective-permute-start.22) | collective-permute-done | bytes 524320 | tf_op jit(solution)/shard_map/ppermute | solution.py:27
  73.5 0.6 residual.5
  74.2 0.5 collective-permute-start.37
  74.9 2.0 %collective-permute-start.44 = (bf16[64,2048]{1,0:T(8,128)(2,1)S(1)}, bf16[64,2048]{1,0:T(8,128)(2,1)S(1)}, u32[]{:S(2)}, u32[]{:S(2)}) collective-permute-start(bf16[64,2048]{1,0:T(8,128)(2,1)S(1)} %get-tuple-element.153), channel_id=1, source_target_pairs={{0,2},{1,3},{2,0},{3,1},{4,6},{5,7},{6,4},{7,5},{8,10},{9,11},{10,... | collective-permute-start | bytes 786440 | tf_op jit(solution)/shard_map/ppermute | solution.py:27
  77.0 3.7 %feed.5 = (bf16[128,2048]{1,0:T(8,128)(2,1)S(1)}, bf16[48,2048]{1,0:T(8,128)(2,1)S(1)}, bf16[48,2048]{1,0:T(8,128)(2,1)S(1)}, bf16[32,2048]{1,0:T(8,128)(2,1)S(1)}) custom-call(bf16[2048,1024]{1,0:T(8,128)(2,1)S(1)} %copy-done.1, bf16[2048,1024]{1,0:T(8,128)(2,1)S(1)} %copy-done.2, bf16[1024,2048]{1,0:T(8,128)(2,1)S(1)} %copy-done.3, ...), custom_call_target="tpu_custom_call" | custom-call | flops 1 | bytes 1 | tf_op jit(solution)/shard_map/feed/pallas_call | solution.py:409
  80.7 0.2 collective-permute-start.40
  80.9 0.3 collective-permute-start.41
  81.4 1.5 %finish.3.refs_0_ = bf16[3,64,2048]{2,1,0:T(8,128)(2,1)} custom-call(s32[3]{0:T(128)S(1)} %copy-done.12, f32[64,2048]{1,0:T(8,128)S(1)} %get-tuple-element.142.res_ref, bf16[64,2048]{1,0:T(8,128)(2,1)S(1)} %get-tuple-element.125.near_ref, bf16[64,2048]{1,0:T(8,128)(2,1)S(1)} %collective-permute-done.39.far_ref, f32[5,2048]{1,0:T(8,128)S(1)} %stack.32.gains_ref), custom_call_target="tpu_custom_call" | custom-call | flops 99999997952 | bytes 1 | tf_op jit(solution)/shard_map/finish/pallas_call | solution.py:433
  83.0 1.2 %collective-permute-start.43 = (bf16[64,2048]{1,0:T(8,128)(2,1)S(1)}, bf16[64,2048]{1,0:T(8,128)(2,1)S(1)}, u32[]{:S(2)}, u32[]{:S(2)}) collective-permute-start(bf16[64,2048]{1,0:T(8,128)(2,1)S(1)} %get-tuple-element.150), channel_id=1, source_target_pairs={{0,2},{1,3},{2,0},{3,1},{4,6},{5,7},{6,4},{7,5},{8,10},{9,11},{10,... | collective-permute-start | bytes 786440 | tf_op jit(solution)/shard_map/ppermute | solution.py:27
  84.4 1.5 %finish.4.refs_0_ = bf16[3,64,2048]{2,1,0:T(8,128)(2,1)} custom-call(s32[3]{0:T(128)S(1)} %copy-done.12, f32[64,2048]{1,0:T(8,128)S(1)} %get-tuple-element.152.res_ref, bf16[64,2048]{1,0:T(8,128)(2,1)S(1)} %get-tuple-element.137.near_ref, bf16[64,2048]{1,0:T(8,128)(2,1)S(1)} %collective-permute-done.44.far_ref, ...), custom_call_target="tpu_custom_call", output_to_operand_aliasing={{}: (5, {})} | custom-call | flops 1 | bytes 1 | tf_op jit(solution)/shard_map/finish/pallas_call | solution.py:433
  85.9 5.7 %collective-permute-done.43.far_ref = bf16[64,2048]{1,0:T(8,128)(2,1)S(1)} collective-permute-done((bf16[64,2048]{1,0:T(8,128)(2,1)S(1)}, bf16[64,2048]{1,0:T(8,128)(2,1)S(1)}, u32[]{:S(2)}, u32[]{:S(2)}) %collective-permute-start.43) | collective-permute-done | bytes 262176 | tf_op jit(solution)/shard_map/ppermute | solution.py:27
  91.6 1.5 %finish.5 = bf16[3,64,2048]{2,1,0:T(8,128)(2,1)} custom-call(s32[3]{0:T(128)S(1)} %copy-done.12, f32[64,2048]{1,0:T(8,128)S(1)} %get-tuple-element.131.res_ref, bf16[64,2048]{1,0:T(8,128)(2,1)S(1)} %get-tuple-element.149.near_ref, bf16[64,2048]{1,0:T(8,128)(2,1)S(1)} %collective-permute-done.43.far_ref, ...), custom_call_target="tpu_custom_call", output_to_operand_aliasing={{}: (5, {})} | custom-call | flops 1 | bytes 1 | tf_op jit(solution)/shard_map/finish/pallas_call | solution.py:433
  (91 shorter events, 3.1 us)
Async XLA Ops:
  0.6 3.2 %copy-start = (bf16[2,128,1024]{2,1,0:T(8,128)(2,1)S(1)}, bf16[2,128,1024]{2,1,0:T(8,128)(2,1)}, u32[]{:S(2)}) copy-start(bf16[2,128,1024]{2,1,0:T(8,128)(2,1)} %param.37) | copy-start | bytes 1572868
  0.6 3.1 %collective-permute-start = (bf16[3,64,2048]{2,1,0:T(8,128)(2,1)}, bf16[3,64,2048]{2,1,0:T(8,128)(2,1)S(1)}, u32[]{:S(2)}, u32[]{:S(2)}) collective-permute-start(bf16[3,64,2048]{2,1,0:T(8,128)(2,1)} %bitcast.11), channel_id=1, source_target_pairs={{0,1},{1,0},{2,3},{3,2},{4,5},{5,4},{6,7},{7,6},{8,9},{9,8},{10,11... | collective-permute-start | bytes 2359304 | tf_op jit(solution)/shard_map/ppermute | solution.py:27
  1.2 20.9 %collective-permute-start.2 = (bf16[3,64,2048]{2,1,0:T(8,128)(2,1)}, bf16[3,64,2048]{2,1,0:T(8,128)(2,1)S(1)}, u32[]{:S(2)}, u32[]{:S(2)}) collective-permute-start(bf16[3,64,2048]{2,1,0:T(8,128)(2,1)} %bitcast.12), channel_id=1, source_target_pairs={{0,2},{1,3},{2,0},{3,1},{4,6},{5,7},{6,4},{7,5},{8,10},{9,11},{10,... | collective-permute-start | bytes 2359304 | tf_op jit(solution)/shard_map/ppermute | solution.py:27
  3.8 7.3 %collective-permute-start.1 = (bf16[1,128,512]{2,1,0:T(8,128)(2,1)S(1)}, bf16[1,128,512]{2,1,0:T(8,128)(2,1)S(1)}, u32[]{:S(2)}, u32[]{:S(2)}) collective-permute-start(bf16[1,128,512]{2,1,0:T(8,128)(2,1)S(1)} %constant_dynamic-slice_fusion), channel_id=1, source_target_pairs={{0,8},{4,12},{8,0},{12,4},{16,24},{20,28},{24,16},{28,20},{1,9},{5... | collective-permute-start | bytes 393224 | tf_op jit(solution)/shard_map/ppermute | solution.py:27
  6.8 12.5 %collective-permute-start.3 = (bf16[1,128,512]{2,1,0:T(8,128)(2,1)S(1)}, bf16[1,128,512]{2,1,0:T(8,128)(2,1)S(1)}, u32[]{:S(2)}, u32[]{:S(2)}) collective-permute-start(bf16[1,128,512]{2,1,0:T(8,128)(2,1)S(1)} %constant_dynamic-slice_fusion), channel_id=1, source_target_pairs={{0,16},{4,20},{8,24},{12,28},{16,0},{20,4},{24,8},{28,12},{1,17},{... | collective-permute-start | bytes 393224 | tf_op jit(solution)/shard_map/ppermute | solution.py:27
  11.0 8.3 %collective-permute-start.4 = (bf16[1,128,512]{2,1,0:T(8,128)(2,1)S(1)}, bf16[1,128,512]{2,1,0:T(8,128)(2,1)S(1)}, u32[]{:S(2)}, u32[]{:S(2)}) collective-permute-start(bf16[1,128,512]{2,1,0:T(8,128)(2,1)S(1)} %constant_dynamic-slice_fusion), channel_id=1, source_target_pairs={{0,24},{4,28},{8,16},{12,20},{16,8},{20,12},{24,0},{28,4},{1,25},{... | collective-permute-start | bytes 393224 | tf_op jit(solution)/shard_map/ppermute | solution.py:27
  11.2 15.8 %collective-permute-start.7 = (bf16[2,128,512]{2,1,0:T(8,128)(2,1)S(1)}, bf16[2,128,512]{2,1,0:T(8,128)(2,1)S(1)}, u32[]{:S(2)}, u32[]{:S(2)}) collective-permute-start(bf16[2,128,512]{2,1,0:T(8,128)(2,1)S(1)} %pad_maximum_fusion.refs_0_), channel_id=1, source_target_pairs={{0,4},{4,0},{8,12},{12,8},{16,20},{20,16},{24,28},{28,24},{1,5},{5... | collective-permute-start | bytes 786440 | tf_op jit(solution)/shard_map/ppermute | solution.py:27
  12.9 1.1 %copy-start.7 = (bf16[64,3,2048]{2,0,1:T(8,128)(2,1)S(1)}, bf16[64,3,2048]{2,0,1:T(8,128)(2,1)}, u32[]{:S(2)}) copy-start(bf16[64,3,2048]{2,0,1:T(8,128)(2,1)} %param.21) | copy-start | bytes 2359300
  14.0 0.9 %copy-start.8 = (bf16[2048,64]{0,1:T(8,128)(2,1)S(1)}, bf16[2048,64]{0,1:T(8,128)(2,1)}, u32[]{:S(2)}) copy-start(bf16[2048,64]{0,1:T(8,128)(2,1)} %param.29) | copy-start | bytes 786436
  15.0 0.9 %copy-start.10 = (bf16[64,2048]{1,0:T(8,128)(2,1)S(1)}, bf16[64,2048]{1,0:T(8,128)(2,1)}, u32[]{:S(2)}) copy-start(bf16[64,2048]{1,0:T(8,128)(2,1)} %right_ref.3) | copy-start | bytes 786436
  15.9 6.2 %copy-start.9 = (bf16[2048,64]{0,1:T(8,128)(2,1)S(1)}, bf16[2048,64]{0,1:T(8,128)(2,1)}, u32[]{:S(2)}) copy-start(bf16[2048,64]{0,1:T(8,128)(2,1)} %param.29) | copy-start | bytes 786436
  15.9 6.2 %copy-start.11 = (bf16[64,2048]{1,0:T(8,128)(2,1)S(1)}, bf16[64,2048]{1,0:T(8,128)(2,1)}, u32[]{:S(2)}) copy-start(bf16[64,2048]{1,0:T(8,128)(2,1)} %right_ref.3) | copy-start | bytes 786436
  19.4 5.0 %copy-start.5 = (bf16[2048,512]{1,0:T(8,128)(2,1)S(1)}, bf16[2048,512]{1,0:T(8,128)(2,1)}, u32[]{:S(2)}) copy-start(bf16[2048,512]{1,0:T(8,128)(2,1)} %wq_ref.5) | copy-start | bytes 6291460
  19.4 5.0 %copy-start.6 = (bf16[2048,256]{1,0:T(8,128)(2,1)S(1)}, bf16[2048,256]{1,0:T(8,128)(2,1)}, u32[]{:S(2)}) copy-start(bf16[2048,256]{1,0:T(8,128)(2,1)} %wkv_ref.5) | copy-start | bytes 3145732
  19.4 5.0 %copy-start.12 = (s32[3]{0:T(128)S(1)}, s32[3]{0:T(128)}, u32[]{:S(2)}) copy-start(s32[3]{0:T(128)} %len_ref.11) | copy-start | bytes 40
  19.4 7.4 %collective-permute-start.8 = (bf16[2,128,512]{2,1,0:T(8,128)(2,1)S(1)}, bf16[2,128,512]{2,1,0:T(8,128)(2,1)S(1)}, u32[]{:S(2)}, u32[]{:S(2)}) collective-permute-start(bf16[2,128,512]{2,1,0:T(8,128)(2,1)S(1)} %constant_dynamic-update-slice_fusion.refs_1_), channel_id=1, source_target_pairs={{0,4},{4,0},{8,12},{12,8},{16,20},{20,16},{24,28},{28,24},{1,5},{5... | collective-permute-start | bytes 786440 | tf_op jit(solution)/shard_map/ppermute | solution.py:27
  22.1 2.3 %collective-permute-start.5 = (bf16[3,64,2048]{2,1,0:T(8,128)(2,1)S(1)}, bf16[3,64,2048]{2,1,0:T(8,128)(2,1)S(1)}, u32[]{:S(2)}, u32[]{:S(2)}) collective-permute-start(bf16[3,64,2048]{2,1,0:T(8,128)(2,1)S(1)} %collective-permute-done.2.hidden_ref.y_ref), channel_id=1, source_target_pairs={{0,1},{1,0},{2,3},{3,2},{4,5},{5,4},{6,7},{7,6},{8,9},{9,8},{10,11... | collective-permute-start | bytes 2359304 | tf_op jit(solution)/shard_map/ppermute | solution.py:27
  23.5 6.4 %collective-permute-start.10 = (bf16[2,128,512]{2,1,0:T(8,128)(2,1)S(1)}, bf16[2,128,512]{2,1,0:T(8,128)(2,1)S(1)}, u32[]{:S(2)}, u32[]{:S(2)}) collective-permute-start(bf16[2,128,512]{2,1,0:T(8,128)(2,1)S(1)} %constant_dynamic-update-slice_fusion.refs_1_), channel_id=1, source_target_pairs={{0,1},{1,0},{2,3},{3,2},{4,5},{5,4},{6,7},{7,6},{8,9},{9,8},{10,11... | collective-permute-start | bytes 786440 | tf_op jit(solution)/shard_map/ppermute | solution.py:27
  24.1 5.9 %collective-permute-start.9 = (bf16[2,128,512]{2,1,0:T(8,128)(2,1)S(1)}, bf16[2,128,512]{2,1,0:T(8,128)(2,1)S(1)}, u32[]{:S(2)}, u32[]{:S(2)}) collective-permute-start(bf16[2,128,512]{2,1,0:T(8,128)(2,1)S(1)} %pad_maximum_fusion.refs_0_), channel_id=1, source_target_pairs={{0,1},{1,0},{2,3},{3,2},{4,5},{5,4},{6,7},{7,6},{8,9},{9,8},{10,11... | collective-permute-start | bytes 786440 | tf_op jit(solution)/shard_map/ppermute | solution.py:27
  26.8 3.1 %collective-permute-start.12 = (bf16[2,128,512]{2,1,0:T(8,128)(2,1)S(1)}, bf16[2,128,512]{2,1,0:T(8,128)(2,1)S(1)}, u32[]{:S(2)}, u32[]{:S(2)}) collective-permute-start(bf16[2,128,512]{2,1,0:T(8,128)(2,1)S(1)} %collective-permute-done.8.refs_3_), channel_id=1, source_target_pairs={{0,1},{1,0},{2,3},{3,2},{4,5},{5,4},{6,7},{7,6},{8,9},{9,8},{10,11... | collective-permute-start | bytes 786440 | tf_op jit(solution)/shard_map/ppermute | solution.py:27
  27.0 2.9 %collective-permute-start.11 = (bf16[2,128,512]{2,1,0:T(8,128)(2,1)S(1)}, bf16[2,128,512]{2,1,0:T(8,128)(2,1)S(1)}, u32[]{:S(2)}, u32[]{:S(2)}) collective-permute-start(bf16[2,128,512]{2,1,0:T(8,128)(2,1)S(1)} %collective-permute-done.7.refs_2_), channel_id=1, source_target_pairs={{0,1},{1,0},{2,3},{3,2},{4,5},{5,4},{6,7},{7,6},{8,9},{9,8},{10,11... | collective-permute-start | bytes 786440 | tf_op jit(solution)/shard_map/ppermute | solution.py:27
  27.3 2.6 %collective-permute-start.6 = (bf16[1,256,256]{2,1,0:T(8,128)(2,1)S(1)}, bf16[1,256,256]{2,1,0:T(8,128)(2,1)S(1)}, u32[]{:S(2)}, u32[]{:S(2)}) collective-permute-start(bf16[1,256,256]{2,1,0:T(8,128)(2,1)S(1)} %get-tuple-element.93.mine_ref), channel_id=1, source_target_pairs={{0,1},{1,0},{2,3},{3,2},{4,5},{5,4},{6,7},{7,6},{8,9},{9,8},{10,11... | collective-permute-start | bytes 393224 | tf_op jit(solution)/shard_map/ppermute | solution.py:27
  27.5 2.4 %copy-start.4 = (bf16[512,2048]{1,0:T(8,128)(2,1)S(1)}, bf16[512,2048]{1,0:T(8,128)(2,1)}, u32[]{:S(2)}) copy-start(bf16[512,2048]{1,0:T(8,128)(2,1)} %wo_ref.5) | copy-start | bytes 6291460
  27.5 2.5 %copy-start.13 = (s32[2,8]{1,0:T(2,128)S(1)}, s32[2,8]{1,0:T(2,128)}, u32[]{:S(2)}) copy-start(s32[2,8]{1,0:T(2,128)} %owner_ref.5) | copy-start | bytes 196
  27.5 2.5 %copy-start.14 = (s32[2,8]{1,0:T(2,128)S(1)}, s32[2,8]{1,0:T(2,128)}, u32[]{:S(2)}) copy-start(s32[2,8]{1,0:T(2,128)} %slot_ref.5) | copy-start | bytes 196
  27.5 2.5 %copy-start.15 = (s32[3]{0:T(128)S(1)}, s32[3]{0:T(128)}, u32[]{:S(2)}) copy-start(s32[3]{0:T(128)} %group_ref.5) | copy-start | bytes 40
  34.3 1.6 %collective-permute-start.13 = (bf16[64,2048]{1,0:T(8,128)(2,1)S(1)}, bf16[64,2048]{1,0:T(8,128)(2,1)S(1)}, u32[]{:S(2)}, u32[]{:S(2)}) collective-permute-start(bf16[64,2048]{1,0:T(8,128)(2,1)S(1)} %get-tuple-element.97), channel_id=1, source_target_pairs={{0,1},{1,0},{2,3},{3,2},{4,5},{5,4},{6,7},{7,6},{8,9},{9,8},{10,11... | collective-permute-start | bytes 786440 | tf_op jit(solution)/shard_map/ppermute | solution.py:27
  34.8 1.5 %collective-permute-start.14 = (bf16[64,2048]{1,0:T(8,128)(2,1)S(1)}, bf16[64,2048]{1,0:T(8,128)(2,1)S(1)}, u32[]{:S(2)}, u32[]{:S(2)}) collective-permute-start(bf16[64,2048]{1,0:T(8,128)(2,1)S(1)} %get-tuple-element.98), channel_id=1, source_target_pairs={{0,1},{1,0},{2,3},{3,2},{4,5},{5,4},{6,7},{7,6},{8,9},{9,8},{10,11... | collective-permute-start | bytes 786440 | tf_op jit(solution)/shard_map/ppermute | solution.py:27
  36.4 16.3 %collective-permute-start.19 = (bf16[128,2048]{1,0:T(8,128)(2,1)S(1)}, bf16[128,2048]{1,0:T(8,128)(2,1)S(1)}, u32[]{:S(2)}, u32[]{:S(2)}) collective-permute-start(bf16[128,2048]{1,0:T(8,128)(2,1)S(1)} %pair_sum.6.refs_0_), channel_id=1, source_target_pairs={{0,2},{1,3},{2,0},{3,1},{4,6},{5,7},{6,4},{7,5},{8,10},{9,11},{10,... | collective-permute-start | bytes 1572872 | tf_op jit(solution)/shard_map/ppermute | solution.py:27
  38.3 2.5 %collective-permute-start.15 = (bf16[1,256,256]{2,1,0:T(8,128)(2,1)S(1)}, bf16[1,256,256]{2,1,0:T(8,128)(2,1)S(1)}, u32[]{:S(2)}, u32[]{:S(2)}) collective-permute-start(bf16[1,256,256]{2,1,0:T(8,128)(2,1)S(1)} %get-tuple-element.103.mine_ref), channel_id=1, source_target_pairs={{0,1},{1,0},{2,3},{3,2},{4,5},{5,4},{6,7},{7,6},{8,9},{9,8},{10,11... | collective-permute-start | bytes 393224 | tf_op jit(solution)/shard_map/ppermute | solution.py:27
  45.2 1.7 %collective-permute-start.16 = (bf16[64,2048]{1,0:T(8,128)(2,1)S(1)}, bf16[64,2048]{1,0:T(8,128)(2,1)S(1)}, u32[]{:S(2)}, u32[]{:S(2)}) collective-permute-start(bf16[64,2048]{1,0:T(8,128)(2,1)S(1)} %get-tuple-element.105), channel_id=1, source_target_pairs={{0,1},{1,0},{2,3},{3,2},{4,5},{5,4},{6,7},{7,6},{8,9},{9,8},{10,11... | collective-permute-start | bytes 786440 | tf_op jit(solution)/shard_map/ppermute | solution.py:27
  45.8 1.5 %collective-permute-start.17 = (bf16[64,2048]{1,0:T(8,128)(2,1)S(1)}, bf16[64,2048]{1,0:T(8,128)(2,1)S(1)}, u32[]{:S(2)}, u32[]{:S(2)}) collective-permute-start(bf16[64,2048]{1,0:T(8,128)(2,1)S(1)} %get-tuple-element.106), channel_id=1, source_target_pairs={{0,1},{1,0},{2,3},{3,2},{4,5},{5,4},{6,7},{7,6},{8,9},{9,8},{10,11... | collective-permute-start | bytes 786440 | tf_op jit(solution)/shard_map/ppermute | solution.py:27
  45.9 2.0 %collective-permute-start.18 = (bf16[1,256,256]{2,1,0:T(8,128)(2,1)S(1)}, bf16[1,256,256]{2,1,0:T(8,128)(2,1)S(1)}, u32[]{:S(2)}, u32[]{:S(2)}) collective-permute-start(bf16[1,256,256]{2,1,0:T(8,128)(2,1)S(1)} %get-tuple-element.108.mine_ref), channel_id=1, source_target_pairs={{0,1},{1,0},{2,3},{3,2},{4,5},{5,4},{6,7},{7,6},{8,9},{9,8},{10,11... | collective-permute-start | bytes 393224 | tf_op jit(solution)/shard_map/ppermute | solution.py:27
  47.5 14.8 %collective-permute-start.23 = (bf16[128,2048]{1,0:T(8,128)(2,1)S(1)}, bf16[128,2048]{1,0:T(8,128)(2,1)S(1)}, u32[]{:S(2)}, u32[]{:S(2)}) collective-permute-start(bf16[128,2048]{1,0:T(8,128)(2,1)S(1)} %pair_sum.7.refs_0_), channel_id=1, source_target_pairs={{0,2},{1,3},{2,0},{3,1},{4,6},{5,7},{6,4},{7,5},{8,10},{9,11},{10,... | collective-permute-start | bytes 1572872 | tf_op jit(solution)/shard_map/ppermute | solution.py:27
  52.1 1.8 %collective-permute-start.20 = (bf16[64,2048]{1,0:T(8,128)(2,1)S(1)}, bf16[64,2048]{1,0:T(8,128)(2,1)S(1)}, u32[]{:S(2)}, u32[]{:S(2)}) collective-permute-start(bf16[64,2048]{1,0:T(8,128)(2,1)S(1)} %get-tuple-element.113), channel_id=1, source_target_pairs={{0,1},{1,0},{2,3},{3,2},{4,5},{5,4},{6,7},{7,6},{8,9},{9,8},{10,11... | collective-permute-start | bytes 786440 | tf_op jit(solution)/shard_map/ppermute | solution.py:27
  52.4 1.7 %collective-permute-start.21 = (bf16[64,2048]{1,0:T(8,128)(2,1)S(1)}, bf16[64,2048]{1,0:T(8,128)(2,1)S(1)}, u32[]{:S(2)}, u32[]{:S(2)}) collective-permute-start(bf16[64,2048]{1,0:T(8,128)(2,1)S(1)} %get-tuple-element.114), channel_id=1, source_target_pairs={{0,1},{1,0},{2,3},{3,2},{4,5},{5,4},{6,7},{7,6},{8,9},{9,8},{10,11... | collective-permute-start | bytes 786440 | tf_op jit(solution)/shard_map/ppermute | solution.py:27
  52.7 3.4 %copy-start.1 = (bf16[2048,1024]{1,0:T(8,128)(2,1)S(1)}, bf16[2048,1024]{1,0:T(8,128)(2,1)}, u32[]{:S(2)}) copy-start(bf16[2048,1024]{1,0:T(8,128)(2,1)} %gate_ref.5) | copy-start | bytes 12582916
  52.7 3.5 %copy-start.2 = (bf16[2048,1024]{1,0:T(8,128)(2,1)S(1)}, bf16[2048,1024]{1,0:T(8,128)(2,1)}, u32[]{:S(2)}) copy-start(bf16[2048,1024]{1,0:T(8,128)(2,1)} %up_ref.5) | copy-start | bytes 12582916
  52.7 4.7 %copy-start.3 = (bf16[1024,2048]{1,0:T(8,128)(2,1)S(1)}, bf16[1024,2048]{1,0:T(8,128)(2,1)}, u32[]{:S(2)}) copy-start(bf16[1024,2048]{1,0:T(8,128)(2,1)} %down_ref.5) | copy-start | bytes 12582916
  53.4 2.7 %collective-permute-start.24 = (bf16[48,2048]{1,0:T(8,128)(2,1)S(1)}, bf16[48,2048]{1,0:T(8,128)(2,1)S(1)}, u32[]{:S(2)}, u32[]{:S(2)}) collective-permute-start(bf16[48,2048]{1,0:T(8,128)(2,1)S(1)} %get-tuple-element.115.refs_0_), channel_id=1, source_target_pairs={{0,1},{1,0},{2,3},{3,2},{4,5},{5,4},{6,7},{7,6},{8,9},{9,8},{10,11... | collective-permute-start | bytes 589832 | tf_op jit(solution)/shard_map/ppermute | solution.py:27
  53.6 2.5 %collective-permute-start.25 = (bf16[48,2048]{1,0:T(8,128)(2,1)S(1)}, bf16[48,2048]{1,0:T(8,128)(2,1)S(1)}, u32[]{:S(2)}, u32[]{:S(2)}) collective-permute-start(bf16[48,2048]{1,0:T(8,128)(2,1)S(1)} %get-tuple-element.116.refs_1_), channel_id=1, source_target_pairs={{0,1},{1,0},{2,3},{3,2},{4,5},{5,4},{6,7},{7,6},{8,9},{9,8},{10,11... | collective-permute-start | bytes 589832 | tf_op jit(solution)/shard_map/ppermute | solution.py:27
  53.9 2.1 %collective-permute-start.26 = (bf16[32,2048]{1,0:T(8,128)(2,1)S(1)}, bf16[32,2048]{1,0:T(8,128)(2,1)S(1)}, u32[]{:S(2)}, u32[]{:S(2)}) collective-permute-start(bf16[32,2048]{1,0:T(8,128)(2,1)S(1)} %get-tuple-element.117.refs_2_), channel_id=1, source_target_pairs={{0,1},{1,0},{2,3},{3,2},{4,5},{5,4},{6,7},{7,6},{8,9},{9,8},{10,11... | collective-permute-start | bytes 393224 | tf_op jit(solution)/shard_map/ppermute | solution.py:27
  54.3 19.3 %collective-permute-start.22 = (bf16[128,2048]{1,0:T(8,128)(2,1)S(1)}, bf16[128,2048]{1,0:T(8,128)(2,1)S(1)}, u32[]{:S(2)}, u32[]{:S(2)}) collective-permute-start(bf16[128,2048]{1,0:T(8,128)(2,1)S(1)} %pair_sum.8.refs_0_), channel_id=1, source_target_pairs={{0,2},{1,3},{2,0},{3,1},{4,6},{5,7},{6,4},{7,5},{8,10},{9,11},{10,... | collective-permute-start | bytes 1572872 | tf_op jit(solution)/shard_map/ppermute | solution.py:27
  60.8 2.7 %collective-permute-start.27 = (bf16[48,2048]{1,0:T(8,128)(2,1)S(1)}, bf16[48,2048]{1,0:T(8,128)(2,1)S(1)}, u32[]{:S(2)}, u32[]{:S(2)}) collective-permute-start(bf16[48,2048]{1,0:T(8,128)(2,1)S(1)} %get-tuple-element.122), channel_id=1, source_target_pairs={{0,1},{1,0},{2,3},{3,2},{4,5},{5,4},{6,7},{7,6},{8,9},{9,8},{10,11... | collective-permute-start | bytes 589832 | tf_op jit(solution)/shard_map/ppermute | solution.py:27
  61.1 2.5 %collective-permute-start.28 = (bf16[48,2048]{1,0:T(8,128)(2,1)S(1)}, bf16[48,2048]{1,0:T(8,128)(2,1)S(1)}, u32[]{:S(2)}, u32[]{:S(2)}) collective-permute-start(bf16[48,2048]{1,0:T(8,128)(2,1)S(1)} %get-tuple-element.123), channel_id=1, source_target_pairs={{0,1},{1,0},{2,3},{3,2},{4,5},{5,4},{6,7},{7,6},{8,9},{9,8},{10,11... | collective-permute-start | bytes 589832 | tf_op jit(solution)/shard_map/ppermute | solution.py:27
  61.4 1.6 %collective-permute-start.29 = (bf16[32,2048]{1,0:T(8,128)(2,1)S(1)}, bf16[32,2048]{1,0:T(8,128)(2,1)S(1)}, u32[]{:S(2)}, u32[]{:S(2)}) collective-permute-start(bf16[32,2048]{1,0:T(8,128)(2,1)S(1)} %get-tuple-element.124), channel_id=1, source_target_pairs={{0,1},{1,0},{2,3},{3,2},{4,5},{5,4},{6,7},{7,6},{8,9},{9,8},{10,11... | collective-permute-start | bytes 393224 | tf_op jit(solution)/shard_map/ppermute | solution.py:27
  62.9 2.8 %collective-permute-start.30 = (bf16[48,2048]{1,0:T(8,128)(2,1)S(1)}, bf16[48,2048]{1,0:T(8,128)(2,1)S(1)}, u32[]{:S(2)}, u32[]{:S(2)}) collective-permute-start(bf16[48,2048]{1,0:T(8,128)(2,1)S(1)} %get-tuple-element.126.refs_0_), channel_id=1, source_target_pairs={{0,1},{1,0},{2,3},{3,2},{4,5},{5,4},{6,7},{7,6},{8,9},{9,8},{10,11... | collective-permute-start | bytes 589832 | tf_op jit(solution)/shard_map/ppermute | solution.py:27
  63.0 2.7 %collective-permute-start.31 = (bf16[48,2048]{1,0:T(8,128)(2,1)S(1)}, bf16[48,2048]{1,0:T(8,128)(2,1)S(1)}, u32[]{:S(2)}, u32[]{:S(2)}) collective-permute-start(bf16[48,2048]{1,0:T(8,128)(2,1)S(1)} %get-tuple-element.127.refs_1_), channel_id=1, source_target_pairs={{0,1},{1,0},{2,3},{3,2},{4,5},{5,4},{6,7},{7,6},{8,9},{9,8},{10,11... | collective-permute-start | bytes 589832 | tf_op jit(solution)/shard_map/ppermute | solution.py:27
  63.5 2.2 %collective-permute-start.32 = (bf16[32,2048]{1,0:T(8,128)(2,1)S(1)}, bf16[32,2048]{1,0:T(8,128)(2,1)S(1)}, u32[]{:S(2)}, u32[]{:S(2)}) collective-permute-start(bf16[32,2048]{1,0:T(8,128)(2,1)S(1)} %get-tuple-element.128.refs_2_), channel_id=1, source_target_pairs={{0,1},{1,0},{2,3},{3,2},{4,5},{5,4},{6,7},{7,6},{8,9},{9,8},{10,11... | collective-permute-start | bytes 393224 | tf_op jit(solution)/shard_map/ppermute | solution.py:27
  63.7 16.9 %collective-permute-start.39 = (bf16[64,2048]{1,0:T(8,128)(2,1)S(1)}, bf16[64,2048]{1,0:T(8,128)(2,1)S(1)}, u32[]{:S(2)}, u32[]{:S(2)}) collective-permute-start(bf16[64,2048]{1,0:T(8,128)(2,1)S(1)} %get-tuple-element.143), channel_id=1, source_target_pairs={{0,2},{1,3},{2,0},{3,1},{4,6},{5,7},{6,4},{7,5},{8,10},{9,11},{10,... | collective-permute-start | bytes 786440 | tf_op jit(solution)/shard_map/ppermute | solution.py:27
  69.2 5.6 %collective-permute-start.33 = (bf16[48,2048]{1,0:T(8,128)(2,1)S(1)}, bf16[48,2048]{1,0:T(8,128)(2,1)S(1)}, u32[]{:S(2)}, u32[]{:S(2)}) collective-permute-start(bf16[48,2048]{1,0:T(8,128)(2,1)S(1)} %get-tuple-element.134), channel_id=1, source_target_pairs={{0,1},{1,0},{2,3},{3,2},{4,5},{5,4},{6,7},{7,6},{8,9},{9,8},{10,11... | collective-permute-start | bytes 589832 | tf_op jit(solution)/shard_map/ppermute | solution.py:27
  69.4 5.4 %collective-permute-start.34 = (bf16[48,2048]{1,0:T(8,128)(2,1)S(1)}, bf16[48,2048]{1,0:T(8,128)(2,1)S(1)}, u32[]{:S(2)}, u32[]{:S(2)}) collective-permute-start(bf16[48,2048]{1,0:T(8,128)(2,1)S(1)} %get-tuple-element.135), channel_id=1, source_target_pairs={{0,1},{1,0},{2,3},{3,2},{4,5},{5,4},{6,7},{7,6},{8,9},{9,8},{10,11... | collective-permute-start | bytes 589832 | tf_op jit(solution)/shard_map/ppermute | solution.py:27
  69.8 4.5 %collective-permute-start.35 = (bf16[32,2048]{1,0:T(8,128)(2,1)S(1)}, bf16[32,2048]{1,0:T(8,128)(2,1)S(1)}, u32[]{:S(2)}, u32[]{:S(2)}) collective-permute-start(bf16[32,2048]{1,0:T(8,128)(2,1)S(1)} %get-tuple-element.136), channel_id=1, source_target_pairs={{0,1},{1,0},{2,3},{3,2},{4,5},{5,4},{6,7},{7,6},{8,9},{9,8},{10,11... | collective-permute-start | bytes 393224 | tf_op jit(solution)/shard_map/ppermute | solution.py:27
  74.1 2.8 %collective-permute-start.36 = (bf16[48,2048]{1,0:T(8,128)(2,1)S(1)}, bf16[48,2048]{1,0:T(8,128)(2,1)S(1)}, u32[]{:S(2)}, u32[]{:S(2)}) collective-permute-start(bf16[48,2048]{1,0:T(8,128)(2,1)S(1)} %get-tuple-element.138.refs_0_), channel_id=1, source_target_pairs={{0,1},{1,0},{2,3},{3,2},{4,5},{5,4},{6,7},{7,6},{8,9},{9,8},{10,11... | collective-permute-start | bytes 589832 | tf_op jit(solution)/shard_map/ppermute | solution.py:27
  74.2 2.7 %collective-permute-start.37 = (bf16[48,2048]{1,0:T(8,128)(2,1)S(1)}, bf16[48,2048]{1,0:T(8,128)(2,1)S(1)}, u32[]{:S(2)}, u32[]{:S(2)}) collective-permute-start(bf16[48,2048]{1,0:T(8,128)(2,1)S(1)} %get-tuple-element.139.refs_1_), channel_id=1, source_target_pairs={{0,1},{1,0},{2,3},{3,2},{4,5},{5,4},{6,7},{7,6},{8,9},{9,8},{10,11... | collective-permute-start | bytes 589832 | tf_op jit(solution)/shard_map/ppermute | solution.py:27
  74.7 2.2 %collective-permute-start.38 = (bf16[32,2048]{1,0:T(8,128)(2,1)S(1)}, bf16[32,2048]{1,0:T(8,128)(2,1)S(1)}, u32[]{:S(2)}, u32[]{:S(2)}) collective-permute-start(bf16[32,2048]{1,0:T(8,128)(2,1)S(1)} %get-tuple-element.140.refs_2_), channel_id=1, source_target_pairs={{0,1},{1,0},{2,3},{3,2},{4,5},{5,4},{6,7},{7,6},{8,9},{9,8},{10,11... | collective-permute-start | bytes 393224 | tf_op jit(solution)/shard_map/ppermute | solution.py:27
  74.9 9.5 %collective-permute-start.44 = (bf16[64,2048]{1,0:T(8,128)(2,1)S(1)}, bf16[64,2048]{1,0:T(8,128)(2,1)S(1)}, u32[]{:S(2)}, u32[]{:S(2)}) collective-permute-start(bf16[64,2048]{1,0:T(8,128)(2,1)S(1)} %get-tuple-element.153), channel_id=1, source_target_pairs={{0,2},{1,3},{2,0},{3,1},{4,6},{5,7},{6,4},{7,5},{8,10},{9,11},{10,... | collective-permute-start | bytes 786440 | tf_op jit(solution)/shard_map/ppermute | solution.py:27
  80.7 2.2 %collective-permute-start.40 = (bf16[48,2048]{1,0:T(8,128)(2,1)S(1)}, bf16[48,2048]{1,0:T(8,128)(2,1)S(1)}, u32[]{:S(2)}, u32[]{:S(2)}) collective-permute-start(bf16[48,2048]{1,0:T(8,128)(2,1)S(1)} %get-tuple-element.146), channel_id=1, source_target_pairs={{0,1},{1,0},{2,3},{3,2},{4,5},{5,4},{6,7},{7,6},{8,9},{9,8},{10,11... | collective-permute-start | bytes 589832 | tf_op jit(solution)/shard_map/ppermute | solution.py:27
  80.9 2.0 %collective-permute-start.41 = (bf16[48,2048]{1,0:T(8,128)(2,1)S(1)}, bf16[48,2048]{1,0:T(8,128)(2,1)S(1)}, u32[]{:S(2)}, u32[]{:S(2)}) collective-permute-start(bf16[48,2048]{1,0:T(8,128)(2,1)S(1)} %get-tuple-element.147), channel_id=1, source_target_pairs={{0,1},{1,0},{2,3},{3,2},{4,5},{5,4},{6,7},{7,6},{8,9},{9,8},{10,11... | collective-permute-start | bytes 589832 | tf_op jit(solution)/shard_map/ppermute | solution.py:27
  81.2 1.6 %collective-permute-start.42 = (bf16[32,2048]{1,0:T(8,128)(2,1)S(1)}, bf16[32,2048]{1,0:T(8,128)(2,1)S(1)}, u32[]{:S(2)}, u32[]{:S(2)}) collective-permute-start(bf16[32,2048]{1,0:T(8,128)(2,1)S(1)} %get-tuple-element.148), channel_id=1, source_target_pairs={{0,1},{1,0},{2,3},{3,2},{4,5},{5,4},{6,7},{7,6},{8,9},{9,8},{10,11... | collective-permute-start | bytes 393224 | tf_op jit(solution)/shard_map/ppermute | solution.py:27
  83.0 8.6 %collective-permute-start.43 = (bf16[64,2048]{1,0:T(8,128)(2,1)S(1)}, bf16[64,2048]{1,0:T(8,128)(2,1)S(1)}, u32[]{:S(2)}, u32[]{:S(2)}) collective-permute-start(bf16[64,2048]{1,0:T(8,128)(2,1)S(1)} %get-tuple-element.150), channel_id=1, source_target_pairs={{0,2},{1,3},{2,0},{3,1},{4,6},{5,7},{6,4},{7,5},{8,10},{9,11},{10,... | collective-permute-start | bytes 786440 | tf_op jit(solution)/shard_map/ppermute | solution.py:27

commit v6 on v4

--- a/solution.py
+++ b/solution.py
@@ -16,6 +16,7 @@
 SCALARS = pl.BlockSpec(memory_space=pltpu.SMEM)
 ANYWHERE = pl.BlockSpec(memory_space=pl.ANY)
 BLOCK_XOR = (0, 2, 1, 3)
+AFTER_FIRST_ATTEND = (8,)
 AFTER_ATTEND = (4, 4)
 AFTER_FEED = (3, 3, 2)
 BEFORE_FEED = (3, 3, 2)
@@ -291,6 +292,7 @@
 
 
 def attend(req, index, offset, rows, sources, group, owner, slot, q, mine, other, wo, pools):
+    pieces = AFTER_ATTEND if req else AFTER_FIRST_ATTEND
     count, head = mine.shape[1:]
     heads = q.shape[1] // count
     page = pools[0].shape[1]
@@ -298,9 +300,9 @@
     keys = n_pages * page + count
     return pl.pallas_call(
         functools.partial(attend_kernel, req, index, offset, rows, sources),
-        out_shape=partial_shapes(rows, wo.shape[1], AFTER_ATTEND),
+        out_shape=partial_shapes(rows, wo.shape[1], pieces),
         in_specs=[SCALARS] * 3 + [ON_CHIP] * 4 + [ANYWHERE] * len(pools),
-        out_specs=[ON_CHIP] * (1 + len(AFTER_ATTEND)),
+        out_specs=[ON_CHIP] * (1 + len(pieces)),
         scratch_shapes=[
             pltpu.VMEM((keys, 2 * head), BF16),
             pltpu.VMEM((len(BLOCK_XOR) * rows, heads * head), BF16),
@@ -399,12 +401,27 @@
 
 
 def finish_kernel(req, len_ref, res_ref, near_ref, far_ref, gains_ref, *refs):
-    out_ref = refs[-1]
+    out_ref, rows_ref, sems = refs[-3:]
     part = res_ref.shape[0]
-    total = near_ref[...].astype(F32) + far_ref[...].astype(F32)
-    output = res_ref[...] + normed(total, gains_ref[4:5, :])
-    position = lax.axis_index("mlp") * part + lax.broadcasted_iota(jnp.int32, (part, 1), 0)
-    out_ref[0] = jnp.where(position < len_ref[req], output, 0.0).astype(BF16)
+    steps = sems.shape[0]
+    rows = part // steps
+    copies = []
+    for i in range(steps):
+        here = slice(i * rows, (i + 1) * rows)
+        total = near_ref[here, :].astype(F32) + far_ref[here, :].astype(F32)
+        output = res_ref[here, :] + normed(total, gains_ref[4:5, :])
+        position = (
+            lax.axis_index("mlp") * part
+            + i * rows
+            + lax.broadcasted_iota(jnp.int32, (rows, 1), 0)
+        )
+        rows_ref[here, :] = jnp.where(position < len_ref[req], output, 0.0).astype(BF16)
+        copies.append(
+            pltpu.make_async_copy(rows_ref.at[here, :], out_ref.at[req, here, :], sems.at[i])
+        )
+        copies[-1].start()
+    for copy in copies:
+        copy.wait()
 
 
 def finish(req, reqs, lens, residual, near, far, gains, before):
@@ -412,11 +429,11 @@
     extra = [] if before is None else [before]
     return pl.pallas_call(
         functools.partial(finish_kernel, req),
-        grid=(1,),
         out_shape=jax.ShapeDtypeStruct((reqs, part, width), BF16),
         in_specs=[SCALARS] + [ON_CHIP] * 4 + [ANYWHERE] * len(extra),
-        out_specs=pl.BlockSpec((1, part, width), lambda i: (req, 0, 0)),
+        out_specs=ANYWHERE,
         input_output_aliases={5: 0} if extra else {},
+        scratch_shapes=[pltpu.VMEM((part, width), BF16), pltpu.SemaphoreType.DMA((4,))],
         cost_estimate=cost(1e11 if req == 0 else 1),
         compiler_params=params(4),
         name="finish",

time: 93.2 us -> 93.4 us (level)
    ppermute x45 -> x44, waiting for transfers between devices: 16.7 us -> 17.2 us  [exchange(): lax.ppermute(value, axis, [(i, i ^ flip) for i in range(lax.axis_size(axi...]
    ppermute x45 -> x44, starting transfers between devices: 28.7 us -> 28.2 us  [exchange(): lax.ppermute(value, axis, [(i, i ^ flip) for i in range(lax.axis_size(axi...]
  transfers between devices with their start and end apart: 45 -> 44, of which waited for: 11 -> 11; matrix products, arithmetic and copies ran while one was open for 2% -> 2% of each run, Pallas kernels for 37% -> 37%
where the time goes in v6:
time: 93.4 us; the launch traced here: 93 us
  Pallas kernels  39.9 us (43%)
  starting transfers between devices  28.2 us (30%)
  waiting for transfers between devices  17.2 us (18%)
  local copies, waits for them, and re-layouts  5.27 us (6%)
  other arithmetic  1.27 us (1%)
  between operations  1.26 us (1%)
    ppermute x44, starting transfers between devices, exchange(): lax.ppermute(value, axis, [(i, i ^ flip) for i in range(lax.axis_size(axi...  28.2 us
    ppermute x44, waiting for transfers between devices, exchange(): lax.ppermute(value, axis, [(i, i ^ flip) for i in range(lax.axis_size(axi...  17.2 us
    pallas_call x3, Pallas kernels, attend(): pl.pallas_call(functools.partial(attend_kernel, req, index, offset, rows,...  13.2 us
    pallas_call x3, Pallas kernels, feed(): pl.pallas_call(functools.partial(feed_kernel, len(pieces)), out_shape=par...  10.5 us
    pallas_call x3, Pallas kernels, project(): pl.pallas_call(functools.partial(project_kernel, reqs, len(extra)), grid=...  6.62 us
    unnamed x37, local copies, waits for them, and re-layouts  4.41 us
    pallas_call x3, Pallas kernels, finish(): pl.pallas_call(functools.partial(finish_kernel, req), out_shape=jax.Shape...  4.24 us
    pallas_call x2, Pallas kernels, make_base(): pl.pallas_call(base_kernel, out_shape=jax.ShapeDtypeStruct(hidden.shape,...  2.73 us
  transfers between devices with their start and end apart: 44, of which 11 were waited for; matrix products, arithmetic and copies ran while one was open for 2% of the time, Pallas kernels for 37%

profile of v6, /device:TPU:0, one launch (start us, length us, event | category | flops | bytes accessed | tf_op | source)
XLA Modules:
  0.0 93.0 jit_solution(8531430565323815105)
XLA Ops:
  0.6 0.5 collective-permute-start
  1.2 2.6 %collective-permute-start.2 = (bf16[3,64,2048]{2,1,0:T(8,128)(2,1)}, bf16[3,64,2048]{2,1,0:T(8,128)(2,1)S(1)}, u32[]{:S(2)}, u32[]{:S(2)}) collective-permute-start(bf16[3,64,2048]{2,1,0:T(8,128)(2,1)} %bitcast.12), channel_id=1, source_target_pairs={{0,2},{1,3},{2,0},{3,1},{4,6},{5,7},{6,4},{7,5},{8,10},{9,11},{10,... | collective-permute-start | bytes 2359304 | tf_op jit(solution)/shard_map/ppermute | solution.py:28
  3.8 2.5 %collective-permute-start.1 = (bf16[1,128,512]{2,1,0:T(8,128)(2,1)S(1)}, bf16[1,128,512]{2,1,0:T(8,128)(2,1)S(1)}, u32[]{:S(2)}, u32[]{:S(2)}) collective-permute-start(bf16[1,128,512]{2,1,0:T(8,128)(2,1)S(1)} %constant_dynamic-slice_fusion), channel_id=1, source_target_pairs={{0,8},{4,12},{8,0},{12,4},{16,24},{20,28},{24,16},{28,20},{1,9},{5... | collective-permute-start | bytes 393224 | tf_op jit(solution)/shard_map/ppermute | solution.py:28
  6.3 0.5 multiply_sine_fusion
  6.9 2.7 %collective-permute-start.3 = (bf16[1,128,512]{2,1,0:T(8,128)(2,1)S(1)}, bf16[1,128,512]{2,1,0:T(8,128)(2,1)S(1)}, u32[]{:S(2)}, u32[]{:S(2)}) collective-permute-start(bf16[1,128,512]{2,1,0:T(8,128)(2,1)S(1)} %constant_dynamic-slice_fusion), channel_id=1, source_target_pairs={{0,16},{4,20},{8,24},{12,28},{16,0},{20,4},{24,8},{28,12},{1,17},{... | collective-permute-start | bytes 393224 | tf_op jit(solution)/shard_map/ppermute | solution.py:28
  9.5 0.7 pad_maximum_fusion.1.head_gains_ref
  10.2 0.8 stack.32.gains_ref
  11.2 1.8 %collective-permute-start.7 = (bf16[2,128,512]{2,1,0:T(8,128)(2,1)S(1)}, bf16[2,128,512]{2,1,0:T(8,128)(2,1)S(1)}, u32[]{:S(2)}, u32[]{:S(2)}) collective-permute-start(bf16[2,128,512]{2,1,0:T(8,128)(2,1)S(1)} %pad_maximum_fusion.refs_0_), channel_id=1, source_target_pairs={{0,4},{4,0},{8,12},{12,8},{16,20},{20,16},{24,28},{28,24},{1,5},{5... | collective-permute-start | bytes 786440 | tf_op jit(solution)/shard_map/ppermute | solution.py:28
  12.9 1.1 %copy-done.6 = bf16[64,3,2048]{2,0,1:T(8,128)(2,1)S(1)} copy-done((bf16[64,3,2048]{2,0,1:T(8,128)(2,1)S(1)}, bf16[64,3,2048]{2,0,1:T(8,128)(2,1)}, u32[]{:S(2)}) %copy-start.6) | copy-done | bytes 786456
  14.1 0.9 %copy-done.9 = bf16[2048,64]{0,1:T(8,128)(2,1)S(1)} copy-done((bf16[2048,64]{0,1:T(8,128)(2,1)S(1)}, bf16[2048,64]{0,1:T(8,128)(2,1)}, u32[]{:S(2)}) %copy-start.9) | copy-done | bytes 262168
  15.0 0.9 %copy-done.11 = bf16[64,2048]{1,0:T(8,128)(2,1)S(1)} copy-done((bf16[64,2048]{1,0:T(8,128)(2,1)S(1)}, bf16[64,2048]{1,0:T(8,128)(2,1)}, u32[]{:S(2)}) %copy-start.11) | copy-done | bytes 262168
  16.0 1.4 %base.2.own_base_ref = f32[3,64,2048]{2,1,0:T(8,128)S(1)} custom-call(bf16[3,64,2048]{2,1,0:T(8,128)(2,1)S(1)} %bitcast.13, f32[5,2048]{1,0:T(8,128)S(1)} %stack.32.gains_ref, bf16[64,2048]{1,0:T(8,128)(2,1)S(1)} %bitcast.17, bf16[64,2048]{1,0:T(8,128)(2,1)S(1)} %copy-done.11), custom_call_target="tpu_custom_call" | custom-call | flops 1 | bytes 1 | tf_op jit(solution)/shard_map/base/pallas_call | solution.py:72
  17.3 2.0 %collective-permute-done.3 = bf16[1,128,512]{2,1,0:T(8,128)(2,1)S(1)} collective-permute-done((bf16[1,128,512]{2,1,0:T(8,128)(2,1)S(1)}, bf16[1,128,512]{2,1,0:T(8,128)(2,1)S(1)}, u32[]{:S(2)}, u32[]{:S(2)}) %collective-permute-start.3) | collective-permute-done | bytes 131104 | tf_op jit(solution)/shard_map/ppermute | solution.py:28
  19.5 1.6 %collective-permute-start.8 = (bf16[2,128,512]{2,1,0:T(8,128)(2,1)S(1)}, bf16[2,128,512]{2,1,0:T(8,128)(2,1)S(1)}, u32[]{:S(2)}, u32[]{:S(2)}) collective-permute-start(bf16[2,128,512]{2,1,0:T(8,128)(2,1)S(1)} %constant_dynamic-update-slice_fusion.refs_1_), channel_id=1, source_target_pairs={{0,4},{4,0},{8,12},{12,8},{16,20},{20,16},{24,28},{28,24},{1,5},{5... | collective-permute-start | bytes 786440 | tf_op jit(solution)/shard_map/ppermute | solution.py:28
  21.0 1.1 %collective-permute-done.2.hidden_ref.y_ref = bf16[3,64,2048]{2,1,0:T(8,128)(2,1)S(1)} collective-permute-done((bf16[3,64,2048]{2,1,0:T(8,128)(2,1)}, bf16[3,64,2048]{2,1,0:T(8,128)(2,1)S(1)}, u32[]{:S(2)}, u32[]{:S(2)}) %collective-permute-start.2) | collective-permute-done | bytes 786464 | tf_op jit(solution)/shard_map/ppermute | solution.py:28
  22.1 1.4 %base.3.y_base_ref = f32[3,64,2048]{2,1,0:T(8,128)S(1)} custom-call(bf16[3,64,2048]{2,1,0:T(8,128)(2,1)S(1)} %collective-permute-done.2.hidden_ref.y_ref, f32[5,2048]{1,0:T(8,128)S(1)} %stack.32.gains_ref, bf16[64,2048]{1,0:T(8,128)(2,1)S(1)} %bitcast.18, bf16[64,2048]{1,0:T(8,128)(2,1)S(1)} %copy-done.12), custom_call_target="tpu_custom_call" | custom-call | flops 99999997952 | bytes 1 | tf_op jit(solution)/shard_map/base/pallas_call | solution.py:72
  23.5 0.6 collective-permute-start.9
  24.1 0.3 collective-permute-done.5.d_ref
  24.4 2.5 %project.3 = (bf16[3,256,256]{2,1,0:T(8,128)(2,1)}, bf16[1,512,256]{2,1,0:T(8,128)(2,1)S(1)}, bf16[1,256,256]{2,1,0:T(8,128)(2,1)S(1)}) custom-call(s32[3]{0:T(128)S(1)} %copy-done.13, bf16[3,64,2048]{2,1,0:T(8,128)(2,1)S(1)} %bitcast.14, bf16[3,64,2048]{2,1,0:T(8,128)(2,1)S(1)} %collective-permute-done.2.hidden_ref.y_ref, ...), custom_call_target="tpu_custom_call" | custom-call | flops 1 | bytes 1 | tf_op jit(solution)/shard_map/project/pallas_call | solution.py:143
  27.0 0.2 collective-permute-start.11
  27.1 0.3 collective-permute-start.12
  27.5 0.2 collective-permute-start.6
  27.7 2.0 %project.4 = (bf16[3,256,256]{2,1,0:T(8,128)(2,1)}, bf16[1,512,256]{2,1,0:T(8,128)(2,1)S(1)}, bf16[1,256,256]{2,1,0:T(8,128)(2,1)S(1)}) custom-call(s32[3]{0:T(128)S(1)} %copy-done.13, bf16[3,64,2048]{2,1,0:T(8,128)(2,1)S(1)} %bitcast.15, bf16[3,64,2048]{2,1,0:T(8,128)(2,1)S(1)} %collective-permute-done.2.hidden_ref.y_ref, ...), custom_call_target="tpu_custom_call", output_to_operand_aliasing={{0}: (11, {})} | custom-call | flops 1 | bytes 1 | tf_op jit(solution)/shard_map/project/pallas_call | solution.py:143
  29.8 4.3 %attend.3 = (bf16[128,2048]{1,0:T(8,128)(2,1)S(1)}, bf16[128,2048]{1,0:T(8,128)(2,1)S(1)}) custom-call(s32[3]{0:T(128)S(1)} %copy-done.17, s32[2,8]{1,0:T(2,128)S(1)} %copy-done.15, s32[2,8]{1,0:T(2,128)S(1)} %copy-done.16, bf16[1,512,256]{2,1,0:T(8,128)(2,1)S(1)} %get-tuple-element.85.q_ref, bf16[1,256,256]{2,1,0:T(8,128)(2,1)S(1)} %get-tuple-element.86.mine_ref, ...), custom_call_target="tpu_custom_call" | custom-call | flops 1 | bytes 1 | tf_op jit(solution)/shard_map/attend/pallas_call | solution.py:301
  34.1 0.5 collective-permute-start.13
  34.6 1.5 %collective-permute-done.13.refs_0_ = bf16[128,2048]{1,0:T(8,128)(2,1)S(1)} collective-permute-done((bf16[128,2048]{1,0:T(8,128)(2,1)S(1)}, bf16[128,2048]{1,0:T(8,128)(2,1)S(1)}, u32[]{:S(2)}, u32[]{:S(2)}) %collective-permute-start.13) | collective-permute-done | bytes 524320 | tf_op jit(solution)/shard_map/ppermute | solution.py:28
  36.2 1.8 %collective-permute-start.18 = (bf16[128,2048]{1,0:T(8,128)(2,1)S(1)}, bf16[128,2048]{1,0:T(8,128)(2,1)S(1)}, u32[]{:S(2)}, u32[]{:S(2)}) collective-permute-start(bf16[128,2048]{1,0:T(8,128)(2,1)S(1)} %pair_sum.6.refs_0_), channel_id=1, source_target_pairs={{0,2},{1,3},{2,0},{3,1},{4,6},{5,7},{6,4},{7,5},{8,10},{9,11},{10,... | collective-permute-start | bytes 1572872 | tf_op jit(solution)/shard_map/ppermute | solution.py:28
  38.2 2.0 %project.5 = (bf16[3,256,256]{2,1,0:T(8,128)(2,1)}, bf16[1,512,256]{2,1,0:T(8,128)(2,1)S(1)}, bf16[1,256,256]{2,1,0:T(8,128)(2,1)S(1)}) custom-call(s32[3]{0:T(128)S(1)} %copy-done.13, bf16[3,64,2048]{2,1,0:T(8,128)(2,1)S(1)} %bitcast.16, bf16[3,64,2048]{2,1,0:T(8,128)(2,1)S(1)} %collective-permute-done.2.hidden_ref.y_ref, ...), custom_call_target="tpu_custom_call", output_to_operand_aliasing={{0}: (11, {})} | custom-call | flops 1 | bytes 1 | tf_op jit(solution)/shard_map/project/pallas_call | solution.py:143
  40.2 4.5 %attend.4 = (bf16[128,2048]{1,0:T(8,128)(2,1)S(1)}, bf16[64,2048]{1,0:T(8,128)(2,1)S(1)}, bf16[64,2048]{1,0:T(8,128)(2,1)S(1)}) custom-call(s32[3]{0:T(128)S(1)} %copy-done.17, s32[2,8]{1,0:T(2,128)S(1)} %copy-done.15, s32[2,8]{1,0:T(2,128)S(1)} %copy-done.16, bf16[1,512,256]{2,1,0:T(8,128)(2,1)S(1)} %get-tuple-element.94.q_ref, ...), custom_call_target="tpu_custom_call" | custom-call | flops 1 | bytes 1 | tf_op jit(solution)/shard_map/attend/pallas_call | solution.py:301
  44.7 0.6 collective-permute-start.15
  45.3 0.4 collective-permute-start.17
  45.8 0.7 collective-permute-done.15.refs_0_
  46.4 0.4 collective-permute-done.16.refs_1_
  46.9 0.3 collective-permute-start.22
  47.3 4.4 %attend.5 = (bf16[128,2048]{1,0:T(8,128)(2,1)S(1)}, bf16[64,2048]{1,0:T(8,128)(2,1)S(1)}, bf16[64,2048]{1,0:T(8,128)(2,1)S(1)}) custom-call(s32[3]{0:T(128)S(1)} %copy-done.17, s32[2,8]{1,0:T(2,128)S(1)} %copy-done.15, s32[2,8]{1,0:T(2,128)S(1)} %copy-done.16, bf16[1,512,256]{2,1,0:T(8,128)(2,1)S(1)} %get-tuple-element.99.q_ref, ...), custom_call_target="tpu_custom_call" | custom-call | flops 1 | bytes 1 | tf_op jit(solution)/shard_map/attend/pallas_call | solution.py:301
  51.8 0.5 collective-permute-start.20
  52.3 0.6 residual.3
  53.0 0.4 collective-permute-start.24
  53.8 1.8 %collective-permute-start.21 = (bf16[128,2048]{1,0:T(8,128)(2,1)S(1)}, bf16[128,2048]{1,0:T(8,128)(2,1)S(1)}, u32[]{:S(2)}, u32[]{:S(2)}) collective-permute-start(bf16[128,2048]{1,0:T(8,128)(2,1)S(1)} %pair_sum.8.refs_0_), channel_id=1, source_target_pairs={{0,2},{1,3},{2,0},{3,1},{4,6},{5,7},{6,4},{7,5},{8,10},{9,11},{10,... | collective-permute-start | bytes 1572872 | tf_op jit(solution)/shard_map/ppermute | solution.py:28
  55.7 1.2 %copy-done.3 = bf16[1024,2048]{1,0:T(8,128)(2,1)S(1)} copy-done((bf16[1024,2048]{1,0:T(8,128)(2,1)S(1)}, bf16[1024,2048]{1,0:T(8,128)(2,1)}, u32[]{:S(2)}) %copy-start.3) | copy-done | bytes 4194328
  56.9 3.4 %feed.3 = (bf16[128,2048]{1,0:T(8,128)(2,1)S(1)}, bf16[48,2048]{1,0:T(8,128)(2,1)S(1)}, bf16[48,2048]{1,0:T(8,128)(2,1)S(1)}, bf16[32,2048]{1,0:T(8,128)(2,1)S(1)}) custom-call(bf16[2048,1024]{1,0:T(8,128)(2,1)S(1)} %copy-done.1, bf16[2048,1024]{1,0:T(8,128)(2,1)S(1)} %copy-done.2, bf16[1024,2048]{1,0:T(8,128)(2,1)S(1)} %copy-done.3, ...), custom_call_target="tpu_custom_call" | custom-call | flops 1 | bytes 1 | tf_op jit(solution)/shard_map/feed/pallas_call | solution.py:391
  60.5 0.4 collective-permute-start.27
  61.0 1.3 %collective-permute-done.22.refs_1_ = bf16[128,2048]{1,0:T(8,128)(2,1)S(1)} collective-permute-done((bf16[128,2048]{1,0:T(8,128)(2,1)S(1)}, bf16[128,2048]{1,0:T(8,128)(2,1)S(1)}, u32[]{:S(2)}, u32[]{:S(2)}) %collective-permute-start.22) | collective-permute-done | bytes 524320 | tf_op jit(solution)/shard_map/ppermute | solution.py:28
  62.3 0.6 residual.4
  63.0 0.5 collective-permute-start.30
  63.7 1.8 %collective-permute-start.38 = (bf16[64,2048]{1,0:T(8,128)(2,1)S(1)}, bf16[64,2048]{1,0:T(8,128)(2,1)S(1)}, u32[]{:S(2)}, u32[]{:S(2)}) collective-permute-start(bf16[64,2048]{1,0:T(8,128)(2,1)S(1)} %get-tuple-element.135), channel_id=1, source_target_pairs={{0,2},{1,3},{2,0},{3,1},{4,6},{5,7},{6,4},{7,5},{8,10},{9,11},{10,... | collective-permute-start | bytes 786440 | tf_op jit(solution)/shard_map/ppermute | solution.py:28
  65.6 3.4 %feed.4 = (bf16[128,2048]{1,0:T(8,128)(2,1)S(1)}, bf16[48,2048]{1,0:T(8,128)(2,1)S(1)}, bf16[48,2048]{1,0:T(8,128)(2,1)S(1)}, bf16[32,2048]{1,0:T(8,128)(2,1)S(1)}) custom-call(bf16[2048,1024]{1,0:T(8,128)(2,1)S(1)} %copy-done.1, bf16[2048,1024]{1,0:T(8,128)(2,1)S(1)} %copy-done.2, bf16[1024,2048]{1,0:T(8,128)(2,1)S(1)} %copy-done.3, ...), custom_call_target="tpu_custom_call" | custom-call | flops 1 | bytes 1 | tf_op jit(solution)/shard_map/feed/pallas_call | solution.py:391
  69.0 0.2 collective-permute-start.32
  69.2 0.4 collective-permute-start.33
  69.6 0.2 collective-permute-start.34
  69.7 3.8 %collective-permute-done.21.refs_1_ = bf16[128,2048]{1,0:T(8,128)(2,1)S(1)} collective-permute-done((bf16[128,2048]{1,0:T(8,128)(2,1)S(1)}, bf16[128,2048]{1,0:T(8,128)(2,1)S(1)}, u32[]{:S(2)}, u32[]{:S(2)}) %collective-permute-start.21) | collective-permute-done | bytes 524320 | tf_op jit(solution)/shard_map/ppermute | solution.py:28
  73.5 0.6 residual.5
  74.2 0.5 collective-permute-start.36
  75.0 1.8 %collective-permute-start.43 = (bf16[64,2048]{1,0:T(8,128)(2,1)S(1)}, bf16[64,2048]{1,0:T(8,128)(2,1)S(1)}, u32[]{:S(2)}, u32[]{:S(2)}) collective-permute-start(bf16[64,2048]{1,0:T(8,128)(2,1)S(1)} %get-tuple-element.145), channel_id=1, source_target_pairs={{0,2},{1,3},{2,0},{3,1},{4,6},{5,7},{6,4},{7,5},{8,10},{9,11},{10,... | collective-permute-start | bytes 786440 | tf_op jit(solution)/shard_map/ppermute | solution.py:28
  76.8 3.7 %feed.5 = (bf16[128,2048]{1,0:T(8,128)(2,1)S(1)}, bf16[48,2048]{1,0:T(8,128)(2,1)S(1)}, bf16[48,2048]{1,0:T(8,128)(2,1)S(1)}, bf16[32,2048]{1,0:T(8,128)(2,1)S(1)}) custom-call(bf16[2048,1024]{1,0:T(8,128)(2,1)S(1)} %copy-done.1, bf16[2048,1024]{1,0:T(8,128)(2,1)S(1)} %copy-done.2, bf16[1024,2048]{1,0:T(8,128)(2,1)S(1)} %copy-done.3, ...), custom_call_target="tpu_custom_call" | custom-call | flops 1 | bytes 1 | tf_op jit(solution)/shard_map/feed/pallas_call | solution.py:391
  80.5 0.2 collective-permute-start.39
  80.7 0.4 collective-permute-start.40
  81.1 0.2 collective-permute-start.41
  81.2 1.4 %finish.3.refs_0_ = bf16[3,64,2048]{2,1,0:T(8,128)(2,1)} custom-call(s32[3]{0:T(128)S(1)} %copy-done.14, f32[64,2048]{1,0:T(8,128)S(1)} %get-tuple-element.134.res_ref, bf16[64,2048]{1,0:T(8,128)(2,1)S(1)} %get-tuple-element.117.near_ref, bf16[64,2048]{1,0:T(8,128)(2,1)S(1)} %collective-permute-done.38.far_ref, f32[5,2048]{1,0:T(8,128)S(1)} %stack.32.gains_ref), custom_call_target="tpu_custom_call" | custom-call | flops 99999997952 | bytes 1 | tf_op jit(solution)/shard_map/finish/pallas_call | solution.py:430
  82.8 1.2 %collective-permute-start.42 = (bf16[64,2048]{1,0:T(8,128)(2,1)S(1)}, bf16[64,2048]{1,0:T(8,128)(2,1)S(1)}, u32[]{:S(2)}, u32[]{:S(2)}) collective-permute-start(bf16[64,2048]{1,0:T(8,128)(2,1)S(1)} %get-tuple-element.142), channel_id=1, source_target_pairs={{0,2},{1,3},{2,0},{3,1},{4,6},{5,7},{6,4},{7,5},{8,10},{9,11},{10,... | collective-permute-start | bytes 786440 | tf_op jit(solution)/shard_map/ppermute | solution.py:28
  84.0 0.2 collective-permute-done.43.far_ref
  84.2 1.4 %finish.4.refs_0_ = bf16[3,64,2048]{2,1,0:T(8,128)(2,1)} custom-call(s32[3]{0:T(128)S(1)} %copy-done.14, f32[64,2048]{1,0:T(8,128)S(1)} %get-tuple-element.144.res_ref, bf16[64,2048]{1,0:T(8,128)(2,1)S(1)} %get-tuple-element.129.near_ref, bf16[64,2048]{1,0:T(8,128)(2,1)S(1)} %collective-permute-done.43.far_ref, ...), custom_call_target="tpu_custom_call", output_to_operand_aliasing={{}: (5, {})} | custom-call | flops 1 | bytes 1 | tf_op jit(solution)/shard_map/finish/pallas_call | solution.py:430
  85.7 5.8 %collective-permute-done.42.far_ref = bf16[64,2048]{1,0:T(8,128)(2,1)S(1)} collective-permute-done((bf16[64,2048]{1,0:T(8,128)(2,1)S(1)}, bf16[64,2048]{1,0:T(8,128)(2,1)S(1)}, u32[]{:S(2)}, u32[]{:S(2)}) %collective-permute-start.42) | collective-permute-done | bytes 262176 | tf_op jit(solution)/shard_map/ppermute | solution.py:28
  91.4 1.4 %finish.5 = bf16[3,64,2048]{2,1,0:T(8,128)(2,1)} custom-call(s32[3]{0:T(128)S(1)} %copy-done.14, f32[64,2048]{1,0:T(8,128)S(1)} %get-tuple-element.123.res_ref, bf16[64,2048]{1,0:T(8,128)(2,1)S(1)} %get-tuple-element.141.near_ref, bf16[64,2048]{1,0:T(8,128)(2,1)S(1)} %collective-permute-done.42.far_ref, ...), custom_call_target="tpu_custom_call", output_to_operand_aliasing={{}: (5, {})} | custom-call | flops 1 | bytes 1 | tf_op jit(solution)/shard_map/finish/pallas_call | solution.py:430
  (92 shorter events, 2.4 us)
Async XLA Ops:
  0.6 3.2 %copy-start = (bf16[2,128,1024]{2,1,0:T(8,128)(2,1)S(1)}, bf16[2,128,1024]{2,1,0:T(8,128)(2,1)}, u32[]{:S(2)}) copy-start(bf16[2,128,1024]{2,1,0:T(8,128)(2,1)} %param.37) | copy-start | bytes 1572868
  0.6 3.1 %collective-permute-start = (bf16[3,64,2048]{2,1,0:T(8,128)(2,1)}, bf16[3,64,2048]{2,1,0:T(8,128)(2,1)S(1)}, u32[]{:S(2)}, u32[]{:S(2)}) collective-permute-start(bf16[3,64,2048]{2,1,0:T(8,128)(2,1)} %bitcast.11), channel_id=1, source_target_pairs={{0,1},{1,0},{2,3},{3,2},{4,5},{5,4},{6,7},{7,6},{8,9},{9,8},{10,11... | collective-permute-start | bytes 2359304 | tf_op jit(solution)/shard_map/ppermute | solution.py:28
  1.2 20.9 %collective-permute-start.2 = (bf16[3,64,2048]{2,1,0:T(8,128)(2,1)}, bf16[3,64,2048]{2,1,0:T(8,128)(2,1)S(1)}, u32[]{:S(2)}, u32[]{:S(2)}) collective-permute-start(bf16[3,64,2048]{2,1,0:T(8,128)(2,1)} %bitcast.12), channel_id=1, source_target_pairs={{0,2},{1,3},{2,0},{3,1},{4,6},{5,7},{6,4},{7,5},{8,10},{9,11},{10,... | collective-permute-start | bytes 2359304 | tf_op jit(solution)/shard_map/ppermute | solution.py:28
  3.8 7.3 %collective-permute-start.1 = (bf16[1,128,512]{2,1,0:T(8,128)(2,1)S(1)}, bf16[1,128,512]{2,1,0:T(8,128)(2,1)S(1)}, u32[]{:S(2)}, u32[]{:S(2)}) collective-permute-start(bf16[1,128,512]{2,1,0:T(8,128)(2,1)S(1)} %constant_dynamic-slice_fusion), channel_id=1, source_target_pairs={{0,8},{4,12},{8,0},{12,4},{16,24},{20,28},{24,16},{28,20},{1,9},{5... | collective-permute-start | bytes 393224 | tf_op jit(solution)/shard_map/ppermute | solution.py:28
  6.8 15.3 %copy-start.10 = (bf16[2048,64]{0,1:T(8,128)(2,1)S(1)}, bf16[2048,64]{0,1:T(8,128)(2,1)}, u32[]{:S(2)}) copy-start(bf16[2048,64]{0,1:T(8,128)(2,1)} %param.29) | copy-start | bytes 786436
  6.9 15.2 %copy-start.12 = (bf16[64,2048]{1,0:T(8,128)(2,1)S(1)}, bf16[64,2048]{1,0:T(8,128)(2,1)}, u32[]{:S(2)}) copy-start(bf16[64,2048]{1,0:T(8,128)(2,1)} %right_ref.3) | copy-start | bytes 786436
  6.9 12.5 %collective-permute-start.3 = (bf16[1,128,512]{2,1,0:T(8,128)(2,1)S(1)}, bf16[1,128,512]{2,1,0:T(8,128)(2,1)S(1)}, u32[]{:S(2)}, u32[]{:S(2)}) collective-permute-start(bf16[1,128,512]{2,1,0:T(8,128)(2,1)S(1)} %constant_dynamic-slice_fusion), channel_id=1, source_target_pairs={{0,16},{4,20},{8,24},{12,28},{16,0},{20,4},{24,8},{28,12},{1,17},{... | collective-permute-start | bytes 393224 | tf_op jit(solution)/shard_map/ppermute | solution.py:28
  11.1 8.3 %collective-permute-start.4 = (bf16[1,128,512]{2,1,0:T(8,128)(2,1)S(1)}, bf16[1,128,512]{2,1,0:T(8,128)(2,1)S(1)}, u32[]{:S(2)}, u32[]{:S(2)}) collective-permute-start(bf16[1,128,512]{2,1,0:T(8,128)(2,1)S(1)} %constant_dynamic-slice_fusion), channel_id=1, source_target_pairs={{0,24},{4,28},{8,16},{12,20},{16,8},{20,12},{24,0},{28,4},{1,25},{... | collective-permute-start | bytes 393224 | tf_op jit(solution)/shard_map/ppermute | solution.py:28
  11.2 15.8 %collective-permute-start.7 = (bf16[2,128,512]{2,1,0:T(8,128)(2,1)S(1)}, bf16[2,128,512]{2,1,0:T(8,128)(2,1)S(1)}, u32[]{:S(2)}, u32[]{:S(2)}) collective-permute-start(bf16[2,128,512]{2,1,0:T(8,128)(2,1)S(1)} %pad_maximum_fusion.refs_0_), channel_id=1, source_target_pairs={{0,4},{4,0},{8,12},{12,8},{16,20},{20,16},{24,28},{28,24},{1,5},{5... | collective-permute-start | bytes 786440 | tf_op jit(solution)/shard_map/ppermute | solution.py:28
  12.9 1.1 %copy-start.6 = (bf16[64,3,2048]{2,0,1:T(8,128)(2,1)S(1)}, bf16[64,3,2048]{2,0,1:T(8,128)(2,1)}, u32[]{:S(2)}) copy-start(bf16[64,3,2048]{2,0,1:T(8,128)(2,1)} %param.21) | copy-start | bytes 2359300
  14.1 0.9 %copy-start.9 = (bf16[2048,64]{0,1:T(8,128)(2,1)S(1)}, bf16[2048,64]{0,1:T(8,128)(2,1)}, u32[]{:S(2)}) copy-start(bf16[2048,64]{0,1:T(8,128)(2,1)} %param.29) | copy-start | bytes 786436
  15.0 0.9 %copy-start.11 = (bf16[64,2048]{1,0:T(8,128)(2,1)S(1)}, bf16[64,2048]{1,0:T(8,128)(2,1)}, u32[]{:S(2)}) copy-start(bf16[64,2048]{1,0:T(8,128)(2,1)} %right_ref.3) | copy-start | bytes 786436
  19.4 5.0 %copy-start.5 = (bf16[2048,512]{1,0:T(8,128)(2,1)S(1)}, bf16[2048,512]{1,0:T(8,128)(2,1)}, u32[]{:S(2)}) copy-start(bf16[2048,512]{1,0:T(8,128)(2,1)} %wq_ref.5) | copy-start | bytes 6291460
  19.4 5.0 %copy-start.7 = (bf16[64,3,2048]{2,0,1:T(8,128)(2,1)S(1)}, bf16[64,3,2048]{2,0,1:T(8,128)(2,1)}, u32[]{:S(2)}) copy-start(bf16[64,3,2048]{2,0,1:T(8,128)(2,1)} %param.21) | copy-start | bytes 2359300
  19.4 5.0 %copy-start.8 = (bf16[2048,256]{1,0:T(8,128)(2,1)S(1)}, bf16[2048,256]{1,0:T(8,128)(2,1)}, u32[]{:S(2)}) copy-start(bf16[2048,256]{1,0:T(8,128)(2,1)} %wkv_ref.5) | copy-start | bytes 3145732
  19.4 5.0 %copy-start.13 = (s32[3]{0:T(128)S(1)}, s32[3]{0:T(128)}, u32[]{:S(2)}) copy-start(s32[3]{0:T(128)} %len_ref.11) | copy-start | bytes 40
  19.5 7.5 %collective-permute-start.8 = (bf16[2,128,512]{2,1,0:T(8,128)(2,1)S(1)}, bf16[2,128,512]{2,1,0:T(8,128)(2,1)S(1)}, u32[]{:S(2)}, u32[]{:S(2)}) collective-permute-start(bf16[2,128,512]{2,1,0:T(8,128)(2,1)S(1)} %constant_dynamic-update-slice_fusion.refs_1_), channel_id=1, source_target_pairs={{0,4},{4,0},{8,12},{12,8},{16,20},{20,16},{24,28},{28,24},{1,5},{5... | collective-permute-start | bytes 786440 | tf_op jit(solution)/shard_map/ppermute | solution.py:28
  22.1 2.3 %collective-permute-start.5 = (bf16[3,64,2048]{2,1,0:T(8,128)(2,1)S(1)}, bf16[3,64,2048]{2,1,0:T(8,128)(2,1)S(1)}, u32[]{:S(2)}, u32[]{:S(2)}) collective-permute-start(bf16[3,64,2048]{2,1,0:T(8,128)(2,1)S(1)} %collective-permute-done.2.hidden_ref.y_ref), channel_id=1, source_target_pairs={{0,1},{1,0},{2,3},{3,2},{4,5},{5,4},{6,7},{7,6},{8,9},{9,8},{10,11... | collective-permute-start | bytes 2359304 | tf_op jit(solution)/shard_map/ppermute | solution.py:28
  23.5 6.2 %collective-permute-start.9 = (bf16[2,128,512]{2,1,0:T(8,128)(2,1)S(1)}, bf16[2,128,512]{2,1,0:T(8,128)(2,1)S(1)}, u32[]{:S(2)}, u32[]{:S(2)}) collective-permute-start(bf16[2,128,512]{2,1,0:T(8,128)(2,1)S(1)} %pad_maximum_fusion.refs_0_), channel_id=1, source_target_pairs={{0,1},{1,0},{2,3},{3,2},{4,5},{5,4},{6,7},{7,6},{8,9},{9,8},{10,11... | collective-permute-start | bytes 786440 | tf_op jit(solution)/shard_map/ppermute | solution.py:28
  24.1 5.7 %collective-permute-start.10 = (bf16[2,128,512]{2,1,0:T(8,128)(2,1)S(1)}, bf16[2,128,512]{2,1,0:T(8,128)(2,1)S(1)}, u32[]{:S(2)}, u32[]{:S(2)}) collective-permute-start(bf16[2,128,512]{2,1,0:T(8,128)(2,1)S(1)} %constant_dynamic-update-slice_fusion.refs_1_), channel_id=1, source_target_pairs={{0,1},{1,0},{2,3},{3,2},{4,5},{5,4},{6,7},{7,6},{8,9},{9,8},{10,11... | collective-permute-start | bytes 786440 | tf_op jit(solution)/shard_map/ppermute | solution.py:28
  27.0 2.8 %collective-permute-start.11 = (bf16[2,128,512]{2,1,0:T(8,128)(2,1)S(1)}, bf16[2,128,512]{2,1,0:T(8,128)(2,1)S(1)}, u32[]{:S(2)}, u32[]{:S(2)}) collective-permute-start(bf16[2,128,512]{2,1,0:T(8,128)(2,1)S(1)} %collective-permute-done.7.refs_2_), channel_id=1, source_target_pairs={{0,1},{1,0},{2,3},{3,2},{4,5},{5,4},{6,7},{7,6},{8,9},{9,8},{10,11... | collective-permute-start | bytes 786440 | tf_op jit(solution)/shard_map/ppermute | solution.py:28
  27.1 2.6 %collective-permute-start.12 = (bf16[2,128,512]{2,1,0:T(8,128)(2,1)S(1)}, bf16[2,128,512]{2,1,0:T(8,128)(2,1)S(1)}, u32[]{:S(2)}, u32[]{:S(2)}) collective-permute-start(bf16[2,128,512]{2,1,0:T(8,128)(2,1)S(1)} %collective-permute-done.8.refs_3_), channel_id=1, source_target_pairs={{0,1},{1,0},{2,3},{3,2},{4,5},{5,4},{6,7},{7,6},{8,9},{9,8},{10,11... | collective-permute-start | bytes 786440 | tf_op jit(solution)/shard_map/ppermute | solution.py:28
  27.5 2.3 %collective-permute-start.6 = (bf16[1,256,256]{2,1,0:T(8,128)(2,1)S(1)}, bf16[1,256,256]{2,1,0:T(8,128)(2,1)S(1)}, u32[]{:S(2)}, u32[]{:S(2)}) collective-permute-start(bf16[1,256,256]{2,1,0:T(8,128)(2,1)S(1)} %get-tuple-element.86.mine_ref), channel_id=1, source_target_pairs={{0,1},{1,0},{2,3},{3,2},{4,5},{5,4},{6,7},{7,6},{8,9},{9,8},{10,11... | collective-permute-start | bytes 393224 | tf_op jit(solution)/shard_map/ppermute | solution.py:28
  27.6 2.1 %copy-start.4 = (bf16[512,2048]{1,0:T(8,128)(2,1)S(1)}, bf16[512,2048]{1,0:T(8,128)(2,1)}, u32[]{:S(2)}) copy-start(bf16[512,2048]{1,0:T(8,128)(2,1)} %wo_ref.5) | copy-start | bytes 6291460
  27.7 2.1 %copy-start.15 = (s32[2,8]{1,0:T(2,128)S(1)}, s32[2,8]{1,0:T(2,128)}, u32[]{:S(2)}) copy-start(s32[2,8]{1,0:T(2,128)} %owner_ref.5) | copy-start | bytes 196
  27.7 2.1 %copy-start.16 = (s32[2,8]{1,0:T(2,128)S(1)}, s32[2,8]{1,0:T(2,128)}, u32[]{:S(2)}) copy-start(s32[2,8]{1,0:T(2,128)} %slot_ref.5) | copy-start | bytes 196
  27.7 2.1 %copy-start.17 = (s32[3]{0:T(128)S(1)}, s32[3]{0:T(128)}, u32[]{:S(2)}) copy-start(s32[3]{0:T(128)} %group_ref.5) | copy-start | bytes 40
  34.1 2.0 %collective-permute-start.13 = (bf16[128,2048]{1,0:T(8,128)(2,1)S(1)}, bf16[128,2048]{1,0:T(8,128)(2,1)S(1)}, u32[]{:S(2)}, u32[]{:S(2)}) collective-permute-start(bf16[128,2048]{1,0:T(8,128)(2,1)S(1)} %get-tuple-element.90), channel_id=1, source_target_pairs={{0,1},{1,0},{2,3},{3,2},{4,5},{5,4},{6,7},{7,6},{8,9},{9,8},{10,11... | collective-permute-start | bytes 1572872 | tf_op jit(solution)/shard_map/ppermute | solution.py:28
  36.2 16.0 %collective-permute-start.18 = (bf16[128,2048]{1,0:T(8,128)(2,1)S(1)}, bf16[128,2048]{1,0:T(8,128)(2,1)S(1)}, u32[]{:S(2)}, u32[]{:S(2)}) collective-permute-start(bf16[128,2048]{1,0:T(8,128)(2,1)S(1)} %pair_sum.6.refs_0_), channel_id=1, source_target_pairs={{0,2},{1,3},{2,0},{3,1},{4,6},{5,7},{6,4},{7,5},{8,10},{9,11},{10,... | collective-permute-start | bytes 1572872 | tf_op jit(solution)/shard_map/ppermute | solution.py:28
  38.1 2.1 %collective-permute-start.14 = (bf16[1,256,256]{2,1,0:T(8,128)(2,1)S(1)}, bf16[1,256,256]{2,1,0:T(8,128)(2,1)S(1)}, u32[]{:S(2)}, u32[]{:S(2)}) collective-permute-start(bf16[1,256,256]{2,1,0:T(8,128)(2,1)S(1)} %get-tuple-element.95.mine_ref), channel_id=1, source_target_pairs={{0,1},{1,0},{2,3},{3,2},{4,5},{5,4},{6,7},{7,6},{8,9},{9,8},{10,11... | collective-permute-start | bytes 393224 | tf_op jit(solution)/shard_map/ppermute | solution.py:28
  44.7 1.7 %collective-permute-start.15 = (bf16[64,2048]{1,0:T(8,128)(2,1)S(1)}, bf16[64,2048]{1,0:T(8,128)(2,1)S(1)}, u32[]{:S(2)}, u32[]{:S(2)}) collective-permute-start(bf16[64,2048]{1,0:T(8,128)(2,1)S(1)} %get-tuple-element.97), channel_id=1, source_target_pairs={{0,1},{1,0},{2,3},{3,2},{4,5},{5,4},{6,7},{7,6},{8,9},{9,8},{10,11... | collective-permute-start | bytes 786440 | tf_op jit(solution)/shard_map/ppermute | solution.py:28
  45.3 1.5 %collective-permute-start.16 = (bf16[64,2048]{1,0:T(8,128)(2,1)S(1)}, bf16[64,2048]{1,0:T(8,128)(2,1)S(1)}, u32[]{:S(2)}, u32[]{:S(2)}) collective-permute-start(bf16[64,2048]{1,0:T(8,128)(2,1)S(1)} %get-tuple-element.98), channel_id=1, source_target_pairs={{0,1},{1,0},{2,3},{3,2},{4,5},{5,4},{6,7},{7,6},{8,9},{9,8},{10,11... | collective-permute-start | bytes 786440 | tf_op jit(solution)/shard_map/ppermute | solution.py:28
  45.3 1.9 %collective-permute-start.17 = (bf16[1,256,256]{2,1,0:T(8,128)(2,1)S(1)}, bf16[1,256,256]{2,1,0:T(8,128)(2,1)S(1)}, u32[]{:S(2)}, u32[]{:S(2)}) collective-permute-start(bf16[1,256,256]{2,1,0:T(8,128)(2,1)S(1)} %get-tuple-element.100.mine_ref), channel_id=1, source_target_pairs={{0,1},{1,0},{2,3},{3,2},{4,5},{5,4},{6,7},{7,6},{8,9},{9,8},{10,11... | collective-permute-start | bytes 393224 | tf_op jit(solution)/shard_map/ppermute | solution.py:28
  46.9 15.4 %collective-permute-start.22 = (bf16[128,2048]{1,0:T(8,128)(2,1)S(1)}, bf16[128,2048]{1,0:T(8,128)(2,1)S(1)}, u32[]{:S(2)}, u32[]{:S(2)}) collective-permute-start(bf16[128,2048]{1,0:T(8,128)(2,1)S(1)} %pair_sum.7.refs_0_), channel_id=1, source_target_pairs={{0,2},{1,3},{2,0},{3,1},{4,6},{5,7},{6,4},{7,5},{8,10},{9,11},{10,... | collective-permute-start | bytes 1572872 | tf_op jit(solution)/shard_map/ppermute | solution.py:28
  51.7 1.8 %collective-permute-start.19 = (bf16[64,2048]{1,0:T(8,128)(2,1)S(1)}, bf16[64,2048]{1,0:T(8,128)(2,1)S(1)}, u32[]{:S(2)}, u32[]{:S(2)}) collective-permute-start(bf16[64,2048]{1,0:T(8,128)(2,1)S(1)} %get-tuple-element.105), channel_id=1, source_target_pairs={{0,1},{1,0},{2,3},{3,2},{4,5},{5,4},{6,7},{7,6},{8,9},{9,8},{10,11... | collective-permute-start | bytes 786440 | tf_op jit(solution)/shard_map/ppermute | solution.py:28
  51.8 1.9 %collective-permute-start.20 = (bf16[64,2048]{1,0:T(8,128)(2,1)S(1)}, bf16[64,2048]{1,0:T(8,128)(2,1)S(1)}, u32[]{:S(2)}, u32[]{:S(2)}) collective-permute-start(bf16[64,2048]{1,0:T(8,128)(2,1)S(1)} %get-tuple-element.106), channel_id=1, source_target_pairs={{0,1},{1,0},{2,3},{3,2},{4,5},{5,4},{6,7},{7,6},{8,9},{9,8},{10,11... | collective-permute-start | bytes 786440 | tf_op jit(solution)/shard_map/ppermute | solution.py:28
  52.3 3.4 %copy-start.1 = (bf16[2048,1024]{1,0:T(8,128)(2,1)S(1)}, bf16[2048,1024]{1,0:T(8,128)(2,1)}, u32[]{:S(2)}) copy-start(bf16[2048,1024]{1,0:T(8,128)(2,1)} %gate_ref.5) | copy-start | bytes 12582916
  52.3 3.5 %copy-start.2 = (bf16[2048,1024]{1,0:T(8,128)(2,1)S(1)}, bf16[2048,1024]{1,0:T(8,128)(2,1)}, u32[]{:S(2)}) copy-start(bf16[2048,1024]{1,0:T(8,128)(2,1)} %up_ref.5) | copy-start | bytes 12582916
  52.3 4.7 %copy-start.3 = (bf16[1024,2048]{1,0:T(8,128)(2,1)S(1)}, bf16[1024,2048]{1,0:T(8,128)(2,1)}, u32[]{:S(2)}) copy-start(bf16[1024,2048]{1,0:T(8,128)(2,1)} %down_ref.5) | copy-start | bytes 12582916
  52.9 2.7 %collective-permute-start.23 = (bf16[48,2048]{1,0:T(8,128)(2,1)S(1)}, bf16[48,2048]{1,0:T(8,128)(2,1)S(1)}, u32[]{:S(2)}, u32[]{:S(2)}) collective-permute-start(bf16[48,2048]{1,0:T(8,128)(2,1)S(1)} %get-tuple-element.107.refs_0_), channel_id=1, source_target_pairs={{0,1},{1,0},{2,3},{3,2},{4,5},{5,4},{6,7},{7,6},{8,9},{9,8},{10,11... | collective-permute-start | bytes 589832 | tf_op jit(solution)/shard_map/ppermute | solution.py:28
  53.0 2.6 %collective-permute-start.24 = (bf16[48,2048]{1,0:T(8,128)(2,1)S(1)}, bf16[48,2048]{1,0:T(8,128)(2,1)S(1)}, u32[]{:S(2)}, u32[]{:S(2)}) collective-permute-start(bf16[48,2048]{1,0:T(8,128)(2,1)S(1)} %get-tuple-element.108.refs_1_), channel_id=1, source_target_pairs={{0,1},{1,0},{2,3},{3,2},{4,5},{5,4},{6,7},{7,6},{8,9},{9,8},{10,11... | collective-permute-start | bytes 589832 | tf_op jit(solution)/shard_map/ppermute | solution.py:28
  53.5 2.1 %collective-permute-start.25 = (bf16[32,2048]{1,0:T(8,128)(2,1)S(1)}, bf16[32,2048]{1,0:T(8,128)(2,1)S(1)}, u32[]{:S(2)}, u32[]{:S(2)}) collective-permute-start(bf16[32,2048]{1,0:T(8,128)(2,1)S(1)} %get-tuple-element.109.refs_2_), channel_id=1, source_target_pairs={{0,1},{1,0},{2,3},{3,2},{4,5},{5,4},{6,7},{7,6},{8,9},{9,8},{10,11... | collective-permute-start | bytes 393224 | tf_op jit(solution)/shard_map/ppermute | solution.py:28
  53.8 19.8 %collective-permute-start.21 = (bf16[128,2048]{1,0:T(8,128)(2,1)S(1)}, bf16[128,2048]{1,0:T(8,128)(2,1)S(1)}, u32[]{:S(2)}, u32[]{:S(2)}) collective-permute-start(bf16[128,2048]{1,0:T(8,128)(2,1)S(1)} %pair_sum.8.refs_0_), channel_id=1, source_target_pairs={{0,2},{1,3},{2,0},{3,1},{4,6},{5,7},{6,4},{7,5},{8,10},{9,11},{10,... | collective-permute-start | bytes 1572872 | tf_op jit(solution)/shard_map/ppermute | solution.py:28
  60.3 3.2 %collective-permute-start.26 = (bf16[48,2048]{1,0:T(8,128)(2,1)S(1)}, bf16[48,2048]{1,0:T(8,128)(2,1)S(1)}, u32[]{:S(2)}, u32[]{:S(2)}) collective-permute-start(bf16[48,2048]{1,0:T(8,128)(2,1)S(1)} %get-tuple-element.114), channel_id=1, source_target_pairs={{0,1},{1,0},{2,3},{3,2},{4,5},{5,4},{6,7},{7,6},{8,9},{9,8},{10,11... | collective-permute-start | bytes 589832 | tf_op jit(solution)/shard_map/ppermute | solution.py:28
  60.5 3.1 %collective-permute-start.27 = (bf16[48,2048]{1,0:T(8,128)(2,1)S(1)}, bf16[48,2048]{1,0:T(8,128)(2,1)S(1)}, u32[]{:S(2)}, u32[]{:S(2)}) collective-permute-start(bf16[48,2048]{1,0:T(8,128)(2,1)S(1)} %get-tuple-element.115), channel_id=1, source_target_pairs={{0,1},{1,0},{2,3},{3,2},{4,5},{5,4},{6,7},{7,6},{8,9},{9,8},{10,11... | collective-permute-start | bytes 589832 | tf_op jit(solution)/shard_map/ppermute | solution.py:28
  60.9 2.1 %collective-permute-start.28 = (bf16[32,2048]{1,0:T(8,128)(2,1)S(1)}, bf16[32,2048]{1,0:T(8,128)(2,1)S(1)}, u32[]{:S(2)}, u32[]{:S(2)}) collective-permute-start(bf16[32,2048]{1,0:T(8,128)(2,1)S(1)} %get-tuple-element.116), channel_id=1, source_target_pairs={{0,1},{1,0},{2,3},{3,2},{4,5},{5,4},{6,7},{7,6},{8,9},{9,8},{10,11... | collective-permute-start | bytes 393224 | tf_op jit(solution)/shard_map/ppermute | solution.py:28
  62.9 2.6 %collective-permute-start.29 = (bf16[48,2048]{1,0:T(8,128)(2,1)S(1)}, bf16[48,2048]{1,0:T(8,128)(2,1)S(1)}, u32[]{:S(2)}, u32[]{:S(2)}) collective-permute-start(bf16[48,2048]{1,0:T(8,128)(2,1)S(1)} %get-tuple-element.118.refs_0_), channel_id=1, source_target_pairs={{0,1},{1,0},{2,3},{3,2},{4,5},{5,4},{6,7},{7,6},{8,9},{9,8},{10,11... | collective-permute-start | bytes 589832 | tf_op jit(solution)/shard_map/ppermute | solution.py:28
  63.0 2.5 %collective-permute-start.30 = (bf16[48,2048]{1,0:T(8,128)(2,1)S(1)}, bf16[48,2048]{1,0:T(8,128)(2,1)S(1)}, u32[]{:S(2)}, u32[]{:S(2)}) collective-permute-start(bf16[48,2048]{1,0:T(8,128)(2,1)S(1)} %get-tuple-element.119.refs_1_), channel_id=1, source_target_pairs={{0,1},{1,0},{2,3},{3,2},{4,5},{5,4},{6,7},{7,6},{8,9},{9,8},{10,11... | collective-permute-start | bytes 589832 | tf_op jit(solution)/shard_map/ppermute | solution.py:28
  63.5 2.0 %collective-permute-start.31 = (bf16[32,2048]{1,0:T(8,128)(2,1)S(1)}, bf16[32,2048]{1,0:T(8,128)(2,1)S(1)}, u32[]{:S(2)}, u32[]{:S(2)}) collective-permute-start(bf16[32,2048]{1,0:T(8,128)(2,1)S(1)} %get-tuple-element.120.refs_2_), channel_id=1, source_target_pairs={{0,1},{1,0},{2,3},{3,2},{4,5},{5,4},{6,7},{7,6},{8,9},{9,8},{10,11... | collective-permute-start | bytes 393224 | tf_op jit(solution)/shard_map/ppermute | solution.py:28
  63.7 16.8 %collective-permute-start.38 = (bf16[64,2048]{1,0:T(8,128)(2,1)S(1)}, bf16[64,2048]{1,0:T(8,128)(2,1)S(1)}, u32[]{:S(2)}, u32[]{:S(2)}) collective-permute-start(bf16[64,2048]{1,0:T(8,128)(2,1)S(1)} %get-tuple-element.135), channel_id=1, source_target_pairs={{0,2},{1,3},{2,0},{3,1},{4,6},{5,7},{6,4},{7,5},{8,10},{9,11},{10,... | collective-permute-start | bytes 786440 | tf_op jit(solution)/shard_map/ppermute | solution.py:28
  69.0 5.7 %collective-permute-start.32 = (bf16[48,2048]{1,0:T(8,128)(2,1)S(1)}, bf16[48,2048]{1,0:T(8,128)(2,1)S(1)}, u32[]{:S(2)}, u32[]{:S(2)}) collective-permute-start(bf16[48,2048]{1,0:T(8,128)(2,1)S(1)} %get-tuple-element.126), channel_id=1, source_target_pairs={{0,1},{1,0},{2,3},{3,2},{4,5},{5,4},{6,7},{7,6},{8,9},{9,8},{10,11... | collective-permute-start | bytes 589832 | tf_op jit(solution)/shard_map/ppermute | solution.py:28
  69.2 5.6 %collective-permute-start.33 = (bf16[48,2048]{1,0:T(8,128)(2,1)S(1)}, bf16[48,2048]{1,0:T(8,128)(2,1)S(1)}, u32[]{:S(2)}, u32[]{:S(2)}) collective-permute-start(bf16[48,2048]{1,0:T(8,128)(2,1)S(1)} %get-tuple-element.127), channel_id=1, source_target_pairs={{0,1},{1,0},{2,3},{3,2},{4,5},{5,4},{6,7},{7,6},{8,9},{9,8},{10,11... | collective-permute-start | bytes 589832 | tf_op jit(solution)/shard_map/ppermute | solution.py:28
  69.6 4.7 %collective-permute-start.34 = (bf16[32,2048]{1,0:T(8,128)(2,1)S(1)}, bf16[32,2048]{1,0:T(8,128)(2,1)S(1)}, u32[]{:S(2)}, u32[]{:S(2)}) collective-permute-start(bf16[32,2048]{1,0:T(8,128)(2,1)S(1)} %get-tuple-element.128), channel_id=1, source_target_pairs={{0,1},{1,0},{2,3},{3,2},{4,5},{5,4},{6,7},{7,6},{8,9},{9,8},{10,11... | collective-permute-start | bytes 393224 | tf_op jit(solution)/shard_map/ppermute | solution.py:28
  74.2 2.6 %collective-permute-start.35 = (bf16[48,2048]{1,0:T(8,128)(2,1)S(1)}, bf16[48,2048]{1,0:T(8,128)(2,1)S(1)}, u32[]{:S(2)}, u32[]{:S(2)}) collective-permute-start(bf16[48,2048]{1,0:T(8,128)(2,1)S(1)} %get-tuple-element.130.refs_0_), channel_id=1, source_target_pairs={{0,1},{1,0},{2,3},{3,2},{4,5},{5,4},{6,7},{7,6},{8,9},{9,8},{10,11... | collective-permute-start | bytes 589832 | tf_op jit(solution)/shard_map/ppermute | solution.py:28
  74.2 2.6 %collective-permute-start.36 = (bf16[48,2048]{1,0:T(8,128)(2,1)S(1)}, bf16[48,2048]{1,0:T(8,128)(2,1)S(1)}, u32[]{:S(2)}, u32[]{:S(2)}) collective-permute-start(bf16[48,2048]{1,0:T(8,128)(2,1)S(1)} %get-tuple-element.131.refs_1_), channel_id=1, source_target_pairs={{0,1},{1,0},{2,3},{3,2},{4,5},{5,4},{6,7},{7,6},{8,9},{9,8},{10,11... | collective-permute-start | bytes 589832 | tf_op jit(solution)/shard_map/ppermute | solution.py:28
  74.7 2.1 %collective-permute-start.37 = (bf16[32,2048]{1,0:T(8,128)(2,1)S(1)}, bf16[32,2048]{1,0:T(8,128)(2,1)S(1)}, u32[]{:S(2)}, u32[]{:S(2)}) collective-permute-start(bf16[32,2048]{1,0:T(8,128)(2,1)S(1)} %get-tuple-element.132.refs_2_), channel_id=1, source_target_pairs={{0,1},{1,0},{2,3},{3,2},{4,5},{5,4},{6,7},{7,6},{8,9},{9,8},{10,11... | collective-permute-start | bytes 393224 | tf_op jit(solution)/shard_map/ppermute | solution.py:28
  75.0 6.3 %copy-start.14 = (s32[3]{0:T(128)S(1)}, s32[3]{0:T(128)}, u32[]{:S(2)}) copy-start(s32[3]{0:T(128)} %len_ref.11) | copy-start | bytes 40
  75.0 9.3 %collective-permute-start.43 = (bf16[64,2048]{1,0:T(8,128)(2,1)S(1)}, bf16[64,2048]{1,0:T(8,128)(2,1)S(1)}, u32[]{:S(2)}, u32[]{:S(2)}) collective-permute-start(bf16[64,2048]{1,0:T(8,128)(2,1)S(1)} %get-tuple-element.145), channel_id=1, source_target_pairs={{0,2},{1,3},{2,0},{3,1},{4,6},{5,7},{6,4},{7,5},{8,10},{9,11},{10,... | collective-permute-start | bytes 786440 | tf_op jit(solution)/shard_map/ppermute | solution.py:28
  80.5 2.2 %collective-permute-start.39 = (bf16[48,2048]{1,0:T(8,128)(2,1)S(1)}, bf16[48,2048]{1,0:T(8,128)(2,1)S(1)}, u32[]{:S(2)}, u32[]{:S(2)}) collective-permute-start(bf16[48,2048]{1,0:T(8,128)(2,1)S(1)} %get-tuple-element.138), channel_id=1, source_target_pairs={{0,1},{1,0},{2,3},{3,2},{4,5},{5,4},{6,7},{7,6},{8,9},{9,8},{10,11... | collective-permute-start | bytes 589832 | tf_op jit(solution)/shard_map/ppermute | solution.py:28
  80.7 2.0 %collective-permute-start.40 = (bf16[48,2048]{1,0:T(8,128)(2,1)S(1)}, bf16[48,2048]{1,0:T(8,128)(2,1)S(1)}, u32[]{:S(2)}, u32[]{:S(2)}) collective-permute-start(bf16[48,2048]{1,0:T(8,128)(2,1)S(1)} %get-tuple-element.139), channel_id=1, source_target_pairs={{0,1},{1,0},{2,3},{3,2},{4,5},{5,4},{6,7},{7,6},{8,9},{9,8},{10,11... | collective-permute-start | bytes 589832 | tf_op jit(solution)/shard_map/ppermute | solution.py:28
  81.1 1.6 %collective-permute-start.41 = (bf16[32,2048]{1,0:T(8,128)(2,1)S(1)}, bf16[32,2048]{1,0:T(8,128)(2,1)S(1)}, u32[]{:S(2)}, u32[]{:S(2)}) collective-permute-start(bf16[32,2048]{1,0:T(8,128)(2,1)S(1)} %get-tuple-element.140), channel_id=1, source_target_pairs={{0,1},{1,0},{2,3},{3,2},{4,5},{5,4},{6,7},{7,6},{8,9},{9,8},{10,11... | collective-permute-start | bytes 393224 | tf_op jit(solution)/shard_map/ppermute | solution.py:28
  82.8 8.6 %collective-permute-start.42 = (bf16[64,2048]{1,0:T(8,128)(2,1)S(1)}, bf16[64,2048]{1,0:T(8,128)(2,1)S(1)}, u32[]{:S(2)}, u32[]{:S(2)}) collective-permute-start(bf16[64,2048]{1,0:T(8,128)(2,1)S(1)} %get-tuple-element.142), channel_id=1, source_target_pairs={{0,2},{1,3},{2,0},{3,1},{4,6},{5,7},{6,4},{7,5},{8,10},{9,11},{10,... | collective-permute-start | bytes 786440 | tf_op jit(solution)/shard_map/ppermute | solution.py:28
